TPU v7x, 32 devices: a whole 2x2x4 slice. The times are simulated.
32 devices in a mesh: section: 2 (over core), dp: 16 (over z, y, x).
Axes of the slice: x: 2, y: 2, z: 4, core: 2. Of those that a mesh axis runs over, the one named last changes fastest.
Arguments:
- tokens: bfloat16 [32, 512, 768], P('dp'), may hold values from -6 to 6
- segment_ids: int32 [32, 512], P('dp'), may hold values from 0 to 7, never falling along the last dimension, each value on 1 to 128 neighbouring positions
- cotangent: bfloat16 [32, 512, 128], P('dp'), may hold values from -48 to 48
- qkv_weight: float32 [2, 768, 2304], P('section', 'dp'), may hold values from -0.21875 to 0.21875
- out_weight: float32 [2, 768, 768], P('section', 'dp'), may hold values from -1.75 to 1.75
- up_weight: float32 [2, 768, 3072], P('section', 'dp'), may hold values from -0.21875 to 0.21875
- down_weight: float32 [2, 3072, 768], P('section', 'dp'), may hold values from -0.109375 to 0.109375
- ln_gains: float32 [2, 2, 768], P('section', None, 'dp'), may hold values from 0.5 to 1.5
- shifts: float32 [2, 6, 768], P('section', None, 'dp'), may hold values from -1.8 to 1.8
- up_bias: float32 [2, 3072], P('section', 'dp'), may hold values from -1.8 to 1.8
- head_weight: float32 [768, 128], P(('section', 'dp')), may hold values from -0.21875 to 0.21875
Outputs:
- qkv_grad: float32 [2, 768, 2304], P('section', 'dp')
- out_grad: float32 [2, 768, 768], P('section', 'dp')
- up_grad: float32 [2, 768, 3072], P('section', 'dp')
- down_grad: float32 [2, 3072, 768], P('section', 'dp')
- gain_grad: float32 [2, 2, 768], P('section', None, 'dp')
- shift_grad: float32 [2, 6, 768], P('section', None, 'dp')
- up_bias_grad: float32 [2, 3072], P('section', 'dp')
- head_grad: float32 [768, 128], P(('section', 'dp'))
- input_grads: float32 [2, 32, 512, 768], P('section', 'dp')
Inputs may be any that keep to these rules, and one draw needn't show every extreme that they name: `segment_ids`: along each row the ids never fall; a passage holds 1 to 128 tokens.
All inputs are finite; a program needn't handle non-finite values.
Results may differ from a plain program's by a relative error of at most 0.02.
Values may be sent and summed in bfloat16 or wider, within the bound.
No kernel may reach another device: no remote copies, remote signals or barrier semaphores. Data moves between devices by JAX's collectives and lax.ppermute only.
A program may use at most 256 MiB of HBM per device.

v0:
```python
import jax
import jax.numpy as jnp
from jax import lax
from jax.sharding import PartitionSpec as P

HEADS = 12
HDIM = 64
MICRO = 2


norm_eps = 1e-06


def from_behind(value, axis, steps):
    count = lax.axis_size(axis)
    first, last = (max(0, -steps), min(count, count - steps))
    return lax.ppermute(value, axis, [(source, source + steps) for source in range(first, last)])


def layer_norm(values, gain, shift):
    center = values - jnp.mean(values, axis=-1, keepdims=True)
    spread = jnp.mean(center * center, axis=-1, keepdims=True)
    return center * lax.rsqrt(spread + norm_eps) * gain + shift


def unit_norm(proj):
    return proj * lax.rsqrt(jnp.sum(proj * proj, axis=-1, keepdims=True) + norm_eps)


def gelu_exact(values):
    return jax.nn.gelu(values, approximate=False)


def layer_forward(acts, seg, weights):
    w_qkv, w_out, w_up, w_down, gains, shift, up_shift = weights
    width = w_out.shape[0]
    rows, length = (acts.shape[0], acts.shape[1])
    bias = jnp.concatenate([shift[0], jnp.zeros_like(shift[0]), shift[1]])
    qkv = (jnp.dot(acts, w_qkv, preferred_element_type=jnp.float32) + bias).astype(jnp.bfloat16)
    heads = qkv.reshape(rows, length, 3, HEADS, HDIM)
    query, keys, value = (heads[:, :, 0], heads[:, :, 1], heads[:, :, 2])
    scores = jnp.einsum(
        "rqhd,rkhd->rhqk", query, keys, preferred_element_type=jnp.float32
    ) * HDIM ** (-0.5)
    same = (seg[:, :, None] == seg[:, None, :])[:, None]
    probs = jax.nn.softmax(jnp.where(same, scores, -1000000000.0), axis=-1)
    probs_low = probs.astype(jnp.bfloat16)
    mixed = jnp.einsum("rhqk,rkhd->rqhd", probs_low, value, preferred_element_type=jnp.float32)
    mixed = mixed.astype(jnp.bfloat16).reshape(rows, length, width)
    branch = jnp.dot(mixed, w_out, preferred_element_type=jnp.float32) + shift[2]
    total = acts.astype(jnp.float32) + branch
    hidden = layer_norm(total, gains[0], shift[4])
    upper = (
        jnp.dot(hidden.astype(jnp.bfloat16), w_up, preferred_element_type=jnp.float32) + up_shift
    )
    active = gelu_exact(upper).astype(jnp.bfloat16)
    second = jnp.dot(active, w_down, preferred_element_type=jnp.float32) + shift[3]
    outcome = layer_norm(hidden + second, gains[1], shift[5])
    return (
        outcome,
        (query, keys, value, probs, probs_low, mixed, total, hidden, upper, active, second),
    )


def layer_backward(acts, weights, d_out, kept):
    w_qkv, w_out, w_up, w_down, gains, shift, up_shift = weights
    query, keys, value, probs, probs_low, mixed, total, hidden, upper, active, second = kept
    width = w_out.shape[0]
    rows, length = (acts.shape[0], acts.shape[1])
    _, second_pull = jax.vjp(layer_norm, hidden + second, gains[1], shift[5])
    d_sum, d_gain_two, d_shift_five = second_pull(d_out)
    d_second = d_sum.astype(jnp.bfloat16)
    grad_down = jnp.einsum("rsf,rsd->fd", active, d_second, preferred_element_type=jnp.float32)
    grad_cdown = jnp.sum(d_second.astype(jnp.float32), axis=(0, 1))
    d_active = jnp.einsum("rsd,fd->rsf", d_second, w_down, preferred_element_type=jnp.float32)
    _, gelu_pull = jax.vjp(gelu_exact, upper)
    d_upper = gelu_pull(d_active)[0].astype(jnp.bfloat16)
    grad_cup = jnp.sum(d_upper.astype(jnp.float32), axis=(0, 1))
    grad_up = jnp.einsum(
        "rsd,rsf->df", hidden.astype(jnp.bfloat16), d_upper, preferred_element_type=jnp.float32
    )
    d_hidden = d_sum + jnp.einsum("rsf,df->rsd", d_upper, w_up, preferred_element_type=jnp.float32)
    _, first_pull = jax.vjp(layer_norm, total, gains[0], shift[4])
    d_total, d_gain_one, d_shift_four = first_pull(d_hidden)
    d_branch = d_total.astype(jnp.bfloat16)
    grad_out = jnp.einsum("rsi,rsd->id", mixed, d_branch, preferred_element_type=jnp.float32)
    grad_cout = jnp.sum(d_branch.astype(jnp.float32), axis=(0, 1))
    d_mixed = jnp.einsum("rsd,id->rsi", d_branch, w_out, preferred_element_type=jnp.float32)
    d_mixed = d_mixed.astype(jnp.bfloat16).reshape(rows, length, HEADS, HDIM)
    grad_value = jnp.einsum(
        "rhqk,rqhd->rkhd", probs_low, d_mixed, preferred_element_type=jnp.float32
    )
    d_probs = jnp.einsum("rqhd,rkhd->rhqk", d_mixed, value, preferred_element_type=jnp.float32)
    d_scores = (probs * (d_probs - jnp.sum(probs * d_probs, axis=-1, keepdims=True))).astype(
        jnp.bfloat16
    )
    grad_query = jnp.einsum(
        "rhqk,rkhd->rqhd", d_scores, keys, preferred_element_type=jnp.float32
    ) * HDIM ** (-0.5)
    grad_keys = jnp.einsum(
        "rhqk,rqhd->rkhd", d_scores, query, preferred_element_type=jnp.float32
    ) * HDIM ** (-0.5)
    d_qkv = (
        jnp.stack([grad_query, grad_keys, grad_value], axis=2)
        .astype(jnp.bfloat16)
        .reshape(rows, length, 3 * width)
    )
    parts = d_qkv.astype(jnp.float32)
    grad_bquery = jnp.sum(parts[..., :width], axis=(0, 1))
    grad_bvalue = jnp.sum(parts[..., 2 * width :], axis=(0, 1))
    grad_qkv = jnp.einsum("rsd,rse->de", acts, d_qkv, preferred_element_type=jnp.float32)
    d_acts = d_total + jnp.einsum("rse,de->rsd", d_qkv, w_qkv, preferred_element_type=jnp.float32)
    grad_gain = jnp.stack([d_gain_one, d_gain_two])
    grad_shift = jnp.stack(
        [grad_bquery, grad_bvalue, grad_cout, grad_cdown, d_shift_four, d_shift_five]
    )
    return (d_acts, (grad_qkv, grad_out, grad_up, grad_down, grad_gain, grad_shift, grad_cup))


def head_backward(outcome, cot, head):
    low_out = outcome.astype(jnp.bfloat16)
    proj = jnp.dot(low_out, head, preferred_element_type=jnp.float32)
    _, pull = jax.vjp(unit_norm, proj)
    d_proj = pull(cot.astype(jnp.float32))[0].astype(jnp.bfloat16)
    grad_head = jnp.einsum("rsd,rsp->dp", low_out, d_proj, preferred_element_type=jnp.float32)
    d_outcome = jnp.einsum("rsp,dp->rsd", d_proj, head, preferred_element_type=jnp.float32)
    return (d_outcome, grad_head)


def shards(
    tokens,
    segment_ids,
    cotangent,
    qkv_weight,
    out_weight,
    up_weight,
    down_weight,
    ln_gains,
    shifts,
    up_bias,
    head_weight,
):
    section_id = lax.axis_index("section")
    first = section_id == 0
    bf = jnp.bfloat16
    full = (
        lax.all_gather(qkv_weight.astype(bf), "dp", axis=1, tiled=True),
        lax.all_gather(out_weight.astype(bf), "dp", axis=1, tiled=True),
        lax.all_gather(up_weight.astype(bf), "dp", axis=1, tiled=True),
        lax.all_gather(down_weight.astype(bf), "dp", axis=1, tiled=True),
        lax.all_gather(ln_gains.astype(bf), "dp", axis=2, tiled=True),
        lax.all_gather(shifts.astype(bf), "dp", axis=2, tiled=True),
        lax.all_gather(up_bias.astype(bf), "dp", axis=1, tiled=True),
    )
    weights = (
        full[0][0],
        full[1][0],
        full[2][0],
        full[3][0],
        full[4][0].astype(jnp.float32),
        full[5][0].astype(jnp.float32),
        full[6][0].astype(jnp.float32),
    )
    head = lax.all_gather(head_weight.astype(bf), ("section", "dp"), axis=0, tiled=True)
    rows_dev, length, width = tokens.shape
    micro_rows = rows_dev // MICRO
    received = jnp.zeros((micro_rows, length, width), bf)
    saved = []
    for step in range(MICRO + 1):
        index = jnp.clip(step - section_id, 0, MICRO - 1) * micro_rows
        own = lax.dynamic_slice_in_dim(tokens, index, micro_rows, 0)
        seg = lax.dynamic_slice_in_dim(segment_ids, index, micro_rows, 0)
        inputs = jnp.where(first, own, received)
        saved.append((inputs, seg))
        if step < MICRO:
            outcome, _ = layer_forward(inputs, seg, weights)
            received = from_behind(outcome.astype(bf), "section", 1)
    totals = tuple((jnp.zeros((1,) + item.shape, jnp.float32) for item in weights))
    head_total = jnp.zeros(head.shape, jnp.float32)
    input_grads = jnp.zeros((rows_dev, length, width), jnp.float32)
    back_recv = jnp.zeros((micro_rows, length, width), bf)
    for step in range(MICRO + 1):
        inputs, seg = saved[MICRO - step]
        micro = MICRO - step - section_id
        valid = (micro >= 0) & (micro < MICRO)
        index = jnp.clip(micro, 0, MICRO - 1) * micro_rows
        outcome, kept = layer_forward(inputs, seg, weights)
        cot = lax.dynamic_slice_in_dim(cotangent, index, micro_rows, 0)
        head_out, grad_head = head_backward(outcome, cot, head)
        d_out = jnp.where(first, back_recv.astype(jnp.float32), head_out)
        d_acts, grads = layer_backward(inputs, weights, d_out, kept)
        head_total = head_total + jnp.where(valid & jnp.logical_not(first), grad_head, 0.0)
        updated = lax.dynamic_update_slice_in_dim(input_grads, d_acts, index, 0)
        input_grads = jnp.where(valid, updated, input_grads)
        step_grads = tuple((jnp.where(valid, item, 0.0)[None] for item in grads))
        totals = tuple((left + right for left, right in zip(totals, step_grads)))
        if step < MICRO:
            back_recv = from_behind(d_acts.astype(bf), "section", -1)
    g_qkv, g_out, g_up, g_down, g_gain, g_shift, g_cup = totals
    totals = (
        lax.psum_scatter(g_qkv, "dp", scatter_dimension=1, tiled=True),
        lax.psum_scatter(g_out, "dp", scatter_dimension=1, tiled=True),
        lax.psum_scatter(g_up, "dp", scatter_dimension=1, tiled=True),
        lax.psum_scatter(g_down, "dp", scatter_dimension=1, tiled=True),
        lax.psum_scatter(g_gain, "dp", scatter_dimension=2, tiled=True),
        lax.psum_scatter(g_shift, "dp", scatter_dimension=2, tiled=True),
        lax.psum_scatter(g_cup, "dp", scatter_dimension=1, tiled=True),
    )
    head_share = lax.psum_scatter(head_total, ("section", "dp"), scatter_dimension=0, tiled=True)
    return (
        totals[0],
        totals[1],
        totals[2],
        totals[3],
        totals[4],
        totals[5],
        totals[6],
        head_share,
        input_grads[None],
    )


def solution(mesh):
    return jax.shard_map(
        shards,
        mesh=mesh,
        in_specs=(
            P("dp", None, None),
            P("dp", None),
            P("dp", None, None),
            P("section", "dp", None),
            P("section", "dp", None),
            P("section", "dp", None),
            P("section", "dp", None),
            P("section", None, "dp"),
            P("section", None, "dp"),
            P("section", "dp"),
            P(("section", "dp"), None),
        ),
        out_specs=(
            P("section", "dp", None),
            P("section", "dp", None),
            P("section", "dp", None),
            P("section", "dp", None),
            P("section", None, "dp"),
            P("section", None, "dp"),
            P("section", "dp"),
            P(("section", "dp"), None),
            P("section", "dp", None, None),
        ),
        check_vma=False,
    )
```

profile of v0, /device:TPU:0, one launch (start us, length us, event | category | flops | bytes accessed | tf_op | source)
XLA Modules:
  0.0 1715.2 jit_solution(574918942565243134)
XLA Ops:
  14.6 46.4 %all_gather.25 = bf16[1,6,768]{1,0,2:T(2,128)(2,1)S(1)} all-gather(bf16[1,6,48]{1,0,2:T(2,128)(2,1)S(1)} %copy.118), channel_id=1, replica_groups=mesh['section'=2,'dp'=16] {'dp'}, dimensions={2}, use_global_device_ids=true | all-gather | bytes 9792 | tf_op jit(solution)/shard_map/all_gather | solution.py:152
  61.5 12.8 slice_reduce_fusion.6
  74.5 65.1 %all_gather.31 = bf16[768,128]{1,0:T(8,128)(2,1)S(1)} all-gather(bf16[24,128]{1,0:T(8,128)(2,1)S(1)} %convert_element_type.454), channel_id=1, replica_groups=mesh['section'=2,'dp'=16] {'section','dp'}, dimensions={0}, use_global_device_ids=true | all-gather | bytes 202752 | tf_op jit(solution)/shard_map/all_gather | solution.py:164
  139.7 40.7 %all_gather.27 = bf16[1,2,768]{1,0,2:T(2,128)(2,1)S(1)} all-gather(bf16[1,2,48]{1,0,2:T(2,128)(2,1)S(1)} %copy.121), channel_id=1, replica_groups=mesh['section'=2,'dp'=16] {'dp'}, dimensions={2}, use_global_device_ids=true | all-gather | bytes 3264 | tf_op jit(solution)/shard_map/all_gather | solution.py:151
  182.3 38.5 %all-reduce = bf16[3072]{0:T(1024)(128)(2,1)S(1)} all-reduce(bf16[3072]{0:T(1024)(128)(2,1)S(1)} %dynamic-update-slice.4), channel_id=1, replica_groups=mesh['section'=2,'dp'=16] {'dp'}, use_global_device_ids=true, to_apply=%add | all-reduce | flops 3072 | bytes 12288
  255.3 19.8 %multiply_convert_fusion.5 = (bf16[512,3072]{1,0:T(8,128)(2,1)}, f32[512,3072]{1,0:T(8,128)}, f32[512,3072]{1,0:T(8,128)}) fusion(f32[3072]{0:T(1024)S(1)} %convert_element_type.504, bf16[1,768,3072]{2,1,0:T(8,128)(2,1)} %all-gather.9.cloned.1.call-done, f32[1,512,768]{2,1,0:T(8,128)S(1)} %get-tuple-element.89, f32[768]{0:T(1024)S(1)} %get-tuple-element.36, ...), kind=kOutput, calls=%fused_computation.61 | convolution fusion | flops 2521694208 | bytes 22042624 | tf_op jit(solution)/shard_map/dot_general | solution.py:54
  275.1 38.8 %all-gather.11.cloned.1.call-done = bf16[1,3072,768]{2,1,0:T(8,128)(2,1)} async-done(((bf16[1,192,768]{2,1,0:T(8,128)(2,1)}), bf16[1,3072,768]{2,1,0:T(8,128)(2,1)}) %all-gather.11.cloned.1.call-update) | async-done | bytes 4718608 | tf_op jit(solution)/shard_map/all_gather | solution.py:150
  346.0 20.2 %multiply_convert_fusion.4 = (bf16[512,3072]{1,0:T(8,128)(2,1)S(1)}, f32[512,3072]{1,0:T(8,128)}, f32[512,3072]{1,0:T(8,128)}) fusion(f32[3072]{0:T(1024)S(1)} %convert_element_type.504, bf16[1,768,3072]{2,1,0:T(8,128)(2,1)} %all-gather.9.cloned.1.call-done, f32[1,512,768]{2,1,0:T(8,128)S(1)} %get-tuple-element.96, f32[512]{0:T(512)S(1)} %fusion.202, ...), kind=kOutput, calls=%fused_computation.47 | convolution fusion | flops 2521694208 | bytes 22042624 | tf_op jit(solution)/shard_map/dot_general | solution.py:54
  396.0 20.6 %multiply_convert_fusion.3 = (bf16[512,3072]{1,0:T(8,128)(2,1)S(1)}, f32[512,3072]{1,0:T(8,128)}, f32[512,3072]{1,0:T(8,128)}) fusion(f32[3072]{0:T(1024)S(1)} %convert_element_type.504, bf16[1,768,3072]{2,1,0:T(8,128)(2,1)} %all-gather.9.cloned.1.call-done, f32[1,512,768]{2,1,0:T(8,128)S(1)} %get-tuple-element.103, f32[512]{0:T(512)S(1)} %fusion.204, ...), kind=kOutput, calls=%fused_computation.33 | convolution fusion | flops 2521694208 | bytes 22042624 | tf_op jit(solution)/shard_map/dot_general | solution.py:54
  423.2 10.4 convert_reduce_fusion.2
  446.2 10.4 multiply_reduce_fusion.2
  506.6 12.0 multiply_reduce_fusion.1
  542.9 9.6 convert_reduce_fusion
  561.9 10.4 multiply_reduce_fusion
  624.2 9.4 add_bitcast_fusion
  643.0 8.6 add_bitcast_fusion.1
  662.0 49.8 %reduce-scatter.25.cloned.1.call-done = f32[48,2]{1,0:T(8,128)} async-done(((f32[768,2]{1,0:T(8,128)}), f32[48,2]{1,0:T(8,128)}) %reduce-scatter.25.cloned.1.call-update) | async-done | bytes 400
  713.2 127.7 %reduce-scatter.29.cloned.1.call-done = f32[192,1]{1,0:T(8,128)} async-done(((f32[3072,1]{1,0:T(8,128)}), f32[192,1]{1,0:T(8,128)}) %reduce-scatter.29.cloned.1.call-update) | async-done | bytes 784
  842.5 124.5 %reduce-scatter.27.cloned.1.call-done = f32[48,6]{1,0:T(8,128)} async-done(((f32[768,6]{1,0:T(8,128)}), f32[48,6]{1,0:T(8,128)}) %reduce-scatter.27.cloned.1.call-update) | async-done | bytes 1168
  968.5 97.9 %reduce-scatter.31.cloned.1.call-done = f32[24,128]{1,0:T(8,128)} async-done(((f32[768,128]{1,0:T(8,128)}), f32[24,128]{1,0:T(8,128)}) %reduce-scatter.31.cloned.1.call-update) | async-done | bytes 12304
  1066.5 132.9 %reduce-scatter.19.cloned.1.call-done = f32[1,48,768]{2,1,0:T(8,128)} async-done(((f32[1,768,768]{2,1,0:T(8,128)}), f32[1,48,768]{2,1,0:T(8,128)}) %reduce-scatter.19.cloned.1.call-update) | async-done | bytes 147472 | tf_op jit(solution)/shard_map/reduce_scatter | solution.py:202
  1199.4 155.4 %reduce-scatter.17.cloned.1.call-done = f32[1,48,2304]{2,1,0:T(8,128)} async-done(((f32[1,768,2304]{2,1,0:T(8,128)}), f32[1,48,2304]{2,1,0:T(8,128)}) %reduce-scatter.17.cloned.1.call-update) | async-done | bytes 442384 | tf_op jit(solution)/shard_map/reduce_scatter | solution.py:201
  1354.8 176.2 %reduce-scatter.23.cloned.1.call-done = f32[1,192,768]{2,1,0:T(8,128)} async-done(((f32[1,3072,768]{2,1,0:T(8,128)}), f32[1,192,768]{2,1,0:T(8,128)}) %reduce-scatter.23.cloned.1.call-update) | async-done | bytes 589840 | tf_op jit(solution)/shard_map/reduce_scatter | solution.py:204
  1531.1 177.1 %reduce-scatter.21.cloned.1.call-done = f32[1,48,3072]{2,1,0:T(8,128)} async-done(((f32[1,768,3072]{2,1,0:T(8,128)}), f32[1,48,3072]{2,1,0:T(8,128)}) %reduce-scatter.21.cloned.1.call-update) | async-done | bytes 589840 | tf_op jit(solution)/shard_map/reduce_scatter | solution.py:203
  (543 shorter events, 282.2 us)
Async XLA Ops:
  7.2 222.0 %all-gather.5.cloned.1.call-start = ((), (), s32[]{:S(2)}) async-start(), calls=%async_computation.8 | async-start | bytes 3760128 | tf_op jit(solution)/shard_map/all_gather | solution.py:147
  9.0 65.4 %copy-start.102 = (f32[24,128]{1,0:T(8,128)S(1)}, f32[24,128]{1,0:T(8,128)}, u32[]{:S(2)}) copy-start(f32[24,128]{1,0:T(8,128)} %param.21) | copy-start | bytes 36868
  9.0 65.4 %copy-start.106 = (s32[2,512]{1,0:T(2,128)S(1)}, s32[2,512]{1,0:T(2,128)}, u32[]{:S(2)}) copy-start(s32[2,512]{1,0:T(2,128)} %param.12) | copy-start | bytes 12292
  9.0 65.4 %copy-start.67 = (bf16[2,512,128]{2,1,0:T(8,128)(2,1)S(1)}, bf16[2,512,128]{2,1,0:T(8,128)(2,1)}, u32[]{:S(2)}) copy-start(bf16[2,512,128]{2,1,0:T(8,128)(2,1)} %param.13) | copy-start | bytes 786436
  9.0 243.3 %all-gather.7.cloned.1.call-start = ((), (), s32[]{:S(2)}) async-start(), calls=%async_computation.9 | async-start | bytes 1253376 | tf_op jit(solution)/shard_map/all_gather | solution.py:148
  10.7 244.6 %all-gather.9.cloned.1.call-start = ((), (), s32[]{:S(2)}) async-start(), calls=%async_computation.10 | async-start | bytes 5013504 | tf_op jit(solution)/shard_map/all_gather | solution.py:149
  12.6 127.0 %copy-start.126 = (f32[1,2,48]{2,1,0:T(2,128)S(1)}, f32[1,2,48]{2,1,0:T(2,128)}, u32[]{:S(2)}) copy-start(f32[1,2,48]{2,1,0:T(2,128)} %param.18) | copy-start | bytes 1156
  12.6 301.3 %all-gather.11.cloned.1.call-start = ((), (), s32[]{:S(2)}) async-start(), calls=%async_computation.11 | async-start | bytes 5013504 | tf_op jit(solution)/shard_map/all_gather | solution.py:150
  14.4 166.4 %copy-start.127 = (u32[32]{0:T(128)S(1)}, u32[32]{0:T(128)}, u32[]{:S(2)}) copy-start(u32[32]{0:T(128)} %constant.135) | copy-start | bytes 388
  14.5 697.4 %reduce-scatter.25.cloned.1.call-start = ((), (), s32[]{:S(2)}) async-start(), calls=%async_computation.16 | async-start | bytes 417792
  61.4 167.7 %copy-start.38 = (bf16[2,512,768]{2,1,0:T(8,128)(2,1)S(1)}, bf16[2,512,768]{2,1,0:T(8,128)(2,1)}, u32[]{:S(2)}) copy-start(bf16[2,512,768]{2,1,0:T(8,128)(2,1)} %param.11) | copy-start | bytes 4718596
  74.3 342.4 %copy-start.99 = (f32[768]{0:T(1024)}, f32[768]{0:T(1024)S(1)}, u32[]{:S(2)}) copy-start(f32[768]{0:T(1024)S(1)} %get-tuple-element.36) | copy-start | bytes 9220
  220.9 202.3 %copy-start.103 = (f32[3072]{0:T(1024)}, f32[3072]{0:T(1024)S(1)}, u32[]{:S(2)}) copy-start(f32[3072]{0:T(1024)S(1)} %convert_element_type.504) | copy-start | bytes 36868
  320.7 3.5 collective-permute-start
  369.7 4.5 collective-permute-start.1
  480.9 6.3 collective-permute-start.2
  536.7 4.4 collective-permute-start.3
  590.6 250.3 %reduce-scatter.29.cloned.1.call-start = ((), (), s32[]{:S(2)}) async-start(), calls=%async_computation.18 | async-start | bytes 1671168
  594.8 372.2 %reduce-scatter.27.cloned.1.call-start = ((), (), s32[]{:S(2)}) async-start(), calls=%async_computation.17 | async-start | bytes 417792
  598.5 468.0 %reduce-scatter.31.cloned.1.call-start = ((), (), s32[]{:S(2)}) async-start(), calls=%async_computation.19 | async-start | bytes 405504
  600.6 598.8 %reduce-scatter.19.cloned.1.call-start = ((), (), s32[]{:S(2)}) async-start(), calls=%async_computation.13 | async-start | bytes 2506752 | tf_op jit(solution)/shard_map/reduce_scatter | solution.py:202
  605.5 749.4 %reduce-scatter.17.cloned.1.call-start = ((), (), s32[]{:S(2)}) async-start(), calls=%async_computation.12 | async-start | bytes 7520256 | tf_op jit(solution)/shard_map/reduce_scatter | solution.py:201
  615.5 915.6 %reduce-scatter.23.cloned.1.call-start = ((), (), s32[]{:S(2)}) async-start(), calls=%async_computation.15 | async-start | bytes 10027008 | tf_op jit(solution)/shard_map/reduce_scatter | solution.py:204
  633.6 1074.5 %reduce-scatter.21.cloned.1.call-start = ((), (), s32[]{:S(2)}) async-start(), calls=%async_computation.14 | async-start | bytes 10027008 | tf_op jit(solution)/shard_map/reduce_scatter | solution.py:203
  (146 other events, 1208.3 us)
Sparse Core Ops, SparseCore 0:
  11.4 76.4 all-gather.4
  91.3 54.6 all-gather.6
  149.4 81.8 all-gather.8
  234.5 79.3 all-gather.10
  590.8 121.0 reduce-scatter.24
  717.2 123.6 reduce-scatter.28
  846.3 120.6 reduce-scatter.26
  972.5 93.9 reduce-scatter.30
  1072.7 126.6 reduce-scatter.18
  1205.1 149.6 reduce-scatter.16
  1361.1 169.9 reduce-scatter.22
  1538.1 169.9 reduce-scatter.20
where the time goes:
time: 1720 us
  waiting for transfers between devices  1080 us (63%)
  matrix products  295 us (17%)
  blocking collectives  191 us (11%)
  local copies, waits for them, and re-layouts  72.8 us (4%)
  other arithmetic  46.9 us (3%)
  between operations  17.6 us (1%)
    unnamed x16, waiting for transfers between devices  400 us
    reduce_scatter x1, waiting for transfers between devices, shards(): lax.psum_scatter(g_up, 'dp', scatter_dimension=1, tiled=True)  177 us
    reduce_scatter x1, waiting for transfers between devices, shards(): lax.psum_scatter(g_down, 'dp', scatter_dimension=1, tiled=True)  176 us
    reduce_scatter x1, waiting for transfers between devices, shards(): lax.psum_scatter(g_qkv, 'dp', scatter_dimension=1, tiled=True)  155 us
    reduce_scatter x1, waiting for transfers between devices, shards(): lax.psum_scatter(g_out, 'dp', scatter_dimension=1, tiled=True)  133 us
    all_gather x1, blocking collectives, shards(): lax.all_gather(head_weight.astype(bf), ('section', 'dp'), axis=0, tiled=T...  65.1 us
    dot_general x3, matrix products, layer_forward(): jnp.dot(hidden.astype(jnp.bfloat16), w_up, preferred_element_type=jnp.flo...  60.6 us
    all_gather x1, blocking collectives, shards(): lax.all_gather(shifts.astype(bf), 'dp', axis=2, tiled=True)  46.4 us
  transfers between devices with their start and end apart: 16, of which 12 were waited for; matrix products, arithmetic and copies ran while one was open for 9% of the time, Pallas kernels for 0%

commit v1 on v0

v1 whole, which is shorter than its diff:
```python
import jax
import jax.numpy as jnp
from jax import lax
from jax.sharding import PartitionSpec as P

HEADS = 12
HDIM = 64
norm_eps = 1e-06
BF = jnp.bfloat16
F32 = jnp.float32
BOTH = ("section", "dp")
PAD = 16


def layer_norm(values, gain, shift):
    center = values - jnp.mean(values, axis=-1, keepdims=True)
    spread = jnp.mean(center * center, axis=-1, keepdims=True)
    return center * lax.rsqrt(spread + norm_eps) * gain + shift


def unit_norm(proj):
    return proj * lax.rsqrt(jnp.sum(proj * proj, axis=-1, keepdims=True) + norm_eps)


def gelu_exact(values):
    return jax.nn.gelu(values, approximate=False)


def flip(value, mask):
    count = lax.axis_size("dp")
    pairs = [(s * count + i, s * count + (i ^ mask)) for s in range(2) for i in range(count)]
    return lax.ppermute(value, BOTH, pairs)


def swap(value):
    count = lax.axis_size("dp")
    pairs = [(s * count + i, (1 - s) * count + i) for s in range(2) for i in range(count)]
    return lax.ppermute(value, BOTH, pairs)


def gather_chunk(block):
    count = lax.axis_size("dp")
    me = lax.axis_index("dp")
    own = block[None]
    bit = 4
    while bit < count:
        other = flip(own, bit)
        high = (me & bit) != 0
        own = jnp.where(high, jnp.concatenate([other, own]), jnp.concatenate([own, other]))
        bit *= 2
    half = own.shape[0] // 2
    from_x = flip(own, 1)
    from_y = flip(own, 2)
    diag = jnp.concatenate([flip(from_y[:half], 1), flip(from_x[half:], 2)])
    quad = me & 3
    whole = jnp.zeros((4,) + own.shape, own.dtype)
    for rel, part in enumerate((own, from_x, from_y, diag)):
        whole = lax.dynamic_update_index_in_dim(whole, part, quad ^ rel, 0)
    return whole


def scatter_chunk(total):
    count = lax.axis_size("dp")
    me = lax.axis_index("dp")
    quad = me & 3
    part = [lax.dynamic_index_in_dim(total, quad ^ rel, 0, keepdims=False) for rel in range(4)]
    half = total.shape[1] // 2
    by_x = flip(part[3][:half].astype(BF), 1)
    by_y = flip(part[3][half:].astype(BF), 2)
    to_y = jnp.concatenate([part[2][:half] + by_x, part[2][half:]])
    to_x = jnp.concatenate([part[1][:half], part[1][half:] + by_y])
    rest = part[0] + flip(to_x.astype(BF), 1) + flip(to_y.astype(BF), 2)
    bit = count // 2
    while bit >= 4:
        size = rest.shape[0] // 2
        high = (me & bit) != 0
        keep = jnp.where(high, rest[size:], rest[:size])
        send = jnp.where(high, rest[:size], rest[size:])
        rest = keep + flip(send.astype(BF), bit)
        bit //= 2
    return rest[0]


def in_order(whole, first, units):
    quad, outer, rows, width = whole.shape
    size = width // (quad * outer)
    piece = whole[:, :, first * size : (first + units) * size]
    return piece.transpose(1, 0, 2, 3).reshape(quad * outer, units, size, width)


def attend(query, keys, value, same):
    scores = jnp.einsum("qhd,khd->hqk", query, keys, preferred_element_type=F32) * HDIM ** (-0.5)
    probs = jax.nn.softmax(jnp.where(same[None], scores, -1000000000.0), axis=-1)
    mixed = jnp.einsum("hqk,khd->qhd", probs.astype(BF), value, preferred_element_type=F32)
    return mixed, probs


def layer_forward(acts, same, weights):
    wq, wk, wv, wo, w_up, w_down, gains, shift, up_shift = weights
    length, width = acts.shape

    def proj(w, b):
        return (jnp.dot(acts, w, preferred_element_type=F32) + b).astype(BF)

    query = proj(wq, shift[0]).reshape(length, HEADS, HDIM)
    keys = proj(wk, 0.0).reshape(length, HEADS, HDIM)
    value = proj(wv, shift[1]).reshape(length, HEADS, HDIM)
    mixed, probs = attend(query, keys, value, same)
    mixed = mixed.astype(BF).reshape(length, width)
    total = acts.astype(F32) + jnp.dot(mixed, wo, preferred_element_type=F32) + shift[2]
    hidden = layer_norm(total, gains[0], shift[4])
    upper = jnp.dot(hidden.astype(BF), w_up, preferred_element_type=F32) + up_shift
    active = gelu_exact(upper).astype(BF)
    summed = hidden + jnp.dot(active, w_down, preferred_element_type=F32) + shift[3]
    outcome = layer_norm(summed, gains[1], shift[5])
    return outcome, (query, keys, value, probs, mixed, total, hidden, upper, active, summed)


def ffn_backward(weights, d_out, kept):
    wq, wk, wv, wo, w_up, w_down, gains, shift, up_shift = weights
    query, keys, value, probs, mixed, total, hidden, upper, active, summed = kept
    _, pull = jax.vjp(layer_norm, summed, gains[1], shift[5])
    d_sum, d_gain_two, d_shift_five = pull(d_out)
    d_second = d_sum.astype(BF)
    g_down = jnp.einsum("sf,sd->fd", active, d_second, preferred_element_type=F32)
    g_cdown = jnp.sum(d_second.astype(F32), axis=0)
    d_active = jnp.einsum("sd,fd->sf", d_second, w_down, preferred_element_type=F32)
    _, gelu_pull = jax.vjp(gelu_exact, upper)
    d_upper = gelu_pull(d_active)[0].astype(BF)
    g_cup = jnp.sum(d_upper.astype(F32), axis=0)
    g_up = jnp.einsum("sd,sf->df", hidden.astype(BF), d_upper, preferred_element_type=F32)
    d_hidden = d_sum + jnp.einsum("sf,df->sd", d_upper, w_up, preferred_element_type=F32)
    return d_hidden, (g_up, g_down, d_gain_two, d_shift_five, g_cdown, g_cup)


def attention_backward(acts, weights, d_hidden, kept):
    wq, wk, wv, wo, w_up, w_down, gains, shift, up_shift = weights
    query, keys, value, probs, mixed, total, hidden, upper, active, summed = kept
    length, width = acts.shape
    _, pull = jax.vjp(layer_norm, total, gains[0], shift[4])
    d_total, d_gain_one, d_shift_four = pull(d_hidden)
    d_branch = d_total.astype(BF)
    g_out = jnp.einsum("si,sd->id", mixed, d_branch, preferred_element_type=F32)
    g_cout = jnp.sum(d_branch.astype(F32), axis=0)
    d_mixed = jnp.einsum("sd,id->si", d_branch, wo, preferred_element_type=F32)
    d_mixed = d_mixed.astype(BF).reshape(length, HEADS, HDIM)
    d_value = jnp.einsum("hqk,qhd->khd", probs.astype(BF), d_mixed, preferred_element_type=F32)
    d_probs = jnp.einsum("qhd,khd->hqk", d_mixed, value, preferred_element_type=F32)
    d_scores = (probs * (d_probs - jnp.sum(probs * d_probs, axis=-1, keepdims=True))).astype(BF)
    scale = HDIM ** (-0.5)
    d_query = jnp.einsum("hqk,khd->qhd", d_scores, keys, preferred_element_type=F32) * scale
    d_keys = jnp.einsum("hqk,qhd->khd", d_scores, query, preferred_element_type=F32) * scale
    low = [item.astype(BF).reshape(length, width) for item in (d_query, d_keys, d_value)]
    g_q, g_k, g_v = [jnp.einsum("sd,se->de", acts, item, preferred_element_type=F32) for item in low]
    g_bq = jnp.sum(low[0].astype(F32), axis=0)
    g_bv = jnp.sum(low[2].astype(F32), axis=0)
    d_acts = d_total
    for item, w in zip(low, (wq, wk, wv)):
        d_acts = d_acts + jnp.einsum("se,de->sd", item, w, preferred_element_type=F32)
    return d_acts, (g_q, g_k, g_v, g_out, d_gain_one, d_shift_four, g_cout, g_bq, g_bv)


def head_backward(outcome, cot, head):
    low_out = outcome.astype(BF)
    proj = jnp.dot(low_out, head, preferred_element_type=F32)
    _, pull = jax.vjp(unit_norm, proj)
    d_proj = pull(cot.astype(F32))[0].astype(BF)
    grad_head = jnp.einsum("sd,sp->dp", low_out, d_proj, preferred_element_type=F32)
    d_outcome = jnp.einsum("sp,dp->sd", d_proj, head, preferred_element_type=F32)
    return d_outcome, grad_head


def shards(tokens, segment_ids, cotangent, qkv_w, out_w, up_w, down_w, gains_w, shifts_w, up_b, head_w):
    count = lax.axis_size("dp")
    section = lax.axis_index("section")
    first = section == 0
    rows_dev, length, width = tokens.shape
    mine = rows_dev // 2
    size = width // count
    ff = up_w.shape[2]
    ups = ff // width

    def cols(array, n):
        return [array[:, j * width : (j + 1) * width] for j in range(n)]

    q_u, k_u, v_u = cols(qkv_w[0].astype(BF), 3)
    up_u = cols(up_w[0].astype(BF), ups)
    plane = (
        jnp.concatenate([q_u, k_u] + up_u),
        jnp.concatenate([v_u, out_w[0].astype(BF), down_w[0].astype(BF)]),
    )
    got = swap(jnp.where(first, plane[1], plane[0]))
    zero = jnp.where(first, plane[0], got)
    one = jnp.where(first, got, plane[1])
    small = jnp.concatenate([gains_w.reshape(-1), shifts_w.reshape(-1), up_b.reshape(-1)]).astype(BF)
    small_n = small.shape[0]
    small_rows = -(-small_n // width)
    head_n = head_w.shape[0] * head_w.shape[1]
    head_rows = -(-head_n // width)
    pad_rows = -(-(small_rows + head_rows) // PAD) * PAD

    def to_rows(flat, rows):
        return jnp.pad(flat, (0, rows * width - flat.shape[0])).reshape(rows, width)

    extra = jnp.concatenate(
        [
            to_rows(small, small_rows),
            to_rows(head_w.astype(BF).reshape(-1), head_rows),
            jnp.zeros((pad_rows - small_rows - head_rows, width), BF),
        ]
    )
    parts = [
        jnp.concatenate([zero[: 2 * size], extra]),
        zero[2 * size :],
        one[: 2 * size],
        one[2 * size :],
    ]
    planes = []
    for item in parts:
        whole = gather_chunk(item)
        other = swap(whole)
        planes.append((jnp.where(first, whole, other), jnp.where(first, other, whole)))

    smalls = []
    heads = []
    for item in planes[0]:
        tail = item[:, :, 2 * size :].transpose(1, 0, 2, 3).reshape(count, pad_rows, width)
        flat = tail[:, :small_rows].reshape(count, -1)[:, :small_n].astype(F32)
        n_g = gains_w.shape[1] * size
        n_s = shifts_w.shape[1] * size
        gains = flat[:, :n_g].reshape(count, -1, size).transpose(1, 0, 2).reshape(-1, width)
        shift = flat[:, n_g : n_g + n_s].reshape(count, -1, size).transpose(1, 0, 2).reshape(-1, width)
        cup = flat[:, n_g + n_s :].reshape(-1)
        smalls.append((gains, shift, cup))
        block = tail[:, small_rows : small_rows + head_rows].reshape(count, -1)[:, :head_n]
        heads.append(block.reshape(count * head_w.shape[0], head_w.shape[1]))
    head = jnp.concatenate(heads)

    def layer_weights(level):
        attn, ffn = planes[2 * level], planes[2 * level + 1]
        wq, wk = [in_order(attn[0], j, 1).reshape(width, width) for j in range(2)]
        wv, wo = [in_order(attn[1], j, 1).reshape(width, width) for j in range(2)]
        w_up = in_order(ffn[0], 0, ups).transpose(0, 2, 1, 3).reshape(width, ff)
        w_down = in_order(ffn[1], 0, ups).reshape(ff, width)
        return (wq, wk, wv, wo, w_up, w_down) + smalls[level]

    weights = [layer_weights(level) for level in range(2)]
    own = lax.dynamic_slice_in_dim(tokens, section * mine, mine, 0)
    seg = lax.dynamic_slice_in_dim(segment_ids, section * mine, mine, 0)
    cot = lax.dynamic_slice_in_dim(cotangent, section * mine, mine, 0)
    add = lambda old, new: new if old is None else jax.tree.map(jnp.add, old, new)
    acc = {}
    first_in, second_in = [], []
    for row in range(mine):
        same = seg[row][:, None] == seg[row][None, :]
        a0 = own[row]
        y0, kept0 = layer_forward(a0, same, weights[0])
        a1 = y0.astype(BF)
        y1, kept1 = layer_forward(a1, same, weights[1])
        d_y1, g_head = head_backward(y1, cot[row], head)
        d_h, ffn1 = ffn_backward(weights[1], d_y1, kept1)
        d_a1, att1 = attention_backward(a1, weights[1], d_h, kept1)
        d_h, ffn0 = ffn_backward(weights[0], d_a1.astype(BF).astype(F32), kept0)
        d_a0, att0 = attention_backward(a0, weights[0], d_h, kept0)
        acc = add(acc or None, dict(head=g_head, ffn1=ffn1, att1=att1, ffn0=ffn0, att0=att0))
        first_in.append(d_a0)
        second_in.append(d_a1)

    def to_units(grad, units):
        block = grad.reshape(count // 4, 4, size, units, width).transpose(1, 0, 3, 2, 4)
        return block.reshape(4, count // 4, units * size, width)

    def by_chip(grad):
        block = grad.reshape(count // 4, 4, -1, width)
        return block.transpose(1, 0, 2, 3)

    def reduce(zero_plane, one_plane):
        keep = jnp.where(first, zero_plane, one_plane)
        send = jnp.where(first, one_plane, zero_plane)
        return scatter_chunk(keep + swap(send.astype(BF)).astype(F32))

    def ffn_chunk(grads):
        g_up, g_down = grads[:2]
        return reduce(to_units(g_up, ups), by_chip(g_down))

    def attn_planes(grads):
        return (
            jnp.concatenate([to_units(item, 1) for item in grads[:2]], axis=2),
            jnp.concatenate([to_units(item, 1) for item in grads[2:4]], axis=2),
        )

    def small_block(att, ffn, head_part):
        g_q, g_k, g_v, g_out, d_gain_one, d_shift_four, g_cout, g_bq, g_bv = att
        g_up, g_down, d_gain_two, d_shift_five, g_cdown, g_cup = ffn
        gains = jnp.stack([d_gain_one, d_gain_two]).reshape(2, count, size).transpose(1, 0, 2)
        shift = jnp.stack([g_bq, g_bv, g_cout, g_cdown, d_shift_four, d_shift_five])
        shift = shift.reshape(6, count, size).transpose(1, 0, 2)
        flat = jnp.concatenate(
            [gains.reshape(count, -1), shift.reshape(count, -1), g_cup.reshape(count, -1)], axis=1
        )
        flat = jnp.pad(flat, ((0, 0), (0, small_rows * width - small_n)))
        piece = jnp.pad(head_part.reshape(count, -1), ((0, 0), (0, head_rows * width - head_n)))
        block = jnp.concatenate(
            [
                flat.reshape(count, small_rows, width),
                piece.reshape(count, head_rows, width),
                jnp.zeros((count, pad_rows - small_rows - head_rows, width), F32),
            ],
            axis=1,
        )
        return by_chip(block)

    done_ffn1 = ffn_chunk(acc["ffn1"])
    done_att1 = reduce(*attn_planes(acc["att1"]))
    done_ffn0 = ffn_chunk(acc["ffn0"])
    half_head = acc["head"].reshape(2, -1, head_w.shape[1])
    last = attn_planes(acc["att0"])
    last = (
        jnp.concatenate([last[0], small_block(acc["att0"], acc["ffn0"], half_head[0])], axis=2),
        jnp.concatenate([last[1], small_block(acc["att1"], acc["ffn1"], half_head[1])], axis=2),
    )
    done_att0 = reduce(*last)

    cut = 2 * size
    sums_zero = jnp.concatenate([done_att0[:cut], done_ffn0])
    sums_one = jnp.concatenate([done_att1, done_ffn1])
    other = swap(jnp.where(first, sums_one, sums_zero))
    low_plane = jnp.where(first, sums_zero, other)
    high_plane = jnp.where(first, other, sums_one)

    def unit(array, j):
        return array[j * size : (j + 1) * size]

    qkv_grad = jnp.concatenate([unit(low_plane, 0), unit(low_plane, 1), unit(high_plane, 0)], axis=1)
    out_grad = unit(high_plane, 1)
    up_grad = jnp.concatenate([unit(low_plane, 2 + j) for j in range(ups)], axis=1)
    down_grad = high_plane[cut:]
    tail = done_att0[cut:]
    flat = tail[:small_rows].reshape(-1)[:small_n]
    n_g = gains_w.shape[1] * size
    n_s = shifts_w.shape[1] * size
    gain_grad = flat[:n_g].reshape(gains_w.shape)
    shift_grad = flat[n_g : n_g + n_s].reshape(shifts_w.shape)
    cup_grad = flat[n_g + n_s :].reshape(up_b.shape)
    head_grad = tail[small_rows : small_rows + head_rows].reshape(-1)[:head_n].reshape(head_w.shape)

    d_first, d_second = jnp.stack(first_in), jnp.stack(second_in)
    got = swap(jnp.where(first, d_second, d_first))
    keep = jnp.where(first, d_first, d_second)
    input_grads = jnp.where(first, jnp.concatenate([keep, got]), jnp.concatenate([got, keep]))
    return (
        qkv_grad[None],
        out_grad[None],
        up_grad[None],
        down_grad[None],
        gain_grad,
        shift_grad,
        cup_grad,
        head_grad,
        input_grads[None],
    )


def solution(mesh):
    return jax.shard_map(
        shards,
        mesh=mesh,
        in_specs=(
            P("dp", None, None),
            P("dp", None),
            P("dp", None, None),
            P("section", "dp", None),
            P("section", "dp", None),
            P("section", "dp", None),
            P("section", "dp", None),
            P("section", None, "dp"),
            P("section", None, "dp"),
            P("section", "dp"),
            P(("section", "dp"), None),
        ),
        out_specs=(
            P("section", "dp", None),
            P("section", "dp", None),
            P("section", "dp", None),
            P("section", "dp", None),
            P("section", None, "dp"),
            P("section", None, "dp"),
            P("section", "dp"),
            P(("section", "dp"), None),
            P("section", "dp", None, None),
        ),
        check_vma=False,
    )
```

time: 1720 us -> 758 us (0.44)
  waiting for transfers between devices: 1080 us -> 253 us
  blocking collectives: 191 us -> 0 us
  matrix products: 295 us -> 191 us
  other arithmetic: 46.9 us -> 106 us
  local copies, waits for them, and re-layouts: 72.8 us -> 130 us
  starting transfers between devices: 8.83 us -> 63.1 us
    reduce_scatter x4 -> x0, waiting for transfers between devices: 642 us -> none  [the longest x1 177 us: shards(): lax.psum_scatter(g_up, 'dp', scatter_dimension=1, tiled=True)]
    unnamed x16 -> x0, waiting for transfers between devices: 400 us -> none
    ppermute x4 -> x59, waiting for transfers between devices: 2.67 us -> 253 us  [the longest x48 253 us: flip(): return lax.ppermute(value, BOTH, pairs)]
    all_gather x3 -> x0, blocking collectives: 152 us -> none  [the longest x1 65.1 us: shards(): lax.all_gather(head_weight.astype(bf), ('section', 'dp'), axis=0, tiled=T...]
    dot_general x60 -> x49, matrix products: 271 us -> 175 us  [the longest x2 37.1 us: layer_forward(): jnp.dot(hidden.astype(BF), w_up, preferred_element_type=F32) + up_shift]
    ppermute x4 -> x59, starting transfers between devices: 7.44 us -> 63.1 us  [the longest x48 60.8 us: flip(): return lax.ppermute(value, BOTH, pairs)]
    reshape x0 -> x21, local copies, waits for them, and re-layouts: none -> 46.8 us  [the longest x4 43.2 us: to_units(): grad.reshape(count // 4, 4, size, units, width).transpose(1, 0, 3, 2, 4)]
    all_gather x4 -> x0, waiting for transfers between devices: 38.8 us -> none  [the longest x1 38.8 us: shards(): lax.all_gather(down_weight.astype(bf), 'dp', axis=1, tiled=True)]
  transfers between devices with their start and end apart: 16 -> 59, of which waited for: 12 -> 28; matrix products, arithmetic and copies ran while one was open for 9% -> 34% of each run, Pallas kernels for 0% -> 0%
where the time goes in v1:
time: 758 us; the launch traced here: 747 us
  waiting for transfers between devices  253 us (33%)
  matrix products  191 us (25%)
  local copies, waits for them, and re-layouts  130 us (17%)
  other arithmetic  106 us (14%)
  starting transfers between devices  63.1 us (8%)
    ppermute x48, waiting for transfers between devices, flip(): return lax.ppermute(value, BOTH, pairs)  253 us
    ppermute x48, starting transfers between devices, flip(): return lax.ppermute(value, BOTH, pairs)  60.8 us
    reshape x4, local copies, waits for them, and re-layouts, to_units(): grad.reshape(count // 4, 4, size, units, width).transpose(1, 0, 3, 2, 4)  43.2 us
    dot_general x2, matrix products, layer_forward(): jnp.dot(hidden.astype(BF), w_up, preferred_element_type=F32) + up_shift  37.1 us
    unnamed x367, local copies, waits for them, and re-layouts  28 us
    convert_element_type x4, other arithmetic, reduce(): return scatter_chunk(keep + swap(send.astype(BF)).astype(F32))  26.3 us
    add x4, other arithmetic, reduce(): return scatter_chunk(keep + swap(send.astype(BF)).astype(F32))  23.4 us
    dot_general x2, matrix products, attention_backward(): jnp.einsum('qhd,khd->hqk', d_mixed, value, preferred_element_type=F32)  22.2 us
  transfers between devices with their start and end apart: 59, of which 28 were waited for; matrix products, arithmetic and copies ran while one was open for 34% of the time, Pallas kernels for 0%

profile of v1, /device:TPU:0, one launch (start us, length us, event | category | flops | bytes accessed | tf_op | source)
XLA Modules:
  0.0 747.3 jit_solution(3878974547036271813)
XLA Ops:
  19.0 10.6 %collective-permute-done.1 = bf16[1,112,768]{2,1,0:T(8,128)(2,1)S(1)} collective-permute-done((bf16[1,112,768]{2,1,0:T(8,128)(2,1)S(1)}, bf16[1,112,768]{2,1,0:T(8,128)(2,1)S(1)}, u32[]{:S(2)}, u32[]{:S(2)}) %collective-permute-start.1) | collective-permute-done | bytes 172064 | tf_op jit(solution)/shard_map/ppermute | solution.py:32
  47.2 32.7 %collective-permute-done.2 = bf16[2,112,768]{2,1,0:T(8,128)(2,1)S(1)} collective-permute-done((bf16[2,112,768]{2,1,0:T(8,128)(2,1)S(1)}, bf16[2,112,768]{2,1,0:T(8,128)(2,1)S(1)}, u32[]{:S(2)}, u32[]{:S(2)}) %collective-permute-start.2) | collective-permute-done | bytes 344096 | tf_op jit(solution)/shard_map/ppermute | solution.py:32
  82.7 9.9 %collective-permute-done.9 = bf16[2,192,768]{2,1,0:T(8,128)(2,1)S(1)} collective-permute-done((bf16[2,192,768]{2,1,0:T(8,128)(2,1)S(1)}, bf16[2,192,768]{2,1,0:T(8,128)(2,1)S(1)}, u32[]{:S(2)}, u32[]{:S(2)}) %collective-permute-start.9) | collective-permute-done | bytes 589856 | tf_op jit(solution)/shard_map/ppermute | solution.py:32
  114.1 22.4 %collective-permute-done.20 = bf16[2,96,768]{2,1,0:T(8,128)(2,1)S(1)} collective-permute-done((bf16[2,96,768]{2,1,0:T(8,128)(2,1)S(1)}, bf16[2,96,768]{2,1,0:T(8,128)(2,1)S(1)}, u32[]{:S(2)}, u32[]{:S(2)}) %collective-permute-start.20) | collective-permute-done | bytes 294944 | tf_op jit(solution)/shard_map/ppermute | solution.py:32
  155.8 12.8 %collective-permute-done.25 = bf16[4,192,768]{2,1,0:T(8,128)(2,1)S(1)} collective-permute-done((bf16[4,192,768]{2,1,0:T(8,128)(2,1)S(1)}, bf16[4,192,768]{2,1,0:T(8,128)(2,1)S(1)}, u32[]{:S(2)}, u32[]{:S(2)}) %collective-permute-start.25) | collective-permute-done | bytes 1179680 | tf_op jit(solution)/shard_map/ppermute | solution.py:32
  174.9 11.1 %collective-permute-done.12 = bf16[2,192,768]{2,1,0:T(8,128)(2,1)S(1)} collective-permute-done((bf16[2,192,768]{2,1,0:T(8,128)(2,1)S(1)}, bf16[2,192,768]{2,1,0:T(8,128)(2,1)S(1)}, u32[]{:S(2)}, u32[]{:S(2)}) %collective-permute-start.12) | collective-permute-done | bytes 589856 | tf_op jit(solution)/shard_map/ppermute | solution.py:32
  250.3 18.6 %multiply_convert_fusion.3 = (bf16[512,3072]{1,0:T(8,128)(2,1)S(1)}, f32[512,3072]{1,0:T(8,128)}, f32[512,3072]{1,0:T(8,128)}) fusion(f32[3072]{0:T(1024)S(1)} %add.390, bf16[768,3072]{1,0:T(8,128)(2,1)S(1)} %bitcast.554, f32[512,768]{1,0:T(8,128)S(1)} %copy-done.39, f32[768]{0:T(1024)S(1)} %add.387, f32[768]{0:T(1024)S(1)} %mul.366, f32[512]{0:T(512)S(1)} %fusion.118, ...), kind=kOutput, calls=%fused_computation.42 | convolution fusion | flops 2521694208 | bytes 22042624 | tf_op jit(solution)/shard_map/dot_general | solution.py:112
  311.3 18.4 %multiply_convert_fusion.2 = (bf16[512,3072]{1,0:T(8,128)(2,1)S(1)}, f32[512,3072]{1,0:T(8,128)}, f32[512,3072]{1,0:T(8,128)}) fusion(f32[3072]{0:T(1024)S(1)} %add.415, bf16[768,3072]{1,0:T(8,128)(2,1)S(1)} %bitcast.562, f32[512,768]{1,0:T(8,128)S(1)} %copy-done.36, f32[768]{0:T(1024)S(1)} %add.412, f32[768]{0:T(1024)S(1)} %mul.382, f32[512]{0:T(512)S(1)} %fusion.120, ...), kind=kOutput, calls=%fused_computation.28 | convolution fusion | flops 2521694208 | bytes 22042624 | tf_op jit(solution)/shard_map/dot_general | solution.py:112
  354.2 10.2 %multiply_reduce_fusion.1 = (f32[12,512]{1,0:T(8,128)S(1)}, f32[12,512,512]{1,2,0:T(8,128)}) fusion(f32[12,512,512]{1,2,0:T(8,128)} %get-tuple-element.150, f32[12,512]{1,0:T(8,128)S(1)} %copy-done.116, bf16[512,12,64]{0,2,1:T(8,128)(2,1)S(1)} %bitcast.605, bf16[512,12,64]{0,2,1:T(8,128)(2,1)S(1)} %bitcast.604), kind=kOutput, calls=%fused_computation.5 | convolution fusion | flops 412084224 | bytes 26787840 | tf_op jit(solution)/shard_map/qhd,khd->hqk/dot_general | solution.py:148
  385.6 8.5 %convert_reduce_fusion.1 = (f32[3072]{0:T(1024)S(1)}, bf16[512,3072]{1,0:T(8,128)(2,1)S(1)}) fusion(f32[512,3072]{1,0:T(8,128)} %get-tuple-element.83, f32[512,3072]{1,0:T(8,128)} %get-tuple-element.146, f32[3072]{0:T(1024)S(1)} %copy-done.131, bf16[512,768]{1,0:T(8,128)(2,1)S(1)} %get-tuple-element.60, bf16[3072,768]{1,0:T(8,128)(2,1)S(1)} %bitcast.561), kind=kOutput, calls=%fused_computation.25 | convolution fusion | flops 2442654720 | bytes 21258240 | tf_op jit(solution)/shard_map/sd,fd->sf/dot_general | solution.py:127
  404.4 12.0 %multiply_reduce_fusion = (f32[12,512]{1,0:T(8,128)S(1)}, f32[12,512,512]{1,2,0:T(8,128)}) fusion(f32[12,512,512]{1,2,0:T(8,128)} %get-tuple-element.143, f32[12,512]{1,0:T(8,128)S(1)} %copy-done.114, bf16[512,12,64]{0,2,1:T(8,128)(2,1)} %bitcast.607, bf16[512,12,64]{0,2,1:T(8,128)(2,1)} %bitcast.602), kind=kOutput, calls=%fused_computation.3 | convolution fusion | flops 412084224 | bytes 26787840 | tf_op jit(solution)/shard_map/qhd,khd->hqk/dot_general | solution.py:148
  458.4 12.9 %reshape.1111 = f32[4,4,48,4,768]{4,3,2,1,0:T(4,128)} reshape(f32[768,3072]{1,0:T(8,128)} %fusion.130) | data formatting | bytes 18874368 | tf_op jit(solution)/shard_map/reshape | solution.py:270
  471.3 8.8 %copy.109 = f32[4,4,48,4,768]{4,2,3,0,1:T(8,128)} copy(f32[4,4,48,4,768]{4,3,2,1,0:T(4,128)} %reshape.1111) | data formatting | bytes 18874368 | tf_op jit(solution)/shard_map/reshape | solution.py:270
  480.1 9.9 %fusion.7 = bf16[4,4,192,768]{3,2,1,0:T(8,128)(2,1)} fusion(f32[4,4,48,4,768]{4,2,3,0,1:T(8,128)} %copy.109, f32[4,4,192,768]{3,2,1,0:T(8,128)} %bitcast.522, pred[]{:T(512)S(6)} %eq.22), kind=kLoop, calls=%fused_computation.21 | loop fusion | flops 2359296 | bytes 23592960 | tf_op jit(solution)/shard_map/convert_element_type | solution.py:280
  506.3 12.4 %reshape.1118 = f32[4,4,48,4,768]{4,3,2,1,0:T(4,128)} reshape(f32[768,3072]{1,0:T(8,128)} %fusion.126) | data formatting | bytes 18874368 | tf_op jit(solution)/shard_map/reshape | solution.py:270
  518.7 9.1 %copy.119 = f32[4,4,48,4,768]{4,2,3,0,1:T(8,128)} copy(f32[4,4,48,4,768]{4,3,2,1,0:T(4,128)} %reshape.1118) | data formatting | bytes 18874368 | tf_op jit(solution)/shard_map/reshape | solution.py:270
  533.0 9.8 %fusion.5 = bf16[4,4,192,768]{3,2,1,0:T(8,128)(2,1)} fusion(f32[4,4,48,4,768]{4,2,3,0,1:T(8,128)} %copy.119, f32[4,4,192,768]{3,2,1,0:T(8,128)} %bitcast.524, pred[]{:T(512)S(6)} %eq.22), kind=kLoop, calls=%fused_computation.17 | loop fusion | flops 2359296 | bytes 23592960 | tf_op jit(solution)/shard_map/convert_element_type | solution.py:280
  568.3 16.5 %collective-permute-done.30 = bf16[2,112,768]{2,1,0:T(8,128)(2,1)S(1)} collective-permute-done((bf16[2,112,768]{2,1,0:T(8,128)(2,1)S(1)}, bf16[2,112,768]{2,1,0:T(8,128)(2,1)S(1)}, u32[]{:S(2)}, u32[]{:S(2)}) %collective-permute-start.30) | collective-permute-done | bytes 344096 | tf_op jit(solution)/shard_map/ppermute | solution.py:32
  598.4 9.4 %collective-permute-done.48 = bf16[2,96,768]{2,1,0:T(8,128)(2,1)S(1)} collective-permute-done((bf16[2,96,768]{2,1,0:T(8,128)(2,1)S(1)}, bf16[2,96,768]{2,1,0:T(8,128)(2,1)S(1)}, u32[]{:S(2)}, u32[]{:S(2)}) %collective-permute-start.48) | collective-permute-done | bytes 294944 | tf_op jit(solution)/shard_map/ppermute | solution.py:32
  609.1 9.5 %fusion.6 = f32[4,4,192,768]{3,2,1,0:T(8,128)} fusion(f32[4,4,48,4,768]{4,2,3,0,1:T(8,128)S(1)} %bitcast.519, bf16[4,4,192,768]{3,2,1,0:T(8,128)(2,1)} %collective-permute-done.36, f32[4,4,192,768]{3,2,1,0:T(8,128)} %bitcast.523, pred[]{:T(512)S(6)} %eq.22), kind=kLoop, calls=%fused_computation.20 | loop fusion | flops 7077888 | bytes 33030144 | tf_op jit(solution)/shard_map/add | solution.py:280
  623.8 9.2 %fusion.4 = f32[4,4,192,768]{3,2,1,0:T(8,128)} fusion(f32[4,4,48,4,768]{4,2,3,0,1:T(8,128)S(1)} %bitcast.521, bf16[4,4,192,768]{3,2,1,0:T(8,128)(2,1)} %collective-permute-done.50, f32[4,4,192,768]{3,2,1,0:T(8,128)} %bitcast.525, pred[]{:T(512)S(6)} %eq.22), kind=kLoop, calls=%fused_computation.16 | loop fusion | flops 7077888 | bytes 33030144 | tf_op jit(solution)/shard_map/add | solution.py:280
  655.3 22.4 %collective-permute-done.38 = bf16[4,192,768]{2,1,0:T(8,128)(2,1)S(1)} collective-permute-done((bf16[4,192,768]{2,1,0:T(8,128)(2,1)S(1)}, bf16[4,192,768]{2,1,0:T(8,128)(2,1)S(1)}, u32[]{:S(2)}, u32[]{:S(2)}) %collective-permute-start.38) | collective-permute-done | bytes 1179680 | tf_op jit(solution)/shard_map/ppermute | solution.py:32
  681.2 18.0 %collective-permute-done.52 = bf16[4,192,768]{2,1,0:T(8,128)(2,1)S(1)} collective-permute-done((bf16[4,192,768]{2,1,0:T(8,128)(2,1)S(1)}, bf16[4,192,768]{2,1,0:T(8,128)(2,1)S(1)}, u32[]{:S(2)}, u32[]{:S(2)}) %collective-permute-start.52) | collective-permute-done | bytes 1179680 | tf_op jit(solution)/shard_map/ppermute | solution.py:32
  711.3 15.0 %collective-permute-done.55 = bf16[2,192,768]{2,1,0:T(8,128)(2,1)S(1)} collective-permute-done((bf16[2,192,768]{2,1,0:T(8,128)(2,1)S(1)}, bf16[2,192,768]{2,1,0:T(8,128)(2,1)S(1)}, u32[]{:S(2)}, u32[]{:S(2)}) %collective-permute-start.55) | collective-permute-done | bytes 589856 | tf_op jit(solution)/shard_map/ppermute | solution.py:32
  (805 shorter events, 413.3 us)
Async XLA Ops:
  29.6 50.3 %collective-permute-start.2 = (bf16[2,112,768]{2,1,0:T(8,128)(2,1)S(1)}, bf16[2,112,768]{2,1,0:T(8,128)(2,1)S(1)}, u32[]{:S(2)}, u32[]{:S(2)}) collective-permute-start(bf16[2,112,768]{2,1,0:T(8,128)(2,1)S(1)} %maximum_select_fusion.11), channel_id=1, source_target_pairs={{0,8},{1,9},{2,10},{3,11},{4,12},{5,13},{6,14},{7,15},{8,0},{9,1},... | collective-permute-start | bytes 1032200 | tf_op jit(solution)/shard_map/ppermute | solution.py:32
  36.3 56.3 %collective-permute-start.9 = (bf16[2,192,768]{2,1,0:T(8,128)(2,1)S(1)}, bf16[2,192,768]{2,1,0:T(8,128)(2,1)S(1)}, u32[]{:S(2)}, u32[]{:S(2)}) collective-permute-start(bf16[2,192,768]{2,1,0:T(8,128)(2,1)S(1)} %maximum_select_fusion.7), channel_id=1, source_target_pairs={{0,8},{1,9},{2,10},{3,11},{4,12},{5,13},{6,14},{7,15},{8,0},{9,1},... | collective-permute-start | bytes 1769480 | tf_op jit(solution)/shard_map/ppermute | solution.py:32
  42.4 59.5 %collective-permute-start.23 = (bf16[2,192,768]{2,1,0:T(8,128)(2,1)S(1)}, bf16[2,192,768]{2,1,0:T(8,128)(2,1)S(1)}, u32[]{:S(2)}, u32[]{:S(2)}) collective-permute-start(bf16[2,192,768]{2,1,0:T(8,128)(2,1)S(1)} %maximum_select_fusion.10), channel_id=1, source_target_pairs={{0,8},{1,9},{2,10},{3,11},{4,12},{5,13},{6,14},{7,15},{8,0},{9,1},... | collective-permute-start | bytes 1769480 | tf_op jit(solution)/shard_map/ppermute | solution.py:32
  44.2 61.2 %collective-permute-start.17 = (bf16[4,96,768]{2,1,0:T(8,128)(2,1)S(1)}, bf16[4,96,768]{2,1,0:T(8,128)(2,1)S(1)}, u32[]{:S(2)}, u32[]{:S(2)}) collective-permute-start(bf16[4,96,768]{2,1,0:T(8,128)(2,1)S(1)} %maximum_select_fusion.9), channel_id=1, source_target_pairs={{0,1},{1,0},{2,3},{3,2},{4,5},{5,4},{6,7},{7,6},{8,9},{9,8},{10,11... | collective-permute-start | bytes 1769480 | tf_op jit(solution)/shard_map/ppermute | solution.py:32
  45.7 58.0 %collective-permute-start.18 = (bf16[4,96,768]{2,1,0:T(8,128)(2,1)S(1)}, bf16[4,96,768]{2,1,0:T(8,128)(2,1)S(1)}, u32[]{:S(2)}, u32[]{:S(2)}) collective-permute-start(bf16[4,96,768]{2,1,0:T(8,128)(2,1)S(1)} %maximum_select_fusion.9), channel_id=1, source_target_pairs={{0,2},{1,3},{2,0},{3,1},{4,6},{5,7},{6,4},{7,5},{8,10},{9,11},{10,... | collective-permute-start | bytes 1769480 | tf_op jit(solution)/shard_map/ppermute | solution.py:32
  101.9 44.2 %collective-permute-start.11 = (bf16[4,192,768]{2,1,0:T(8,128)(2,1)S(1)}, bf16[4,192,768]{2,1,0:T(8,128)(2,1)S(1)}, u32[]{:S(2)}, u32[]{:S(2)}) collective-permute-start(bf16[4,192,768]{2,1,0:T(8,128)(2,1)S(1)} %maximum_select_fusion.2), channel_id=1, source_target_pairs={{0,2},{1,3},{2,0},{3,1},{4,6},{5,7},{6,4},{7,5},{8,10},{9,11},{10,... | collective-permute-start | bytes 3538952 | tf_op jit(solution)/shard_map/ppermute | solution.py:32
  106.0 44.2 %collective-permute-start.10 = (bf16[4,192,768]{2,1,0:T(8,128)(2,1)S(1)}, bf16[4,192,768]{2,1,0:T(8,128)(2,1)S(1)}, u32[]{:S(2)}, u32[]{:S(2)}) collective-permute-start(bf16[4,192,768]{2,1,0:T(8,128)(2,1)S(1)} %maximum_select_fusion.2), channel_id=1, source_target_pairs={{0,1},{1,0},{2,3},{3,2},{4,5},{5,4},{6,7},{7,6},{8,9},{9,8},{10,11... | collective-permute-start | bytes 3538952 | tf_op jit(solution)/shard_map/ppermute | solution.py:32
  106.5 36.0 %collective-permute-start.5 = (bf16[2,112,768]{2,1,0:T(8,128)(2,1)S(1)}, bf16[2,112,768]{2,1,0:T(8,128)(2,1)S(1)}, u32[]{:S(2)}, u32[]{:S(2)}) collective-permute-start(bf16[2,112,768]{2,1,0:T(8,128)(2,1)S(1)} %slice.606), channel_id=1, source_target_pairs={{0,1},{1,0},{2,3},{3,2},{4,5},{5,4},{6,7},{7,6},{8,9},{9,8},{10,11... | collective-permute-start | bytes 1032200 | tf_op jit(solution)/shard_map/ppermute | solution.py:32
  136.5 60.5 %collective-permute-start.21 = (bf16[4,4,96,768]{3,2,1,0:T(8,128)(2,1)S(1)}, bf16[4,4,96,768]{3,2,1,0:T(8,128)(2,1)S(1)}, u32[]{:S(2)}, u32[]{:S(2)}) collective-permute-start(bf16[4,4,96,768]{3,2,1,0:T(8,128)(2,1)S(1)} %fusion.100), channel_id=1, source_target_pairs={{0,16},{1,17},{2,18},{3,19},{4,20},{5,21},{6,22},{7,23},{8,24},{9,... | collective-permute-start | bytes 7077896 | tf_op jit(solution)/shard_map/ppermute | solution.py:38
  146.1 56.2 %collective-permute-start.7 = (bf16[4,4,112,768]{3,2,0,1:T(8,128)(2,1)S(1)}, bf16[4,4,112,768]{3,2,0,1:T(8,128)(2,1)S(1)}, u32[]{:S(2)}, u32[]{:S(2)}) collective-permute-start(bf16[4,4,112,768]{3,2,0,1:T(8,128)(2,1)S(1)} %fusion.87), channel_id=1, source_target_pairs={{0,16},{1,17},{2,18},{3,19},{4,20},{5,21},{6,22},{7,23},{8,24},{9,... | collective-permute-start | bytes 8257544 | tf_op jit(solution)/shard_map/ppermute | solution.py:38
  150.2 35.8 %collective-permute-start.12 = (bf16[2,192,768]{2,1,0:T(8,128)(2,1)S(1)}, bf16[2,192,768]{2,1,0:T(8,128)(2,1)S(1)}, u32[]{:S(2)}, u32[]{:S(2)}) collective-permute-start(bf16[2,192,768]{2,1,0:T(8,128)(2,1)S(1)} %slice.623), channel_id=1, source_target_pairs={{0,1},{1,0},{2,3},{3,2},{4,5},{5,4},{6,7},{7,6},{8,9},{9,8},{10,11... | collective-permute-start | bytes 1769480 | tf_op jit(solution)/shard_map/ppermute | solution.py:32
  189.5 50.0 %collective-permute-start.14 = (bf16[4,4,192,768]{3,2,1,0:T(8,128)(2,1)}, bf16[4,4,192,768]{3,2,1,0:T(8,128)(2,1)}, u32[]{:S(2)}, u32[]{:S(2)}) collective-permute-start(bf16[4,4,192,768]{3,2,1,0:T(8,128)(2,1)} %fusion.68), channel_id=1, source_target_pairs={{0,16},{1,17},{2,18},{3,19},{4,20},{5,21},{6,22},{7,23},{8,24},{9,... | collective-permute-start | bytes 14155784 | tf_op jit(solution)/shard_map/ppermute | solution.py:38
  197.0 103.4 %collective-permute-start.28 = (bf16[4,4,192,768]{3,2,1,0:T(8,128)(2,1)}, bf16[4,4,192,768]{3,2,1,0:T(8,128)(2,1)}, u32[]{:S(2)}, u32[]{:S(2)}) collective-permute-start(bf16[4,4,192,768]{3,2,1,0:T(8,128)(2,1)} %fusion.70), channel_id=1, source_target_pairs={{0,16},{1,17},{2,18},{3,19},{4,20},{5,21},{6,22},{7,23},{8,24},{9,... | collective-permute-start | bytes 14155784 | tf_op jit(solution)/shard_map/ppermute | solution.py:38
  457.8 107.0 %collective-permute-start.29 = (bf16[4,4,112,768]{3,2,0,1:T(8,128)(2,1)}, bf16[4,4,112,768]{3,2,0,1:T(8,128)(2,1)}, u32[]{:S(2)}, u32[]{:S(2)}) collective-permute-start(bf16[4,4,112,768]{3,2,0,1:T(8,128)(2,1)} %select_convert_fusion), channel_id=1, source_target_pairs={{0,16},{1,17},{2,18},{3,19},{4,20},{5,21},{6,22},{7,23},{8,24},{9,... | collective-permute-start | bytes 8257544 | tf_op jit(solution)/shard_map/ppermute | solution.py:38
  490.0 119.1 %collective-permute-start.36 = (bf16[4,4,192,768]{3,2,1,0:T(8,128)(2,1)}, bf16[4,4,192,768]{3,2,1,0:T(8,128)(2,1)}, u32[]{:S(2)}, u32[]{:S(2)}) collective-permute-start(bf16[4,4,192,768]{3,2,1,0:T(8,128)(2,1)} %fusion.7), channel_id=1, source_target_pairs={{0,16},{1,17},{2,18},{3,19},{4,20},{5,21},{6,22},{7,23},{8,24},{9,... | collective-permute-start | bytes 14155784 | tf_op jit(solution)/shard_map/ppermute | solution.py:38
  499.0 49.1 %collective-permute-start.43 = (bf16[4,4,96,768]{3,2,1,0:T(8,128)(2,1)}, bf16[4,4,96,768]{3,2,1,0:T(8,128)(2,1)}, u32[]{:S(2)}, u32[]{:S(2)}) collective-permute-start(bf16[4,4,96,768]{3,2,1,0:T(8,128)(2,1)} %select_convert_fusion.1), channel_id=1, source_target_pairs={{0,16},{1,17},{2,18},{3,19},{4,20},{5,21},{6,22},{7,23},{8,24},{9,... | collective-permute-start | bytes 7077896 | tf_op jit(solution)/shard_map/ppermute | solution.py:38
  542.8 81.0 %collective-permute-start.50 = (bf16[4,4,192,768]{3,2,1,0:T(8,128)(2,1)}, bf16[4,4,192,768]{3,2,1,0:T(8,128)(2,1)}, u32[]{:S(2)}, u32[]{:S(2)}) collective-permute-start(bf16[4,4,192,768]{3,2,1,0:T(8,128)(2,1)} %fusion.5), channel_id=1, source_target_pairs={{0,16},{1,17},{2,18},{3,19},{4,20},{5,21},{6,22},{7,23},{8,24},{9,... | collective-permute-start | bytes 14155784 | tf_op jit(solution)/shard_map/ppermute | solution.py:38
  560.7 32.9 %collective-permute-start.45 = (bf16[4,96,768]{2,1,0:T(8,128)(2,1)}, bf16[4,96,768]{2,1,0:T(8,128)(2,1)}, u32[]{:S(2)}, u32[]{:S(2)}) collective-permute-start(bf16[4,96,768]{2,1,0:T(8,128)(2,1)} %pad_maximum_fusion.12), channel_id=1, source_target_pairs={{0,1},{1,0},{2,3},{3,2},{4,5},{5,4},{6,7},{7,6},{8,9},{9,8},{10,11... | collective-permute-start | bytes 1769480 | tf_op jit(solution)/shard_map/ppermute | solution.py:32
  563.3 31.9 %collective-permute-start.47 = (bf16[4,96,768]{2,1,0:T(8,128)(2,1)}, bf16[4,96,768]{2,1,0:T(8,128)(2,1)}, u32[]{:S(2)}, u32[]{:S(2)}) collective-permute-start(bf16[4,96,768]{2,1,0:T(8,128)(2,1)} %pad_maximum_fusion.13), channel_id=1, source_target_pairs={{0,2},{1,3},{2,0},{3,1},{4,6},{5,7},{6,4},{7,5},{8,10},{9,11},{10,... | collective-permute-start | bytes 1769480 | tf_op jit(solution)/shard_map/ppermute | solution.py:32
  607.9 46.1 %collective-permute-start.49 = (bf16[1,96,768]{2,1,0:T(8,128)(2,1)S(1)}, bf16[1,96,768]{2,1,0:T(8,128)(2,1)S(1)}, u32[]{:S(2)}, u32[]{:S(2)}) collective-permute-start(bf16[1,96,768]{2,1,0:T(8,128)(2,1)S(1)} %select_convert_fusion.9), channel_id=1, source_target_pairs={{0,4},{1,5},{2,6},{3,7},{4,0},{5,1},{6,2},{7,3},{8,12},{9,13},{10,... | collective-permute-start | bytes 442376 | tf_op jit(solution)/shard_map/ppermute | solution.py:32
  643.9 33.7 %collective-permute-start.38 = (bf16[4,192,768]{2,1,0:T(8,128)(2,1)S(1)}, bf16[4,192,768]{2,1,0:T(8,128)(2,1)S(1)}, u32[]{:S(2)}, u32[]{:S(2)}) collective-permute-start(bf16[4,192,768]{2,1,0:T(8,128)(2,1)S(1)} %pad_maximum_fusion.4), channel_id=1, source_target_pairs={{0,1},{1,0},{2,3},{3,2},{4,5},{5,4},{6,7},{7,6},{8,9},{9,8},{10,11... | collective-permute-start | bytes 3538952 | tf_op jit(solution)/shard_map/ppermute | solution.py:32
  652.8 46.4 %collective-permute-start.52 = (bf16[4,192,768]{2,1,0:T(8,128)(2,1)S(1)}, bf16[4,192,768]{2,1,0:T(8,128)(2,1)S(1)}, u32[]{:S(2)}, u32[]{:S(2)}) collective-permute-start(bf16[4,192,768]{2,1,0:T(8,128)(2,1)S(1)} %pad_maximum_fusion.6), channel_id=1, source_target_pairs={{0,1},{1,0},{2,3},{3,2},{4,5},{5,4},{6,7},{7,6},{8,9},{9,8},{10,11... | collective-permute-start | bytes 3538952 | tf_op jit(solution)/shard_map/ppermute | solution.py:32
  654.0 45.2 %collective-permute-start.54 = (bf16[4,192,768]{2,1,0:T(8,128)(2,1)S(1)}, bf16[4,192,768]{2,1,0:T(8,128)(2,1)S(1)}, u32[]{:S(2)}, u32[]{:S(2)}) collective-permute-start(bf16[4,192,768]{2,1,0:T(8,128)(2,1)S(1)} %pad_maximum_fusion.7), channel_id=1, source_target_pairs={{0,2},{1,3},{2,0},{3,1},{4,6},{5,7},{6,4},{7,5},{8,10},{9,11},{10,... | collective-permute-start | bytes 3538952 | tf_op jit(solution)/shard_map/ppermute | solution.py:32
  655.0 80.8 %collective-permute-start.58 = (f32[1,512,768]{2,1,0:T(8,128)S(1)}, f32[1,512,768]{2,1,0:T(8,128)S(1)}, u32[]{:S(2)}, u32[]{:S(2)}) collective-permute-start(f32[1,512,768]{2,1,0:T(8,128)S(1)} %copy-done.68), channel_id=1, source_target_pairs={{0,16},{1,17},{2,18},{3,19},{4,20},{5,21},{6,22},{7,23},{8,24},{9,... | collective-permute-start | bytes 4718600 | tf_op jit(solution)/shard_map/ppermute | solution.py:38
  (216 other events, 2480.8 us)

commit v2 on v1

v2 whole, which is shorter than its diff:
```python
import jax
import jax.numpy as jnp
from jax import lax
from jax.experimental import pallas as pl
from jax.experimental.pallas import tpu as pltpu
from jax.sharding import PartitionSpec as P

HEADS = 12
HDIM = 64
GROUP = 4
BLOCK = 128
PAD = 16
norm_eps = 1e-06
BF = jnp.bfloat16
F32 = jnp.float32
BOTH = ("section", "dp")
SCALE = HDIM ** (-0.5)

ERF_SCALE = 0.425
ERF_POLY = (
    0.11985147519825406,
    0.12072713574380309,
    0.10159474513684189,
    0.12334456743816431,
    -0.0435293372534038,
    0.19486821903107854,
    -0.15132025578595443,
    0.03446332841595847,
)


def dot(left, right, over_left=1, over_right=0):
    return lax.dot_general(
        left, right, (((over_left,), (over_right,)), ((), ())), preferred_element_type=F32
    )


def shape_of(shape, dtype):
    return jax.ShapeDtypeStruct(shape, dtype)


def whole_block(*shape):
    return pl.BlockSpec(shape, lambda g: (0,) * len(shape))


def gelu_pair(u):
    bell = jnp.exp(u * u * -0.5)
    t = 1.0 / (1.0 + (ERF_SCALE * 0.7071067811865476) * jnp.abs(u))
    poly = ERF_POLY[-1]
    for item in ERF_POLY[-2::-1]:
        poly = poly * t + item
    tail = bell * (poly * t)
    cdf = jnp.where(u < 0.0, tail, 1.0 - tail)
    return u * cdf, cdf + u * bell * 0.3989422804014327


def norm_stats(v):
    center = v - jnp.mean(v, axis=-1, keepdims=True)
    t = lax.rsqrt(jnp.mean(center * center, axis=-1, keepdims=True) + norm_eps)
    return center * t, t


def norm_back(dy, n, t, gain):
    dn = dy * gain
    mean = jnp.mean(dn, axis=-1, keepdims=True)
    along = jnp.mean(dn * n, axis=-1, keepdims=True)
    return t * (dn - mean - n * along)


def colsum(v):
    return jnp.sum(v, axis=0, keepdims=True)


def near(b, blocks):
    return max(0, b - 1) * BLOCK, min(blocks, b + 2) * BLOCK


def attn_fwd_kernel(
    a_ref, sq_ref, sk_ref, wq_ref, wk_ref, wv_ref, wo_ref, bias_ref, shift_ref,
    q_ref, k_ref, v_ref, o_ref, n_ref, t_ref, acc,
):
    step = pl.program_id(0)
    blocks = a_ref.shape[0] // BLOCK
    a = a_ref[...]
    q_ref[...] = (dot(a, wq_ref[0]) + bias_ref[0:1]).astype(BF)
    k_ref[...] = dot(a, wk_ref[0]).astype(BF)
    v_ref[...] = (dot(a, wv_ref[0]) + bias_ref[1:2]).astype(BF)
    lane = lax.broadcasted_iota(jnp.int32, (BLOCK, 2 * HDIM), 1)
    for b in range(blocks):
        lo, hi = near(b, blocks)
        rows = slice(b * BLOCK, (b + 1) * BLOCK)
        same = sq_ref[rows, 0:1] == sk_ref[0:1, lo:hi]
        for pair in range(GROUP // 2):
            lanes = slice(pair * 2 * HDIM, (pair + 1) * 2 * HDIM)
            query = q_ref[rows, lanes]
            keys = k_ref[lo:hi, lanes]
            value = v_ref[lo:hi, lanes]
            out = []
            for mine in (lane < HDIM, lane >= HDIM):
                scores = dot(jnp.where(mine, query, jnp.zeros_like(query)), keys, 1, 1) * SCALE
                scores = jnp.where(same, scores, -1000000000.0)
                grown = jnp.exp(scores - jnp.max(scores, axis=-1, keepdims=True))
                probs = grown * (1.0 / jnp.sum(grown, axis=-1, keepdims=True))
                out.append(dot(probs.astype(BF), value))
            o_ref[rows, lanes] = jnp.where(lane < HDIM, out[0], out[1]).astype(BF)
    part = dot(o_ref[...], wo_ref[0])

    @pl.when(step == 0)
    def _():
        acc[...] = a.astype(F32) + shift_ref[2:3] + part

    @pl.when(step != 0)
    def _():
        acc[...] += part

    @pl.when(step == pl.num_programs(0) - 1)
    def _():
        n, t = norm_stats(acc[...])
        n_ref[...] = n
        t_ref[...] = jnp.broadcast_to(t, t_ref.shape)


def attn_weight_blocks(width, cols):
    def column(j):
        return pl.BlockSpec((1, width, cols), lambda g: (j, 0, g))

    return [column(0), column(1), column(2), pl.BlockSpec((1, cols, width), lambda g: (3, g, 0))]


def attn_fwd(a, seg_col, seg_row, w4, shift):
    length, width = a.shape
    cols = GROUP * HDIM
    group = pl.BlockSpec((length, cols), lambda g: (0, g))
    return pl.pallas_call(
        attn_fwd_kernel,
        grid=(HEADS // GROUP,),
        in_specs=[whole_block(length, width), whole_block(length, 128), whole_block(8, length)]
        + attn_weight_blocks(width, cols)
        + [pl.BlockSpec((8, cols), lambda g: (0, g)), whole_block(8, width)],
        out_specs=[group] * 4 + [whole_block(length, width), whole_block(length, 128)],
        out_shape=[shape_of((length, width), BF)] * 4
        + [shape_of((length, width), F32), shape_of((length, 128), F32)],
        scratch_shapes=[pltpu.VMEM((length, width), F32)],
        name="attn_fwd",
    )(a, seg_col, seg_row, w4, w4, w4, w4, shift, shift)


def ffn_fwd_kernel(
    n1_ref, up_ref, cup_ref, down_ref, gain_ref, shift_ref,
    g_ref, gp_ref, n_ref, t_ref, y_ref, h1, acc,
):
    step = pl.program_id(0)
    half = n1_ref.shape[0] // 2

    @pl.when(step == 0)
    def _():
        hidden = n1_ref[...] * gain_ref[0:1] + shift_ref[4:5]
        h1[...] = hidden.astype(BF)
        acc[...] = hidden + shift_ref[3:4]

    for r in range(2):
        rows = slice(r * half, (r + 1) * half)
        g, slope = gelu_pair(dot(h1[rows], up_ref[0]) + cup_ref[0])
        g = g.astype(BF)
        g_ref[rows] = g
        gp_ref[rows] = slope.astype(BF)
        acc[rows] += dot(g, down_ref[...])

    @pl.when(step == pl.num_programs(0) - 1)
    def _():
        n, t = norm_stats(acc[...])
        n_ref[...] = n
        t_ref[...] = jnp.broadcast_to(t, t_ref.shape)
        y_ref[...] = (n * gain_ref[1:2] + shift_ref[5:6]).astype(BF)


def ffn_fwd(n1, up, cup, down, gain, shift):
    length, width = n1.shape
    units = up.shape[0]
    column = pl.BlockSpec((length, width), lambda g: (0, g))
    return pl.pallas_call(
        ffn_fwd_kernel,
        grid=(units,),
        in_specs=[
            whole_block(length, width),
            pl.BlockSpec((1, width, width), lambda g: (g, 0, 0)),
            pl.BlockSpec((1, 1, width), lambda g: (g, 0, 0)),
            pl.BlockSpec((width, width), lambda g: (g, 0)),
            whole_block(8, width),
            whole_block(8, width),
        ],
        out_specs=[column, column, whole_block(length, width), whole_block(length, 128), whole_block(length, width)],
        out_shape=[shape_of((length, units * width), BF)] * 2
        + [shape_of((length, width), F32), shape_of((length, 128), F32), shape_of((length, width), BF)],
        scratch_shapes=[pltpu.VMEM((length, width), BF), pltpu.VMEM((length, width), F32)],
        name="ffn_fwd",
    )(n1, up, cup.reshape(units, 1, width), down, gain, shift)


def by_section(section, action):
    for plane in range(2):
        pl.when(section == plane)(lambda plane=plane: action(plane))


def copy_all(copies, start):
    for item in copies:
        if start:
            item.start()
        else:
            item.wait()


def ffn_bwd_kernel(
    place_ref, dy_ref, n2_ref, t2_ref, g_ref, gp_ref, up_ref, down_ref, n1_ref, t1_ref, gain_ref, shift_ref,
    keep_ref, send_ref, dr1_ref, sums_ref, cup_ref, h1, df, acc, gup, gdown, sem,
):
    step = pl.program_id(0)
    last = pl.num_programs(0) - 1
    quads = keep_ref.shape[0]
    outer = keep_ref.shape[1]
    width = h1.shape[1]
    size = width // (quads * outer)

    @pl.when(step == 0)
    def _():
        n2 = n2_ref[...]
        dy = dy_ref[...].astype(F32)
        dr2 = norm_back(dy, n2, t2_ref[:, 0:1], gain_ref[1:2])
        low = dr2.astype(BF)
        df[...] = low
        acc[...] = dr2
        h1[...] = (n1_ref[...] * gain_ref[0:1] + shift_ref[4:5]).astype(BF)
        sums_ref[...] = jnp.zeros_like(sums_ref)
        sums_ref[1:2] = colsum(dy * n2)
        sums_ref[2:3] = colsum(dy)
        sums_ref[3:4] = colsum(low.astype(F32))

    d = df[...]
    down = dot(g_ref[...], d, 0, 0).astype(BF)
    gdown[step] = down.reshape(quads, width // quads, width)
    du = (dot(d, down_ref[...], 1, 1) * gp_ref[...].astype(F32)).astype(BF)
    cup_ref[0] = colsum(du.astype(F32))
    up = dot(h1[...], du, 0, 0).astype(BF)
    gup[step] = up.reshape(outer, quads, size, width)
    acc[...] += dot(du, up_ref[0], 1, 1)

    def copies(j, plane):
        up_to, down_to = (keep_ref, send_ref) if plane == 0 else (send_ref, keep_ref)
        out = []
        for q in range(quads):
            rel = q ^ place_ref[0]
            out.append(
                pltpu.make_async_copy(
                    gup.at[j, :, q], up_to.at[rel, :, j * size : (j + 1) * size, :], sem.at[j, 0, q]
                )
            )
            out.append(pltpu.make_async_copy(gdown.at[j, q], down_to.at[rel, j], sem.at[j, 1, q]))
        return out

    for j in range(gup.shape[0]):
        @pl.when(step == j)
        def _(j=j):
            by_section(place_ref[1], lambda plane: copy_all(copies(j, plane), True))

    @pl.when(step == last)
    def _():
        dh = acc[...]
        n1 = n1_ref[...]
        dr1_ref[...] = norm_back(dh, n1, t1_ref[:, 0:1], gain_ref[0:1])
        sums_ref[0:1] = colsum(dh * n1)
        sums_ref[4:5] = colsum(dh)

        def finish(plane):
            for j in range(gup.shape[0]):
                copy_all(copies(j, plane), False)

        by_section(place_ref[1], finish)


def ffn_bwd(place, outer, dy, n2, t2, g, gp, up, down, n1, t1, gain, shift):
    length, width = n1.shape
    units = up.shape[0]
    size = width // (4 * outer)
    column = pl.BlockSpec((length, width), lambda g: (0, g))
    chunk = shape_of((4, outer, units * size, width), BF)
    return pl.pallas_call(
        ffn_bwd_kernel,
        grid=(units,),
        in_specs=[
            pl.BlockSpec(memory_space=pltpu.SMEM),
            whole_block(length, width),
            whole_block(length, width),
            whole_block(length, 128),
            column,
            column,
            pl.BlockSpec((1, width, width), lambda g: (g, 0, 0)),
            pl.BlockSpec((width, width), lambda g: (g, 0)),
            whole_block(length, width),
            whole_block(length, 128),
            whole_block(8, width),
            whole_block(8, width),
        ],
        out_specs=[
            pl.BlockSpec(memory_space=pl.ANY),
            pl.BlockSpec(memory_space=pl.ANY),
            whole_block(length, width),
            whole_block(8, width),
            pl.BlockSpec((1, 1, width), lambda g: (g, 0, 0)),
        ],
        out_shape=[chunk, chunk, shape_of((length, width), F32), shape_of((8, width), F32), shape_of((units, 1, width), F32)],
        scratch_shapes=[
            pltpu.VMEM((length, width), BF),
            pltpu.VMEM((length, width), BF),
            pltpu.VMEM((length, width), F32),
            pltpu.VMEM((units, outer, 4, size, width), BF),
            pltpu.VMEM((units, 4, width // 4, width), BF),
            pltpu.SemaphoreType.DMA((units, 2, 4)),
        ],
        name="ffn_bwd",
    )(place, dy, n2, t2, g, gp, up, down, n1, t1, gain, shift)


def attn_bwd_kernel(
    place_ref, dr_ref, a_ref, sq_ref, sk_ref, q_ref, k_ref, v_ref, o_ref, wq_ref, wk_ref, wv_ref, wo_ref,
    keep_ref, send_ref, da_ref, sums_ref, sumo_ref, dat, do_sc, dq, dk, dv, grads, sem,
):
    step = pl.program_id(0)
    length, width = a_ref.shape
    blocks = length // BLOCK
    quads = keep_ref.shape[0]
    outer = keep_ref.shape[1]
    size = width // (quads * outer)
    cols = GROUP * HDIM

    @pl.when(step == 0)
    def _():
        low = dr_ref[...].astype(BF)
        dat[...] = low
        da_ref[...] = dr_ref[...]
        sumo_ref[...] = jnp.zeros_like(sumo_ref)
        sumo_ref[0:1] = colsum(low.astype(F32))

    d = dat[...]
    grad_o = dot(o_ref[...], d, 0, 0).astype(BF)
    do_sc[...] = dot(d, wo_ref[0], 1, 1).astype(BF)
    dk[...] = jnp.zeros_like(dk)
    dv[...] = jnp.zeros_like(dv)
    lane = lax.broadcasted_iota(jnp.int32, (BLOCK, 2 * HDIM), 1)
    for b in range(blocks):
        lo, hi = near(b, blocks)
        rows = slice(b * BLOCK, (b + 1) * BLOCK)
        same = sk_ref[lo:hi, 0:1] == sq_ref[0:1, rows]
        for pair in range(GROUP // 2):
            lanes = slice(pair * 2 * HDIM, (pair + 1) * 2 * HDIM)
            query = q_ref[rows, lanes]
            d_out = do_sc[rows, lanes]
            keys = k_ref[lo:hi, lanes]
            value = v_ref[lo:hi, lanes]
            dqs, dks, dvs = [], [], []
            for mine in (lane < HDIM, lane >= HDIM):
                q_head = jnp.where(mine, query, jnp.zeros_like(query))
                do_head = jnp.where(mine, d_out, jnp.zeros_like(d_out))
                scores = jnp.where(same, dot(keys, q_head, 1, 1) * SCALE, -1000000000.0)
                grown = jnp.exp(scores - jnp.max(scores, axis=0, keepdims=True))
                probs = grown * (1.0 / jnp.sum(grown, axis=0, keepdims=True))
                d_probs = dot(value, do_head, 1, 1)
                d_scores = probs * (d_probs - jnp.sum(probs * d_probs, axis=0, keepdims=True))
                d_scores = d_scores.astype(BF)
                dvs.append(dot(probs.astype(BF), do_head))
                dks.append(dot(d_scores, q_head))
                dqs.append(dot(d_scores, keys, 0, 0))
            dq[rows, lanes] = jnp.where(lane < HDIM, dqs[0], dqs[1]) * SCALE
            dv[lo:hi, lanes] += dvs[0] + dvs[1]
            dk[lo:hi, lanes] += dks[0] + dks[1]
    a = a_ref[...]
    out = da_ref[...]
    lows = (dq[...].astype(BF), (dk[...] * SCALE).astype(BF), dv[...].astype(BF))
    made = []
    for low, w_ref in zip(lows, (wq_ref, wk_ref, wv_ref)):
        made.append(dot(a, low, 0, 0).astype(BF))
        out = out + dot(low, w_ref[0], 1, 1)
    da_ref[...] = out
    sums_ref[...] = jnp.zeros_like(sums_ref)
    sums_ref[0:1] = colsum(lows[0].astype(F32))
    sums_ref[1:2] = colsum(lows[2].astype(F32))
    steps = HEADS // GROUP
    for j in range(steps):
        @pl.when(step == j)
        def _(j=j):
            here = slice(j * cols, (j + 1) * cols)
            for unit in range(3):
                grads[unit, :, here] = made[unit]
            grads[3, here, :] = grad_o

    @pl.when(step == steps - 1)
    def _():
        def copies(plane):
            out = []
            for unit in range(4):
                to = keep_ref if unit // 2 == plane else send_ref
                at = (unit % 2) * size
                for block in range(quads * outer):
                    rel = (block % quads) ^ place_ref[0]
                    out.append(
                        pltpu.make_async_copy(
                            grads.at[unit, block * size : (block + 1) * size, :],
                            to.at[rel, block // quads, at : at + size, :],
                            sem.at[unit, block],
                        )
                    )
            return out

        def move(plane):
            items = copies(plane)
            copy_all(items, True)
            copy_all(items, False)

        by_section(place_ref[1], move)


def attn_bwd(place, outer, dr, a, seg_col, seg_row, q, k, v, o, w4):
    length, width = a.shape
    size = width // (4 * outer)
    cols = GROUP * HDIM
    group = pl.BlockSpec((length, cols), lambda g: (0, g))
    chunk = shape_of((4, outer, 2 * size, width), BF)
    return pl.pallas_call(
        attn_bwd_kernel,
        grid=(HEADS // GROUP,),
        in_specs=[
            pl.BlockSpec(memory_space=pltpu.SMEM),
            whole_block(length, width),
            whole_block(length, width),
            whole_block(8, length),
            whole_block(length, 128),
        ]
        + [group] * 4
        + attn_weight_blocks(width, cols),
        out_specs=[
            pl.BlockSpec(memory_space=pl.ANY),
            pl.BlockSpec(memory_space=pl.ANY),
            whole_block(length, width),
            pl.BlockSpec((8, cols), lambda g: (0, g)),
            whole_block(8, width),
        ],
        out_shape=[chunk, chunk, shape_of((length, width), F32), shape_of((8, width), F32), shape_of((8, width), F32)],
        scratch_shapes=[pltpu.VMEM((length, width), BF), pltpu.VMEM((length, cols), BF)]
        + [pltpu.VMEM((length, cols), F32)] * 3
        + [pltpu.VMEM((4, width, width), BF), pltpu.SemaphoreType.DMA((4, 4 * outer))],
        name="attn_bwd",
    )(place, dr, a, seg_row, seg_col, q, k, v, o, w4, w4, w4, w4)


def flip(value, mask):
    count = lax.axis_size("dp")
    pairs = [(s * count + i, s * count + (i ^ mask)) for s in range(2) for i in range(count)]
    return lax.ppermute(value, BOTH, pairs)


def swap(value):
    count = lax.axis_size("dp")
    pairs = [(s * count + i, (1 - s) * count + i) for s in range(2) for i in range(count)]
    return lax.ppermute(value, BOTH, pairs)


def after(values, *done):
    leaves, tree = jax.tree.flatten(values)
    return jax.tree.unflatten(tree, lax.optimization_barrier((*leaves, *done))[: len(leaves)])


def double(own, bit):
    other = flip(own, bit)
    high = (lax.axis_index("dp") & bit) != 0
    return jnp.where(high, jnp.concatenate([other, own]), jnp.concatenate([own, other]))


def outer_first(block):
    own, bit = block[None], 4
    while bit < lax.axis_size("dp") // 2:
        own = double(own, bit)
        bit *= 2
    return own


def outer_last(own):
    return double(own, lax.axis_size("dp") // 2)


def near_quad(own):
    return flip(own, 1), flip(own, 2)


def far_quad(from_x, from_y):
    half = from_x.shape[0] // 2
    return flip(from_y[:half], 1), flip(from_x[half:], 2)


def spread(own, quads):
    (from_x, from_y), (diag_low, diag_high) = quads
    half = own.shape[0] // 2
    return ((own, 0, 0), (from_x, 0, 1), (from_y, 0, 2), (diag_low, 0, 3), (diag_high, half, 3))


def assemble_kernel(attn, units, size, layout, place_ref, *refs):
    pieces = len(layout)
    mine, other = refs[:pieces], refs[pieces : 2 * pieces]
    outs, sem = refs[2 * pieces : -1], refs[-1]

    def copies(plane):
        out = []
        count = 0
        for which, group in ((plane, mine), (1 - plane, other)):
            for (outer, start, rel), ref in zip(layout, group):
                q = rel ^ place_ref[0]
                span = slice(start, start + outer)
                if attn:
                    moves = [
                        (ref.at[:, u * size : (u + 1) * size, :], outs[0].at[2 * which + u, span, q])
                        for u in range(2)
                    ]
                elif which == 0:
                    moves = [
                        (ref.at[:, u * size : (u + 1) * size, :], outs[0].at[u, span, q]) for u in range(units)
                    ]
                else:
                    moves = [(ref, outs[1].at[span, q])]
                for source, target in moves:
                    out.append(pltpu.make_async_copy(source, target, sem.at[count]))
                    count += 1
        return out

    def move(plane):
        items = copies(plane)
        copy_all(items, True)
        copy_all(items, False)

    by_section(place_ref[1], move)


def assemble(attn, place, units, size, own_quads, other_quads):
    own, other = spread(*own_quads), spread(*other_quads)
    layout = tuple((piece.shape[0], start, rel) for piece, start, rel in own)
    outer, _, width = own[0][0].shape
    if size % PAD == 0:
        if attn:
            shapes = [(4, outer, 4, size, width)]
        else:
            shapes = [(units, outer, 4, size, width), (outer, 4, units * size, width)]
        anywhere = pl.BlockSpec(memory_space=pl.ANY)
        outs = pl.pallas_call(
            lambda *refs: assemble_kernel(attn, units, size, layout, *refs),
            in_specs=[pl.BlockSpec(memory_space=pltpu.SMEM)] + [anywhere] * (2 * len(layout)),
            out_specs=[pl.BlockSpec(memory_space=pltpu.VMEM)] * len(shapes),
            out_shape=[shape_of(shape, BF) for shape in shapes],
            scratch_shapes=[pltpu.SemaphoreType.DMA((2 * len(layout) * units,))],
            name="assemble",
        )(place, *[piece for piece, _, _ in own], *[piece for piece, _, _ in other])
    else:
        planes = []
        for pieces in (own, other):
            whole = jnp.zeros((outer, 4) + own[0][0].shape[1:], BF)
            for piece, start, rel in pieces:
                whole = lax.dynamic_update_slice(whole, piece[:, None], (start, place[0] ^ rel, 0, 0))
            planes.append(whole.reshape(4 * outer, -1, width))
        first = place[1] == 0
        low = jnp.where(first, planes[0], planes[1])
        high = jnp.where(first, planes[1], planes[0])

        def unit(array, j):
            return array[:, j * size : (j + 1) * size].reshape(width, width)

        if attn:
            outs = [jnp.stack([unit(low, 0), unit(low, 1), unit(high, 0), unit(high, 1)])]
        else:
            outs = [jnp.stack([unit(low, j) for j in range(units)]), high]
    if attn:
        return outs[0].reshape(4, width, width)
    return outs[0].reshape(units, width, width), outs[1].reshape(units * width, width)


def in_chips(chunk, place, units, count):
    if count == 16:
        return chunk
    quads, outer, rows, width = chunk.shape
    size = width // count
    natural = chunk.reshape(quads, outer, units, -1, width).transpose(2, 1, 0, 3, 4)
    block = natural.reshape(units, count // 4, 4, size, width).transpose(2, 1, 0, 3, 4)
    return relative(block.reshape(4, count // 4, units * size, width), place)


def down_in_chips(chunk, place, count):
    if count == 16:
        return chunk
    width = chunk.shape[3]
    natural = chunk.transpose(1, 0, 2, 3).reshape(count // 4, 4, -1, width)
    return relative(natural.transpose(1, 0, 2, 3), place)


def relative(block, place):
    return jnp.stack([lax.dynamic_index_in_dim(block, place[0] ^ rel, 0, False) for rel in range(4)])


def low(value):
    return value.astype(BF)


class Reduce:
    def __init__(self, keep, send):
        self.keep, self.got = keep, swap(send)

    def part(self, rel, span=slice(None)):
        return self.keep[rel, span].astype(F32) + self.got[rel, span].astype(F32)

    def start_far(self):
        half = self.keep.shape[1] // 2
        self.halves = (slice(0, half), slice(half, None))
        self.far = [low(self.part(3, span)) for span in self.halves]
        self.by = [flip(item, mask) for item, mask in zip(self.far, (1, 2))]
        return self.far

    def start_near(self):
        first, second = self.halves
        to_y = jnp.concatenate([low(self.part(2, first) + self.by[0]), low(self.part(2, second))])
        to_x = jnp.concatenate([low(self.part(1, first)), low(self.part(1, second) + self.by[1])])
        self.near = [to_x, to_y]
        self.quad = [flip(to_x, 1), flip(to_y, 2)]
        return self.near

    def start_outer(self):
        rest = self.part(0) + self.quad[0].astype(F32) + self.quad[1].astype(F32)
        self.bit = lax.axis_size("dp") // 2
        return self.halve(rest)

    def halve(self, rest):
        size = rest.shape[0] // 2
        high = (lax.axis_index("dp") & self.bit) != 0
        self.rest = jnp.where(high, rest[size:], rest[:size])
        sent = low(jnp.where(high, rest[:size], rest[size:]))
        self.there = flip(sent, self.bit)
        return [sent]

    def next_outer(self):
        self.bit //= 2
        return self.halve(self.rest + self.there.astype(F32))

    def finish(self):
        while self.bit > 4:
            self.next_outer()
        return (self.rest + self.there.astype(F32))[0]


def shards(tokens, segment_ids, cotangent, qkv_w, out_w, up_w, down_w, gains_w, shifts_w, up_b, head_w):
    count = lax.axis_size("dp")
    section = lax.axis_index("section")
    me = lax.axis_index("dp")
    first = section == 0
    place = jnp.stack([me & 3, section]).astype(jnp.int32)
    grad_place = place if count == 16 else jnp.stack([jnp.zeros_like(section), section]).astype(jnp.int32)
    rows_dev, length, width = tokens.shape
    mine = rows_dev // 2
    size = width // count
    ff = up_w.shape[2]
    units = ff // width

    def cols(array, n):
        return [array[:, j * width : (j + 1) * width] for j in range(n)]

    q_u, k_u, v_u = cols(low(qkv_w[0]), 3)
    plane = (
        jnp.concatenate([q_u, k_u] + cols(low(up_w[0]), units)),
        jnp.concatenate([v_u, low(out_w[0]), low(down_w[0])]),
    )
    got = swap(jnp.where(first, plane[1], plane[0]))
    zero = jnp.where(first, plane[0], got)
    one = jnp.where(first, got, plane[1])
    small = low(jnp.concatenate([gains_w.reshape(-1), shifts_w.reshape(-1), up_b.reshape(-1)]))
    small_n = small.shape[0]
    small_rows = -(-small_n // width)
    head_n = head_w.shape[0] * head_w.shape[1]
    head_rows = -(-head_n // width)
    pad_rows = -(-(small_rows + head_rows) // PAD) * PAD

    def to_rows(flat, rows):
        return jnp.pad(flat, (0, rows * width - flat.shape[0])).reshape(rows, width)

    extra = jnp.concatenate(
        [
            to_rows(small, small_rows),
            to_rows(low(head_w).reshape(-1), head_rows),
            jnp.zeros((pad_rows - small_rows - head_rows, width), BF),
        ]
    )
    cut = 2 * size

    a0_one = outer_first(jnp.concatenate([zero[:cut], extra]))
    f0_one = outer_first(after(zero[cut:], a0_one))
    a0_own = outer_last(a0_one)
    a1_one = outer_first(after(one[:cut], a0_own))
    f0_own = outer_last(f0_one)
    f1_one = outer_first(after(one[cut:], f0_own))
    a1_own = outer_last(a1_one)
    f1_own = outer_last(f1_one)

    def both(own, near, far):
        return (own, (near, far)), jax.tree.map(swap, (own, (near, far)))

    a0_near = near_quad(a0_own)
    a0_all = both(a0_own, a0_near, far_quad(*a0_near))
    w4_0 = assemble(True, place, 2, size, *a0_all)

    smalls, heads = [], []
    tails = [jax.tree.map(lambda item: item[:, cut:], item) for item in a0_all]
    tails_full = []
    for own, quads in tails:
        whole = jnp.zeros((4,) + own.shape, BF)
        for piece, start, rel in spread(own, quads):
            whole = lax.dynamic_update_slice(whole, piece[None], (place[0] ^ rel, start, 0, 0))
        tails_full.append(whole.transpose(1, 0, 2, 3).reshape(count, pad_rows, width))
    tails_full = (
        jnp.where(first, tails_full[0], tails_full[1]),
        jnp.where(first, tails_full[1], tails_full[0]),
    )
    n_g = gains_w.shape[1] * size
    n_s = shifts_w.shape[1] * size
    for tail in tails_full:
        flat = tail[:, :small_rows].reshape(count, -1)[:, :small_n].astype(F32)
        gains = flat[:, :n_g].reshape(count, -1, size).transpose(1, 0, 2).reshape(-1, width)
        shift = flat[:, n_g : n_g + n_s].reshape(count, -1, size).transpose(1, 0, 2).reshape(-1, width)
        cup = flat[:, n_g + n_s :].reshape(-1)
        eight = lambda item: jnp.pad(item, ((0, 8 - item.shape[0]), (0, 0)))
        smalls.append((eight(gains), eight(shift), cup))
        block = tail[:, small_rows : small_rows + head_rows].reshape(count, -1)[:, :head_n]
        heads.append(block.reshape(count * head_w.shape[0], head_w.shape[1]))
    head = jnp.concatenate(heads)
    (gain0, shift0, cup0), (gain1, shift1, cup1) = smalls

    own = lax.dynamic_slice_in_dim(tokens, section * mine, mine, 0)
    seg = lax.dynamic_slice_in_dim(segment_ids, section * mine, mine, 0)
    cot = lax.dynamic_slice_in_dim(cotangent, section * mine, mine, 0)
    rows = range(mine)
    seg_col = [jnp.broadcast_to(seg[r][:, None], (length, 128)) for r in rows]
    seg_row = [jnp.broadcast_to(seg[r][None], (8, length)) for r in rows]

    f0_near = near_quad(f0_own)
    a0 = after([own[r] for r in rows], f0_own, a1_one)
    kept_a0 = [attn_fwd(a0[r], seg_col[r], seg_row[r], w4_0, shift0) for r in rows]
    n1 = [kept[4] for kept in kept_a0]
    f0_near = after(f0_near, *n1)
    a1_own = after(a1_own, *n1)
    f1_one = after(f1_one, *n1)
    f0_all = both(f0_own, f0_near, far_quad(*f0_near))
    a1_near = near_quad(a1_own)
    f1_own = outer_last(f1_one)
    up0, down0 = assemble(False, place, units, size, *f0_all)
    n1 = after(n1, a1_own, f1_one)
    kept_f0 = [ffn_fwd(n1[r], up0, cup0, down0, gain0, shift0) for r in rows]
    a1 = [kept[4] for kept in kept_f0]
    a1_near = after(a1_near, *a1)
    f1_own = after(f1_own, *a1)
    a1_all = both(a1_own, a1_near, far_quad(*a1_near))
    f1_near = near_quad(f1_own)
    w4_1 = assemble(True, place, 2, size, *a1_all)
    a1 = after(a1, f1_own)
    kept_a1 = [attn_fwd(a1[r], seg_col[r], seg_row[r], w4_1, shift1) for r in rows]
    n1 = [kept[4] for kept in kept_a1]
    f1_near = after(f1_near, *n1)
    f1_all = both(f1_own, f1_near, far_quad(*f1_near))
    up1, down1 = assemble(False, place, units, size, *f1_all)
    kept_f1 = [ffn_fwd(n1[r], up1, cup1, down1, gain1, shift1) for r in rows]

    d_y1, g_head = [], 0.0
    for r in rows:
        y1 = kept_f1[r][4]
        proj = dot(y1, head)
        rho = lax.rsqrt(jnp.sum(proj * proj, axis=-1, keepdims=True) + norm_eps)
        c = cot[r].astype(F32)
        d_proj = low(rho * c - rho * rho * rho * proj * jnp.sum(proj * c, axis=-1, keepdims=True))
        g_head = g_head + dot(y1, d_proj, 0, 0)
        d_y1.append(dot(d_proj, head, 1, 1))

    def total(items):
        out = items[0]
        for item in items[1:]:
            out = jax.tree.map(lambda x, y: (x.astype(F32) + y.astype(F32)).astype(x.dtype), out, item)
        return out

    def ffn_back(d_out, kept_a, kept_f, up, down, gain, shift):
        outs = [
            ffn_bwd(grad_place, 4, d_out[r], *kept_f[r][2:4], *kept_f[r][:2], up, down, *kept_a[r][4:6], gain, shift)
            for r in rows
        ]
        keep, send, sums, cup = total([(o[0], o[1], o[3], o[4]) for o in outs])
        if count != 16:
            as_up = [in_chips(item, place, units, count) for item in (keep, send)]
            as_down = [down_in_chips(item, place, count) for item in (keep, send)]
            keep = jnp.where(first, as_up[0], as_down[0])
            send = jnp.where(first, as_down[1], as_up[1])
        return keep, send, [o[2] for o in outs], sums, cup

    def attn_back(d_out, a, kept, w4):
        outs = [attn_bwd(grad_place, 4, d_out[r], a[r], seg_col[r], seg_row[r], *kept[r][:4], w4) for r in rows]
        keep, send, sums, sumo = total([(o[0], o[1], o[3], o[4]) for o in outs])
        keep, send = [in_chips(item, place, 2, count) for item in (keep, send)]
        return keep, send, [o[2] for o in outs], sums, sumo

    keep, send, d_r, sums_f1, g_cup1 = ffn_back(d_y1, kept_a1, kept_f1, up1, down1, gain1, shift1)
    red_f1 = Reduce(keep, send)
    d_r = after(d_r, *red_f1.start_far())
    keep, send, d_a1, sums_a1, sumo_a1 = attn_back(d_r, a1, kept_a1, w4_1)
    red_f1.by = after(red_f1.by, *d_a1)
    d_y0 = after([low(item) for item in d_a1], *red_f1.start_near())
    red_a1 = Reduce(keep, send)
    d_y0 = after(d_y0, *red_a1.start_far())
    keep, send, d_r, sums_f0, g_cup0 = ffn_back(d_y0, kept_a0, kept_f0, up0, down0, gain0, shift0)
    red_f1.quad = after(red_f1.quad, *d_r)
    red_a1.by = after(red_a1.by, *d_r)
    d_r = after(d_r, *red_f1.start_outer(), *red_a1.start_near())
    red_f0 = Reduce(keep, send)
    d_r = after(d_r, *red_f0.start_far())
    keep, send, d_a0, sums_a0, sumo_a0 = attn_back(d_r, a0, kept_a0, w4_0)
    red_f1.there = after(red_f1.there, *d_a0)
    red_a1.quad = after(red_a1.quad, *d_a0)
    red_f0.by = after(red_f0.by, *d_a0)

    def small_block(sums_a, sumo, sums_f, g_cup, head_part):
        gains = jnp.stack([sums_f[0], sums_f[1]]).reshape(2, count, size).transpose(1, 0, 2)
        shift = jnp.stack([sums_a[0], sums_a[1], sumo[0], sums_f[3], sums_f[4], sums_f[2]])
        shift = shift.reshape(6, count, size).transpose(1, 0, 2)
        flat = jnp.concatenate(
            [gains.reshape(count, -1), shift.reshape(count, -1), g_cup.reshape(count, -1)], axis=1
        )
        flat = jnp.pad(flat, ((0, 0), (0, small_rows * width - small_n)))
        piece = jnp.pad(head_part.reshape(count, -1), ((0, 0), (0, head_rows * width - head_n)))
        block = jnp.concatenate(
            [
                flat.reshape(count, small_rows, width),
                piece.reshape(count, head_rows, width),
                jnp.zeros((count, pad_rows - small_rows - head_rows, width), F32),
            ],
            axis=1,
        )
        return relative(low(block).reshape(count // 4, 4, pad_rows, width).transpose(1, 0, 2, 3), place)

    half_head = g_head.reshape(2, -1, head_w.shape[1])
    tail0 = small_block(sums_a0, sumo_a0, sums_f0, g_cup0, half_head[0])
    tail1 = small_block(sums_a1, sumo_a1, sums_f1, g_cup1, half_head[1])
    keep = jnp.concatenate([keep, jnp.where(first, tail0, tail1)], axis=2)
    send = jnp.concatenate([send, jnp.where(first, tail1, tail0)], axis=2)
    red_a0 = Reduce(keep, send)
    red_f0.start_near()
    red_a0.start_far()
    red_f1.next_outer()
    red_a1.start_outer()
    red_a0.start_near()
    red_f0.start_outer()
    done_f1 = red_f1.finish()
    done_a1 = red_a1.finish()
    red_a0.start_outer()
    done_f0 = red_f0.finish()
    done_a0 = red_a0.finish()

    sums_zero = jnp.concatenate([done_a0[:cut], done_f0])
    sums_one = jnp.concatenate([done_a1, done_f1])
    other = swap(jnp.where(first, sums_one, sums_zero))
    low_plane = jnp.where(first, sums_zero, other)
    high_plane = jnp.where(first, other, sums_one)

    def unit(array, j):
        return array[j * size : (j + 1) * size]

    qkv_grad = jnp.concatenate([unit(low_plane, 0), unit(low_plane, 1), unit(high_plane, 0)], axis=1)
    out_grad = unit(high_plane, 1)
    up_grad = jnp.concatenate([unit(low_plane, 2 + j) for j in range(units)], axis=1)
    down_grad = high_plane[cut:]
    tail = done_a0[cut:]
    flat = tail[:small_rows].reshape(-1)[:small_n]
    gain_grad = flat[:n_g].reshape(gains_w.shape)
    shift_grad = flat[n_g : n_g + n_s].reshape(shifts_w.shape)
    cup_grad = flat[n_g + n_s :].reshape(up_b.shape)
    head_grad = tail[small_rows : small_rows + head_rows].reshape(-1)[:head_n].reshape(head_w.shape)

    d_first, d_second = jnp.stack(d_a0), jnp.stack(d_a1)
    got = swap(jnp.where(first, d_second, d_first))
    keep = jnp.where(first, d_first, d_second)
    input_grads = jnp.where(first, jnp.concatenate([keep, got]), jnp.concatenate([got, keep]))
    return (
        qkv_grad[None],
        out_grad[None],
        up_grad[None],
        down_grad[None],
        gain_grad,
        shift_grad,
        cup_grad,
        head_grad,
        input_grads[None],
    )


def solution(mesh):
    return jax.shard_map(
        shards,
        mesh=mesh,
        in_specs=(
            P("dp", None, None),
            P("dp", None),
            P("dp", None, None),
            P("section", "dp", None),
            P("section", "dp", None),
            P("section", "dp", None),
            P("section", "dp", None),
            P("section", None, "dp"),
            P("section", None, "dp"),
            P("section", "dp"),
            P(("section", "dp"), None),
        ),
        out_specs=(
            P("section", "dp", None),
            P("section", "dp", None),
            P("section", "dp", None),
            P("section", "dp", None),
            P("section", None, "dp"),
            P("section", None, "dp"),
            P("section", "dp"),
            P(("section", "dp"), None),
            P("section", "dp", None, None),
        ),
        check_vma=False,
    )
```

time: 758 us -> 656 us (0.87)
  Pallas kernels: 0 us -> 205 us
  matrix products: 191 us -> 3.57 us
  local copies, waits for them, and re-layouts: 130 us -> 68 us
  other arithmetic: 106 us -> 50.3 us
  waiting for transfers between devices: 253 us -> 261 us
    pallas_call x0 -> x12, Pallas kernels: none -> 205 us  [the longest x2 62.3 us: attn_bwd(): pl.pallas_call(attn_bwd_kernel, grid=(HEADS // GROUP,), in_specs=[pl.Bloc...]
    dot_general x49 -> x3, matrix products: 175 us -> 3.57 us  [dot(): lax.dot_general(left, right, (((over_left,), (over_right,)), ((), ())), p...]
    reshape x4 -> x8, local copies, waits for them, and re-layouts: 43.2 us -> 2.37 us  [the longest x4 2.17 us: small_block(): shift = shift.reshape(6, count, size).transpose(1, 0, 2)]
    convert_element_type x22 -> x23, other arithmetic: 44.6 us -> 20.5 us  [low(): return value.astype(BF)]
    add x13 -> x9, other arithmetic: 27 us -> 8.25 us  [the longest x4 6.56 us: start_outer(): rest = self.part(0) + self.quad[0].astype(F32) + self.quad[1].astype(F32)]
    sub x2 -> x0, matrix products: 15.4 us -> none  [attend(): jax.nn.softmax(jnp.where(same[None], scores, -1000000000.0), axis=-1)]
    unnamed x367 -> x130, local copies, waits for them, and re-layouts: 28 us -> 16.4 us
    convert_element_type x12 -> x0, local copies, waits for them, and re-layouts: 11.1 us -> none  [the longest x6 6.2 us: proj(): return (jnp.dot(acts, w, preferred_element_type=F32) + b).astype(BF)]
  transfers between devices with their start and end apart: 59 -> 75, of which waited for: 28 -> 30; matrix products, arithmetic and copies ran while one was open for 34% -> 14% of each run, Pallas kernels for 0% -> 17%
where the time goes in v2:
time: 656 us; the launch traced here: 647 us
  waiting for transfers between devices  261 us (40%)
  Pallas kernels  205 us (31%)
  local copies, waits for them, and re-layouts  68 us (10%)
  starting transfers between devices  55.9 us (9%)
  other arithmetic  50.3 us (8%)
    ppermute x48, waiting for transfers between devices, flip(): return lax.ppermute(value, BOTH, pairs)  251 us
    pallas_call x2, Pallas kernels, attn_bwd(): pl.pallas_call(attn_bwd_kernel, grid=(HEADS // GROUP,), in_specs=[pl.Bloc...  62.3 us
    ppermute x48, starting transfers between devices, flip(): return lax.ppermute(value, BOTH, pairs)  51.6 us
    pallas_call x2, Pallas kernels, attn_fwd(): pl.pallas_call(attn_fwd_kernel, grid=(HEADS // GROUP,), in_specs=[whole_b...  45.1 us
    pallas_call x2, Pallas kernels, ffn_bwd(): pl.pallas_call(ffn_bwd_kernel, grid=(units,), in_specs=[pl.BlockSpec(memo...  38.1 us
    pallas_call x2, Pallas kernels, ffn_fwd(): pl.pallas_call(ffn_fwd_kernel, grid=(units,), in_specs=[whole_block(lengt...  32.2 us
    pallas_call x4, Pallas kernels, assemble(): pl.pallas_call(lambda *refs: assemble_kernel(attn, units, size, layout, *...  27.6 us
    convert_element_type x23, other arithmetic, low(): return value.astype(BF)  20.5 us
  transfers between devices with their start and end apart: 75, of which 30 were waited for; matrix products, arithmetic and copies ran while one was open for 14% of the time, Pallas kernels for 17%

profile of v2, /device:TPU:0, one launch (start us, length us, event | category | flops | bytes accessed | tf_op | source)
XLA Modules:
  0.0 646.9 jit_solution(5056928345876864909)
XLA Ops:
  19.7 10.4 %collective-permute-done.2 = bf16[1,192,768]{2,1,0:T(8,128)(2,1)S(1)} collective-permute-done((bf16[1,192,768]{2,1,0:T(8,128)(2,1)S(1)}, bf16[1,192,768]{2,1,0:T(8,128)(2,1)S(1)}, u32[]{:S(2)}, u32[]{:S(2)}) %collective-permute-start.2) | collective-permute-done | bytes 294944 | tf_op jit(solution)/shard_map/ppermute | solution.py:457
  30.7 17.5 %collective-permute-done.4 = bf16[2,112,768]{2,1,0:T(8,128)(2,1)S(1)} collective-permute-done((bf16[2,112,768]{2,1,0:T(8,128)(2,1)S(1)}, bf16[2,112,768]{2,1,0:T(8,128)(2,1)S(1)}, u32[]{:S(2)}, u32[]{:S(2)}) %collective-permute-start.4) | collective-permute-done | bytes 344096 | tf_op jit(solution)/shard_map/ppermute | solution.py:457
  54.3 8.6 %collective-permute-done.5 = bf16[1,96,768]{2,1,0:T(8,128)(2,1)S(1)} collective-permute-done((bf16[1,96,768]{2,1,0:T(8,128)(2,1)S(1)}, bf16[1,96,768]{2,1,0:T(8,128)(2,1)S(1)}, u32[]{:S(2)}, u32[]{:S(2)}) %collective-permute-start.5) | collective-permute-done | bytes 147488 | tf_op jit(solution)/shard_map/ppermute | solution.py:457
  97.8 22.6 %attn_fwd.2 = (bf16[512,768]{1,0:T(8,128)(2,1)}, bf16[512,768]{1,0:T(8,128)(2,1)}, bf16[512,768]{1,0:T(8,128)(2,1)}, bf16[512,768]{1,0:T(8,128)(2,1)}, f32[512,768]{1,0:T(8,128)}, /*index=5*/f32[512,128]{1,0:T(8,128)}) custom-call(bf16[512,768]{1,0:T(8,128)(2,1)} %dynamic-slice_bitcast_fusion.a_ref, s32[512,128]{1,0:T(8,128)} %broadcast_in_dim.77.sq_ref.sk_ref, ...), custom_call_target="tpu_custom_call" | custom-call | tf_op jit(solution)/shard_map/attn_fwd/pallas_call | solution.py:134
  123.2 6.9 %collective-permute-done.16 = bf16[1,192,768]{2,1,0:T(8,128)(2,1)S(1)} collective-permute-done((bf16[1,192,768]{2,1,0:T(8,128)(2,1)}, bf16[1,192,768]{2,1,0:T(8,128)(2,1)S(1)}, u32[]{:S(2)}, u32[]{:S(2)}) %collective-permute-start.16) | collective-permute-done | bytes 294944 | tf_op jit(solution)/shard_map/ppermute | solution.py:457
  139.1 21.2 %collective-permute-done.26 = bf16[2,192,768]{2,1,0:T(8,128)(2,1)S(1)} collective-permute-done((bf16[2,192,768]{2,1,0:T(8,128)(2,1)S(1)}, bf16[2,192,768]{2,1,0:T(8,128)(2,1)S(1)}, u32[]{:S(2)}, u32[]{:S(2)}) %collective-permute-start.26) | collective-permute-done | bytes 589856 | tf_op jit(solution)/shard_map/ppermute | solution.py:457
  166.5 8.4 %assemble.5 = (bf16[4,4,4,48,768]{4,3,2,1,0:T(8,128)(2,1)}, bf16[4,4,192,768]{3,2,1,0:T(8,128)(2,1)}) custom-call(s32[2]{0:T(128)} %pad_add_fusion.refs_0_.place_ref, bf16[4,192,768]{2,1,0:T(8,128)(2,1)} %copy-done.4, bf16[4,192,768]{2,1,0:T(8,128)(2,1)} %copy-done.11, bf16[4,192,768]{2,1,0:T(8,128)(2,1)} %copy-done.9, bf16[2,192,768]{2,1,0:T(8,128)(2,1)} %copy-done.35, ...), custom_call_target="tpu_custom_call" | custom-call | tf_op jit(solution)/shard_map/assemble/pallas_call | solution.py:550
  175.0 16.1 %ffn_fwd.2 = (bf16[512,3072]{1,0:T(8,128)(2,1)}, bf16[512,3072]{1,0:T(8,128)(2,1)}, f32[512,768]{1,0:T(8,128)}, f32[512,128]{1,0:T(8,128)}, bf16[512,768]{1,0:T(8,128)(2,1)}) custom-call(f32[512,768]{1,0:T(8,128)} %get-tuple-element.93.n1_ref, bf16[4,768,768]{2,1,0:T(8,128)(2,1)} %bitcast.237, f32[4,1,768]{2,1,0:T(1,128)} %reshape_reshape.15.cup_ref, ...), custom_call_target="tpu_custom_call" | custom-call | tf_op jit(solution)/shard_map/ffn_fwd/pallas_call | solution.py:181
  197.3 29.8 %collective-permute-done.29.refs_4_ = bf16[2,96,768]{2,1,0:T(8,128)(2,1)} collective-permute-done((bf16[2,96,768]{2,1,0:T(8,128)(2,1)S(1)}, bf16[2,96,768]{2,1,0:T(8,128)(2,1)}, u32[]{:S(2)}, u32[]{:S(2)}) %collective-permute-start.29) | collective-permute-done | bytes 294944 | tf_op jit(solution)/shard_map/ppermute | solution.py:457
  241.6 22.5 %attn_fwd.3 = (bf16[512,768]{1,0:T(8,128)(2,1)}, bf16[512,768]{1,0:T(8,128)(2,1)}, bf16[512,768]{1,0:T(8,128)(2,1)}, bf16[512,768]{1,0:T(8,128)(2,1)}, f32[512,768]{1,0:T(8,128)}, /*index=5*/f32[512,128]{1,0:T(8,128)}) custom-call(bf16[512,768]{1,0:T(8,128)(2,1)} %get-tuple-element.100.a_ref, s32[512,128]{1,0:T(8,128)} %broadcast_in_dim.77.sq_ref.sk_ref, ...), custom_call_target="tpu_custom_call" | custom-call | tf_op jit(solution)/shard_map/attn_fwd/pallas_call | solution.py:134
  266.6 13.5 %collective-permute-done.38.refs_4_ = bf16[2,192,768]{2,1,0:T(8,128)(2,1)} collective-permute-done((bf16[2,192,768]{2,1,0:T(8,128)(2,1)S(1)}, bf16[2,192,768]{2,1,0:T(8,128)(2,1)}, u32[]{:S(2)}, u32[]{:S(2)}) %collective-permute-start.38) | collective-permute-done | bytes 589856 | tf_op jit(solution)/shard_map/ppermute | solution.py:457
  297.9 8.6 %assemble.7 = (bf16[4,4,4,48,768]{4,3,2,1,0:T(8,128)(2,1)}, bf16[4,4,192,768]{3,2,1,0:T(8,128)(2,1)}) custom-call(s32[2]{0:T(128)} %pad_add_fusion.refs_0_.place_ref, bf16[4,192,768]{2,1,0:T(8,128)(2,1)} %copy-done.5, bf16[4,192,768]{2,1,0:T(8,128)(2,1)} %copy-done.12, bf16[4,192,768]{2,1,0:T(8,128)(2,1)} %copy-done.10, ...), custom_call_target="tpu_custom_call" | custom-call | tf_op jit(solution)/shard_map/assemble/pallas_call | solution.py:550
  306.6 16.1 %ffn_fwd.3 = (bf16[512,3072]{1,0:T(8,128)(2,1)}, bf16[512,3072]{1,0:T(8,128)(2,1)}, f32[512,768]{1,0:T(8,128)}, f32[512,128]{1,0:T(8,128)}, bf16[512,768]{1,0:T(8,128)(2,1)}) custom-call(f32[512,768]{1,0:T(8,128)} %get-tuple-element.103.n1_ref, bf16[4,768,768]{2,1,0:T(8,128)(2,1)} %bitcast.241, f32[4,1,768]{2,1,0:T(1,128)} %reshape_reshape.16.cup_ref, ...), custom_call_target="tpu_custom_call" | custom-call | tf_op jit(solution)/shard_map/ffn_fwd/pallas_call | solution.py:181
  326.0 19.0 %ffn_bwd.2 = (bf16[4,4,192,768]{3,2,1,0:T(8,128)(2,1)}, bf16[4,4,192,768]{3,2,1,0:T(8,128)(2,1)}, f32[512,768]{1,0:T(8,128)}, f32[8,768]{1,0:T(8,128)}, f32[4,1,768]{2,1,0:T(1,128)}) custom-call(s32[2]{0:T(128)} %pad_add_fusion.refs_0_.place_ref, f32[512,768]{1,0:T(8,128)} %fusion.70.dy_ref, f32[512,768]{1,0:T(8,128)} %get-tuple-element.109.n2_ref, ...), custom_call_target="tpu_custom_call" | custom-call | tf_op jit(solution)/shard_map/ffn_bwd/pallas_call | solution.py:286
  345.5 7.8 %collective-permute-done.45 = bf16[4,4,192,768]{3,2,1,0:T(8,128)(2,1)S(1)} collective-permute-done((bf16[4,4,192,768]{3,2,1,0:T(8,128)(2,1)}, bf16[4,4,192,768]{3,2,1,0:T(8,128)(2,1)S(1)}, u32[]{:S(2)}, u32[]{:S(2)}) %collective-permute-start.45) | collective-permute-done | bytes 4718624 | tf_op jit(solution)/shard_map/ppermute | solution.py:463
  357.7 31.0 %attn_bwd.2 = (bf16[4,4,96,768]{3,2,1,0:T(8,128)(2,1)}, bf16[4,4,96,768]{3,2,1,0:T(8,128)(2,1)}, f32[512,768]{1,0:T(8,128)}, f32[8,768]{1,0:T(8,128)}, f32[8,768]{1,0:T(8,128)}) custom-call(s32[2]{0:T(128)} %pad_add_fusion.refs_0_.place_ref, f32[512,768]{1,0:T(8,128)} %get-tuple-element.117.dr_ref, bf16[512,768]{1,0:T(8,128)(2,1)} %get-tuple-element.100.a_ref, ...), custom_call_target="tpu_custom_call" | custom-call | tf_op jit(solution)/shard_map/attn_bwd/pallas_call | solution.py:427
  393.5 11.0 %collective-permute-done.47 = bf16[2,192,768]{2,1,0:T(8,128)(2,1)S(1)} collective-permute-done((bf16[2,192,768]{2,1,0:T(8,128)(2,1)S(1)}, bf16[2,192,768]{2,1,0:T(8,128)(2,1)S(1)}, u32[]{:S(2)}, u32[]{:S(2)}) %collective-permute-start.47) | collective-permute-done | bytes 589856 | tf_op jit(solution)/shard_map/ppermute | solution.py:457
  412.0 19.1 %ffn_bwd.3 = (bf16[4,4,192,768]{3,2,1,0:T(8,128)(2,1)}, bf16[4,4,192,768]{3,2,1,0:T(8,128)(2,1)}, f32[512,768]{1,0:T(8,128)}, f32[8,768]{1,0:T(8,128)}, f32[4,1,768]{2,1,0:T(1,128)}) custom-call(s32[2]{0:T(128)} %pad_add_fusion.refs_0_.place_ref, bf16[512,768]{1,0:T(8,128)(2,1)} %convert_element_type.523.dy_ref, f32[512,768]{1,0:T(8,128)} %get-tuple-element.129.n2_ref, ...), custom_call_target="tpu_custom_call" | custom-call | tf_op jit(solution)/shard_map/ffn_bwd/pallas_call | solution.py:286
  440.6 19.7 %collective-permute-done.49 = bf16[4,192,768]{2,1,0:T(8,128)(2,1)S(1)} collective-permute-done((bf16[4,192,768]{2,1,0:T(8,128)(2,1)}, bf16[4,192,768]{2,1,0:T(8,128)(2,1)S(1)}, u32[]{:S(2)}, u32[]{:S(2)}) %collective-permute-start.49) | collective-permute-done | bytes 1179680 | tf_op jit(solution)/shard_map/ppermute | solution.py:457
  477.1 31.3 %attn_bwd.3 = (bf16[4,4,96,768]{3,2,1,0:T(8,128)(2,1)}, bf16[4,4,96,768]{3,2,1,0:T(8,128)(2,1)}, f32[512,768]{1,0:T(8,128)}, f32[8,768]{1,0:T(8,128)}, f32[8,768]{1,0:T(8,128)}) custom-call(s32[2]{0:T(128)} %pad_add_fusion.refs_0_.place_ref, f32[512,768]{1,0:T(8,128)} %get-tuple-element.142.dr_ref, bf16[512,768]{1,0:T(8,128)(2,1)} %dynamic-slice_bitcast_fusion.a_ref, ...), custom_call_target="tpu_custom_call" | custom-call | tf_op jit(solution)/shard_map/attn_bwd/pallas_call | solution.py:427
  530.4 14.6 %collective-permute-done.69 = bf16[2,96,768]{2,1,0:T(8,128)(2,1)S(1)} collective-permute-done((bf16[2,96,768]{2,1,0:T(8,128)(2,1)S(1)}, bf16[2,96,768]{2,1,0:T(8,128)(2,1)S(1)}, u32[]{:S(2)}, u32[]{:S(2)}) %collective-permute-start.69) | collective-permute-done | bytes 294944 | tf_op jit(solution)/shard_map/ppermute | solution.py:457
  552.0 30.5 %collective-permute-done.57 = bf16[2,112,768]{2,1,0:T(8,128)(2,1)S(1)} collective-permute-done((bf16[2,112,768]{2,1,0:T(8,128)(2,1)S(1)}, bf16[2,112,768]{2,1,0:T(8,128)(2,1)S(1)}, u32[]{:S(2)}, u32[]{:S(2)}) %collective-permute-start.57) | collective-permute-done | bytes 344096 | tf_op jit(solution)/shard_map/ppermute | solution.py:457
  589.0 8.8 %collective-permute-done.58 = bf16[4,112,768]{2,1,0:T(8,128)(2,1)S(1)} collective-permute-done((bf16[4,112,768]{2,1,0:T(8,128)(2,1)S(1)}, bf16[4,112,768]{2,1,0:T(8,128)(2,1)S(1)}, u32[]{:S(2)}, u32[]{:S(2)}) %collective-permute-start.58) | collective-permute-done | bytes 688160 | tf_op jit(solution)/shard_map/ppermute | solution.py:457
  598.6 22.7 %collective-permute-done.65 = bf16[2,192,768]{2,1,0:T(8,128)(2,1)S(1)} collective-permute-done((bf16[2,192,768]{2,1,0:T(8,128)(2,1)S(1)}, bf16[2,192,768]{2,1,0:T(8,128)(2,1)S(1)}, u32[]{:S(2)}, u32[]{:S(2)}) %collective-permute-start.65) | collective-permute-done | bytes 589856 | tf_op jit(solution)/shard_map/ppermute | solution.py:457
  (466 shorter events, 226.5 us)
Async XLA Ops:
  30.2 34.0 %collective-permute-start.3 = (bf16[2,192,768]{2,1,0:T(8,128)(2,1)S(1)}, bf16[2,192,768]{2,1,0:T(8,128)(2,1)S(1)}, u32[]{:S(2)}, u32[]{:S(2)}) collective-permute-start(bf16[2,192,768]{2,1,0:T(8,128)(2,1)S(1)} %maximum_select_fusion.4), channel_id=1, source_target_pairs={{0,8},{1,9},{2,10},{3,11},{4,12},{5,13},{6,14},{7,15},{8,0},{9,1},... | collective-permute-start | bytes 1769480 | tf_op jit(solution)/shard_map/ppermute | solution.py:457
  63.7 59.5 %collective-permute-start.15 = (bf16[2,96,768]{2,1,0:T(8,128)(2,1)}, bf16[2,96,768]{2,1,0:T(8,128)(2,1)}, u32[]{:S(2)}, u32[]{:S(2)}) collective-permute-start(bf16[2,96,768]{2,1,0:T(8,128)(2,1)} %maximum_select_fusion.8), channel_id=1, source_target_pairs={{0,8},{1,9},{2,10},{3,11},{4,12},{5,13},{6,14},{7,15},{8,0},{9,1},... | collective-permute-start | bytes 884744 | tf_op jit(solution)/shard_map/ppermute | solution.py:457
  76.0 44.4 %collective-permute-start.18 = (bf16[4,192,768]{2,1,0:T(8,128)(2,1)S(1)}, bf16[4,192,768]{2,1,0:T(8,128)(2,1)S(1)}, u32[]{:S(2)}, u32[]{:S(2)}) collective-permute-start(bf16[4,192,768]{2,1,0:T(8,128)(2,1)S(1)} %maximum_select_fusion.1.refs_1_), channel_id=1, source_target_pairs={{0,2},{1,3},{2,0},{3,1},{4,6},{5,7},{6,4},{7,5},{8,10},{9,11},{10,... | collective-permute-start | bytes 3538952 | tf_op jit(solution)/shard_map/ppermute | solution.py:457
  77.5 42.9 %collective-permute-start.17 = (bf16[4,192,768]{2,1,0:T(8,128)(2,1)S(1)}, bf16[4,192,768]{2,1,0:T(8,128)(2,1)S(1)}, u32[]{:S(2)}, u32[]{:S(2)}) collective-permute-start(bf16[4,192,768]{2,1,0:T(8,128)(2,1)S(1)} %maximum_select_fusion.1.refs_1_), channel_id=1, source_target_pairs={{0,1},{1,0},{2,3},{3,2},{4,5},{5,4},{6,7},{7,6},{8,9},{9,8},{10,11... | collective-permute-start | bytes 3538952 | tf_op jit(solution)/shard_map/ppermute | solution.py:457
  80.8 49.4 %collective-permute-start.21 = (bf16[4,192,768]{2,1,0:T(8,128)(2,1)S(1)}, bf16[4,192,768]{2,1,0:T(8,128)(2,1)}, u32[]{:S(2)}, u32[]{:S(2)}) collective-permute-start(bf16[4,192,768]{2,1,0:T(8,128)(2,1)S(1)} %maximum_select_fusion.1.refs_1_), channel_id=1, source_target_pairs={{0,16},{1,17},{2,18},{3,19},{4,20},{5,21},{6,22},{7,23},{8,24},{9,... | collective-permute-start | bytes 3538952 | tf_op jit(solution)/shard_map/ppermute | solution.py:463
  123.2 43.3 %collective-permute-start.22 = (bf16[4,192,768]{2,1,0:T(8,128)(2,1)S(1)}, bf16[4,192,768]{2,1,0:T(8,128)(2,1)}, u32[]{:S(2)}, u32[]{:S(2)}) collective-permute-start(bf16[4,192,768]{2,1,0:T(8,128)(2,1)S(1)} %collective-permute-done.17.refs_2_), channel_id=1, source_target_pairs={{0,16},{1,17},{2,18},{3,19},{4,20},{5,21},{6,22},{7,23},{8,24},{9,... | collective-permute-start | bytes 3538952 | tf_op jit(solution)/shard_map/ppermute | solution.py:463
  130.1 36.4 %collective-permute-start.23 = (bf16[4,192,768]{2,1,0:T(8,128)(2,1)S(1)}, bf16[4,192,768]{2,1,0:T(8,128)(2,1)}, u32[]{:S(2)}, u32[]{:S(2)}) collective-permute-start(bf16[4,192,768]{2,1,0:T(8,128)(2,1)S(1)} %collective-permute-done.18.refs_3_), channel_id=1, source_target_pairs={{0,16},{1,17},{2,18},{3,19},{4,20},{5,21},{6,22},{7,23},{8,24},{9,... | collective-permute-start | bytes 3538952 | tf_op jit(solution)/shard_map/ppermute | solution.py:463
  160.3 32.8 %collective-permute-start.28 = (bf16[4,96,768]{2,1,0:T(8,128)(2,1)}, bf16[4,96,768]{2,1,0:T(8,128)(2,1)}, u32[]{:S(2)}, u32[]{:S(2)}) collective-permute-start(bf16[4,96,768]{2,1,0:T(8,128)(2,1)} %maximum_select_fusion.5.refs_1_), channel_id=1, source_target_pairs={{0,2},{1,3},{2,0},{3,1},{4,6},{5,7},{6,4},{7,5},{8,10},{9,11},{10,... | collective-permute-start | bytes 1769480 | tf_op jit(solution)/shard_map/ppermute | solution.py:457
  191.0 73.1 %collective-permute-start.37 = (bf16[4,192,768]{2,1,0:T(8,128)(2,1)S(1)}, bf16[4,192,768]{2,1,0:T(8,128)(2,1)S(1)}, u32[]{:S(2)}, u32[]{:S(2)}) collective-permute-start(bf16[4,192,768]{2,1,0:T(8,128)(2,1)S(1)} %maximum_select_fusion.2.refs_1_), channel_id=1, source_target_pairs={{0,2},{1,3},{2,0},{3,1},{4,6},{5,7},{6,4},{7,5},{8,10},{9,11},{10,... | collective-permute-start | bytes 3538952 | tf_op jit(solution)/shard_map/ppermute | solution.py:457
  192.6 71.5 %collective-permute-start.36 = (bf16[4,192,768]{2,1,0:T(8,128)(2,1)S(1)}, bf16[4,192,768]{2,1,0:T(8,128)(2,1)S(1)}, u32[]{:S(2)}, u32[]{:S(2)}) collective-permute-start(bf16[4,192,768]{2,1,0:T(8,128)(2,1)S(1)} %maximum_select_fusion.2.refs_1_), channel_id=1, source_target_pairs={{0,1},{1,0},{2,3},{3,2},{4,5},{5,4},{6,7},{7,6},{8,9},{9,8},{10,11... | collective-permute-start | bytes 3538952 | tf_op jit(solution)/shard_map/ppermute | solution.py:457
  194.1 32.9 %collective-permute-start.29 = (bf16[2,96,768]{2,1,0:T(8,128)(2,1)S(1)}, bf16[2,96,768]{2,1,0:T(8,128)(2,1)}, u32[]{:S(2)}, u32[]{:S(2)}) collective-permute-start(bf16[2,96,768]{2,1,0:T(8,128)(2,1)S(1)} %slice.504), channel_id=1, source_target_pairs={{0,1},{1,0},{2,3},{3,2},{4,5},{5,4},{6,7},{7,6},{8,9},{9,8},{10,11... | collective-permute-start | bytes 884744 | tf_op jit(solution)/shard_map/ppermute | solution.py:457
  195.7 31.9 %collective-permute-start.32 = (bf16[4,96,768]{2,1,0:T(8,128)(2,1)}, bf16[4,96,768]{2,1,0:T(8,128)(2,1)S(1)}, u32[]{:S(2)}, u32[]{:S(2)}) collective-permute-start(bf16[4,96,768]{2,1,0:T(8,128)(2,1)} %collective-permute-done.27.refs_2_), channel_id=1, source_target_pairs={{0,16},{1,17},{2,18},{3,19},{4,20},{5,21},{6,22},{7,23},{8,24},{9,... | collective-permute-start | bytes 1769480 | tf_op jit(solution)/shard_map/ppermute | solution.py:463
  236.3 61.0 %collective-permute-start.40 = (bf16[4,192,768]{2,1,0:T(8,128)(2,1)S(1)}, bf16[4,192,768]{2,1,0:T(8,128)(2,1)}, u32[]{:S(2)}, u32[]{:S(2)}) collective-permute-start(bf16[4,192,768]{2,1,0:T(8,128)(2,1)S(1)} %maximum_select_fusion.2.refs_1_), channel_id=1, source_target_pairs={{0,16},{1,17},{2,18},{3,19},{4,20},{5,21},{6,22},{7,23},{8,24},{9,... | collective-permute-start | bytes 3538952 | tf_op jit(solution)/shard_map/ppermute | solution.py:463
  266.1 31.8 %collective-permute-start.42 = (bf16[4,192,768]{2,1,0:T(8,128)(2,1)S(1)}, bf16[4,192,768]{2,1,0:T(8,128)(2,1)}, u32[]{:S(2)}, u32[]{:S(2)}) collective-permute-start(bf16[4,192,768]{2,1,0:T(8,128)(2,1)S(1)} %collective-permute-done.37.refs_3_), channel_id=1, source_target_pairs={{0,16},{1,17},{2,18},{3,19},{4,20},{5,21},{6,22},{7,23},{8,24},{9,... | collective-permute-start | bytes 3538952 | tf_op jit(solution)/shard_map/ppermute | solution.py:463
  431.1 42.0 %collective-permute-start.53 = (bf16[4,4,192,768]{3,2,1,0:T(8,128)(2,1)}, bf16[4,4,192,768]{3,2,1,0:T(8,128)(2,1)}, u32[]{:S(2)}, u32[]{:S(2)}) collective-permute-start(bf16[4,4,192,768]{3,2,1,0:T(8,128)(2,1)} %get-tuple-element.141), channel_id=1, source_target_pairs={{0,16},{1,17},{2,18},{3,19},{4,20},{5,21},{6,22},{7,23},{8,24},{9,... | collective-permute-start | bytes 14155784 | tf_op jit(solution)/shard_map/ppermute | solution.py:463
  467.6 54.8 %collective-permute-start.71 = (bf16[2,192,768]{2,1,0:T(8,128)(2,1)}, bf16[2,192,768]{2,1,0:T(8,128)(2,1)}, u32[]{:S(2)}, u32[]{:S(2)}) collective-permute-start(bf16[2,192,768]{2,1,0:T(8,128)(2,1)} %select_convert_fusion.1), channel_id=1, source_target_pairs={{0,8},{1,9},{2,10},{3,11},{4,12},{5,13},{6,14},{7,15},{8,0},{9,1},... | collective-permute-start | bytes 1769480 | tf_op jit(solution)/shard_map/ppermute | solution.py:457
  470.2 52.9 %collective-permute-start.67 = (bf16[4,96,768]{2,1,0:T(8,128)(2,1)}, bf16[4,96,768]{2,1,0:T(8,128)(2,1)}, u32[]{:S(2)}, u32[]{:S(2)}) collective-permute-start(bf16[4,96,768]{2,1,0:T(8,128)(2,1)} %pad_maximum_fusion.9), channel_id=1, source_target_pairs={{0,1},{1,0},{2,3},{3,2},{4,5},{5,4},{6,7},{7,6},{8,9},{9,8},{10,11... | collective-permute-start | bytes 1769480 | tf_op jit(solution)/shard_map/ppermute | solution.py:457
  472.4 50.7 %collective-permute-start.68 = (bf16[4,96,768]{2,1,0:T(8,128)(2,1)}, bf16[4,96,768]{2,1,0:T(8,128)(2,1)}, u32[]{:S(2)}, u32[]{:S(2)}) collective-permute-start(bf16[4,96,768]{2,1,0:T(8,128)(2,1)} %pad_maximum_fusion.10), channel_id=1, source_target_pairs={{0,2},{1,3},{2,0},{3,1},{4,6},{5,7},{6,4},{7,5},{8,10},{9,11},{10,... | collective-permute-start | bytes 1769480 | tf_op jit(solution)/shard_map/ppermute | solution.py:457
  547.1 36.4 %collective-permute-start.64 = (bf16[4,192,768]{2,1,0:T(8,128)(2,1)S(1)}, bf16[4,192,768]{2,1,0:T(8,128)(2,1)S(1)}, u32[]{:S(2)}, u32[]{:S(2)}) collective-permute-start(bf16[4,192,768]{2,1,0:T(8,128)(2,1)S(1)} %pad_maximum_fusion.4), channel_id=1, source_target_pairs={{0,2},{1,3},{2,0},{3,1},{4,6},{5,7},{6,4},{7,5},{8,10},{9,11},{10,... | collective-permute-start | bytes 3538952 | tf_op jit(solution)/shard_map/ppermute | solution.py:457
  548.8 36.1 %collective-permute-start.63 = (bf16[4,192,768]{2,1,0:T(8,128)(2,1)S(1)}, bf16[4,192,768]{2,1,0:T(8,128)(2,1)S(1)}, u32[]{:S(2)}, u32[]{:S(2)}) collective-permute-start(bf16[4,192,768]{2,1,0:T(8,128)(2,1)S(1)} %pad_maximum_fusion.3), channel_id=1, source_target_pairs={{0,1},{1,0},{2,3},{3,2},{4,5},{5,4},{6,7},{7,6},{8,9},{9,8},{10,11... | collective-permute-start | bytes 3538952 | tf_op jit(solution)/shard_map/ppermute | solution.py:457
  549.8 32.8 %collective-permute-start.57 = (bf16[2,112,768]{2,1,0:T(8,128)(2,1)S(1)}, bf16[2,112,768]{2,1,0:T(8,128)(2,1)S(1)}, u32[]{:S(2)}, u32[]{:S(2)}) collective-permute-start(bf16[2,112,768]{2,1,0:T(8,128)(2,1)S(1)} %get-tuple-element.206), channel_id=1, source_target_pairs={{0,1},{1,0},{2,3},{3,2},{4,5},{5,4},{6,7},{7,6},{8,9},{9,8},{10,11... | collective-permute-start | bytes 1032200 | tf_op jit(solution)/shard_map/ppermute | solution.py:457
  551.3 31.2 %collective-permute-start.55 = (bf16[2,112,768]{2,1,0:T(8,128)(2,1)S(1)}, bf16[2,112,768]{2,1,0:T(8,128)(2,1)S(1)}, u32[]{:S(2)}, u32[]{:S(2)}) collective-permute-start(bf16[2,112,768]{2,1,0:T(8,128)(2,1)S(1)} %get-tuple-element.207), channel_id=1, source_target_pairs={{0,2},{1,3},{2,0},{3,1},{4,6},{5,7},{6,4},{7,5},{8,10},{9,11},{10,... | collective-permute-start | bytes 1032200 | tf_op jit(solution)/shard_map/ppermute | solution.py:457
  551.8 86.7 %collective-permute-start.74 = (f32[1,512,768]{2,1,0:T(8,128)S(1)}, f32[1,512,768]{2,1,0:T(8,128)S(1)}, u32[]{:S(2)}, u32[]{:S(2)}) collective-permute-start(f32[1,512,768]{2,1,0:T(8,128)S(1)} %get-tuple-element.217), channel_id=1, source_target_pairs={{0,16},{1,17},{2,18},{3,19},{4,20},{5,21},{6,22},{7,23},{8,24},{9,... | collective-permute-start | bytes 4718600 | tf_op jit(solution)/shard_map/ppermute | solution.py:463
  586.8 34.5 %collective-permute-start.65 = (bf16[2,192,768]{2,1,0:T(8,128)(2,1)S(1)}, bf16[2,192,768]{2,1,0:T(8,128)(2,1)S(1)}, u32[]{:S(2)}, u32[]{:S(2)}) collective-permute-start(bf16[2,192,768]{2,1,0:T(8,128)(2,1)S(1)} %select_convert_fusion), channel_id=1, source_target_pairs={{0,8},{1,9},{2,10},{3,11},{4,12},{5,13},{6,14},{7,15},{8,0},{9,1},... | collective-permute-start | bytes 1769480 | tf_op jit(solution)/shard_map/ppermute | solution.py:457
  (114 other events, 1552.5 us)

commit v3 on v2

v3 whole, which is shorter than its diff:
```python
import jax
import jax.numpy as jnp
from jax import lax
from jax.experimental import pallas as pl
from jax.experimental.pallas import tpu as pltpu
from jax.sharding import PartitionSpec as P

HEADS = 12
HDIM = 64
GROUP = 4
BLOCK = 128
PAD = 16
norm_eps = 1e-06
BF = jnp.bfloat16
F32 = jnp.float32
BOTH = ("section", "dp")
SCALE = HDIM ** (-0.5)

ERF_SCALE = 0.425
ERF_POLY = (
    0.11985147519825406,
    0.12072713574380309,
    0.10159474513684189,
    0.12334456743816431,
    -0.0435293372534038,
    0.19486821903107854,
    -0.15132025578595443,
    0.03446332841595847,
)


def dot(left, right, over_left=1, over_right=0):
    return lax.dot_general(
        left, right, (((over_left,), (over_right,)), ((), ())), preferred_element_type=F32
    )


def shape_of(shape, dtype):
    return jax.ShapeDtypeStruct(shape, dtype)


def whole_block(*shape):
    return pl.BlockSpec(shape, lambda g: (0,) * len(shape))


def gelu_pair(u):
    bell = jnp.exp(u * u * -0.5)
    t = 1.0 / (1.0 + (ERF_SCALE * 0.7071067811865476) * jnp.abs(u))
    poly = ERF_POLY[-1]
    for item in ERF_POLY[-2::-1]:
        poly = poly * t + item
    tail = bell * (poly * t)
    cdf = jnp.where(u < 0.0, tail, 1.0 - tail)
    return u * cdf, cdf + u * bell * 0.3989422804014327


def norm_stats(v):
    center = v - jnp.mean(v, axis=-1, keepdims=True)
    t = lax.rsqrt(jnp.mean(center * center, axis=-1, keepdims=True) + norm_eps)
    return center * t, t


def norm_back(dy, n, t, gain):
    dn = dy * gain
    mean = jnp.mean(dn, axis=-1, keepdims=True)
    along = jnp.mean(dn * n, axis=-1, keepdims=True)
    return t * (dn - mean - n * along)


def colsum(v):
    return jnp.sum(v, axis=0, keepdims=True)


def near(b, blocks):
    return max(0, b - 1) * BLOCK, min(blocks, b + 2) * BLOCK


def pick(flag, left, right):
    return jnp.where(flag, left, right)


def attn_weights(first, refs):
    own_0, own_1, own_rows, other_0, other_1, other_rows = refs
    query = pick(first, own_0[...], other_0[...])
    keys = pick(first, own_1[...], other_1[...])
    value = pick(first, other_0[...], own_0[...])
    out = pick(first, other_rows[...], own_rows[...])
    return query, keys, value, out


def block_of(b, pair):
    return slice(b * BLOCK, (b + 1) * BLOCK), slice(pair * 2 * HDIM, (pair + 1) * 2 * HDIM)


def two_heads(pair, lane):
    zero = jnp.zeros_like(pair)
    return jnp.concatenate([jnp.where(lane < HDIM, pair, zero), jnp.where(lane >= HDIM, pair, zero)])


def attn_fwd_kernel(
    place_ref, a_ref, sq_ref, sk_ref, w0, w1, w2, w3, w4, w5, bias_ref, shift_ref,
    q_ref, k_ref, v_ref, o_ref, n_ref, t_ref, acc,
):
    step = pl.program_id(0)
    blocks = a_ref.shape[0] // BLOCK
    a = a_ref[...]
    wq, wk, wv, wo = attn_weights(place_ref[1] == 0, (w0, w1, w2, w3, w4, w5))
    q_ref[...] = (dot(a, wq) + bias_ref[0:1]).astype(BF)
    k_ref[...] = dot(a, wk).astype(BF)
    v_ref[...] = (dot(a, wv) + bias_ref[1:2]).astype(BF)
    lane = lax.broadcasted_iota(jnp.int32, (BLOCK, 2 * HDIM), 1)
    tiles = [(b, pair) for b in range(blocks) for pair in range(GROUP // 2)]

    def scores_of(b, pair):
        lo, hi = near(b, blocks)
        rows, lanes = block_of(b, pair)
        same = sq_ref[rows, 0:1] == sk_ref[0:1, lo:hi]
        scores = dot(two_heads(q_ref[rows, lanes] * SCALE, lane), k_ref[lo:hi, lanes], 1, 1)
        return jnp.where(jnp.concatenate([same, same]), scores, -1000000000.0)

    ahead = scores_of(*tiles[0])
    for j, (b, pair) in enumerate(tiles):
        lo, hi = near(b, blocks)
        rows, lanes = block_of(b, pair)
        scores = ahead
        if j + 1 < len(tiles):
            ahead = scores_of(*tiles[j + 1])
        grown = jnp.exp(scores - jnp.max(scores, axis=-1, keepdims=True))
        scale = 1.0 / jnp.sum(grown, axis=-1, keepdims=True)
        out = dot((grown * scale).astype(BF), v_ref[lo:hi, lanes])
        o_ref[rows, lanes] = jnp.where(lane < HDIM, out[:BLOCK], out[BLOCK:]).astype(BF)
    part = dot(o_ref[...], wo)

    @pl.when(step == 0)
    def _():
        acc[...] = a.astype(F32) + shift_ref[2:3] + part

    @pl.when(step != 0)
    def _():
        acc[...] += part

    @pl.when(step == pl.num_programs(0) - 1)
    def _():
        n, t = norm_stats(acc[...])
        n_ref[...] = n
        t_ref[...] = jnp.broadcast_to(t, t_ref.shape)


SCALARS = pl.BlockSpec(memory_space=pltpu.SMEM)
NO_COST = pl.CostEstimate(flops=0, bytes_accessed=0, transcendentals=0)


def attn_weight_blocks(width, cols):
    def column(j):
        return pl.BlockSpec((width, cols), lambda g: (j, g))

    return [column(0), column(1), pl.BlockSpec((cols, width), lambda g: (width // cols + g, 0))] * 2


def attn_weight_args(planes):
    own, other = planes
    return (own, own, own, other, other, other)


def attn_fwd(place, a, seg_col, seg_row, planes, shift):
    length, width = a.shape
    cols = GROUP * HDIM
    group = pl.BlockSpec((length, cols), lambda g: (0, g))
    return pl.pallas_call(
        attn_fwd_kernel,
        grid=(HEADS // GROUP,),
        in_specs=[SCALARS, whole_block(length, width), whole_block(length, 128), whole_block(8, length)]
        + attn_weight_blocks(width, cols)
        + [pl.BlockSpec((8, cols), lambda g: (0, g)), whole_block(8, width)],
        out_specs=[group] * 4 + [whole_block(length, width), whole_block(length, 128)],
        out_shape=[shape_of((length, width), BF)] * 4
        + [shape_of((length, width), F32), shape_of((length, 128), F32)],
        scratch_shapes=[pltpu.VMEM((length, width), F32)],
        cost_estimate=NO_COST,
        name="attn_fwd",
    )(place, a, seg_col, seg_row, *attn_weight_args(planes), shift, shift)


def ffn_fwd_kernel(
    place_ref, n1_ref, own_ref, other_ref, cup_ref, gain_ref, shift_ref,
    g_ref, gp_ref, n_ref, t_ref, y_ref, h1, acc,
):
    step = pl.program_id(0)

    @pl.when(step == 0)
    def _():
        hidden = n1_ref[...] * gain_ref[0:1] + shift_ref[4:5]
        h1[...] = hidden.astype(BF)
        acc[...] = hidden + shift_ref[3:4]

    first = place_ref[1] == 0
    up = pick(first, own_ref[0], other_ref[0])
    down = pick(first, other_ref[0], own_ref[0])
    wide = 256
    parts = h1.shape[1] // wide

    def upper(j):
        cols = slice(j * wide, (j + 1) * wide)
        return dot(h1[...], up[:, cols]) + cup_ref[0, :, cols]

    ahead = upper(0)
    total = acc[...]
    for j in range(parts):
        cols = slice(j * wide, (j + 1) * wide)
        here = ahead
        if j + 1 < parts:
            ahead = upper(j + 1)
        g, slope = gelu_pair(here)
        g = g.astype(BF)
        g_ref[:, cols] = g
        gp_ref[:, cols] = slope.astype(BF)
        total = total + dot(g, down[cols])
    acc[...] = total

    @pl.when(step == pl.num_programs(0) - 1)
    def _():
        n, t = norm_stats(acc[...])
        n_ref[...] = n
        t_ref[...] = jnp.broadcast_to(t, t_ref.shape)
        y_ref[...] = (n * gain_ref[1:2] + shift_ref[5:6]).astype(BF)


def ffn_fwd(place, n1, planes, cup, gain, shift):
    length, width = n1.shape
    units = planes[0].shape[0]
    unit = pl.BlockSpec((1, width, width), lambda g: (g, 0, 0))
    column = pl.BlockSpec((length, width), lambda g: (0, g))
    return pl.pallas_call(
        ffn_fwd_kernel,
        grid=(units,),
        in_specs=[
            SCALARS,
            whole_block(length, width),
            unit,
            unit,
            pl.BlockSpec((1, 1, width), lambda g: (g, 0, 0)),
            whole_block(8, width),
            whole_block(8, width),
        ],
        out_specs=[column, column, whole_block(length, width), whole_block(length, 128), whole_block(length, width)],
        out_shape=[shape_of((length, units * width), BF)] * 2
        + [shape_of((length, width), F32), shape_of((length, 128), F32), shape_of((length, width), BF)],
        scratch_shapes=[pltpu.VMEM((length, width), BF), pltpu.VMEM((length, width), F32)],
        cost_estimate=NO_COST,
        name="ffn_fwd",
    )(place, n1, *planes, cup.reshape(units, 1, width), gain, shift)


def send_index(q, place_ref, core):
    rel = q ^ place_ref[0]
    x, y = rel & 1, rel >> 1
    return x * (1 + core) + y * (2 - core)


def outer_index(z, core):
    return z + core * ((z >> 1) + 2 * (z & 1) - z)


def by_section(section, action):
    for plane in range(2):
        pl.when(section == plane)(lambda plane=plane: action(plane))


def copy_all(copies, start):
    for item in copies:
        if start:
            item.start()
        else:
            item.wait()


def ffn_bwd_kernel(
    place_ref, dy_ref, n2_ref, t2_ref, g_ref, gp_ref, own_ref, other_ref, n1_ref, t1_ref, gain_ref, shift_ref,
    keep_ref, send_ref, dr1_ref, sums_ref, cup_ref, h1, df, acc, gup, gdown, sem,
):
    step = pl.program_id(0)
    last = pl.num_programs(0) - 1
    quads = keep_ref.shape[0]
    outer = keep_ref.shape[1]
    width = h1.shape[1]
    size = width // (quads * outer)

    @pl.when(step == 0)
    def _():
        n2 = n2_ref[...]
        dy = dy_ref[...].astype(F32)
        dr2 = norm_back(dy, n2, t2_ref[:, 0:1], gain_ref[1:2])
        low = dr2.astype(BF)
        df[...] = low
        acc[...] = dr2
        h1[...] = (n1_ref[...] * gain_ref[0:1] + shift_ref[4:5]).astype(BF)
        sums_ref[...] = jnp.zeros_like(sums_ref)
        sums_ref[1:2] = colsum(dy * n2)
        sums_ref[2:3] = colsum(dy)
        sums_ref[3:4] = colsum(low.astype(F32))

    d = df[...]
    first = place_ref[1] == 0
    w_up = pick(first, own_ref[0], other_ref[0])
    w_down = pick(first, other_ref[0], own_ref[0])
    down = dot(g_ref[...], d, 0, 0).astype(BF)
    gdown[step] = down.reshape(quads, width // quads, width)
    du = (dot(d, w_down, 1, 1) * gp_ref[...].astype(F32)).astype(BF)
    cup_ref[0] = colsum(du.astype(F32))
    up = dot(h1[...], du, 0, 0).astype(BF)
    gup[step] = up.reshape(outer, quads, size, width)
    acc[...] += dot(du, w_up, 1, 1)

    def copies(j, plane):
        up_to, down_to = (keep_ref, send_ref) if plane == 0 else (send_ref, keep_ref)
        out = []
        for q in range(quads):
            rel = send_index(q, place_ref, 0)
            for z in range(outer):
                to = up_to.at[rel, z, j * size : (j + 1) * size, :]
                out.append(pltpu.make_async_copy(gup.at[j, z, q], to, sem.at[j, z, q]))
            to = down_to.at[send_index(q, place_ref, 1), outer_index(j, 1)]
            out.append(pltpu.make_async_copy(gdown.at[j, q], to, sem.at[j, outer, q]))
        return out

    for j in range(gup.shape[0]):
        @pl.when(step == j)
        def _(j=j):
            by_section(place_ref[1], lambda plane: copy_all(copies(j, plane), True))

    @pl.when(step == last)
    def _():
        dh = acc[...]
        n1 = n1_ref[...]
        dr1_ref[...] = norm_back(dh, n1, t1_ref[:, 0:1], gain_ref[0:1])
        sums_ref[0:1] = colsum(dh * n1)
        sums_ref[4:5] = colsum(dh)

        def finish(plane):
            for j in range(gup.shape[0]):
                copy_all(copies(j, plane), False)

        by_section(place_ref[1], finish)


def ffn_bwd(place, outer, dy, n2, t2, g, gp, planes, n1, t1, gain, shift):
    length, width = n1.shape
    units = planes[0].shape[0]
    unit = pl.BlockSpec((1, width, width), lambda g: (g, 0, 0))
    size = width // (4 * outer)
    column = pl.BlockSpec((length, width), lambda g: (0, g))
    chunk = shape_of((4, outer, units * size, width), BF)
    return pl.pallas_call(
        ffn_bwd_kernel,
        grid=(units,),
        in_specs=[
            pl.BlockSpec(memory_space=pltpu.SMEM),
            whole_block(length, width),
            whole_block(length, width),
            whole_block(length, 128),
            column,
            column,
            unit,
            unit,
            whole_block(length, width),
            whole_block(length, 128),
            whole_block(8, width),
            whole_block(8, width),
        ],
        out_specs=[
            pl.BlockSpec(memory_space=pl.ANY),
            pl.BlockSpec(memory_space=pl.ANY),
            whole_block(length, width),
            whole_block(8, width),
            pl.BlockSpec((1, 1, width), lambda g: (g, 0, 0)),
        ],
        out_shape=[chunk, chunk, shape_of((length, width), F32), shape_of((8, width), F32), shape_of((units, 1, width), F32)],
        scratch_shapes=[
            pltpu.VMEM((length, width), BF),
            pltpu.VMEM((length, width), BF),
            pltpu.VMEM((length, width), F32),
            pltpu.VMEM((units, outer, 4, size, width), BF),
            pltpu.VMEM((units, 4, width // 4, width), BF),
            pltpu.SemaphoreType.DMA((units, outer + 1, 4)),
        ],
        cost_estimate=NO_COST,
        name="ffn_bwd",
    )(place, dy, n2, t2, g, gp, *planes, n1, t1, gain, shift)


def attn_bwd_kernel(
    place_ref, dr_ref, a_ref, sq_ref, sk_ref, q_ref, k_ref, v_ref, o_ref, w0, w1, w2, w3, w4, w5,
    keep_ref, send_ref, da_ref, sums_ref, sumo_ref, dat, do_sc, dq, dk, dv, grads, sem,
):
    step = pl.program_id(0)
    length, width = a_ref.shape
    blocks = length // BLOCK
    quads = keep_ref.shape[0]
    outer = keep_ref.shape[1]
    size = width // (quads * outer)
    cols = GROUP * HDIM

    @pl.when(step == 0)
    def _():
        low = dr_ref[...].astype(BF)
        dat[...] = low
        da_ref[...] = dr_ref[...]
        sumo_ref[...] = jnp.zeros_like(sumo_ref)
        sumo_ref[0:1] = colsum(low.astype(F32))

    d = dat[...]
    grad_o = dot(o_ref[...], d, 0, 0).astype(BF)
    wq, wk, wv, wo = attn_weights(place_ref[1] == 0, (w0, w1, w2, w3, w4, w5))
    do_sc[...] = dot(d, wo, 1, 1).astype(BF)
    dk[...] = jnp.zeros_like(dk)
    dv[...] = jnp.zeros_like(dv)
    lane = lax.broadcasted_iota(jnp.int32, (BLOCK, 2 * HDIM), 1)
    tiles = [(b, pair) for b in range(blocks) for pair in range(GROUP // 2)]

    def products(b, pair):
        lo, hi = near(b, blocks)
        rows, lanes = block_of(b, pair)
        same = sk_ref[lo:hi, 0:1] == sq_ref[0:1, rows]
        query = two_heads(q_ref[rows, lanes] * SCALE, lane)
        d_out = two_heads(do_sc[rows, lanes], lane)
        scores = dot(k_ref[lo:hi, lanes], query, 1, 1)
        scores = jnp.where(jnp.concatenate([same, same], axis=1), scores, -1000000000.0)
        return query, d_out, scores, dot(v_ref[lo:hi, lanes], d_out, 1, 1)

    ahead = products(*tiles[0])
    for j, (b, pair) in enumerate(tiles):
        lo, hi = near(b, blocks)
        rows, lanes = block_of(b, pair)
        query, d_out, scores, d_probs = ahead
        if j + 1 < len(tiles):
            ahead = products(*tiles[j + 1])
        grown = jnp.exp(scores - jnp.max(scores, axis=0, keepdims=True))
        probs = grown * (1.0 / jnp.sum(grown, axis=0, keepdims=True))
        d_scores = probs * (d_probs - jnp.sum(probs * d_probs, axis=0, keepdims=True))
        d_scores = d_scores.astype(BF)
        dv[lo:hi, lanes] += dot(probs.astype(BF), d_out)
        dk[lo:hi, lanes] += dot(d_scores, query)
        d_query = dot(d_scores, k_ref[lo:hi, lanes], 0, 0)
        dq[rows, lanes] = jnp.where(lane < HDIM, d_query[:BLOCK], d_query[BLOCK:]) * SCALE
    a = a_ref[...]
    out = da_ref[...]
    lows = (dq[...].astype(BF), dk[...].astype(BF), dv[...].astype(BF))
    made = []
    for low, weight in zip(lows, (wq, wk, wv)):
        made.append(dot(a, low, 0, 0).astype(BF))
        out = out + dot(low, weight, 1, 1)
    da_ref[...] = out
    sums_ref[...] = jnp.zeros_like(sums_ref)
    sums_ref[0:1] = colsum(lows[0].astype(F32))
    sums_ref[1:2] = colsum(lows[2].astype(F32))
    steps = HEADS // GROUP
    for j in range(steps):
        @pl.when(step == j)
        def _(j=j):
            here = slice(j * cols, (j + 1) * cols)
            for unit in range(3):
                grads[unit, :, here] = made[unit]
            grads[3, here, :] = grad_o

    @pl.when(step == steps - 1)
    def _():
        def copies(plane):
            out = []
            for unit in range(4):
                to = keep_ref if unit // 2 == plane else send_ref
                at = (unit % 2) * size
                core = unit // 2
                for block in range(quads * outer):
                    rel = send_index(block % quads, place_ref, core)
                    out.append(
                        pltpu.make_async_copy(
                            grads.at[unit, block * size : (block + 1) * size, :],
                            to.at[rel, outer_index(block // quads, core), at : at + size, :],
                            sem.at[unit, block],
                        )
                    )
            return out

        def move(plane):
            items = copies(plane)
            copy_all(items, True)
            copy_all(items, False)

        by_section(place_ref[1], move)


def attn_bwd(place, outer, dr, a, seg_col, seg_row, q, k, v, o, planes):
    length, width = a.shape
    size = width // (4 * outer)
    cols = GROUP * HDIM
    group = pl.BlockSpec((length, cols), lambda g: (0, g))
    chunk = shape_of((4, outer, 2 * size, width), BF)
    return pl.pallas_call(
        attn_bwd_kernel,
        grid=(HEADS // GROUP,),
        in_specs=[
            pl.BlockSpec(memory_space=pltpu.SMEM),
            whole_block(length, width),
            whole_block(length, width),
            whole_block(8, length),
            whole_block(length, 128),
        ]
        + [group] * 4
        + attn_weight_blocks(width, cols),
        out_specs=[
            pl.BlockSpec(memory_space=pl.ANY),
            pl.BlockSpec(memory_space=pl.ANY),
            whole_block(length, width),
            pl.BlockSpec((8, cols), lambda g: (0, g)),
            whole_block(8, width),
        ],
        out_shape=[chunk, chunk, shape_of((length, width), F32), shape_of((8, width), F32), shape_of((8, width), F32)],
        scratch_shapes=[pltpu.VMEM((length, width), BF), pltpu.VMEM((length, cols), BF)]
        + [pltpu.VMEM((length, cols), F32)] * 3
        + [pltpu.VMEM((4, width, width), BF), pltpu.SemaphoreType.DMA((4, 4 * outer))],
        cost_estimate=NO_COST,
        name="attn_bwd",
    )(place, dr, a, seg_row, seg_col, q, k, v, o, *attn_weight_args(planes))


def flip(value, mask, other=None):
    count = lax.axis_size("dp")
    masks = (mask, mask if other is None else other)
    pairs = [(s * count + i, s * count + (i ^ masks[s])) for s in range(2) for i in range(count)]
    return lax.ppermute(value, BOTH, pairs)


def swap(value):
    count = lax.axis_size("dp")
    pairs = [(s * count + i, (1 - s) * count + i) for s in range(2) for i in range(count)]
    return lax.ppermute(value, BOTH, pairs)


class Order:
    def __init__(self, mark):
        self.mark = mark

    def wait(self, *values):
        leaves, tree = jax.tree.flatten(values)
        *leaves, self.mark = lax.optimization_barrier((*leaves, self.mark))
        out = jax.tree.unflatten(tree, leaves)
        return out[0] if len(values) == 1 else out

    def now(self, *values):
        leaves, tree = jax.tree.flatten(values)
        leaves = lax.optimization_barrier((*leaves, self.mark))[:-1]
        out = jax.tree.unflatten(tree, leaves)
        return out[0] if len(values) == 1 else out


class Gather:
    def __init__(self, order, block):
        self.order, self.own, self.bit = order, block[None], 4

    def bits(self):
        return (self.bit, 12 - self.bit) if is_small(lax.axis_size("dp")) else (self.bit, self.bit)

    def outer(self):
        self.got = flip(self.order.now(self.own), *self.bits())

    def outer_done(self):
        bits = self.bits()
        me, section = lax.axis_index("dp"), lax.axis_index("section")
        self.join((me & jnp.where(section == 0, *bits)) != 0)
        self.bit *= 2

    def join(self, high):
        own, got = self.own, self.got
        self.own = jnp.where(high, jnp.concatenate([got, own]), jnp.concatenate([own, got]))

    def rest_of_outer(self):
        while self.bit < lax.axis_size("dp") // 2:
            self.outer()
            self.outer_done()

    def first(self):
        self.got = flip(self.order.now(self.own), 1, 2)

    def first_done(self):
        me = lax.axis_index("dp")
        self.own, self.got = self.own[None], self.got[None]
        self.join(jnp.where(lax.axis_index("section") == 0, me & 1, me >> 1 & 1) != 0)

    def second(self):
        self.got = flip(self.order.now(self.own), 2, 1)

    def wait(self):
        self.got = self.order.wait(self.got)

    def assembled(self, place, units, size):
        return assemble(place, units, size, self.own, self.got)


def assemble_kernel(units, size, place_ref, own_ref, got_ref, out, sem):
    outer = own_ref.shape[1]
    attn = len(out.shape) == 3
    section = place_ref[1]
    bit = (place_ref[0] >> (1 - section)) & 1

    def move(plane):
        moves = []
        for p, ref in enumerate((own_ref, got_ref)):
            for i in range(2):
                q = i * (1 + section) + (bit ^ p) * (2 - section)
                if attn:
                    tiles = size // PAD
                    chips = 4 * outer
                    more = ref.shape[2] - units * tiles
                    for z in range(outer):
                        chip = outer_index(z, section) * 4 + q
                        for u in range(units):
                            to = pl.ds((u * chips + chip) * tiles, tiles)
                            moves.append((ref.at[i, z, u * tiles : (u + 1) * tiles], out.at[to]))
                        if more:
                            to = pl.ds(units * chips * tiles + chip * more, more)
                            moves.append((ref.at[i, z, units * tiles :], out.at[to]))
                else:
                    for z in range(outer):
                        at = outer_index(z, section)
                        if plane == 0:
                            moves += [(ref.at[i, z, u], out.at[u, at, q]) for u in range(units)]
                        else:
                            moves.append((ref.at[i, z], out.at[at, q]))
        copies = [pltpu.make_async_copy(*item, sem.at[j]) for j, item in enumerate(moves)]
        copy_all(copies, True)
        copy_all(copies, False)

    if attn:
        move(0)
    else:
        by_section(section, move)


def assemble(place, units, size, own, got):
    _, outer, rows, width = own.shape
    attn = units == 2
    if is_small(4 * outer):
        if attn:
            shape = (4 * outer * rows // PAD, PAD, width)
            inner = (rows // PAD, PAD, width)
        else:
            shape = (units, outer, 4, size, width)
            inner = (units, size, width)
        whole = pl.pallas_call(
            lambda *refs: assemble_kernel(units, size, *refs),
            in_specs=[SCALARS] + [pl.BlockSpec(memory_space=pl.ANY)] * 2,
            out_specs=pl.BlockSpec(memory_space=pltpu.VMEM),
            out_shape=shape_of(shape, BF),
            scratch_shapes=[pltpu.SemaphoreType.DMA((4 * outer * (units + 1),))],
            cost_estimate=NO_COST,
            name="assemble",
        )(place, own.reshape((2, outer) + inner), got.reshape((2, outer) + inner))
        return whole.reshape((-1, width) if attn else (units, width, width))
    section = place[1]
    bit = (place[0] >> (1 - section)) & 1
    whole = jnp.zeros((outer, 4, rows, width), BF)
    for p, half in enumerate((own, got)):
        for i in range(2):
            q = i * (1 + section) + (bit ^ p) * (2 - section)
            whole = lax.dynamic_update_slice(whole, half[i][:, None], (0, q, 0, 0))
    whole = whole.reshape(4 * outer, rows, width)
    by_unit = [whole[:, j * size : (j + 1) * size].reshape(width, width) for j in range(units)]
    if attn:
        return jnp.concatenate(by_unit + [whole[:, units * size :].reshape(-1, width)])
    return jnp.where(section == 0, jnp.stack(by_unit), whole.reshape(units, width, width))


SWAPPED = (0, 2, 1, 3)


def is_small(count):
    return count == 16


def in_chips(chunk, place, units, count, core):
    quads, outer, rows, width = chunk.shape
    size = width // count
    if core:
        chunk = jnp.stack([chunk[:, z] for z in SWAPPED], axis=1)
        chunk = jnp.stack([chunk[q] for q in SWAPPED])
    if units:
        natural = chunk.reshape(quads, outer, units, -1, width).transpose(2, 1, 0, 3, 4)
        block = natural.reshape(units, count // 4, 4, size, width).transpose(2, 1, 0, 3, 4)
        block = block.reshape(4, count // 4, units * size, width)
    else:
        natural = chunk.transpose(1, 0, 2, 3).reshape(count // 4, 4, -1, width)
        block = natural.transpose(1, 0, 2, 3)
    return relative(block, place, core)


def in_planes(keep, send, place, units, count):
    if is_small(count):
        return keep, send
    first = place[1] == 0
    keeps, sends = [[in_chips(item, place, units[core], count, core) for core in range(2)] for item in (keep, send)]
    return jnp.where(first, *keeps), jnp.where(first, sends[1], sends[0])


def relative(block, place, core):
    at = [place[0] ^ (SWAPPED[rel] if core else rel) for rel in range(4)]
    block = jnp.stack([lax.dynamic_index_in_dim(block, q, 0, False) for q in at])
    if core == 0 or not is_small(lax.axis_size("dp")):
        return block
    return jnp.stack([block[:, z] for z in SWAPPED], axis=1)


def low(value):
    return value.astype(BF)


class Reduce:
    def __init__(self, order, keep, send):
        self.order = order
        self.keep = keep.reshape((2, 2) + keep.shape[1:])
        self.got = swap(order.now(send)).reshape(self.keep.shape)

    def wait(self):
        self.got = self.order.wait(self.got)

    def send(self, value, *masks):
        self.got = flip(self.order.now(low(value)), *masks)

    def second(self):
        self.terms = (self.keep, self.got)
        self.send(self.total(1), 2, 1)

    def total(self, which):
        return sum((item[which].astype(F32) for item in self.terms), 0.0)

    def first(self):
        self.terms = (self.terms[0][0], self.terms[1][0], self.got)
        self.send(self.total(1), 1, 2)

    def outer(self):
        self.rest = self.total(0) + self.got.astype(F32)
        self.bit = lax.axis_size("dp") // 2
        self.halve()

    def halve(self):
        size = self.rest.shape[0] // 2
        me, section = lax.axis_index("dp"), lax.axis_index("section")
        bits = (self.bit, 12 - self.bit) if is_small(lax.axis_size("dp")) else (self.bit, self.bit)
        high = (me & jnp.where(section == 0, *bits)) != 0
        low_half, high_half = self.rest[:size], self.rest[size:]
        self.rest = jnp.where(high, high_half, low_half)
        self.send(jnp.where(high, low_half, high_half), *bits)

    def next_outer(self):
        self.rest = self.rest + self.got.astype(F32)
        self.bit //= 2
        self.halve()

    def rest_of_outer(self):
        while self.bit > 8:
            self.next_outer()
        if self.bit > 4:
            self.next_outer()

    def finish(self):
        return (self.rest + self.got.astype(F32))[0]


def shards(tokens, segment_ids, cotangent, qkv_w, out_w, up_w, down_w, gains_w, shifts_w, up_b, head_w):
    count = lax.axis_size("dp")
    section = lax.axis_index("section")
    me = lax.axis_index("dp")
    first = section == 0
    place = jnp.stack([me & 3, section]).astype(jnp.int32)
    grad_place = place if is_small(count) else jnp.stack([jnp.zeros_like(section), section]).astype(jnp.int32)
    rows_dev, length, width = tokens.shape
    mine = rows_dev // 2
    size = width // count
    ff = up_w.shape[2]
    units = ff // width

    def cols(array, n):
        return [array[:, j * width : (j + 1) * width] for j in range(n)]

    q_u, k_u, v_u = cols(low(qkv_w[0]), 3)
    plane = (
        jnp.concatenate([q_u, k_u] + cols(low(up_w[0]), units)),
        jnp.concatenate([v_u, low(out_w[0]), low(down_w[0])]),
    )
    got = swap(jnp.where(first, plane[1], plane[0]))
    zero = jnp.where(first, plane[0], got)
    one = jnp.where(first, got, plane[1])
    small = low(jnp.concatenate([gains_w.reshape(-1), shifts_w.reshape(-1), up_b.reshape(-1)]))
    small_n = small.shape[0]
    small_rows = -(-small_n // width)
    head_n = head_w.shape[0] * head_w.shape[1]
    head_rows = -(-head_n // width)
    pad_rows = -(-(small_rows + head_rows) // PAD) * PAD

    def to_rows(flat, rows):
        return jnp.pad(flat, (0, rows * width - flat.shape[0])).reshape(rows, width)

    extra = jnp.concatenate(
        [
            to_rows(small, small_rows),
            to_rows(low(head_w).reshape(-1), head_rows),
            jnp.zeros((pad_rows - small_rows - head_rows, width), BF),
        ]
    )
    cut = 2 * size

    order = Order(place)
    a0_g = Gather(order, jnp.concatenate([zero[:cut], extra]))
    f0_g, a1_g, f1_g = Gather(order, zero[cut:]), Gather(order, one[:cut]), Gather(order, one[cut:])

    def both(chunk, units):
        own = chunk.assembled(place, units, size)
        return own, swap(order.now(own))

    a0_g.outer()
    a0_g.wait()
    a0_g.outer_done()
    a0_g.rest_of_outer()
    a0_g.outer()
    a0_g.wait()
    a0_g.outer_done()
    a0_g.first()
    f0_g.outer()
    a0_g.got, f0_g.got = order.wait(a0_g.got, f0_g.got)
    a0_g.first_done()
    f0_g.outer_done()
    f0_g.rest_of_outer()
    a0_g.second()
    f0_g.outer()
    a1_g.outer()
    a0_g.got, f0_g.got, a1_g.got = order.wait(a0_g.got, f0_g.got, a1_g.got)
    f0_g.outer_done()
    f0_g.first()
    a1_g.outer_done()
    a1_g.rest_of_outer()
    a1_g.outer()
    f1_g.outer()
    planes_a0 = both(a0_g, 2)
    planes_a0, f0_g.got, a1_g.got, f1_g.got = order.wait(planes_a0, f0_g.got, a1_g.got, f1_g.got)
    f0_g.first_done()
    f0_g.second()
    a1_g.outer_done()
    a1_g.first()
    f1_g.outer_done()
    f1_g.rest_of_outer()
    f1_g.outer()
    tails = [item[2 * width :] for item in planes_a0]

    smalls, heads = [], []
    tails_full = (jnp.where(first, tails[0], tails[1]), jnp.where(first, tails[1], tails[0]))
    tails_full = [item.reshape(count, pad_rows, width) for item in tails_full]
    n_g = gains_w.shape[1] * size
    n_s = shifts_w.shape[1] * size
    for tail in tails_full:
        flat = tail[:, :small_rows].reshape(count, -1)[:, :small_n].astype(F32)
        gains = flat[:, :n_g].reshape(count, -1, size).transpose(1, 0, 2).reshape(-1, width)
        shift = flat[:, n_g : n_g + n_s].reshape(count, -1, size).transpose(1, 0, 2).reshape(-1, width)
        cup = flat[:, n_g + n_s :].reshape(-1)
        eight = lambda item: jnp.pad(item, ((0, 8 - item.shape[0]), (0, 0)))
        smalls.append((eight(gains), eight(shift), cup))
        block = tail[:, small_rows : small_rows + head_rows].reshape(count, -1)[:, :head_n]
        heads.append(block.reshape(count * head_w.shape[0], head_w.shape[1]))
    head = jnp.concatenate(heads)
    (gain0, shift0, cup0), (gain1, shift1, cup1) = smalls

    own = lax.dynamic_slice_in_dim(tokens, section * mine, mine, 0)
    seg = lax.dynamic_slice_in_dim(segment_ids, section * mine, mine, 0)
    cot = lax.dynamic_slice_in_dim(cotangent, section * mine, mine, 0)
    rows = range(mine)
    seg_col = [jnp.broadcast_to(seg[r][:, None], (length, 128)) for r in rows]
    seg_row = [jnp.broadcast_to(seg[r][None], (8, length)) for r in rows]

    a0 = order.now([own[r] for r in rows])
    kept_a0 = [attn_fwd(place, a0[r], seg_col[r], seg_row[r], planes_a0, shift0) for r in rows]
    kept_a0, f0_g.got, a1_g.got, f1_g.got = order.wait(kept_a0, f0_g.got, a1_g.got, f1_g.got)
    a1_g.first_done()
    a1_g.second()
    f1_g.outer_done()
    f1_g.first()
    planes_f0 = order.wait(both(f0_g, units))
    n1 = [kept[4] for kept in kept_a0]
    n1 = order.now(n1)
    kept_f0 = [ffn_fwd(place, n1[r], planes_f0, cup0, gain0, shift0) for r in rows]
    kept_f0, a1_g.got, f1_g.got = order.wait(kept_f0, a1_g.got, f1_g.got)
    f1_g.first_done()
    f1_g.second()
    planes_a1 = order.wait(both(a1_g, 2))
    a1 = [kept[4] for kept in kept_f0]
    a1 = order.now(a1)
    kept_a1 = [attn_fwd(place, a1[r], seg_col[r], seg_row[r], planes_a1, shift1) for r in rows]
    kept_a1, f1_g.got = order.wait(kept_a1, f1_g.got)
    planes_f1 = both(f1_g, units)
    n1 = [kept[4] for kept in kept_a1]
    kept_f1 = [ffn_fwd(place, n1[r], planes_f1, cup1, gain1, shift1) for r in rows]

    d_y1, g_head = [], 0.0
    for r in rows:
        y1 = kept_f1[r][4]
        proj = dot(y1, head)
        rho = lax.rsqrt(jnp.sum(proj * proj, axis=-1, keepdims=True) + norm_eps)
        c = cot[r].astype(F32)
        d_proj = low(rho * c - rho * rho * rho * proj * jnp.sum(proj * c, axis=-1, keepdims=True))
        g_head = g_head + dot(y1, d_proj, 0, 0)
        d_y1.append(dot(d_proj, head, 1, 1))

    def total(items):
        out = items[0]
        for item in items[1:]:
            out = jax.tree.map(lambda x, y: (x.astype(F32) + y.astype(F32)).astype(x.dtype), out, item)
        return out

    def ffn_back(d_out, kept_a, kept_f, planes, gain, shift):
        outs = [
            ffn_bwd(grad_place, 4, d_out[r], *kept_f[r][2:4], *kept_f[r][:2], planes, *kept_a[r][4:6], gain, shift)
            for r in rows
        ]
        keep, send, sums, cup = total([(o[0], o[1], o[3], o[4]) for o in outs])
        keep, send = in_planes(keep, send, place, (units, 0), count)
        return keep, send, [o[2] for o in outs], sums, cup

    def attn_back(d_out, a, kept, planes):
        outs = [attn_bwd(grad_place, 4, d_out[r], a[r], seg_col[r], seg_row[r], *kept[r][:4], planes) for r in rows]
        keep, send, sums, sumo = total([(o[0], o[1], o[3], o[4]) for o in outs])
        keep, send = in_planes(keep, send, place, (2, 2), count)
        return keep, send, [o[2] for o in outs], sums, sumo

    keep, send, d_r, sums_f1, g_cup1 = ffn_back(d_y1, kept_a1, kept_f1, planes_f1, gain1, shift1)
    f1_r = Reduce(order, keep, send)
    f1_r.wait()
    f1_r.second()
    d_r = order.now(d_r)
    keep, send, d_a1, sums_a1, sumo_a1 = attn_back(d_r, a1, kept_a1, planes_a1)
    d_a1, f1_r.got = order.wait(d_a1, f1_r.got)
    a1_r = Reduce(order, keep, send)
    f1_r.first()
    a1_r.wait()
    a1_r.second()
    d_y0 = order.now([low(item) for item in d_a1])
    keep, send, d_r, sums_f0, g_cup0 = ffn_back(d_y0, kept_a0, kept_f0, planes_f0, gain0, shift0)
    d_r, f1_r.got, a1_r.got = order.wait(d_r, f1_r.got, a1_r.got)
    f0_r = Reduce(order, keep, send)
    f1_r.outer()
    a1_r.first()
    f0_r.wait()
    f0_r.second()
    d_r = order.now(d_r)
    keep, send, d_a0, sums_a0, sumo_a0 = attn_back(d_r, a0, kept_a0, planes_a0)

    f1_r.got, a1_r.got, f0_r.got, d_a0 = order.wait(f1_r.got, a1_r.got, f0_r.got, d_a0)

    def small_block(sums_a, sumo, sums_f, g_cup, head_part, core):
        gains = jnp.stack([sums_f[0], sums_f[1]]).reshape(2, count, size).transpose(1, 0, 2)
        shift = jnp.stack([sums_a[0], sums_a[1], sumo[0], sums_f[3], sums_f[4], sums_f[2]])
        shift = shift.reshape(6, count, size).transpose(1, 0, 2)
        flat = jnp.concatenate(
            [gains.reshape(count, -1), shift.reshape(count, -1), g_cup.reshape(count, -1)], axis=1
        )
        flat = jnp.pad(flat, ((0, 0), (0, small_rows * width - small_n)))
        piece = jnp.pad(head_part.reshape(count, -1), ((0, 0), (0, head_rows * width - head_n)))
        block = jnp.concatenate(
            [
                flat.reshape(count, small_rows, width),
                piece.reshape(count, head_rows, width),
                jnp.zeros((count, pad_rows - small_rows - head_rows, width), F32),
            ],
            axis=1,
        )
        return relative(low(block).reshape(count // 4, 4, pad_rows, width).transpose(1, 0, 2, 3), place, core)

    half_head = g_head.reshape(2, -1, head_w.shape[1])
    tail0 = small_block(sums_a0, sumo_a0, sums_f0, g_cup0, half_head[0], 0)
    tail1 = small_block(sums_a1, sumo_a1, sums_f1, g_cup1, half_head[1], 1)
    keep = jnp.concatenate([keep, jnp.where(first, tail0, tail1)], axis=2)
    send = jnp.concatenate([send, jnp.where(first, tail1, tail0)], axis=2)
    a0_r = Reduce(order, keep, send)
    f1_r.rest_of_outer()
    a1_r.outer()
    f0_r.first()
    a0_r.wait()
    a0_r.second()
    a1_r.got, f1_r.got, f0_r.got = order.wait(a1_r.got, f1_r.got, f0_r.got)
    a1_r.rest_of_outer()
    f0_r.outer()
    a0_r.wait()
    a0_r.first()
    a1_r.got, f0_r.got, a0_r.got = order.wait(a1_r.got, f0_r.got, a0_r.got)
    f0_r.rest_of_outer()
    a0_r.outer()
    a0_r.got, f0_r.got = order.wait(a0_r.got, f0_r.got)
    a0_r.rest_of_outer()
    done_f1, done_a1, done_f0, done_a0 = [item.finish() for item in (f1_r, a1_r, f0_r, a0_r)]

    sums_zero = jnp.concatenate([done_a0[:cut], done_f0])
    sums_one = jnp.concatenate([done_a1, done_f1])
    other = swap(jnp.where(first, sums_one, sums_zero))
    low_plane = jnp.where(first, sums_zero, other)
    high_plane = jnp.where(first, other, sums_one)

    def unit(array, j):
        return array[j * size : (j + 1) * size]

    qkv_grad = jnp.concatenate([unit(low_plane, 0), unit(low_plane, 1), unit(high_plane, 0)], axis=1)
    out_grad = unit(high_plane, 1)
    up_grad = jnp.concatenate([unit(low_plane, 2 + j) for j in range(units)], axis=1)
    down_grad = high_plane[cut:]
    tail = done_a0[cut:]
    flat = tail[:small_rows].reshape(-1)[:small_n]
    gain_grad = flat[:n_g].reshape(gains_w.shape)
    shift_grad = flat[n_g : n_g + n_s].reshape(shifts_w.shape)
    cup_grad = flat[n_g + n_s :].reshape(up_b.shape)
    head_grad = tail[small_rows : small_rows + head_rows].reshape(-1)[:head_n].reshape(head_w.shape)

    d_first, d_second = jnp.stack(d_a0), jnp.stack(d_a1)
    got = swap(jnp.where(first, d_second, d_first))
    keep = jnp.where(first, d_first, d_second)
    input_grads = jnp.where(first, jnp.concatenate([keep, got]), jnp.concatenate([got, keep]))
    return (
        qkv_grad[None],
        out_grad[None],
        up_grad[None],
        down_grad[None],
        gain_grad,
        shift_grad,
        cup_grad,
        head_grad,
        input_grads[None],
    )


def solution(mesh):
    return jax.shard_map(
        shards,
        mesh=mesh,
        in_specs=(
            P("dp", None, None),
            P("dp", None),
            P("dp", None, None),
            P("section", "dp", None),
            P("section", "dp", None),
            P("section", "dp", None),
            P("section", "dp", None),
            P("section", None, "dp"),
            P("section", None, "dp"),
            P("section", "dp"),
            P(("section", "dp"), None),
        ),
        out_specs=(
            P("section", "dp", None),
            P("section", "dp", None),
            P("section", "dp", None),
            P("section", "dp", None),
            P("section", None, "dp"),
            P("section", None, "dp"),
            P("section", "dp"),
            P(("section", "dp"), None),
            P("section", "dp", None, None),
        ),
        check_vma=False,
    )
```

time: 656 us -> 480 us (0.73)
  waiting for transfers between devices: 261 us -> 158 us
  Pallas kernels: 205 us -> 164 us
  local copies, waits for them, and re-layouts: 68 us -> 29.6 us
  other arithmetic: 50.3 us -> 71.9 us
  starting transfers between devices: 55.9 us -> 41.6 us
    ppermute x48 -> x32, waiting for transfers between devices: 251 us -> 140 us  [flip(): return lax.ppermute(value, BOTH, pairs)]
    pallas_call x8, Pallas kernels: 105 us -> 82.5 us  [the longest x2 32.2 us: ffn_fwd(): pl.pallas_call(ffn_fwd_kernel, grid=(units,), in_specs=[SCALARS, whole_bl...]
    pallas_call x2, Pallas kernels: 62.3 us -> 42.1 us  [attn_bwd(): pl.pallas_call(attn_bwd_kernel, grid=(HEADS // GROUP,), in_specs=[pl.Bloc...]
    select_n x9 -> x25, other arithmetic: 6.03 us -> 26.1 us  [the longest x24 24.2 us: join(): jnp.where(high, jnp.concatenate([got, own]), jnp.concatenate([own, got]))]
    ppermute x48 -> x32, starting transfers between devices: 51.6 us -> 39.5 us  [flip(): return lax.ppermute(value, BOTH, pairs)]
    unnamed x130 -> x122, local copies, waits for them, and re-layouts: 16.4 us -> 7.51 us
    ppermute x27 -> x11, waiting for transfers between devices: 9.86 us -> 17.8 us  [swap(): return lax.ppermute(value, BOTH, pairs)]
  transfers between devices with their start and end apart: 75 -> 43, of which waited for: 30 -> 25; matrix products, arithmetic and copies ran while one was open for 14% -> 15% of each run, Pallas kernels for 17% -> 23%
where the time goes in v3:
time: 480 us; the launch traced here: 471 us
  Pallas kernels  164 us (34%)
  waiting for transfers between devices  158 us (33%)
  other arithmetic  71.9 us (15%)
  starting transfers between devices  41.6 us (9%)
  local copies, waits for them, and re-layouts  29.6 us (6%)
    ppermute x32, waiting for transfers between devices, flip(): return lax.ppermute(value, BOTH, pairs)  140 us
    pallas_call x2, Pallas kernels, attn_bwd(): pl.pallas_call(attn_bwd_kernel, grid=(HEADS // GROUP,), in_specs=[pl.Bloc...  42.1 us
    ppermute x32, starting transfers between devices, flip(): return lax.ppermute(value, BOTH, pairs)  39.5 us
    pallas_call x2, Pallas kernels, ffn_bwd(): pl.pallas_call(ffn_bwd_kernel, grid=(units,), in_specs=[pl.BlockSpec(memo...  39.5 us
    pallas_call x2, Pallas kernels, ffn_fwd(): pl.pallas_call(ffn_fwd_kernel, grid=(units,), in_specs=[SCALARS, whole_bl...  32.2 us
    pallas_call x2, Pallas kernels, attn_fwd(): pl.pallas_call(attn_fwd_kernel, grid=(HEADS // GROUP,), in_specs=[SCALARS...  28.7 us
    convert_element_type x23, other arithmetic, low(): return value.astype(BF)  25.9 us
    select_n x24, other arithmetic, join(): jnp.where(high, jnp.concatenate([got, own]), jnp.concatenate([own, got]))  24.2 us
  transfers between devices with their start and end apart: 43, of which 25 were waited for; matrix products, arithmetic and copies ran while one was open for 15% of the time, Pallas kernels for 23%

profile of v3, /device:TPU:0, one launch (start us, length us, event | category | flops | bytes accessed | tf_op | source)
XLA Modules:
  0.0 471.2 jit_solution(190417856001177882)
XLA Ops:
  19.1 7.7 %collective-permute-done.2 = bf16[2,112,768]{2,1,0:T(8,128)(2,1)S(1)} collective-permute-done((bf16[2,112,768]{2,1,0:T(8,128)(2,1)S(1)}, bf16[2,112,768]{2,1,0:T(8,128)(2,1)S(1)}, u32[]{:S(2)}, u32[]{:S(2)}) %collective-permute-start.2) | collective-permute-done | bytes 344096 | tf_op jit(solution)/shard_map/ppermute | solution.py:530
  33.2 8.1 %collective-permute-done.4 = bf16[1,192,768]{2,1,0:T(8,128)(2,1)S(1)} collective-permute-done((bf16[1,192,768]{2,1,0:T(8,128)(2,1)S(1)}, bf16[1,192,768]{2,1,0:T(8,128)(2,1)S(1)}, u32[]{:S(2)}, u32[]{:S(2)}) %collective-permute-start.4) | collective-permute-done | bytes 294944 | tf_op jit(solution)/shard_map/ppermute | solution.py:530
  51.3 7.0 %collective-permute-done.7 = bf16[1,96,768]{2,1,0:T(8,128)(2,1)S(1)} collective-permute-done((bf16[1,96,768]{2,1,0:T(8,128)(2,1)S(1)}, bf16[1,96,768]{2,1,0:T(8,128)(2,1)S(1)}, u32[]{:S(2)}, u32[]{:S(2)}) %collective-permute-start.7) | collective-permute-done | bytes 147488 | tf_op jit(solution)/shard_map/ppermute | solution.py:530
  76.6 12.2 %collective-permute-done.10 = bf16[2,96,768]{2,1,0:T(8,128)(2,1)S(1)} collective-permute-done((bf16[2,96,768]{2,1,0:T(8,128)(2,1)S(1)}, bf16[2,96,768]{2,1,0:T(8,128)(2,1)S(1)}, u32[]{:S(2)}, u32[]{:S(2)}) %collective-permute-start.10) | collective-permute-done | bytes 294944 | tf_op jit(solution)/shard_map/ppermute | solution.py:530
  101.0 14.3 %attn_fwd.2 = (bf16[512,768]{1,0:T(8,128)(2,1)}, bf16[512,768]{1,0:T(8,128)(2,1)}, bf16[512,768]{1,0:T(8,128)(2,1)}, bf16[512,768]{1,0:T(8,128)(2,1)}, f32[512,768]{1,0:T(8,128)}, /*index=5*/f32[512,128]{1,0:T(8,128)}) custom-call(s32[2]{0:T(128)} %pad_add_fusion.refs_0_.place_ref, bf16[512,768]{1,0:T(8,128)(2,1)} %dynamic-slice_bitcast_fusion.a_ref, ...), custom_call_target="tpu_custom_call" | custom-call | tf_op jit(solution)/shard_map/attn_fwd/pallas_call | solution.py:169
  119.3 7.5 %collective-permute-done.12 = bf16[2,4,192,768]{3,2,1,0:T(8,128)(2,1)} collective-permute-done((bf16[2,4,192,768]{3,2,1,0:T(8,128)(2,1)}, bf16[2,4,192,768]{3,2,1,0:T(8,128)(2,1)}, u32[]{:S(2)}, u32[]{:S(2)}) %collective-permute-start.12) | collective-permute-done | bytes 2359328 | tf_op jit(solution)/shard_map/ppermute | solution.py:530
  126.8 6.3 %assemble.5 = bf16[4,4,4,48,768]{4,3,2,1,0:T(8,128)(2,1)} custom-call(s32[2]{0:T(128)} %pad_add_fusion.refs_0_.place_ref, bf16[2,4,4,48,768]{4,3,2,1,0:T(8,128)(2,1)} %maximum_select_fusion.2.refs_1_, bf16[2,4,4,48,768]{4,3,2,1,0:T(8,128)(2,1)} %bitcast.33.refs_2_), custom_call_target="tpu_custom_call" | custom-call | tf_op jit(solution)/shard_map/assemble/pallas_call | solution.py:649
  145.3 16.1 %ffn_fwd.2 = (bf16[512,3072]{1,0:T(8,128)(2,1)}, bf16[512,3072]{1,0:T(8,128)(2,1)}, f32[512,768]{1,0:T(8,128)}, f32[512,128]{1,0:T(8,128)}, bf16[512,768]{1,0:T(8,128)(2,1)}) custom-call(s32[2]{0:T(128)} %pad_add_fusion.refs_0_.place_ref, f32[512,768]{1,0:T(8,128)} %get-tuple-element.220.n1_ref, bf16[4,768,768]{2,1,0:T(8,128)(2,1)} %bitcast.254, ...), custom_call_target="tpu_custom_call" | custom-call | tf_op jit(solution)/shard_map/ffn_fwd/pallas_call | solution.py:233
  161.4 5.9 %collective-permute-done.16 = bf16[2,4,96,768]{3,2,1,0:T(8,128)(2,1)} collective-permute-done((bf16[2,4,96,768]{3,2,1,0:T(8,128)(2,1)}, bf16[2,4,96,768]{3,2,1,0:T(8,128)(2,1)}, u32[]{:S(2)}, u32[]{:S(2)}) %collective-permute-start.16) | collective-permute-done | bytes 1179680 | tf_op jit(solution)/shard_map/ppermute | solution.py:530
  179.4 14.4 %attn_fwd.3 = (bf16[512,768]{1,0:T(8,128)(2,1)}, bf16[512,768]{1,0:T(8,128)(2,1)}, bf16[512,768]{1,0:T(8,128)(2,1)}, bf16[512,768]{1,0:T(8,128)(2,1)}, f32[512,768]{1,0:T(8,128)}, /*index=5*/f32[512,128]{1,0:T(8,128)}) custom-call(s32[2]{0:T(128)} %pad_add_fusion.refs_0_.place_ref, bf16[512,768]{1,0:T(8,128)(2,1)} %get-tuple-element.237.a_ref, ...), custom_call_target="tpu_custom_call" | custom-call | tf_op jit(solution)/shard_map/attn_fwd/pallas_call | solution.py:169
  193.8 10.5 %collective-permute-done.19 = bf16[2,4,192,768]{3,2,1,0:T(8,128)(2,1)} collective-permute-done((bf16[2,4,192,768]{3,2,1,0:T(8,128)(2,1)}, bf16[2,4,192,768]{3,2,1,0:T(8,128)(2,1)}, u32[]{:S(2)}, u32[]{:S(2)}) %collective-permute-start.19) | collective-permute-done | bytes 2359328 | tf_op jit(solution)/shard_map/ppermute | solution.py:530
  204.3 6.4 %assemble.7 = bf16[4,4,4,48,768]{4,3,2,1,0:T(8,128)(2,1)} custom-call(s32[2]{0:T(128)} %pad_add_fusion.refs_0_.place_ref, bf16[2,4,4,48,768]{4,3,2,1,0:T(8,128)(2,1)} %maximum_select_fusion.4.refs_1_, bf16[2,4,4,48,768]{4,3,2,1,0:T(8,128)(2,1)} %bitcast.57.refs_2_), custom_call_target="tpu_custom_call" | custom-call | tf_op jit(solution)/shard_map/assemble/pallas_call | solution.py:649
  219.1 16.1 %ffn_fwd.3 = (bf16[512,3072]{1,0:T(8,128)(2,1)}, bf16[512,3072]{1,0:T(8,128)(2,1)}, f32[512,768]{1,0:T(8,128)}, f32[512,128]{1,0:T(8,128)}, bf16[512,768]{1,0:T(8,128)(2,1)}) custom-call(s32[2]{0:T(128)} %pad_add_fusion.refs_0_.place_ref, f32[512,768]{1,0:T(8,128)} %get-tuple-element.248.n1_ref, bf16[4,768,768]{2,1,0:T(8,128)(2,1)} %bitcast.257, ...), custom_call_target="tpu_custom_call" | custom-call | tf_op jit(solution)/shard_map/ffn_fwd/pallas_call | solution.py:233
  238.4 19.7 %ffn_bwd.2 = (bf16[4,4,192,768]{3,2,1,0:T(8,128)(2,1)}, bf16[4,4,192,768]{3,2,1,0:T(8,128)(2,1)}, f32[512,768]{1,0:T(8,128)}, f32[8,768]{1,0:T(8,128)}, f32[4,1,768]{2,1,0:T(1,128)}) custom-call(s32[2]{0:T(128)} %pad_add_fusion.refs_0_.place_ref, f32[512,768]{1,0:T(8,128)} %fusion.48.dy_ref, f32[512,768]{1,0:T(8,128)} %get-tuple-element.253.n2_ref, ...), custom_call_target="tpu_custom_call" | custom-call | tf_op jit(solution)/shard_map/ffn_bwd/pallas_call | solution.py:353
  258.3 7.9 %collective-permute-done.21 = bf16[4,4,192,768]{3,2,1,0:T(8,128)(2,1)S(1)} collective-permute-done((bf16[4,4,192,768]{3,2,1,0:T(8,128)(2,1)}, bf16[4,4,192,768]{3,2,1,0:T(8,128)(2,1)S(1)}, u32[]{:S(2)}, u32[]{:S(2)}) %collective-permute-start.21) | collective-permute-done | bytes 4718624 | tf_op jit(solution)/shard_map/ppermute | solution.py:536
  272.1 21.0 %attn_bwd.2 = (bf16[4,4,96,768]{3,2,1,0:T(8,128)(2,1)}, bf16[4,4,96,768]{3,2,1,0:T(8,128)(2,1)}, f32[512,768]{1,0:T(8,128)}, f32[8,768]{1,0:T(8,128)}, f32[8,768]{1,0:T(8,128)}) custom-call(s32[2]{0:T(128)} %pad_add_fusion.refs_0_.place_ref, f32[512,768]{1,0:T(8,128)} %get-tuple-element.262.dr_ref, bf16[512,768]{1,0:T(8,128)(2,1)} %get-tuple-element.237.a_ref, ...), custom_call_target="tpu_custom_call" | custom-call | tf_op jit(solution)/shard_map/attn_bwd/pallas_call | solution.py:498
  293.1 7.7 %collective-permute-done.22 = bf16[2,4,192,768]{3,2,1,0:T(8,128)(2,1)} collective-permute-done((bf16[2,4,192,768]{3,2,1,0:T(8,128)(2,1)}, bf16[2,4,192,768]{3,2,1,0:T(8,128)(2,1)}, u32[]{:S(2)}, u32[]{:S(2)}) %collective-permute-start.22) | collective-permute-done | bytes 2359328 | tf_op jit(solution)/shard_map/ppermute | solution.py:530
  309.4 19.8 %ffn_bwd.3 = (bf16[4,4,192,768]{3,2,1,0:T(8,128)(2,1)}, bf16[4,4,192,768]{3,2,1,0:T(8,128)(2,1)}, f32[512,768]{1,0:T(8,128)}, f32[8,768]{1,0:T(8,128)}, f32[4,1,768]{2,1,0:T(1,128)}) custom-call(s32[2]{0:T(128)} %pad_add_fusion.refs_0_.place_ref, bf16[512,768]{1,0:T(8,128)(2,1)} %convert_element_type.343.dy_ref, f32[512,768]{1,0:T(8,128)} %get-tuple-element.277.n2_ref, ...), custom_call_target="tpu_custom_call" | custom-call | tf_op jit(solution)/shard_map/ffn_bwd/pallas_call | solution.py:353
  354.6 21.1 %attn_bwd.3 = (bf16[4,4,96,768]{3,2,1,0:T(8,128)(2,1)}, bf16[4,4,96,768]{3,2,1,0:T(8,128)(2,1)}, f32[512,768]{1,0:T(8,128)}, f32[8,768]{1,0:T(8,128)}, f32[8,768]{1,0:T(8,128)}) custom-call(s32[2]{0:T(128)} %pad_add_fusion.refs_0_.place_ref, f32[512,768]{1,0:T(8,128)} %get-tuple-element.293.dr_ref, bf16[512,768]{1,0:T(8,128)(2,1)} %dynamic-slice_bitcast_fusion.a_ref, ...), custom_call_target="tpu_custom_call" | custom-call | tf_op jit(solution)/shard_map/attn_bwd/pallas_call | solution.py:498
  391.7 12.9 %collective-permute-done.33 = bf16[1,192,768]{2,1,0:T(8,128)(2,1)S(1)} collective-permute-done((bf16[1,192,768]{2,1,0:T(8,128)(2,1)S(1)}, bf16[1,192,768]{2,1,0:T(8,128)(2,1)S(1)}, u32[]{:S(2)}, u32[]{:S(2)}) %collective-permute-start.33) | collective-permute-done | bytes 294944 | tf_op jit(solution)/shard_map/ppermute | solution.py:530
  417.8 10.7 %collective-permute-done.35 = bf16[1,96,768]{2,1,0:T(8,128)(2,1)S(1)} collective-permute-done((bf16[1,96,768]{2,1,0:T(8,128)(2,1)S(1)}, bf16[1,96,768]{2,1,0:T(8,128)(2,1)S(1)}, u32[]{:S(2)}, u32[]{:S(2)}) %collective-permute-start.35) | collective-permute-done | bytes 147488 | tf_op jit(solution)/shard_map/ppermute | solution.py:530
  428.5 10.0 %collective-permute-done.36 = bf16[2,192,768]{2,1,0:T(8,128)(2,1)S(1)} collective-permute-done((bf16[2,192,768]{2,1,0:T(8,128)(2,1)S(1)}, bf16[2,192,768]{2,1,0:T(8,128)(2,1)S(1)}, u32[]{:S(2)}, u32[]{:S(2)}) %collective-permute-start.36) | collective-permute-done | bytes 589856 | tf_op jit(solution)/shard_map/ppermute | solution.py:530
  441.5 6.0 %collective-permute-done.39 = bf16[1,192,768]{2,1,0:T(8,128)(2,1)S(1)} collective-permute-done((bf16[1,192,768]{2,1,0:T(8,128)(2,1)S(1)}, bf16[1,192,768]{2,1,0:T(8,128)(2,1)S(1)}, u32[]{:S(2)}, u32[]{:S(2)}) %collective-permute-start.39) | collective-permute-done | bytes 294944 | tf_op jit(solution)/shard_map/ppermute | solution.py:530
  447.6 7.4 %collective-permute-done.38 = bf16[2,112,768]{2,1,0:T(8,128)(2,1)S(1)} collective-permute-done((bf16[2,112,768]{2,1,0:T(8,128)(2,1)S(1)}, bf16[2,112,768]{2,1,0:T(8,128)(2,1)S(1)}, u32[]{:S(2)}, u32[]{:S(2)}) %collective-permute-start.38) | collective-permute-done | bytes 344096 | tf_op jit(solution)/shard_map/ppermute | solution.py:530
  (388 shorter events, 192.1 us)
Async XLA Ops:
  41.5 22.0 %collective-permute-start.5 = (bf16[2,4,112,768]{3,2,1,0:T(8,128)(2,1)S(1)}, bf16[2,4,112,768]{3,2,1,0:T(8,128)(2,1)S(1)}, u32[]{:S(2)}, u32[]{:S(2)}) collective-permute-start(bf16[2,4,112,768]{3,2,1,0:T(8,128)(2,1)S(1)} %maximum_select_fusion.6), channel_id=1, source_target_pairs={{0,2},{1,3},{2,0},{3,1},{4,6},{5,7},{6,4},{7,5},{8,10},{9,11},{10,... | collective-permute-start | bytes 4128776 | tf_op jit(solution)/shard_map/ppermute | solution.py:530
  44.7 18.8 %collective-permute-start.6 = (bf16[2,192,768]{2,1,0:T(8,128)(2,1)S(1)}, bf16[2,192,768]{2,1,0:T(8,128)(2,1)S(1)}, u32[]{:S(2)}, u32[]{:S(2)}) collective-permute-start(bf16[2,192,768]{2,1,0:T(8,128)(2,1)S(1)} %maximum_select_fusion.18), channel_id=1, source_target_pairs={{0,8},{1,9},{2,10},{3,11},{4,12},{5,13},{6,14},{7,15},{8,0},{9,1},... | collective-permute-start | bytes 1769480 | tf_op jit(solution)/shard_map/ppermute | solution.py:530
  69.2 20.3 %collective-permute-start.8 = (bf16[1792,768]{1,0:T(8,128)(2,1)}, bf16[1792,768]{1,0:T(8,128)(2,1)}, u32[]{:S(2)}, u32[]{:S(2)}) collective-permute-start(bf16[1792,768]{1,0:T(8,128)(2,1)} %bitcast.238), channel_id=1, source_target_pairs={{0,16},{1,17},{2,18},{3,19},{4,20},{5,21},{6,22},{7,23},{8,24},{9,... | collective-permute-start | bytes 8257544 | tf_op jit(solution)/shard_map/ppermute | solution.py:536
  69.5 19.2 %collective-permute-start.9 = (bf16[4,192,768]{2,1,0:T(8,128)(2,1)S(1)}, bf16[4,192,768]{2,1,0:T(8,128)(2,1)S(1)}, u32[]{:S(2)}, u32[]{:S(2)}) collective-permute-start(bf16[4,192,768]{2,1,0:T(8,128)(2,1)S(1)} %maximum_select_fusion.7), channel_id=1, source_target_pairs={{0,1},{1,0},{2,3},{3,2},{4,5},{5,4},{6,7},{7,6},{8,9},{9,8},{10,11... | collective-permute-start | bytes 3538952 | tf_op jit(solution)/shard_map/ppermute | solution.py:530
  72.2 16.5 %collective-permute-start.10 = (bf16[2,96,768]{2,1,0:T(8,128)(2,1)S(1)}, bf16[2,96,768]{2,1,0:T(8,128)(2,1)S(1)}, u32[]{:S(2)}, u32[]{:S(2)}) collective-permute-start(bf16[2,96,768]{2,1,0:T(8,128)(2,1)S(1)} %maximum_select_fusion.27), channel_id=1, source_target_pairs={{0,8},{1,9},{2,10},{3,11},{4,12},{5,13},{6,14},{7,15},{8,0},{9,1},... | collective-permute-start | bytes 884744 | tf_op jit(solution)/shard_map/ppermute | solution.py:530
  72.3 16.5 %collective-permute-start.11 = (bf16[1,192,768]{2,1,0:T(8,128)(2,1)S(1)}, bf16[1,192,768]{2,1,0:T(8,128)(2,1)S(1)}, u32[]{:S(2)}, u32[]{:S(2)}) collective-permute-start(bf16[1,192,768]{2,1,0:T(8,128)(2,1)S(1)} %get-tuple-element.198), channel_id=1, source_target_pairs={{0,4},{1,5},{2,6},{3,7},{4,0},{5,1},{6,2},{7,3},{8,12},{9,13},{10,... | collective-permute-start | bytes 884744 | tf_op jit(solution)/shard_map/ppermute | solution.py:530
  91.3 35.5 %collective-permute-start.12 = (bf16[2,4,192,768]{3,2,1,0:T(8,128)(2,1)}, bf16[2,4,192,768]{3,2,1,0:T(8,128)(2,1)}, u32[]{:S(2)}, u32[]{:S(2)}) collective-permute-start(bf16[2,4,192,768]{3,2,1,0:T(8,128)(2,1)} %maximum_select_fusion.1), channel_id=1, source_target_pairs={{0,2},{1,3},{2,0},{3,1},{4,6},{5,7},{6,4},{7,5},{8,10},{9,11},{10,... | collective-permute-start | bytes 7077896 | tf_op jit(solution)/shard_map/ppermute | solution.py:530
  94.7 24.6 %collective-permute-start.14 = (bf16[2,192,768]{2,1,0:T(8,128)(2,1)}, bf16[2,192,768]{2,1,0:T(8,128)(2,1)S(1)}, u32[]{:S(2)}, u32[]{:S(2)}) collective-permute-start(bf16[2,192,768]{2,1,0:T(8,128)(2,1)} %maximum_select_fusion.20), channel_id=1, source_target_pairs={{0,8},{1,9},{2,10},{3,11},{4,12},{5,13},{6,14},{7,15},{8,0},{9,1},... | collective-permute-start | bytes 1769480 | tf_op jit(solution)/shard_map/ppermute | solution.py:530
  96.2 23.1 %collective-permute-start.13 = (bf16[4,96,768]{2,1,0:T(8,128)(2,1)}, bf16[4,96,768]{2,1,0:T(8,128)(2,1)}, u32[]{:S(2)}, u32[]{:S(2)}) collective-permute-start(bf16[4,96,768]{2,1,0:T(8,128)(2,1)} %maximum_select_fusion.19), channel_id=1, source_target_pairs={{0,1},{1,0},{2,3},{3,2},{4,5},{5,4},{6,7},{7,6},{8,9},{9,8},{10,11... | collective-permute-start | bytes 1769480 | tf_op jit(solution)/shard_map/ppermute | solution.py:530
  138.5 28.8 %collective-permute-start.16 = (bf16[2,4,96,768]{3,2,1,0:T(8,128)(2,1)}, bf16[2,4,96,768]{3,2,1,0:T(8,128)(2,1)}, u32[]{:S(2)}, u32[]{:S(2)}) collective-permute-start(bf16[2,4,96,768]{3,2,1,0:T(8,128)(2,1)} %maximum_select_fusion.10), channel_id=1, source_target_pairs={{0,2},{1,3},{2,0},{3,1},{4,6},{5,7},{6,4},{7,5},{8,10},{9,11},{10,... | collective-permute-start | bytes 3538952 | tf_op jit(solution)/shard_map/ppermute | solution.py:530
  138.8 28.4 %collective-permute-start.17 = (bf16[4,192,768]{2,1,0:T(8,128)(2,1)}, bf16[4,192,768]{2,1,0:T(8,128)(2,1)S(1)}, u32[]{:S(2)}, u32[]{:S(2)}) collective-permute-start(bf16[4,192,768]{2,1,0:T(8,128)(2,1)} %maximum_select_fusion.11), channel_id=1, source_target_pairs={{0,1},{1,0},{2,3},{3,2},{4,5},{5,4},{6,7},{7,6},{8,9},{9,8},{10,11... | collective-permute-start | bytes 3538952 | tf_op jit(solution)/shard_map/ppermute | solution.py:530
  175.2 29.2 %collective-permute-start.19 = (bf16[2,4,192,768]{3,2,1,0:T(8,128)(2,1)}, bf16[2,4,192,768]{3,2,1,0:T(8,128)(2,1)}, u32[]{:S(2)}, u32[]{:S(2)}) collective-permute-start(bf16[2,4,192,768]{3,2,1,0:T(8,128)(2,1)} %maximum_select_fusion.3), channel_id=1, source_target_pairs={{0,2},{1,3},{2,0},{3,1},{4,6},{5,7},{6,4},{7,5},{8,10},{9,11},{10,... | collective-permute-start | bytes 7077896 | tf_op jit(solution)/shard_map/ppermute | solution.py:530
  271.6 29.2 %collective-permute-start.22 = (bf16[2,4,192,768]{3,2,1,0:T(8,128)(2,1)}, bf16[2,4,192,768]{3,2,1,0:T(8,128)(2,1)}, u32[]{:S(2)}, u32[]{:S(2)}) collective-permute-start(bf16[2,4,192,768]{3,2,1,0:T(8,128)(2,1)} %fusion.1), channel_id=1, source_target_pairs={{0,2},{1,3},{2,0},{3,1},{4,6},{5,7},{6,4},{7,5},{8,10},{9,11},{10,... | collective-permute-start | bytes 7077896 | tf_op jit(solution)/shard_map/ppermute | solution.py:530
  304.3 26.9 %collective-permute-start.24 = (bf16[4,192,768]{2,1,0:T(8,128)(2,1)}, bf16[4,192,768]{2,1,0:T(8,128)(2,1)}, u32[]{:S(2)}, u32[]{:S(2)}) collective-permute-start(bf16[4,192,768]{2,1,0:T(8,128)(2,1)} %fusion.7), channel_id=1, source_target_pairs={{0,1},{1,0},{2,3},{3,2},{4,5},{5,4},{6,7},{7,6},{8,9},{9,8},{10,11... | collective-permute-start | bytes 3538952 | tf_op jit(solution)/shard_map/ppermute | solution.py:530
  307.7 25.2 %collective-permute-start.25 = (bf16[2,4,96,768]{3,2,1,0:T(8,128)(2,1)}, bf16[2,4,96,768]{3,2,1,0:T(8,128)(2,1)}, u32[]{:S(2)}, u32[]{:S(2)}) collective-permute-start(bf16[2,4,96,768]{3,2,1,0:T(8,128)(2,1)} %fusion.6), channel_id=1, source_target_pairs={{0,2},{1,3},{2,0},{3,1},{4,6},{5,7},{6,4},{7,5},{8,10},{9,11},{10,... | collective-permute-start | bytes 3538952 | tf_op jit(solution)/shard_map/ppermute | solution.py:530
  345.6 35.5 %collective-permute-start.29 = (bf16[2,4,192,768]{3,2,1,0:T(8,128)(2,1)}, bf16[2,4,192,768]{3,2,1,0:T(8,128)(2,1)}, u32[]{:S(2)}, u32[]{:S(2)}) collective-permute-start(bf16[2,4,192,768]{3,2,1,0:T(8,128)(2,1)} %fusion), channel_id=1, source_target_pairs={{0,2},{1,3},{2,0},{3,1},{4,6},{5,7},{6,4},{7,5},{8,10},{9,11},{10,... | collective-permute-start | bytes 7077896 | tf_op jit(solution)/shard_map/ppermute | solution.py:530
  352.8 27.1 %collective-permute-start.28 = (bf16[4,96,768]{2,1,0:T(8,128)(2,1)}, bf16[4,96,768]{2,1,0:T(8,128)(2,1)}, u32[]{:S(2)}, u32[]{:S(2)}) collective-permute-start(bf16[4,96,768]{2,1,0:T(8,128)(2,1)} %fusion.12), channel_id=1, source_target_pairs={{0,1},{1,0},{2,3},{3,2},{4,5},{5,4},{6,7},{7,6},{8,9},{9,8},{10,11... | collective-permute-start | bytes 1769480 | tf_op jit(solution)/shard_map/ppermute | solution.py:530
  354.0 25.9 %collective-permute-start.27 = (bf16[2,192,768]{2,1,0:T(8,128)(2,1)}, bf16[2,192,768]{2,1,0:T(8,128)(2,1)S(1)}, u32[]{:S(2)}, u32[]{:S(2)}) collective-permute-start(bf16[2,192,768]{2,1,0:T(8,128)(2,1)} %select_convert_fusion.1), channel_id=1, source_target_pairs={{0,8},{1,9},{2,10},{3,11},{4,12},{5,13},{6,14},{7,15},{8,0},{9,1},... | collective-permute-start | bytes 1769480 | tf_op jit(solution)/shard_map/ppermute | solution.py:530
  383.5 26.6 %collective-permute-start.34 = (bf16[4,192,768]{2,1,0:T(8,128)(2,1)S(1)}, bf16[4,192,768]{2,1,0:T(8,128)(2,1)S(1)}, u32[]{:S(2)}, u32[]{:S(2)}) collective-permute-start(bf16[4,192,768]{2,1,0:T(8,128)(2,1)S(1)} %fusion.4), channel_id=1, source_target_pairs={{0,1},{1,0},{2,3},{3,2},{4,5},{5,4},{6,7},{7,6},{8,9},{9,8},{10,11... | collective-permute-start | bytes 3538952 | tf_op jit(solution)/shard_map/ppermute | solution.py:530
  387.4 26.7 %collective-permute-start.31 = (bf16[2,4,112,768]{3,2,1,0:T(8,128)(2,1)S(1)}, bf16[2,4,112,768]{3,2,1,0:T(8,128)(2,1)S(1)}, u32[]{:S(2)}, u32[]{:S(2)}) collective-permute-start(bf16[2,4,112,768]{3,2,1,0:T(8,128)(2,1)S(1)} %fusion.2), channel_id=1, source_target_pairs={{0,2},{1,3},{2,0},{3,1},{4,6},{5,7},{6,4},{7,5},{8,10},{9,11},{10,... | collective-permute-start | bytes 4128776 | tf_op jit(solution)/shard_map/ppermute | solution.py:530
  412.8 25.7 %collective-permute-start.36 = (bf16[2,192,768]{2,1,0:T(8,128)(2,1)S(1)}, bf16[2,192,768]{2,1,0:T(8,128)(2,1)S(1)}, u32[]{:S(2)}, u32[]{:S(2)}) collective-permute-start(bf16[2,192,768]{2,1,0:T(8,128)(2,1)S(1)} %select_convert_fusion), channel_id=1, source_target_pairs={{0,8},{1,9},{2,10},{3,11},{4,12},{5,13},{6,14},{7,15},{8,0},{9,1},... | collective-permute-start | bytes 1769480 | tf_op jit(solution)/shard_map/ppermute | solution.py:530
  414.4 24.1 %collective-permute-start.37 = (bf16[4,112,768]{2,1,0:T(8,128)(2,1)S(1)}, bf16[4,112,768]{2,1,0:T(8,128)(2,1)S(1)}, u32[]{:S(2)}, u32[]{:S(2)}) collective-permute-start(bf16[4,112,768]{2,1,0:T(8,128)(2,1)S(1)} %fusion.9), channel_id=1, source_target_pairs={{0,1},{1,0},{2,3},{3,2},{4,5},{5,4},{6,7},{7,6},{8,9},{9,8},{10,11... | collective-permute-start | bytes 2064392 | tf_op jit(solution)/shard_map/ppermute | solution.py:530
  417.3 44.4 %collective-permute-start.42 = (f32[1,512,768]{2,1,0:T(8,128)S(1)}, f32[1,512,768]{2,1,0:T(8,128)S(1)}, u32[]{:S(2)}, u32[]{:S(2)}) collective-permute-start(f32[1,512,768]{2,1,0:T(8,128)S(1)} %get-tuple-element.368), channel_id=1, source_target_pairs={{0,16},{1,17},{2,18},{3,19},{4,20},{5,21},{6,22},{7,23},{8,24},{9,... | collective-permute-start | bytes 4718600 | tf_op jit(solution)/shard_map/ppermute | solution.py:536
  439.3 15.6 %collective-permute-start.38 = (bf16[2,112,768]{2,1,0:T(8,128)(2,1)S(1)}, bf16[2,112,768]{2,1,0:T(8,128)(2,1)S(1)}, u32[]{:S(2)}, u32[]{:S(2)}) collective-permute-start(bf16[2,112,768]{2,1,0:T(8,128)(2,1)S(1)} %select_convert_fusion.2), channel_id=1, source_target_pairs={{0,8},{1,9},{2,10},{3,11},{4,12},{5,13},{6,14},{7,15},{8,0},{9,1},... | collective-permute-start | bytes 1032200 | tf_op jit(solution)/shard_map/ppermute | solution.py:530
  (76 other events, 549.0 us)

commit v4 on v3

v4 whole, which is shorter than its diff:
```python
import jax
import jax.numpy as jnp
from jax import lax
from jax.experimental import pallas as pl
from jax.experimental.pallas import tpu as pltpu
from jax.sharding import PartitionSpec as P

HEADS = 12
HDIM = 64
GROUP = 4
BLOCK = 128
PAD = 16
norm_eps = 1e-06
BF = jnp.bfloat16
F32 = jnp.float32
BOTH = ("section", "dp")
SCALE = HDIM ** (-0.5)

ERF_SCALE = 0.425
ERF_POLY = (
    0.11985147519825406,
    0.12072713574380309,
    0.10159474513684189,
    0.12334456743816431,
    -0.0435293372534038,
    0.19486821903107854,
    -0.15132025578595443,
    0.03446332841595847,
)


def dot(left, right, over_left=1, over_right=0):
    return lax.dot_general(
        left, right, (((over_left,), (over_right,)), ((), ())), preferred_element_type=F32
    )


def shape_of(shape, dtype):
    return jax.ShapeDtypeStruct(shape, dtype)


def whole_block(*shape):
    return pl.BlockSpec(shape, lambda g: (0,) * len(shape))


def gelu_pair(u):
    bell = jnp.exp(u * u * -0.5)
    t = 1.0 / (1.0 + (ERF_SCALE * 0.7071067811865476) * jnp.abs(u))
    poly = ERF_POLY[-1]
    for item in ERF_POLY[-2::-1]:
        poly = poly * t + item
    tail = bell * (poly * t)
    cdf = jnp.where(u < 0.0, tail, 1.0 - tail)
    return u * cdf, cdf + u * bell * 0.3989422804014327


def norm_stats(v):
    center = v - jnp.mean(v, axis=-1, keepdims=True)
    t = lax.rsqrt(jnp.mean(center * center, axis=-1, keepdims=True) + norm_eps)
    return center * t, t


def norm_back(dy, n, t, gain):
    dn = dy * gain
    mean = jnp.mean(dn, axis=-1, keepdims=True)
    along = jnp.mean(dn * n, axis=-1, keepdims=True)
    return t * (dn - mean - n * along)


def colsum(v):
    return jnp.sum(v, axis=0, keepdims=True)


def near(b, blocks):
    return max(0, b - 1) * BLOCK, min(blocks, b + 2) * BLOCK


def is_small(count):
    return count == 16


def steps_of(count, core, near_first):
    outer = [4 << j for j in range((count // 4).bit_length() - 1)]
    quad = [1, 2]
    if core:
        quad = [2, 1]
        if is_small(count):
            outer = outer[::-1]
    return quad + outer if near_first else outer + quad


def bit_of(me, mask):
    return (me >> (mask.bit_length() - 1)) & 1


def send_index(chip_z, chip_q, me, core, near_first):
    index = 0
    rel = (chip_z * 4 + chip_q) ^ me
    for j, mask in enumerate(steps_of(16, core, near_first)):
        index = index + bit_of(rel, mask) * (1 << j)
    return index


def each(count, body):
    lax.fori_loop(0, count, lambda j, _: (body(j), 0)[1], 0)


class Loads:
    def __init__(self, near_first, place_ref, own, other, targets, sem):
        self.near_first, self.place, self.planes = near_first, place_ref, (own, other)
        self.targets, self.sem = targets, sem

    def at(self, plane, unit, chip):
        target = self.targets[plane]
        if len(target.shape) == 5:
            return target.at[unit, chip >> 2, chip & 3]
        return target.at[chip >> 2, chip & 3]

    def start(self, plane, unit, first, count):
        order = steps_of(16, plane, self.near_first)
        target = self.targets[plane]
        size = target.shape[-2]

        def by_chip(section, chip):
            pieces = self.planes[0] if plane == section else self.planes[1]
            to, sem = self.at(plane, unit, chip), self.sem.at[plane, unit, chip]
            if len(pieces) == 1:
                source = pieces[0].reshape(*target.shape)
                at = source.at[unit] if len(target.shape) == 5 else source
                pltpu.make_async_copy(at.at[chip >> 2, chip & 3], to, sem).start()
                return
            index = sum(bit_of(chip, order[j]) << j for j in range(3))
            far = bit_of(chip ^ self.place[0], order[3])
            for p in range(2):
                @pl.when(far == p)
                def _():
                    rows = pl.ds(pl.multiple_of(unit * size, PAD), size)
                    pltpu.make_async_copy(pieces[p].at[index, rows, :], to, sem).start()

        by_section(self.place[1], lambda section: each(count, lambda j: by_chip(section, first + j)))

    def wait(self, plane, unit, first, count):
        def by_chip(chip):
            to = self.at(plane, unit, chip)
            pltpu.make_async_copy(to, to, self.sem.at[plane, unit, chip]).wait()

        each(count, lambda j: by_chip(first + j))


def block_of(b, pair):
    return slice(b * BLOCK, (b + 1) * BLOCK), slice(pair * 2 * HDIM, (pair + 1) * 2 * HDIM)


def two_heads(pair, lane):
    zero = jnp.zeros_like(pair)
    return jnp.concatenate([jnp.where(lane < HDIM, pair, zero), jnp.where(lane >= HDIM, pair, zero)])


def attn_fwd_kernel(near_first, halves, place_ref, *refs):
    own, other = refs[:halves], refs[halves : 2 * halves]
    a_ref, sq_ref, sk_ref, bias_ref, shift_ref = refs[2 * halves : 2 * halves + 5]
    q_ref, k_ref, v_ref, o_ref, n_ref, t_ref, acc, low_w, high_w, sem = refs[2 * halves + 5 :]
    step = pl.program_id(0)
    length, width = a_ref.shape
    blocks = length // BLOCK
    a = a_ref[...]
    loads = Loads(near_first, place_ref, own, other, (low_w, high_w), sem)

    @pl.when(step == 0)
    def _():
        for plane, unit in ((0, 0), (0, 1), (1, 0), (1, 1)):
            loads.start(plane, unit, 0, 16)
        for plane, unit in ((0, 0), (0, 1), (1, 0)):
            loads.wait(plane, unit, 0, 16)

    cols = GROUP * HDIM
    here = pl.ds(pl.multiple_of(step * cols, cols), cols)

    def column(ref, j):
        return ref[j, :, :, :, here].reshape(width, cols)

    q_ref[...] = (dot(a, column(low_w, 0)) + bias_ref[2:3]).astype(BF)
    k_ref[...] = dot(a, column(low_w, 1)).astype(BF)
    v_ref[...] = (dot(a, column(high_w, 0)) + bias_ref[3:4]).astype(BF)
    lane = lax.broadcasted_iota(jnp.int32, (BLOCK, 2 * HDIM), 1)
    tiles = [(b, pair) for b in range(blocks) for pair in range(GROUP // 2)]

    def scores_of(b, pair):
        lo, hi = near(b, blocks)
        rows, lanes = block_of(b, pair)
        same = sq_ref[rows, 0:1] == sk_ref[0:1, lo:hi]
        scores = dot(two_heads(q_ref[rows, lanes] * SCALE, lane), k_ref[lo:hi, lanes], 1, 1)
        return jnp.where(jnp.concatenate([same, same]), scores, -1000000000.0)

    ahead = scores_of(*tiles[0])
    for j, (b, pair) in enumerate(tiles):
        lo, hi = near(b, blocks)
        rows, lanes = block_of(b, pair)
        scores = ahead
        if j + 1 < len(tiles):
            ahead = scores_of(*tiles[j + 1])
        grown = jnp.exp(scores - jnp.max(scores, axis=-1, keepdims=True))
        scale = 1.0 / jnp.sum(grown, axis=-1, keepdims=True)
        out = dot((grown * scale).astype(BF), v_ref[lo:hi, lanes])
        o_ref[rows, lanes] = jnp.where(lane < HDIM, out[:BLOCK], out[BLOCK:]).astype(BF)
    @pl.when(step == 0)
    def _():
        loads.wait(1, 1, 0, 16)

    part = dot(o_ref[...], high_w.at[1].reshape(width, width)[here, :])

    @pl.when(step == 0)
    def _():
        acc[...] = a.astype(F32) + shift_ref[4:5] + part

    @pl.when(step != 0)
    def _():
        acc[...] += part

    @pl.when(step == pl.num_programs(0) - 1)
    def _():
        n, t = norm_stats(acc[...])
        n_ref[...] = n
        t_ref[...] = jnp.broadcast_to(t, t_ref.shape)


SCALARS = pl.BlockSpec(memory_space=pltpu.SMEM)
NO_COST = pl.CostEstimate(flops=0, bytes_accessed=0, transcendentals=0)


ANYWHERE = pl.BlockSpec(memory_space=pl.ANY)


def attn_fwd(near_first, place, a, seg_col, seg_row, planes, shift):
    length, width = a.shape
    cols = GROUP * HDIM
    group = pl.BlockSpec((length, cols), lambda g: (0, g))
    half = (2, 4, 4, width // 16, width)
    halves = len(planes[0])
    return pl.pallas_call(
        lambda *refs: attn_fwd_kernel(near_first, halves, *refs),
        grid=(HEADS // GROUP,),
        in_specs=[SCALARS]
        + [ANYWHERE] * (2 * halves)
        + [whole_block(length, width), whole_block(length, 128), whole_block(8, length)]
        + [pl.BlockSpec((8, cols), lambda g: (0, g)), whole_block(8, width)],
        out_specs=[group] * 4 + [whole_block(length, width), whole_block(length, 128)],
        out_shape=[shape_of((length, width), BF)] * 4
        + [shape_of((length, width), F32), shape_of((length, 128), F32)],
        scratch_shapes=[
            pltpu.VMEM((length, width), F32),
            pltpu.VMEM(half, BF),
            pltpu.VMEM(half, BF),
            pltpu.SemaphoreType.DMA((2, 2, 16)),
        ],
        cost_estimate=NO_COST,
        name="attn_fwd",
    )(place, *planes[0], *planes[1], a, seg_col, seg_row, shift, shift)


def ffn_fwd_kernel(near_first, halves, place_ref, *refs):
    own, other = refs[:halves], refs[halves : 2 * halves]
    n1_ref, cup_ref, gain_ref, shift_ref = refs[2 * halves : 2 * halves + 4]
    g_ref, gp_ref, n_ref, t_ref, y_ref = refs[2 * halves + 4 : 2 * halves + 9]
    h1, acc, up_w, down_w, sem = refs[2 * halves + 9 :]
    step = pl.program_id(0)
    width = n1_ref.shape[1]
    loads = Loads(near_first, place_ref, own, other, (up_w, down_w), sem)
    units = up_w.shape[0]

    @pl.when(step == 0)
    def _():
        loads.start(0, 0, 0, 16)
        loads.start(1, 0, 0, 4)

    @pl.when(step == 0)
    def _():
        hidden = n1_ref[...] * gain_ref[0:1] + shift_ref[6:7]
        h1[...] = hidden.astype(BF)
        acc[...] = hidden + shift_ref[5:6]

    loads.wait(0, step, 0, 16)

    @pl.when(step + 1 < units)
    def _():
        loads.start(0, step + 1, 0, 16)
        loads.start(1, 0, 4 * (step + 1), 4)

    loads.wait(1, 0, 4 * step, 4)
    up = up_w[step].reshape(width, width)
    down = down_w[step].reshape(width, width)
    wide = 256
    parts = h1.shape[1] // wide

    def upper(j):
        cols = slice(j * wide, (j + 1) * wide)
        return dot(h1[...], up[:, cols]) + cup_ref[0, :, cols]

    ahead = upper(0)
    total = acc[...]
    for j in range(parts):
        cols = slice(j * wide, (j + 1) * wide)
        here = ahead
        if j + 1 < parts:
            ahead = upper(j + 1)
        g, slope = gelu_pair(here)
        g = g.astype(BF)
        g_ref[:, cols] = g
        gp_ref[:, cols] = slope.astype(BF)
        total = total + dot(g, down[cols])
    acc[...] = total

    @pl.when(step == pl.num_programs(0) - 1)
    def _():
        n, t = norm_stats(acc[...])
        n_ref[...] = n
        t_ref[...] = jnp.broadcast_to(t, t_ref.shape)
        y_ref[...] = (n * gain_ref[1:2] + shift_ref[7:8]).astype(BF)


def ffn_fwd(near_first, place, n1, planes, cup, gain, shift):
    length, width = n1.shape
    units = cup.shape[0]
    column = pl.BlockSpec((length, width), lambda g: (0, g))
    up = (units, 4, 4, width // 16, width)
    down = (4, 4, units * width // 16, width)
    halves = len(planes[0])
    return pl.pallas_call(
        lambda *refs: ffn_fwd_kernel(near_first, halves, *refs),
        grid=(units,),
        in_specs=[SCALARS]
        + [ANYWHERE] * (2 * halves)
        + [
            whole_block(length, width),
            pl.BlockSpec((1, 1, width), lambda g: (g, 0, 0)),
            whole_block(8, width),
            whole_block(8, width),
        ],
        out_specs=[column, column, whole_block(length, width), whole_block(length, 128), whole_block(length, width)],
        out_shape=[shape_of((length, units * width), BF)] * 2
        + [shape_of((length, width), F32), shape_of((length, 128), F32), shape_of((length, width), BF)],
        scratch_shapes=[
            pltpu.VMEM((length, width), BF),
            pltpu.VMEM((length, width), F32),
            pltpu.VMEM(up, BF),
            pltpu.VMEM(down, BF),
            pltpu.SemaphoreType.DMA((2, units, 16)),
        ],
        cost_estimate=NO_COST,
        name="ffn_fwd",
    )(place, *planes[0], *planes[1], n1, cup, gain, shift)


def by_section(section, action):
    for plane in range(2):
        pl.when(section == plane)(lambda plane=plane: action(plane))


def ffn_bwd_kernel(near_first, halves, place_ref, *refs):
    own, other = refs[:halves], refs[halves : 2 * halves]
    dy_ref, n2_ref, t2_ref, g_ref, gp_ref, n1_ref, t1_ref, gain_ref, shift_ref = refs[2 * halves : 2 * halves + 9]
    keep_ref, send_ref, dr1_ref, sums_ref, cup_ref = refs[2 * halves + 9 : 2 * halves + 14]
    h1, df, acc, gup, gdown, up_w, down_w, sem, load_sem = refs[2 * halves + 14 :]
    step = pl.program_id(0)
    loads = Loads(near_first, place_ref, own, other, (up_w, down_w), load_sem)

    @pl.when(step == 0)
    def _():
        loads.start(1, 0, 0, 4)
        loads.start(0, 0, 0, 16)

    last = pl.num_programs(0) - 1
    quads = outer = 4
    width = h1.shape[1]
    size = width // (quads * outer)

    @pl.when(step == 0)
    def _():
        n2 = n2_ref[...]
        dy = dy_ref[...].astype(F32)
        dr2 = norm_back(dy, n2, t2_ref[:, 0:1], gain_ref[1:2])
        low = dr2.astype(BF)
        df[...] = low
        acc[...] = dr2
        h1[...] = (n1_ref[...] * gain_ref[0:1] + shift_ref[6:7]).astype(BF)
        sums_ref[...] = jnp.zeros_like(sums_ref)
        sums_ref[1:2] = colsum(dy * n2)
        sums_ref[2:3] = colsum(dy)
        sums_ref[3:4] = colsum(low.astype(F32))

    loads.wait(1, 0, 4 * step, 4)
    loads.wait(0, step, 0, 16)

    @pl.when(step < last)
    def _():
        loads.start(1, 0, 4 * (step + 1), 4)
        loads.start(0, step + 1, 0, 16)

    d = df[...]
    down = dot(g_ref[...], d, 0, 0).astype(BF)
    gdown[step] = down.reshape(quads, width // quads, width)
    du = (dot(d, down_w[step].reshape(width, width), 1, 1) * gp_ref[...].astype(F32)).astype(BF)
    cup_ref[0] = colsum(du.astype(F32))
    up = dot(h1[...], du, 0, 0).astype(BF)
    gup[step] = up.reshape(outer, quads, size, width)
    acc[...] += dot(du, up_w[step].reshape(width, width), 1, 1)

    def up_copy(section, j, chip):
        to = (keep_ref if section == 0 else send_ref).at[send_index(chip >> 2, chip & 3, place_ref[0], 0, near_first)]
        rows = pl.ds(pl.multiple_of(j * size, PAD), size)
        return pltpu.make_async_copy(gup.at[j, chip >> 2, chip & 3], to.at[rows, :], sem.at[j, chip])

    def down_copy(section, j, q):
        to = (send_ref if section == 0 else keep_ref).at[send_index(j, q, place_ref[0], 1, near_first)]
        return pltpu.make_async_copy(gdown.at[j, q], to, sem.at[j, 16 + q])

    def begin(section):
        each(16, lambda chip: up_copy(section, step, chip).start())
        each(4, lambda q: down_copy(section, step, q).start())

    by_section(place_ref[1], begin)

    @pl.when(step == last)
    def _():
        dh = acc[...]
        n1 = n1_ref[...]
        dr1_ref[...] = norm_back(dh, n1, t1_ref[:, 0:1], gain_ref[0:1])
        sums_ref[0:1] = colsum(dh * n1)
        sums_ref[4:5] = colsum(dh)

        def finish(section):
            def one(j):
                each(16, lambda chip: up_copy(section, j, chip).wait())
                each(4, lambda q: down_copy(section, j, q).wait())

            each(gup.shape[0], one)

        by_section(place_ref[1], finish)


def ffn_bwd(near_first, place, dy, n2, t2, g, gp, planes, n1, t1, gain, shift):
    length, width = n1.shape
    units = g.shape[1] // width
    outer, size = 4, width // 16
    halves = len(planes[0])
    up = (units, outer, 4, size, width)
    down = (outer, 4, units * size, width)
    column = pl.BlockSpec((length, width), lambda g: (0, g))
    chunk = shape_of((16, units * size, width), BF)
    return pl.pallas_call(
        lambda *refs: ffn_bwd_kernel(near_first, halves, *refs),
        grid=(units,),
        in_specs=[
            SCALARS,
            *[ANYWHERE] * (2 * halves),
            whole_block(length, width),
            whole_block(length, width),
            whole_block(length, 128),
            column,
            column,
            whole_block(length, width),
            whole_block(length, 128),
            whole_block(8, width),
            whole_block(8, width),
        ],
        out_specs=[
            pl.BlockSpec(memory_space=pl.ANY),
            pl.BlockSpec(memory_space=pl.ANY),
            whole_block(length, width),
            whole_block(8, width),
            pl.BlockSpec((1, 1, width), lambda g: (g, 0, 0)),
        ],
        out_shape=[chunk, chunk, shape_of((length, width), F32), shape_of((8, width), F32), shape_of((units, 1, width), F32)],
        scratch_shapes=[
            pltpu.VMEM((length, width), BF),
            pltpu.VMEM((length, width), BF),
            pltpu.VMEM((length, width), F32),
            pltpu.VMEM((units, outer, 4, size, width), BF),
            pltpu.VMEM((units, 4, width // 4, width), BF),
            pltpu.VMEM(up, BF),
            pltpu.VMEM(down, BF),
            pltpu.SemaphoreType.DMA((units, 20)),
            pltpu.SemaphoreType.DMA((2, units, 16)),
        ],
        cost_estimate=NO_COST,
        name="ffn_bwd",
    )(place, *planes[0], *planes[1], dy, n2, t2, g, gp, n1, t1, gain, shift)


def attn_bwd_kernel(near_first, halves, place_ref, *refs):
    own, other = refs[:halves], refs[halves : 2 * halves]
    dr_ref, a_ref, sq_ref, sk_ref, q_ref, k_ref, v_ref, o_ref = refs[2 * halves : 2 * halves + 8]
    keep_ref, send_ref, da_ref, sums_ref, sumo_ref = refs[2 * halves + 8 : 2 * halves + 13]
    dat, do_sc, dq, dk, dv, grads, low_w, high_w, sem, load_sem = refs[2 * halves + 13 :]
    step = pl.program_id(0)
    loads = Loads(near_first, place_ref, own, other, (low_w, high_w), load_sem)

    @pl.when(step == 0)
    def _():
        for plane, unit in ((1, 1), (0, 0), (0, 1), (1, 0)):
            loads.start(plane, unit, 0, 16)

    length, width = a_ref.shape
    blocks = length // BLOCK
    quads = outer = 4
    size = width // (quads * outer)
    cols = GROUP * HDIM

    @pl.when(step == 0)
    def _():
        low = dr_ref[...].astype(BF)
        dat[...] = low
        da_ref[...] = dr_ref[...]
        sumo_ref[...] = jnp.zeros_like(sumo_ref)
        sumo_ref[0:1] = colsum(low.astype(F32))

    d = dat[...]
    grad_o = dot(o_ref[...], d, 0, 0).astype(BF)

    @pl.when(step == 0)
    def _():
        loads.wait(1, 1, 0, 16)

    now = pl.ds(pl.multiple_of(step * cols, cols), cols)
    do_sc[...] = dot(d, high_w.at[1].reshape(width, width)[now, :], 1, 1).astype(BF)
    dk[...] = jnp.zeros_like(dk)
    dv[...] = jnp.zeros_like(dv)
    lane = lax.broadcasted_iota(jnp.int32, (BLOCK, 2 * HDIM), 1)
    tiles = [(b, pair) for b in range(blocks) for pair in range(GROUP // 2)]

    def products(b, pair):
        lo, hi = near(b, blocks)
        rows, lanes = block_of(b, pair)
        same = sk_ref[lo:hi, 0:1] == sq_ref[0:1, rows]
        query = two_heads(q_ref[rows, lanes] * SCALE, lane)
        d_out = two_heads(do_sc[rows, lanes], lane)
        scores = dot(k_ref[lo:hi, lanes], query, 1, 1)
        scores = jnp.where(jnp.concatenate([same, same], axis=1), scores, -1000000000.0)
        return query, d_out, scores, dot(v_ref[lo:hi, lanes], d_out, 1, 1)

    ahead = products(*tiles[0])
    for j, (b, pair) in enumerate(tiles):
        lo, hi = near(b, blocks)
        rows, lanes = block_of(b, pair)
        query, d_out, scores, d_probs = ahead
        if j + 1 < len(tiles):
            ahead = products(*tiles[j + 1])
        grown = jnp.exp(scores - jnp.max(scores, axis=0, keepdims=True))
        probs = grown * (1.0 / jnp.sum(grown, axis=0, keepdims=True))
        d_scores = probs * (d_probs - jnp.sum(probs * d_probs, axis=0, keepdims=True))
        d_scores = d_scores.astype(BF)
        dv[lo:hi, lanes] += dot(probs.astype(BF), d_out)
        dk[lo:hi, lanes] += dot(d_scores, query)
        d_query = dot(d_scores, k_ref[lo:hi, lanes], 0, 0)
        dq[rows, lanes] = jnp.where(lane < HDIM, d_query[:BLOCK], d_query[BLOCK:]) * SCALE
    a = a_ref[...]
    out = da_ref[...]
    lows = (dq[...].astype(BF), dk[...].astype(BF), dv[...].astype(BF))
    made = []

    @pl.when(step == 0)
    def _():
        for plane, unit in ((0, 0), (0, 1), (1, 0)):
            loads.wait(plane, unit, 0, 16)

    for low, (w_ref, j) in zip(lows, ((low_w, 0), (low_w, 1), (high_w, 0))):
        made.append(dot(a, low, 0, 0).astype(BF))
        out = out + dot(low, w_ref[j, :, :, :, now].reshape(width, cols), 1, 1)
    da_ref[...] = out
    sums_ref[...] = jnp.zeros_like(sums_ref)
    sums_ref[0:1] = colsum(lows[0].astype(F32))
    sums_ref[1:2] = colsum(lows[2].astype(F32))
    steps = HEADS // GROUP
    for j in range(steps):
        @pl.when(step == j)
        def _(j=j):
            here = slice(j * cols, (j + 1) * cols)
            for unit in range(3):
                grads[unit, :, here] = made[unit]
            grads[3, here, :] = grad_o

    @pl.when(step == steps - 1)
    def _():
        def copy(section, unit, chip):
            core = unit // 2
            to = (keep_ref if core == section else send_ref).at[
                send_index(chip >> 2, chip & 3, place_ref[0], core, near_first)
            ]
            rows = pl.ds(pl.multiple_of(chip * size, PAD), size)
            at = (unit % 2) * size
            return pltpu.make_async_copy(grads.at[unit, rows, :], to.at[at : at + size, :], sem.at[unit, chip])

        def move(section):
            for unit in range(4):
                each(16, lambda chip: copy(section, unit, chip).start())
            for unit in range(4):
                each(16, lambda chip: copy(section, unit, chip).wait())

        by_section(place_ref[1], move)


def attn_bwd(near_first, more, place, dr, a, seg_col, seg_row, q, k, v, o, planes):
    length, width = a.shape
    outer, size = 4, width // 16
    halves = len(planes[0])
    half = (2, outer, 4, size, width)
    cols = GROUP * HDIM
    group = pl.BlockSpec((length, cols), lambda g: (0, g))
    chunk = shape_of((16, 2 * size + more, width), BF)
    return pl.pallas_call(
        lambda *refs: attn_bwd_kernel(near_first, halves, *refs),
        grid=(HEADS // GROUP,),
        in_specs=[
            SCALARS,
            *[ANYWHERE] * (2 * halves),
            whole_block(length, width),
            whole_block(length, width),
            whole_block(8, length),
            whole_block(length, 128),
        ]
        + [group] * 4,
        out_specs=[
            pl.BlockSpec(memory_space=pl.ANY),
            pl.BlockSpec(memory_space=pl.ANY),
            whole_block(length, width),
            pl.BlockSpec((8, cols), lambda g: (0, g)),
            whole_block(8, width),
        ],
        out_shape=[chunk, chunk, shape_of((length, width), F32), shape_of((8, width), F32), shape_of((8, width), F32)],
        scratch_shapes=[pltpu.VMEM((length, width), BF), pltpu.VMEM((length, cols), BF)]
        + [pltpu.VMEM((length, cols), F32)] * 3
        + [pltpu.VMEM((4, width, width), BF), pltpu.VMEM(half, BF), pltpu.VMEM(half, BF)]
        + [pltpu.SemaphoreType.DMA((4, 4 * outer)), pltpu.SemaphoreType.DMA((2, 2, 16))],
        cost_estimate=NO_COST,
        name="attn_bwd",
    )(place, *planes[0], *planes[1], dr, a, seg_row, seg_col, q, k, v, o)


def flip(value, mask, other=None):
    count = lax.axis_size("dp")
    masks = (mask, mask if other is None else other)
    pairs = [(s * count + i, s * count + (i ^ masks[s])) for s in range(2) for i in range(count)]
    return lax.ppermute(value, BOTH, pairs)


def swap(value):
    count = lax.axis_size("dp")
    pairs = [(s * count + i, (1 - s) * count + i) for s in range(2) for i in range(count)]
    return lax.ppermute(value, BOTH, pairs)


def across(value, source):
    count = lax.axis_size("dp")
    return lax.ppermute(value, BOTH, [(source * count + i, (1 - source) * count + i) for i in range(count)])


class Order:
    def __init__(self, mark):
        self.mark = mark

    def wait(self, *values):
        leaves, tree = jax.tree.flatten(values)
        *leaves, self.mark = lax.optimization_barrier((*leaves, self.mark))
        out = jax.tree.unflatten(tree, leaves)
        return out[0] if len(values) == 1 else out

    def now(self, *values):
        leaves, tree = jax.tree.flatten(values)
        leaves = lax.optimization_barrier((*leaves, self.mark))[:-1]
        out = jax.tree.unflatten(tree, leaves)
        return out[0] if len(values) == 1 else out


class Gather:
    def __init__(self, order, block, near_first=False):
        self.order, self.own, self.near_first = order, block[None], near_first
        self.left = list(zip(*[steps_of(lax.axis_size("dp"), core, near_first) for core in range(2)]))

    def start(self):
        self.got = flip(self.order.now(self.own), *self.left[0])

    def start_part(self, part):
        half = self.own.shape[0] // 2
        return flip(self.order.now(self.own[part * half : (part + 1) * half]), *self.left[0])

    def done(self):
        masks = self.left.pop(0)
        high = (lax.axis_index("dp") & jnp.where(lax.axis_index("section") == 0, *masks)) != 0
        own, got = self.own, self.got
        self.own = jnp.where(high, jnp.concatenate([got, own]), jnp.concatenate([own, got]))

    def spare(self, steps):
        while len(self.left) > steps:
            self.start()
            self.done()

    def wait(self):
        self.got = self.order.wait(self.got)

    def swap_own(self):
        self.other_own = swap(self.order.now(self.own))

    def swap_got(self):
        self.other_got = swap(self.order.now(self.got))

    def halves(self, place, units, size):
        pairs = tuple(
            (own,) + (got if isinstance(got, tuple) else (got,))
            for own, got in ((self.own, self.got), (self.other_own, self.other_got))
        )
        if is_small(lax.axis_size("dp")):
            return pairs
        return natural_planes(place, units, size, self.near_first, *pairs)


def natural_planes(place, units, size, near_first, own, other):
    count = lax.axis_size("dp")
    out = []
    for section, halves in ((place[1], own), (1 - place[1], other)):
        both = jnp.concatenate(halves)
        at = []
        for core in range(2):
            order = steps_of(count, core, near_first)
            chips = jnp.arange(count)
            index = sum(bit_of(chips, mask) << j for j, mask in enumerate(order))
            at.append(index ^ (bit_of(place[0], order[-1]) << (len(order) - 1)))
        whole = jnp.take(both, jnp.where(section == 0, *at), axis=0)
        rows, width = whole.shape[1:]
        if size:
            by_unit = jnp.stack([whole[:, j * size : (j + 1) * size].reshape(width, width) for j in range(units)])
            if units != 2:
                flat = whole.reshape(units, width, width)
                by_unit = jnp.where(section == 0, by_unit.reshape(flat.shape), flat)
            whole = by_unit.reshape(units, 4, 4, width // 16, width)
        out.append((whole,))
    return out


def tail_kernel(cut, place_ref, *refs):
    halves, (vec_ref, cup_ref, head_ref, pieces, sem) = refs[:4], refs[4:]

    def move(section):
        for start in (True, False):
            for plane in range(2):
                order = steps_of(16, plane, False)
                for p in range(2):
                    source = halves[p if plane == section else 2 + p].at[:, cut:, :]

                    def by_index(index):
                        chip = sum(bit_of(index, 1 << j) * order[j] for j in range(3))
                        chip = chip + order[3] * (bit_of(place_ref[0], order[3]) ^ p)
                        to = pieces.at[plane, chip >> 2, chip & 3]
                        copy = pltpu.make_async_copy(source.at[index], to, sem.at[plane, 8 * p + index])
                        copy.start() if start else copy.wait()

                    each(8, by_index)

    by_section(place_ref[1], move)
    size = vec_ref.shape[2] // 16
    wide = cup_ref.shape[1] * size
    height = head_ref.shape[0] // 32
    for plane in range(2):
        for chip in range(16):
            piece = pieces[plane, chip // 4, chip % 4].astype(F32)
            vec_ref[plane, :, chip * size : (chip + 1) * size] = piece[:8, :size]
            at = (chip % 4) * wide
            cup_ref[plane, chip // 4, :, at : at + wide] = piece[8:9, :wide]
            for k in range(height // 8):
                row = (plane * 16 + chip) * height + 8 * k
                head_ref[row : row + 8, :] = piece[:8, 384 + 128 * k : 512 + 128 * k]


def tails_of(place, cut, units, own, other):
    width = own[0].shape[2]
    return pl.pallas_call(
        lambda *refs: tail_kernel(cut, *refs),
        in_specs=[SCALARS] + [ANYWHERE] * 4,
        out_specs=[pl.BlockSpec(memory_space=pltpu.VMEM)] * 3,
        out_shape=[shape_of((2, 8, width), F32), shape_of((2, units, 1, width), F32), shape_of((width, 128), F32)],
        scratch_shapes=[pltpu.VMEM((2, 4, 4, PAD, width), BF), pltpu.SemaphoreType.DMA((2, 16))],
        cost_estimate=NO_COST,
        name="tails",
    )(place, *own, *other)


def natural_tails(place, cut, own, other):
    own, other = jax.tree.map(lambda item: item[:, cut:], (own, other))
    (mine,), (there,) = natural_planes(place, 0, 0, False, own, other)
    first = place[1] == 0
    return jnp.where(first, mine, there), jnp.where(first, there, mine)


def pack_kernel(cut, place_ref, *refs):
    sums = (refs[0:4], refs[4:8])
    head_ref, _, _, keep_ref, send_ref, pieces, sem = refs[8:]
    width = pieces.shape[3]
    size = width // 16
    height = head_ref.shape[0] // 32
    pieces[...] = jnp.zeros_like(pieces)
    for plane, (attn, out, ffn, cup) in enumerate(sums):
        wide = cup.shape[0] * size
        rows = [ffn[0:1], ffn[1:2], attn[0:1], attn[1:2], out[0:1], ffn[3:4], ffn[4:5], ffn[2:3]]
        vec = jnp.concatenate(rows)
        for chip in range(16):
            pieces[plane, chip, :8, :size] = vec[:, chip * size : (chip + 1) * size].astype(BF)
            at = (chip % 4) * wide
            pieces[plane, chip, 8:9, :wide] = cup[chip // 4, :, at : at + wide].astype(BF)
            for k in range(height // 8):
                row = (plane * 16 + chip) * height + 8 * k
                pieces[plane, chip, :8, 384 + 128 * k : 512 + 128 * k] = head_ref[row : row + 8, :].astype(BF)

    def move(section):
        for start in (True, False):
            for plane in range(2):
                to = keep_ref if plane == section else send_ref

                def by_chip(chip):
                    at = send_index(chip >> 2, chip & 3, place_ref[0], plane, False)
                    copy = pltpu.make_async_copy(pieces.at[plane, chip], to.at[at, cut:, :], sem.at[plane, chip])
                    copy.start() if start else copy.wait()

                each(16, by_chip)

    by_section(place_ref[1], move)


def pack_tails(place, cut, layer0, layer1, g_head, keep, send):
    return pl.pallas_call(
        lambda *refs: pack_kernel(cut, *refs),
        in_specs=[SCALARS] + [pl.BlockSpec(memory_space=pltpu.VMEM)] * 9 + [ANYWHERE] * 2,
        out_specs=[ANYWHERE] * 2,
        out_shape=[shape_of(keep.shape, BF)] * 2,
        input_output_aliases={10: 0, 11: 1},
        scratch_shapes=[pltpu.VMEM((2, 16, PAD, keep.shape[2]), BF), pltpu.SemaphoreType.DMA((2, 16))],
        cost_estimate=NO_COST,
        name="pack",
    )(place, *layer0, *layer1, g_head, keep, send)


def in_chips(chunk, place, units, count, core, near_first):
    chips = jnp.arange(16)
    at = sum(bit_of(chips, mask) << j for j, mask in enumerate(steps_of(16, core, near_first)))
    chunk = jnp.take(chunk, at, axis=0)
    width = chunk.shape[2]
    if units:
        natural = chunk.reshape(16, units, -1, width).transpose(1, 0, 2, 3).reshape(units, count, -1, width)
        natural = natural.transpose(1, 0, 2, 3).reshape(count, -1, width)
    else:
        natural = chunk.reshape(count, -1, width)
    return relative(natural, place, core, near_first)


def in_planes(keep, send, place, units, count, near_first):
    if is_small(count):
        return keep, send
    first = place[1] == 0
    keeps, sends = [
        [in_chips(item, place, units[core], count, core, near_first) for core in range(2)] for item in (keep, send)
    ]
    return jnp.where(first, *keeps), jnp.where(first, sends[1], sends[0])


def relative(block, place, core, near_first=False):
    order = steps_of(block.shape[0], core, near_first)
    index = jnp.arange(block.shape[0])
    chips = sum(bit_of(index, 1 << j) * mask for j, mask in enumerate(order))
    return jnp.take(block, chips ^ place[0], axis=0)


def low(value):
    return value.astype(BF)


def add_low(terms, start, count):
    return low(sum(item[start : start + count].astype(F32) for item in terms))


class Reduce:
    def __init__(self, order, keep, send, near_first=False):
        self.order = order
        self.left = list(zip(*[steps_of(lax.axis_size("dp"), core, near_first) for core in range(2)]))
        self.terms = [keep]
        self.got = swap(order.now(send))

    def wait(self):
        self.got = self.order.wait(self.got)

    def start(self):
        self.terms.append(self.got)
        half = self.got.shape[0] // 2
        self.got = flip(self.order.now(add_low(self.terms, half, half)), *self.left.pop())

    def start_upper(self):
        self.terms.append(self.got)
        self.part = self.got.shape[0] // 4
        self.masks = self.left.pop()
        self.upper = flip(self.order.now(add_low(self.terms, 3 * self.part, self.part)), *self.masks)

    def start_lower(self):
        self.got = flip(self.order.now(add_low(self.terms, 2 * self.part, self.part)), *self.masks)

    def start_from_upper(self):
        part = self.part
        terms = [item[part : 2 * part] for item in self.terms] + [self.upper]
        self.ahead = flip(self.order.now(add_low(terms, 0, part)), *self.left.pop())

    def join(self):
        self.terms.append(self.got)
        self.got = self.ahead

    def spare(self, steps):
        while len(self.left) > steps:
            self.start()

    def finish(self):
        return sum(item[0].astype(F32) for item in self.terms + [self.got])


def shards(tokens, segment_ids, cotangent, qkv_w, out_w, up_w, down_w, gains_w, shifts_w, up_b, head_w):
    count = lax.axis_size("dp")
    section = lax.axis_index("section")
    me = lax.axis_index("dp")
    first = section == 0
    place = jnp.stack([me, section]).astype(jnp.int32)
    grad_place = place if is_small(count) else jnp.stack([jnp.zeros_like(section), section]).astype(jnp.int32)
    rows_dev, length, width = tokens.shape
    mine = rows_dev // 2
    size = width // count
    ff = up_w.shape[2]
    units = ff // width

    def cols(array, n):
        return [array[:, j * width : (j + 1) * width] for j in range(n)]

    def planes_of(low_units, high_units):
        low_plane, high_plane = jnp.concatenate(low_units), jnp.concatenate(high_units)
        got = swap(jnp.where(first, high_plane, low_plane))
        return jnp.where(first, low_plane, got), jnp.where(first, got, high_plane)

    q_u, k_u, v_u = cols(low(qkv_w[0]), 3)
    a_zero, a_one = planes_of([q_u, k_u], [v_u, low(out_w[0])])
    f_zero, f_one = planes_of(cols(low(up_w[0]), units), [low(down_w[0])])
    small = low(jnp.concatenate([gains_w.reshape(-1), shifts_w.reshape(-1), up_b.reshape(-1)]))
    small_n = small.shape[0]
    small_rows = -(-small_n // width)
    head_n = head_w.shape[0] * head_w.shape[1]
    head_rows = -(-head_n // width)
    pad_rows = -(-(small_rows + head_rows) // PAD) * PAD

    def to_rows(flat, rows):
        return jnp.pad(flat, (0, rows * width - flat.shape[0])).reshape(rows, width)

    if is_small(count):
        vec = jnp.concatenate([low(gains_w[0]), low(shifts_w[0])])
        eights = [low(head_w[8 * k : 8 * k + 8]) for k in range(3)]
        above = jnp.concatenate([jnp.pad(vec, ((0, 0), (0, 384 - size)))] + eights, axis=1)
        extra = jnp.concatenate([above, jnp.pad(low(up_b), ((0, 7), (0, width - up_b.shape[1])))])
    else:
        extra = jnp.concatenate(
            [
                to_rows(small, small_rows),
                to_rows(low(head_w).reshape(-1), head_rows),
                jnp.zeros((pad_rows - small_rows - head_rows, width), BF),
            ]
        )
    cut = 2 * size

    order = Order(place)
    a0_g = Gather(order, jnp.concatenate([a_zero, extra]))
    f0_g, a1_g, f1_g = Gather(order, f_zero), Gather(order, a_one, True), Gather(order, f_one)
    a0_g.spare(4)
    f0_g.spare(4)
    f1_g.spare(4)
    a0_g.start()
    a1_g.start()
    a0_g.got, a1_g.got = order.wait(a0_g.got, a1_g.got)
    a0_g.done()
    a0_g.start()
    f0_g.start()
    a1_g.done()
    a1_g.start()
    a0_g.got, f0_g.got, a1_g.got = order.wait(a0_g.got, f0_g.got, a1_g.got)
    a0_g.done()
    a0_g.start()
    f0_g.done()
    f0_g.start()
    a1_g.done()
    a1_g.spare(2)
    a0_g.got, f0_g.got = order.wait(a0_g.got, f0_g.got)
    a0_g.done()
    a0_g.start()
    f0_g.done()
    f0_g.start()
    a1_g.start()
    f1_g.start()
    a0_g.swap_own()
    a0_g.got, f0_g.got, a1_g.got, a0_g.other_own, f1_g.got = order.wait(
        a0_g.got, f0_g.got, a1_g.got, a0_g.other_own, f1_g.got
    )
    f0_g.done()
    f0_g.start()
    a1_g.done()
    f1_g.done()
    f1_g.start()
    a0_g.swap_got()
    a0_g.other_got = order.wait(a0_g.other_got)
    a0_half = a0_g.halves(place, 2, size)
    n_g = gains_w.shape[1] * size
    n_s = shifts_w.shape[1] * size
    tail_halves = (a0_g.own, a0_g.got), (a0_g.other_own, a0_g.other_got)
    if is_small(count):
        vecs, cups, head = tails_of(place, cut, units, *tail_halves)
        head = low(head)
    else:
        vecs, cups, heads = [], [], []
        for tail in natural_tails(place, cut, *tail_halves):
            flat = tail[:, :small_rows].reshape(count, -1)[:, :small_n].astype(F32)
            vec = flat[:, : n_g + n_s].reshape(count, -1, size).transpose(1, 0, 2).reshape(-1, width)
            vecs.append(vec)
            cups.append(flat[:, n_g + n_s :].reshape(units, 1, width))
            block = tail[:, small_rows : small_rows + head_rows].reshape(count, -1)[:, :head_n]
            heads.append(block.reshape(count * head_w.shape[0], head_w.shape[1]))
        head = jnp.concatenate(heads)
    gain0 = shift0 = vecs[0]
    gain1 = shift1 = vecs[1]
    cup0, cup1 = cups[0], cups[1]

    own = lax.dynamic_slice_in_dim(tokens, section * mine, mine, 0)
    seg = lax.dynamic_slice_in_dim(segment_ids, section * mine, mine, 0)
    cot = lax.dynamic_slice_in_dim(cotangent, section * mine, mine, 0)
    rows = range(mine)
    seg_col = [jnp.broadcast_to(seg[r][:, None], (length, 128)) for r in rows]
    seg_row = [jnp.broadcast_to(seg[r][None], (8, length)) for r in rows]

    a0 = order.now([own[r] for r in rows])
    kept_a0 = [attn_fwd(False, place, a0[r], seg_col[r], seg_row[r], a0_half, shift0) for r in rows]
    kept_a0, f0_g.got, f1_g.got = order.wait(kept_a0, f0_g.got, f1_g.got)
    f0_g.swap_own()
    f0_g.swap_got()
    a1_g.start()
    f1_g.done()
    f1_g.start()
    f0_g.other_own, f0_g.other_got = order.wait(f0_g.other_own, f0_g.other_got)
    n1 = order.now([kept[4] for kept in kept_a0])
    f0_half = f0_g.halves(place, units, size)
    a1_g.swap_own()
    kept_f0 = [ffn_fwd(False, place, n1[r], f0_half, cup0, gain0, shift0) for r in rows]
    kept_f0, a1_g.other_own, a1_g.got, f1_g.got = order.wait(kept_f0, a1_g.other_own, a1_g.got, f1_g.got)
    a1_g.swap_got()
    f1_g.done()
    f1_g.start()
    a1_g.other_got = order.wait(a1_g.other_got)
    a1 = order.now([kept[4] for kept in kept_f0])
    a1_half = a1_g.halves(place, 2, size)
    f1_g.swap_own()
    kept_a1 = [attn_fwd(True, place, a1[r], seg_col[r], seg_row[r], a1_half, shift1) for r in rows]
    kept_a1, f1_g.other_own, f1_g.got = order.wait(kept_a1, f1_g.other_own, f1_g.got)
    f1_g.swap_got()
    n1 = [kept[4] for kept in kept_a1]
    f1_half = f1_g.halves(place, units, size)
    kept_f1 = [ffn_fwd(False, place, n1[r], f1_half, cup1, gain1, shift1) for r in rows]

    d_y1, g_head = [], 0.0
    for r in rows:
        y1 = kept_f1[r][4]
        proj = dot(y1, head)
        rho = lax.rsqrt(jnp.sum(proj * proj, axis=-1, keepdims=True) + norm_eps)
        c = cot[r].astype(F32)
        d_proj = low(rho * c - rho * rho * rho * proj * jnp.sum(proj * c, axis=-1, keepdims=True))
        g_head = g_head + dot(y1, d_proj, 0, 0)
        d_y1.append(dot(d_proj, head, 1, 1))

    def total(items):
        out = items[0]
        for item in items[1:]:
            out = jax.tree.map(lambda x, y: (x.astype(F32) + y.astype(F32)).astype(x.dtype), out, item)
        return out

    def ffn_back(near_first, d_out, kept_a, kept_f, planes, gain, shift):
        outs = [
            ffn_bwd(near_first, grad_place, d_out[r], *kept_f[r][2:4], *kept_f[r][:2], planes, *kept_a[r][4:6], gain, shift)
            for r in rows
        ]
        keep, send, sums, cup = total([(o[0], o[1], o[3], o[4]) for o in outs])
        keep, send = in_planes(keep, send, place, (units, 0), count, near_first)
        return keep, send, [o[2] for o in outs], sums, cup

    def attn_back(near_first, more, d_out, a, kept, planes):
        outs = [attn_bwd(near_first, more, grad_place, d_out[r], a[r], seg_col[r], seg_row[r], *kept[r][:4], planes) for r in rows]
        keep, send, sums, sumo = total([(o[0], o[1], o[3], o[4]) for o in outs])
        keep, send = in_planes(keep, send, place, (2, 2), count, near_first)
        return keep, send, [o[2] for o in outs], sums, sumo

    keep, send, d_r, sums_f1, g_cup1 = ffn_back(False, d_y1, kept_a1, kept_f1, f1_half, gain1, shift1)
    f1_r = Reduce(order, keep, send)
    f1_r.wait()
    f1_r.start_upper()
    d_r = order.now(d_r)
    keep, send, d_a1, sums_a1, sumo_a1 = attn_back(True, 0, d_r, a1, kept_a1, a1_half)
    d_a1, f1_r.upper = order.wait(d_a1, f1_r.upper)
    a1_r = Reduce(order, keep, send, True)
    f1_r.start_lower()
    f1_r.start_from_upper()
    a1_r.wait()
    a1_r.spare(4)
    a1_r.start_upper()
    d_y0 = order.now([low(item) for item in d_a1])
    keep, send, d_r, sums_f0, g_cup0 = ffn_back(False, d_y0, kept_a0, kept_f0, f0_half, gain0, shift0)
    d_r, f1_r.got, f1_r.ahead, a1_r.upper = order.wait(d_r, f1_r.got, f1_r.ahead, a1_r.upper)
    f0_r = Reduce(order, keep, send)
    f1_r.join()
    f1_r.start()
    a1_r.start_lower()
    f0_r.wait()
    f0_r.start()
    d_r = order.now(d_r)
    keep, send, d_a0, sums_a0, sumo_a0 = attn_back(
        False, PAD if is_small(count) else 0, d_r, a0, kept_a0, a0_half
    )
    d_a0, a1_r.got, f1_r.got, f0_r.got = order.wait(d_a0, a1_r.got, f1_r.got, f0_r.got)

    def small_block(sums_a, sumo, sums_f, g_cup, head_part, core):
        gains = jnp.stack([sums_f[0], sums_f[1]]).reshape(2, count, size).transpose(1, 0, 2)
        shift = jnp.stack([sums_a[0], sums_a[1], sumo[0], sums_f[3], sums_f[4], sums_f[2]])
        shift = shift.reshape(6, count, size).transpose(1, 0, 2)
        flat = jnp.concatenate(
            [gains.reshape(count, -1), shift.reshape(count, -1), g_cup.reshape(count, -1)], axis=1
        )
        flat = jnp.pad(flat, ((0, 0), (0, small_rows * width - small_n)))
        piece = jnp.pad(head_part.reshape(count, -1), ((0, 0), (0, head_rows * width - head_n)))
        block = jnp.concatenate(
            [
                flat.reshape(count, small_rows, width),
                piece.reshape(count, head_rows, width),
                jnp.zeros((count, pad_rows - small_rows - head_rows, width), F32),
            ],
            axis=1,
        )
        return relative(low(block), place, core)

    if is_small(count):
        layer0 = (sums_a0, sumo_a0, sums_f0, g_cup0)
        layer1 = (sums_a1, sumo_a1, sums_f1, g_cup1)
        keep, send = pack_tails(place, cut, layer0, layer1, g_head, keep, send)
    else:
        half_head = g_head.reshape(2, -1, head_w.shape[1])
        tail0 = small_block(sums_a0, sumo_a0, sums_f0, g_cup0, half_head[0], 0)
        tail1 = small_block(sums_a1, sumo_a1, sums_f1, g_cup1, half_head[1], 1)
        keep = jnp.concatenate([keep, jnp.where(first, tail0, tail1)], axis=1)
        send = jnp.concatenate([send, jnp.where(first, tail1, tail0)], axis=1)
    a0_r = Reduce(order, keep, send)
    a0_r.wait()
    a0_r.start()
    f0_r.start()
    f1_r.spare(1)
    f1_r.start()
    a1_r.start_from_upper()
    d_first, d_second = jnp.stack(d_a0), jnp.stack(d_a1)
    a0_r.got, a1_r.ahead, f1_r.got = order.wait(a0_r.got, a1_r.ahead, f1_r.got)
    a0_r.start()
    a1_r.join()
    f0_r.wait()
    f0_r.start()
    a1_r.start()
    got = across(order.now(d_first), 1), across(order.now(d_second), 0)
    a0_r.got, a1_r.got = order.wait(a0_r.got, a1_r.got)
    a0_r.spare(2)
    a0_r.start()
    done_f1 = f1_r.finish()
    a1_r.start()
    f0_r.got, got, done_f1 = order.wait(f0_r.got, got, done_f1)
    f0_r.spare(1)
    f0_r.start()
    input_grads = jnp.where(first, jnp.concatenate([d_first, got[0]]), jnp.concatenate([got[1], d_second]))
    a0_r.got, a1_r.got, input_grads = order.wait(a0_r.got, a1_r.got, input_grads)
    a0_r.spare(1)
    a0_r.start()
    done_a1 = a1_r.finish()
    f0_r.got, done_a1 = order.wait(f0_r.got, done_a1)
    done_f0 = f0_r.finish()

    def unite(zero_part, one_part):
        got = swap(jnp.where(first, one_part, zero_part))
        return jnp.where(first, zero_part, got), jnp.where(first, got, one_part)

    up_plane, down_plane = unite(done_f0, done_f1)
    a0_r.got, up_plane, down_plane = order.wait(a0_r.got, up_plane, down_plane)
    done_a0 = a0_r.finish()
    low_plane, high_plane = unite(done_a0[:cut], done_a1)

    def unit(array, j):
        return array[j * size : (j + 1) * size]

    qkv_grad = jnp.concatenate([unit(low_plane, 0), unit(low_plane, 1), unit(high_plane, 0)], axis=1)
    out_grad = unit(high_plane, 1)
    up_grad = jnp.concatenate([unit(up_plane, j) for j in range(units)], axis=1)
    down_grad = down_plane
    tail = done_a0[cut:]
    if is_small(count):
        gain_grad = tail[None, :2, :size]
        shift_grad = tail[None, 2:8, :size]
        cup_grad = tail[8:9, : up_b.shape[1]]
        head_grad = jnp.concatenate([tail[:8, 384 + 128 * k : 512 + 128 * k] for k in range(3)])
    else:
        flat = tail[:small_rows].reshape(-1)[:small_n]
        gain_grad = flat[:n_g].reshape(gains_w.shape)
        shift_grad = flat[n_g : n_g + n_s].reshape(shifts_w.shape)
        cup_grad = flat[n_g + n_s :].reshape(up_b.shape)
        head_grad = tail[small_rows : small_rows + head_rows].reshape(-1)[:head_n].reshape(head_w.shape)

    return (
        qkv_grad[None],
        out_grad[None],
        up_grad[None],
        down_grad[None],
        gain_grad,
        shift_grad,
        cup_grad,
        head_grad,
        input_grads[None],
    )


def solution(mesh):
    return jax.shard_map(
        shards,
        mesh=mesh,
        in_specs=(
            P("dp", None, None),
            P("dp", None),
            P("dp", None, None),
            P("section", "dp", None),
            P("section", "dp", None),
            P("section", "dp", None),
            P("section", "dp", None),
            P("section", None, "dp"),
            P("section", None, "dp"),
            P("section", "dp"),
            P(("section", "dp"), None),
        ),
        out_specs=(
            P("section", "dp", None),
            P("section", "dp", None),
            P("section", "dp", None),
            P("section", "dp", None),
            P("section", None, "dp"),
            P("section", None, "dp"),
            P("section", "dp"),
            P(("section", "dp"), None),
            P("section", "dp", None, None),
        ),
        check_vma=False,
    )
```

time: 480 us -> 451 us (0.940)
  local copies, waits for them, and re-layouts: 29.6 us -> 12.9 us
  waiting for transfers between devices: 158 us -> 145 us
  other arithmetic: 71.9 us -> 61.2 us
  starting transfers between devices: 41.6 us -> 52.2 us
  Pallas kernels: 164 us -> 169 us
    ppermute x32 -> x34, waiting for transfers between devices: 140 us -> 115 us  [flip(): return lax.ppermute(value, BOTH, pairs)]
    ppermute x11 -> x16, waiting for transfers between devices: 17.8 us -> 30.5 us  [swap(): return lax.ppermute(value, BOTH, pairs)]
    select_n x31 -> x19, other arithmetic: 31.5 us -> 21.5 us  [the longest x12 15 us: done(): jnp.where(high, jnp.concatenate([got, own]), jnp.concatenate([own, got]))]
    slice x26 -> x3, local copies, waits for them, and re-layouts: 9.37 us -> 0.57 us  [the longest x1 0.56 us: shards(): cup_grad = tail[8:9, :up_b.shape[1]]]
    convert_element_type x23, other arithmetic: 25.9 us -> 33.1 us  [low(): return value.astype(BF)]
    ppermute x32 -> x34, starting transfers between devices: 39.5 us -> 45.6 us  [flip(): return lax.ppermute(value, BOTH, pairs)]
    add x9 -> x3, other arithmetic: 8.29 us -> 2.64 us  [finish(): return sum((item[0].astype(F32) for item in self.terms + [self.got]))]
    pallas_call x12 -> x10, Pallas kernels: 164 us -> 169 us  [the longest x2 47.3 us: attn_bwd(): pl.pallas_call(lambda *refs: attn_bwd_kernel(near_first, halves, *refs),...]
  transfers between devices with their start and end apart: 43 -> 52, of which waited for: 25 -> 27; matrix products, arithmetic and copies ran while one was open for 15% -> 11% of each run, Pallas kernels for 23% -> 29%
where the time goes in v4:
time: 451 us; the launch traced here: 447 us
  Pallas kernels  169 us (37%)
  waiting for transfers between devices  145 us (32%)
  other arithmetic  61.2 us (14%)
  starting transfers between devices  52.2 us (12%)
  local copies, waits for them, and re-layouts  12.9 us (3%)
    ppermute x34, waiting for transfers between devices, flip(): return lax.ppermute(value, BOTH, pairs)  115 us
    pallas_call x2, Pallas kernels, attn_bwd(): pl.pallas_call(lambda *refs: attn_bwd_kernel(near_first, halves, *refs),...  47.3 us
    pallas_call x2, Pallas kernels, ffn_bwd(): pl.pallas_call(lambda *refs: ffn_bwd_kernel(near_first, halves, *refs), g...  46.1 us
    ppermute x34, starting transfers between devices, flip(): return lax.ppermute(value, BOTH, pairs)  45.6 us
    pallas_call x2, Pallas kernels, ffn_fwd(): pl.pallas_call(lambda *refs: ffn_fwd_kernel(near_first, halves, *refs), g...  37 us
    pallas_call x2, Pallas kernels, attn_fwd(): pl.pallas_call(lambda *refs: attn_fwd_kernel(near_first, halves, *refs),...  33.3 us
    convert_element_type x23, other arithmetic, low(): return value.astype(BF)  33.1 us
    ppermute x16, waiting for transfers between devices, swap(): return lax.ppermute(value, BOTH, pairs)  30.5 us
  transfers between devices with their start and end apart: 52, of which 27 were waited for; matrix products, arithmetic and copies ran while one was open for 11% of the time, Pallas kernels for 29%

profile of v4, /device:TPU:0, one launch (start us, length us, event | category | flops | bytes accessed | tf_op | source)
XLA Modules:
  0.0 446.7 jit_solution(14813533662745584111)
XLA Ops:
  12.5 3.8 collective-permute-done.1
  22.4 8.8 %collective-permute-done.5 = bf16[1,192,768]{2,1,0:T(8,128)(2,1)} collective-permute-done((bf16[1,192,768]{2,1,0:T(8,128)(2,1)S(1)}, bf16[1,192,768]{2,1,0:T(8,128)(2,1)}, u32[]{:S(2)}, u32[]{:S(2)}) %collective-permute-start.5) | collective-permute-done | bytes 294944 | tf_op jit(solution)/shard_map/ppermute | solution.py:643
  37.3 15.8 %collective-permute-done.8 = bf16[2,192,768]{2,1,0:T(8,128)(2,1)S(1)} collective-permute-done((bf16[2,192,768]{2,1,0:T(8,128)(2,1)S(1)}, bf16[2,192,768]{2,1,0:T(8,128)(2,1)S(1)}, u32[]{:S(2)}, u32[]{:S(2)}) %collective-permute-start.8) | collective-permute-done | bytes 589856 | tf_op jit(solution)/shard_map/ppermute | solution.py:643
  60.3 20.5 %collective-permute-done.13 = bf16[1,192,768]{2,1,0:T(8,128)(2,1)S(1)} collective-permute-done((bf16[1,192,768]{2,1,0:T(8,128)(2,1)S(1)}, bf16[1,192,768]{2,1,0:T(8,128)(2,1)S(1)}, u32[]{:S(2)}, u32[]{:S(2)}) %collective-permute-start.13) | collective-permute-done | bytes 294944 | tf_op jit(solution)/shard_map/ppermute | solution.py:643
  84.3 3.6 maximum_select_fusion.1.refs_1_
  100.6 16.4 %attn_fwd.2 = (bf16[512,768]{1,0:T(8,128)(2,1)}, bf16[512,768]{1,0:T(8,128)(2,1)}, bf16[512,768]{1,0:T(8,128)(2,1)}, bf16[512,768]{1,0:T(8,128)(2,1)}, f32[512,768]{1,0:T(8,128)}, /*index=5*/f32[512,128]{1,0:T(8,128)}) custom-call(s32[2]{0:T(128)} %pad_add_fusion.refs_0_, bf16[8,112,768]{2,1,0:T(8,128)(2,1)} %copy-done.2, ...), custom_call_target="tpu_custom_call" | custom-call | tf_op jit(solution)/shard_map/attn_fwd/pallas_call | solution.py:240
  126.2 18.5 %ffn_fwd.2 = (bf16[512,3072]{1,0:T(8,128)(2,1)}, bf16[512,3072]{1,0:T(8,128)(2,1)}, f32[512,768]{1,0:T(8,128)}, f32[512,128]{1,0:T(8,128)}, bf16[512,768]{1,0:T(8,128)(2,1)}) custom-call(s32[2]{0:T(128)} %pad_add_fusion.refs_0_, bf16[8,192,768]{2,1,0:T(8,128)(2,1)} %maximum_select_fusion.1.refs_1_, bf16[8,192,768]{2,1,0:T(8,128)(2,1)} %collective-permute-done.15.refs_2_, ...), custom_call_target="tpu_custom_call" | custom-call | tf_op jit(solution)/shard_map/ffn_fwd/pallas_call | solution.py:328
  144.7 7.7 %collective-permute-done.20.refs_2_ = bf16[8,96,768]{2,1,0:T(8,128)(2,1)} collective-permute-done((bf16[8,96,768]{2,1,0:T(8,128)(2,1)S(1)}, bf16[8,96,768]{2,1,0:T(8,128)(2,1)}, u32[]{:S(2)}, u32[]{:S(2)}) %collective-permute-start.20) | collective-permute-done | bytes 1179680 | tf_op jit(solution)/shard_map/ppermute | solution.py:643
  157.8 16.9 %attn_fwd.3 = (bf16[512,768]{1,0:T(8,128)(2,1)}, bf16[512,768]{1,0:T(8,128)(2,1)}, bf16[512,768]{1,0:T(8,128)(2,1)}, bf16[512,768]{1,0:T(8,128)(2,1)}, f32[512,768]{1,0:T(8,128)}, /*index=5*/f32[512,128]{1,0:T(8,128)}) custom-call(s32[2]{0:T(128)} %pad_add_fusion.refs_0_, bf16[8,96,768]{2,1,0:T(8,128)(2,1)} %copy-done.6, ...), custom_call_target="tpu_custom_call" | custom-call | tf_op jit(solution)/shard_map/attn_fwd/pallas_call | solution.py:240
  174.7 9.3 %collective-permute-done.24.refs_2_ = bf16[8,192,768]{2,1,0:T(8,128)(2,1)} collective-permute-done((bf16[8,192,768]{2,1,0:T(8,128)(2,1)S(1)}, bf16[8,192,768]{2,1,0:T(8,128)(2,1)}, u32[]{:S(2)}, u32[]{:S(2)}) %collective-permute-start.24) | collective-permute-done | bytes 2359328 | tf_op jit(solution)/shard_map/ppermute | solution.py:643
  185.0 3.7 collective-permute-done.25.refs_4_
  190.2 18.5 %ffn_fwd.3 = (bf16[512,3072]{1,0:T(8,128)(2,1)}, bf16[512,3072]{1,0:T(8,128)(2,1)}, f32[512,768]{1,0:T(8,128)}, f32[512,128]{1,0:T(8,128)}, bf16[512,768]{1,0:T(8,128)(2,1)}) custom-call(s32[2]{0:T(128)} %pad_add_fusion.refs_0_, bf16[8,192,768]{2,1,0:T(8,128)(2,1)} %copy-done.3, bf16[8,192,768]{2,1,0:T(8,128)(2,1)} %collective-permute-done.24.refs_2_, ...), custom_call_target="tpu_custom_call" | custom-call | tf_op jit(solution)/shard_map/ffn_fwd/pallas_call | solution.py:328
  211.9 23.2 %ffn_bwd.2 = (bf16[16,192,768]{2,1,0:T(8,128)(2,1)}, bf16[16,192,768]{2,1,0:T(8,128)(2,1)}, f32[512,768]{1,0:T(8,128)}, f32[8,768]{1,0:T(8,128)}, f32[4,1,768]{2,1,0:T(1,128)}) custom-call(s32[2]{0:T(128)} %pad_add_fusion.refs_0_, bf16[8,192,768]{2,1,0:T(8,128)(2,1)} %copy-done.3, bf16[8,192,768]{2,1,0:T(8,128)(2,1)} %collective-permute-done.24.refs_2_, ...), custom_call_target="tpu_custom_call" | custom-call | tf_op jit(solution)/shard_map/ffn_bwd/pallas_call | solution.py:450
  235.3 8.2 %collective-permute-done.26 = bf16[16,192,768]{2,1,0:T(8,128)(2,1)} collective-permute-done((bf16[16,192,768]{2,1,0:T(8,128)(2,1)}, bf16[16,192,768]{2,1,0:T(8,128)(2,1)}, u32[]{:S(2)}, u32[]{:S(2)}) %collective-permute-start.26) | collective-permute-done | bytes 4718624 | tf_op jit(solution)/shard_map/ppermute | solution.py:649
  247.1 23.6 %attn_bwd.2 = (bf16[16,96,768]{2,1,0:T(8,128)(2,1)}, bf16[16,96,768]{2,1,0:T(8,128)(2,1)}, f32[512,768]{1,0:T(8,128)}, f32[8,768]{1,0:T(8,128)}, f32[8,768]{1,0:T(8,128)}) custom-call(s32[2]{0:T(128)} %pad_add_fusion.refs_0_, bf16[8,96,768]{2,1,0:T(8,128)(2,1)} %copy-done.6, bf16[8,96,768]{2,1,0:T(8,128)(2,1)} %collective-permute-done.20.refs_2_, ...), custom_call_target="tpu_custom_call" | custom-call | tf_op jit(solution)/shard_map/attn_bwd/pallas_call | solution.py:610
  270.8 4.5 %add_convert_fusion.3 = (bf16[4,192,768]{2,1,0:T(8,128)(2,1)}, bf16[4,192,768]{2,1,0:T(8,128)(2,1)}) fusion(bf16[4,192,768]{2,1,0:T(8,128)(2,1)S(1)} %collective-permute-done.27, bf16[16,192,768]{2,1,0:T(8,128)(2,1)} %collective-permute-done.26, bf16[16,192,768]{2,1,0:T(8,128)(2,1)} %get-tuple-element.301), kind=kLoop, calls=%fused_computation.6 | loop fusion | flops 5898240 | bytes 8257536 | tf_op jit(solution)/shard_map/convert_element_type | solution.py:871
  281.2 22.9 %ffn_bwd.3 = (bf16[16,192,768]{2,1,0:T(8,128)(2,1)}, bf16[16,192,768]{2,1,0:T(8,128)(2,1)}, f32[512,768]{1,0:T(8,128)}, f32[8,768]{1,0:T(8,128)}, f32[4,1,768]{2,1,0:T(1,128)}) custom-call(s32[2]{0:T(128)} %pad_add_fusion.refs_0_, bf16[8,192,768]{2,1,0:T(8,128)(2,1)} %maximum_select_fusion.1.refs_1_, bf16[8,192,768]{2,1,0:T(8,128)(2,1)} %collective-permute-done.15.refs_2_, ...), custom_call_target="tpu_custom_call" | custom-call | tf_op jit(solution)/shard_map/ffn_bwd/pallas_call | solution.py:450
  304.3 8.1 %collective-permute-done.32 = bf16[16,192,768]{2,1,0:T(8,128)(2,1)S(1)} collective-permute-done((bf16[16,192,768]{2,1,0:T(8,128)(2,1)}, bf16[16,192,768]{2,1,0:T(8,128)(2,1)S(1)}, u32[]{:S(2)}, u32[]{:S(2)}) %collective-permute-start.32) | collective-permute-done | bytes 4718624 | tf_op jit(solution)/shard_map/ppermute | solution.py:649
  312.4 5.5 %add_convert_fusion = bf16[8,192,768]{2,1,0:T(8,128)(2,1)} fusion(bf16[16,192,768]{2,1,0:T(8,128)(2,1)S(1)} %collective-permute-done.32, bf16[16,192,768]{2,1,0:T(8,128)(2,1)} %get-tuple-element.349), kind=kLoop, calls=%fused_computation | loop fusion | flops 4718592 | bytes 7077888 | tf_op jit(solution)/shard_map/convert_element_type | solution.py:871
  327.7 23.7 %attn_bwd.3 = (bf16[16,112,768]{2,1,0:T(8,128)(2,1)}, bf16[16,112,768]{2,1,0:T(8,128)(2,1)}, f32[512,768]{1,0:T(8,128)}, f32[8,768]{1,0:T(8,128)}, f32[8,768]{1,0:T(8,128)}) custom-call(s32[2]{0:T(128)} %pad_add_fusion.refs_0_, bf16[8,112,768]{2,1,0:T(8,128)(2,1)} %copy-done.2, bf16[8,112,768]{2,1,0:T(8,128)(2,1)} %collective-permute-done.9.refs_2_, ...), custom_call_target="tpu_custom_call" | custom-call | tf_op jit(solution)/shard_map/attn_bwd/pallas_call | solution.py:610
  354.0 5.3 %collective-permute-done.36 = bf16[16,112,768]{2,1,0:T(8,128)(2,1)S(1)} collective-permute-done((bf16[16,112,768]{2,1,0:T(8,128)(2,1)}, bf16[16,112,768]{2,1,0:T(8,128)(2,1)S(1)}, u32[]{:S(2)}, u32[]{:S(2)}) %collective-permute-start.36) | collective-permute-done | bytes 2752544 | tf_op jit(solution)/shard_map/ppermute | solution.py:649
  369.5 18.2 %collective-permute-done.39 = bf16[1,192,768]{2,1,0:T(8,128)(2,1)S(1)} collective-permute-done((bf16[1,192,768]{2,1,0:T(8,128)(2,1)S(1)}, bf16[1,192,768]{2,1,0:T(8,128)(2,1)S(1)}, u32[]{:S(2)}, u32[]{:S(2)}) %collective-permute-start.39) | collective-permute-done | bytes 294944 | tf_op jit(solution)/shard_map/ppermute | solution.py:643
  387.7 3.6 collective-permute-done.37
  423.0 8.3 %collective-permute-done.43 = bf16[2,112,768]{2,1,0:T(8,128)(2,1)S(1)} collective-permute-done((bf16[2,112,768]{2,1,0:T(8,128)(2,1)S(1)}, bf16[2,112,768]{2,1,0:T(8,128)(2,1)S(1)}, u32[]{:S(2)}, u32[]{:S(2)}) %collective-permute-start.43) | collective-permute-done | bytes 344096 | tf_op jit(solution)/shard_map/ppermute | solution.py:643
  (233 shorter events, 146.5 us)
Async XLA Ops:
  53.4 30.9 %collective-permute-start.12 = (bf16[8,112,768]{2,1,0:T(8,128)(2,1)S(1)}, bf16[8,112,768]{2,1,0:T(8,128)(2,1)}, u32[]{:S(2)}, u32[]{:S(2)}) collective-permute-start(bf16[8,112,768]{2,1,0:T(8,128)(2,1)S(1)} %maximum_select_fusion.3.refs_1_), channel_id=1, source_target_pairs={{0,16},{1,17},{2,18},{3,19},{4,20},{5,21},{6,22},{7,23},{8,24},{9,... | collective-permute-start | bytes 4128776 | tf_op jit(solution)/shard_map/ppermute | solution.py:649
  53.5 30.8 %collective-permute-start.9 = (bf16[8,112,768]{2,1,0:T(8,128)(2,1)S(1)}, bf16[8,112,768]{2,1,0:T(8,128)(2,1)}, u32[]{:S(2)}, u32[]{:S(2)}) collective-permute-start(bf16[8,112,768]{2,1,0:T(8,128)(2,1)S(1)} %maximum_select_fusion.3.refs_1_), channel_id=1, source_target_pairs={{0,2},{1,3},{2,0},{3,1},{4,6},{5,7},{6,4},{7,5},{8,10},{9,11},{10,... | collective-permute-start | bytes 4128776 | tf_op jit(solution)/shard_map/ppermute | solution.py:643
  56.6 27.7 %collective-permute-start.10 = (bf16[4,192,768]{2,1,0:T(8,128)(2,1)}, bf16[4,192,768]{2,1,0:T(8,128)(2,1)}, u32[]{:S(2)}, u32[]{:S(2)}) collective-permute-start(bf16[4,192,768]{2,1,0:T(8,128)(2,1)} %maximum_select_fusion.4), channel_id=1, source_target_pairs={{0,1},{1,0},{2,3},{3,2},{4,5},{5,4},{6,7},{7,6},{8,9},{9,8},{10,11... | collective-permute-start | bytes 3538952 | tf_op jit(solution)/shard_map/ppermute | solution.py:643
  58.2 22.6 %collective-permute-start.11 = (bf16[4,96,768]{2,1,0:T(8,128)(2,1)S(1)}, bf16[4,96,768]{2,1,0:T(8,128)(2,1)S(1)}, u32[]{:S(2)}, u32[]{:S(2)}) collective-permute-start(bf16[4,96,768]{2,1,0:T(8,128)(2,1)S(1)} %maximum_select_fusion.9), channel_id=1, source_target_pairs={{0,4},{1,5},{2,6},{3,7},{4,0},{5,1},{6,2},{7,3},{8,12},{9,13},{10,... | collective-permute-start | bytes 1769480 | tf_op jit(solution)/shard_map/ppermute | solution.py:643
  58.3 22.5 %collective-permute-start.13 = (bf16[1,192,768]{2,1,0:T(8,128)(2,1)S(1)}, bf16[1,192,768]{2,1,0:T(8,128)(2,1)S(1)}, u32[]{:S(2)}, u32[]{:S(2)}) collective-permute-start(bf16[1,192,768]{2,1,0:T(8,128)(2,1)S(1)} %get-tuple-element.223), channel_id=1, source_target_pairs={{0,4},{1,5},{2,6},{3,7},{4,0},{5,1},{6,2},{7,3},{8,12},{9,13},{10,... | collective-permute-start | bytes 884744 | tf_op jit(solution)/shard_map/ppermute | solution.py:643
  87.9 29.3 %collective-permute-start.15 = (bf16[8,192,768]{2,1,0:T(8,128)(2,1)}, bf16[8,192,768]{2,1,0:T(8,128)(2,1)}, u32[]{:S(2)}, u32[]{:S(2)}) collective-permute-start(bf16[8,192,768]{2,1,0:T(8,128)(2,1)} %maximum_select_fusion.1.refs_1_), channel_id=1, source_target_pairs={{0,2},{1,3},{2,0},{3,1},{4,6},{5,7},{6,4},{7,5},{8,10},{9,11},{10,... | collective-permute-start | bytes 7077896 | tf_op jit(solution)/shard_map/ppermute | solution.py:643
  90.2 26.9 %collective-permute-start.16 = (bf16[2,192,768]{2,1,0:T(8,128)(2,1)S(1)}, bf16[2,192,768]{2,1,0:T(8,128)(2,1)}, u32[]{:S(2)}, u32[]{:S(2)}) collective-permute-start(bf16[2,192,768]{2,1,0:T(8,128)(2,1)S(1)} %maximum_select_fusion.10), channel_id=1, source_target_pairs={{0,8},{1,9},{2,10},{3,11},{4,12},{5,13},{6,14},{7,15},{8,0},{9,1},... | collective-permute-start | bytes 1769480 | tf_op jit(solution)/shard_map/ppermute | solution.py:643
  122.6 29.8 %collective-permute-start.20 = (bf16[8,96,768]{2,1,0:T(8,128)(2,1)S(1)}, bf16[8,96,768]{2,1,0:T(8,128)(2,1)}, u32[]{:S(2)}, u32[]{:S(2)}) collective-permute-start(bf16[8,96,768]{2,1,0:T(8,128)(2,1)S(1)} %maximum_select_fusion.5.refs_1_), channel_id=1, source_target_pairs={{0,8},{1,9},{2,10},{3,11},{4,12},{5,13},{6,14},{7,15},{8,0},{9,1},... | collective-permute-start | bytes 3538952 | tf_op jit(solution)/shard_map/ppermute | solution.py:643
  123.3 29.2 %collective-permute-start.21 = (bf16[4,192,768]{2,1,0:T(8,128)(2,1)}, bf16[4,192,768]{2,1,0:T(8,128)(2,1)}, u32[]{:S(2)}, u32[]{:S(2)}) collective-permute-start(bf16[4,192,768]{2,1,0:T(8,128)(2,1)} %maximum_select_fusion.6), channel_id=1, source_target_pairs={{0,1},{1,0},{2,3},{3,2},{4,5},{5,4},{6,7},{7,6},{8,9},{9,8},{10,11... | collective-permute-start | bytes 3538952 | tf_op jit(solution)/shard_map/ppermute | solution.py:643
  125.5 27.0 %collective-permute-start.19 = (bf16[8,96,768]{2,1,0:T(8,128)(2,1)S(1)}, bf16[8,96,768]{2,1,0:T(8,128)(2,1)}, u32[]{:S(2)}, u32[]{:S(2)}) collective-permute-start(bf16[8,96,768]{2,1,0:T(8,128)(2,1)S(1)} %maximum_select_fusion.5.refs_1_), channel_id=1, source_target_pairs={{0,16},{1,17},{2,18},{3,19},{4,20},{5,21},{6,22},{7,23},{8,24},{9,... | collective-permute-start | bytes 3538952 | tf_op jit(solution)/shard_map/ppermute | solution.py:649
  155.0 29.0 %collective-permute-start.24 = (bf16[8,192,768]{2,1,0:T(8,128)(2,1)S(1)}, bf16[8,192,768]{2,1,0:T(8,128)(2,1)}, u32[]{:S(2)}, u32[]{:S(2)}) collective-permute-start(bf16[8,192,768]{2,1,0:T(8,128)(2,1)S(1)} %maximum_select_fusion.2.refs_1_), channel_id=1, source_target_pairs={{0,2},{1,3},{2,0},{3,1},{4,6},{5,7},{6,4},{7,5},{8,10},{9,11},{10,... | collective-permute-start | bytes 7077896 | tf_op jit(solution)/shard_map/ppermute | solution.py:643
  156.7 27.3 %collective-permute-start.23 = (bf16[8,192,768]{2,1,0:T(8,128)(2,1)S(1)}, bf16[8,192,768]{2,1,0:T(8,128)(2,1)}, u32[]{:S(2)}, u32[]{:S(2)}) collective-permute-start(bf16[8,192,768]{2,1,0:T(8,128)(2,1)S(1)} %maximum_select_fusion.2.refs_1_), channel_id=1, source_target_pairs={{0,16},{1,17},{2,18},{3,19},{4,20},{5,21},{6,22},{7,23},{8,24},{9,... | collective-permute-start | bytes 7077896 | tf_op jit(solution)/shard_map/ppermute | solution.py:649
  245.4 25.4 %collective-permute-start.27 = (bf16[4,192,768]{2,1,0:T(8,128)(2,1)S(1)}, bf16[4,192,768]{2,1,0:T(8,128)(2,1)S(1)}, u32[]{:S(2)}, u32[]{:S(2)}) collective-permute-start(bf16[4,192,768]{2,1,0:T(8,128)(2,1)S(1)} %add_convert_fusion.5), channel_id=1, source_target_pairs={{0,2},{1,3},{2,0},{3,1},{4,6},{5,7},{6,4},{7,5},{8,10},{9,11},{10,... | collective-permute-start | bytes 3538952 | tf_op jit(solution)/shard_map/ppermute | solution.py:643
  275.3 28.9 %collective-permute-start.29 = (bf16[4,192,768]{2,1,0:T(8,128)(2,1)}, bf16[4,192,768]{2,1,0:T(8,128)(2,1)S(1)}, u32[]{:S(2)}, u32[]{:S(2)}) collective-permute-start(bf16[4,192,768]{2,1,0:T(8,128)(2,1)} %get-tuple-element.316), channel_id=1, source_target_pairs={{0,2},{1,3},{2,0},{3,1},{4,6},{5,7},{6,4},{7,5},{8,10},{9,11},{10,... | collective-permute-start | bytes 3538952 | tf_op jit(solution)/shard_map/ppermute | solution.py:643
  275.7 28.6 %collective-permute-start.30 = (bf16[4,192,768]{2,1,0:T(8,128)(2,1)}, bf16[4,192,768]{2,1,0:T(8,128)(2,1)}, u32[]{:S(2)}, u32[]{:S(2)}) collective-permute-start(bf16[4,192,768]{2,1,0:T(8,128)(2,1)} %get-tuple-element.318), channel_id=1, source_target_pairs={{0,1},{1,0},{2,3},{3,2},{4,5},{5,4},{6,7},{7,6},{8,9},{9,8},{10,11... | collective-permute-start | bytes 3538952 | tf_op jit(solution)/shard_map/ppermute | solution.py:643
  280.1 24.1 %collective-permute-start.31 = (bf16[4,96,768]{2,1,0:T(8,128)(2,1)S(1)}, bf16[4,96,768]{2,1,0:T(8,128)(2,1)}, u32[]{:S(2)}, u32[]{:S(2)}) collective-permute-start(bf16[4,96,768]{2,1,0:T(8,128)(2,1)S(1)} %add_convert_fusion.11), channel_id=1, source_target_pairs={{0,8},{1,9},{2,10},{3,11},{4,12},{5,13},{6,14},{7,15},{8,0},{9,1},... | collective-permute-start | bytes 1769480 | tf_op jit(solution)/shard_map/ppermute | solution.py:643
  317.9 36.1 %collective-permute-start.35 = (bf16[8,192,768]{2,1,0:T(8,128)(2,1)}, bf16[8,192,768]{2,1,0:T(8,128)(2,1)}, u32[]{:S(2)}, u32[]{:S(2)}) collective-permute-start(bf16[8,192,768]{2,1,0:T(8,128)(2,1)} %add_convert_fusion), channel_id=1, source_target_pairs={{0,2},{1,3},{2,0},{3,1},{4,6},{5,7},{6,4},{7,5},{8,10},{9,11},{10,... | collective-permute-start | bytes 7077896 | tf_op jit(solution)/shard_map/ppermute | solution.py:643
  321.1 32.9 %collective-permute-start.34 = (bf16[2,192,768]{2,1,0:T(8,128)(2,1)}, bf16[2,192,768]{2,1,0:T(8,128)(2,1)S(1)}, u32[]{:S(2)}, u32[]{:S(2)}) collective-permute-start(bf16[2,192,768]{2,1,0:T(8,128)(2,1)} %add_convert_fusion.9), channel_id=1, source_target_pairs={{0,8},{1,9},{2,10},{3,11},{4,12},{5,13},{6,14},{7,15},{8,0},{9,1},... | collective-permute-start | bytes 1769480 | tf_op jit(solution)/shard_map/ppermute | solution.py:643
  326.4 27.5 %collective-permute-start.33 = (bf16[4,96,768]{2,1,0:T(8,128)(2,1)}, bf16[4,96,768]{2,1,0:T(8,128)(2,1)}, u32[]{:S(2)}, u32[]{:S(2)}) collective-permute-start(bf16[4,96,768]{2,1,0:T(8,128)(2,1)} %get-tuple-element.345), channel_id=1, source_target_pairs={{0,8},{1,9},{2,10},{3,11},{4,12},{5,13},{6,14},{7,15},{8,0},{9,1},... | collective-permute-start | bytes 1769480 | tf_op jit(solution)/shard_map/ppermute | solution.py:643
  361.0 30.3 %collective-permute-start.37 = (bf16[8,112,768]{2,1,0:T(8,128)(2,1)S(1)}, bf16[8,112,768]{2,1,0:T(8,128)(2,1)S(1)}, u32[]{:S(2)}, u32[]{:S(2)}) collective-permute-start(bf16[8,112,768]{2,1,0:T(8,128)(2,1)S(1)} %add_convert_fusion.1), channel_id=1, source_target_pairs={{0,2},{1,3},{2,0},{3,1},{4,6},{5,7},{6,4},{7,5},{8,10},{9,11},{10,... | collective-permute-start | bytes 4128776 | tf_op jit(solution)/shard_map/ppermute | solution.py:643
  365.0 26.3 %collective-permute-start.41 = (bf16[4,192,768]{2,1,0:T(8,128)(2,1)S(1)}, bf16[4,192,768]{2,1,0:T(8,128)(2,1)S(1)}, u32[]{:S(2)}, u32[]{:S(2)}) collective-permute-start(bf16[4,192,768]{2,1,0:T(8,128)(2,1)S(1)} %add_convert_fusion.2), channel_id=1, source_target_pairs={{0,1},{1,0},{2,3},{3,2},{4,5},{5,4},{6,7},{7,6},{8,9},{9,8},{10,11... | collective-permute-start | bytes 3538952 | tf_op jit(solution)/shard_map/ppermute | solution.py:643
  365.6 22.1 %collective-permute-start.38 = (bf16[4,96,768]{2,1,0:T(8,128)(2,1)S(1)}, bf16[4,96,768]{2,1,0:T(8,128)(2,1)S(1)}, u32[]{:S(2)}, u32[]{:S(2)}) collective-permute-start(bf16[4,96,768]{2,1,0:T(8,128)(2,1)S(1)} %copy-done.26), channel_id=1, source_target_pairs={{0,4},{1,5},{2,6},{3,7},{4,0},{5,1},{6,2},{7,3},{8,12},{9,13},{10,... | collective-permute-start | bytes 1769480 | tf_op jit(solution)/shard_map/ppermute | solution.py:643
  391.3 26.8 %collective-permute-start.46 = (f32[1,512,768]{2,1,0:T(8,128)S(1)}, f32[1,512,768]{2,1,0:T(8,128)S(1)}, u32[]{:S(2)}, u32[]{:S(2)}) collective-permute-start(f32[1,512,768]{2,1,0:T(8,128)S(1)} %bitcast.80), channel_id=1, source_target_pairs={{16,0},{17,1},{18,2},{19,3},{20,4},{21,5},{22,6},{23,7},{24,8},{25... | collective-permute-start | bytes 4718600 | tf_op jit(solution)/shard_map/ppermute | solution.py:654
  392.6 25.5 %collective-permute-start.47 = (f32[1,512,768]{2,1,0:T(8,128)S(1)}, f32[1,512,768]{2,1,0:T(8,128)S(1)}, u32[]{:S(2)}, u32[]{:S(2)}) collective-permute-start(f32[1,512,768]{2,1,0:T(8,128)S(1)} %bitcast.73), channel_id=1, source_target_pairs={{0,16},{1,17},{2,18},{3,19},{4,20},{5,21},{6,22},{7,23},{8,24},{9,... | collective-permute-start | bytes 4718600 | tf_op jit(solution)/shard_map/ppermute | solution.py:654
  (61 other events, 702.9 us)

commit v5 on v4

--- a/solution.py
+++ b/solution.py
@@ -105,46 +105,67 @@
     lax.fori_loop(0, count, lambda j, _: (body(j), 0)[1], 0)
 
 
+CHIP_BITS = (8, 4, 2, 1)
+
+
 class Loads:
     def __init__(self, near_first, place_ref, own, other, targets, sem):
         self.near_first, self.place, self.planes = near_first, place_ref, (own, other)
         self.targets, self.sem = targets, sem
 
-    def at(self, plane, unit, chip):
-        target = self.targets[plane]
-        if len(target.shape) == 5:
-            return target.at[unit, chip >> 2, chip & 3]
-        return target.at[chip >> 2, chip & 3]
-
-    def start(self, plane, unit, first, count):
+    def groups(self, plane, unit):
         order = steps_of(16, plane, self.near_first)
-        target = self.targets[plane]
-        size = target.shape[-2]
-
-        def by_chip(section, chip):
+        together = len(self.targets[plane].shape) == 6
+        out = []
+        for p in range(2):
+            for b2 in range(2):
+                fixed = {order[3]: bit_of(self.place[0], order[3]) ^ p, order[2]: b2}
+                if together:
+                    assert plane and not self.near_first
+                    fixed.update({8: unit >> 1, 4: unit & 1})
+                    bits = [(unit & 1, unit >> 1)]
+                elif plane == 0:
+                    bits = [()]
+                else:
+                    bits = [(0,), (1,)]
+                for lead in bits:
+                    if lead and not together:
+                        fixed = {**fixed, order[1]: lead[0]}
+                    chips = tuple(fixed.get(mask, slice(None)) for mask in CHIP_BITS)
+                    out.append((p, b2, lead, chips if together else (unit,) + chips))
+        return out
+
+    def start(self, plane, unit):
+        size = self.targets[plane].shape[-2]
+
+        def begin(section):
             pieces = self.planes[0] if plane == section else self.planes[1]
-            to, sem = self.at(plane, unit, chip), self.sem.at[plane, unit, chip]
             if len(pieces) == 1:
-                source = pieces[0].reshape(*target.shape)
-                at = source.at[unit] if len(target.shape) == 5 else source
-                pltpu.make_async_copy(at.at[chip >> 2, chip & 3], to, sem).start()
-                return
-            index = sum(bit_of(chip, order[j]) << j for j in range(3))
-            far = bit_of(chip ^ self.place[0], order[3])
-            for p in range(2):
-                @pl.when(far == p)
-                def _():
-                    rows = pl.ds(pl.multiple_of(unit * size, PAD), size)
-                    pltpu.make_async_copy(pieces[p].at[index, rows, :], to, sem).start()
-
-        by_section(self.place[1], lambda section: each(count, lambda j: by_chip(section, first + j)))
-
-    def wait(self, plane, unit, first, count):
-        def by_chip(chip):
-            to = self.at(plane, unit, chip)
-            pltpu.make_async_copy(to, to, self.sem.at[plane, unit, chip]).wait()
-
-        each(count, lambda j: by_chip(first + j))
+                source = pieces[0].reshape(*self.targets[plane].shape)
+            for k, (p, b2, lead, at) in enumerate(self.groups(plane, unit)):
+                if len(pieces) == 1:
+                    piece = source.at[at]
+                else:
+                    piece = pieces[1 + b2] if p and len(pieces) == 3 else pieces[p].at[b2]
+                    for bit in lead:
+                        piece = piece.at[bit]
+                    if len(at) == 5:
+                        rows = pl.ds(pl.multiple_of(unit * size, PAD), size)
+                        piece = piece.at[(slice(None),) * (len(piece.shape) - 2) + (rows,)]
+                pltpu.make_async_copy(piece, self.targets[plane].at[at], self.sem.at[plane, unit, k]).start()
+
+        by_section(self.place[1], begin)
+
+    def wait(self, plane, unit):
+        for k, (_, _, _, at) in enumerate(self.groups(plane, unit)):
+            to = self.targets[plane].at[at]
+            pltpu.make_async_copy(to, to, self.sem.at[plane, unit, k]).wait()
+
+
+def halves_view(pieces):
+    if len(pieces) == 1:
+        return pieces
+    return [item.reshape((2,) * (item.shape[0].bit_length() - 1) + item.shape[1:]) for item in pieces]
 
 
 def block_of(b, pair):
@@ -169,15 +190,15 @@
     @pl.when(step == 0)
     def _():
         for plane, unit in ((0, 0), (0, 1), (1, 0), (1, 1)):
-            loads.start(plane, unit, 0, 16)
+            loads.start(plane, unit)
         for plane, unit in ((0, 0), (0, 1), (1, 0)):
-            loads.wait(plane, unit, 0, 16)
+            loads.wait(plane, unit)
 
     cols = GROUP * HDIM
     here = pl.ds(pl.multiple_of(step * cols, cols), cols)
 
     def column(ref, j):
-        return ref[j, :, :, :, here].reshape(width, cols)
+        return ref[j, :, :, :, :, :, here].reshape(width, cols)
 
     q_ref[...] = (dot(a, column(low_w, 0)) + bias_ref[2:3]).astype(BF)
     k_ref[...] = dot(a, column(low_w, 1)).astype(BF)
@@ -205,7 +226,7 @@
         o_ref[rows, lanes] = jnp.where(lane < HDIM, out[:BLOCK], out[BLOCK:]).astype(BF)
     @pl.when(step == 0)
     def _():
-        loads.wait(1, 1, 0, 16)
+        loads.wait(1, 1)
 
     part = dot(o_ref[...], high_w.at[1].reshape(width, width)[here, :])
 
@@ -235,7 +256,7 @@
     length, width = a.shape
     cols = GROUP * HDIM
     group = pl.BlockSpec((length, cols), lambda g: (0, g))
-    half = (2, 4, 4, width // 16, width)
+    half = (2, 2, 2, 2, 2, width // 16, width)
     halves = len(planes[0])
     return pl.pallas_call(
         lambda *refs: attn_fwd_kernel(near_first, halves, *refs),
@@ -251,11 +272,11 @@
             pltpu.VMEM((length, width), F32),
             pltpu.VMEM(half, BF),
             pltpu.VMEM(half, BF),
-            pltpu.SemaphoreType.DMA((2, 2, 16)),
+            pltpu.SemaphoreType.DMA((2, 2, 8)),
         ],
         cost_estimate=NO_COST,
         name="attn_fwd",
-    )(place, *planes[0], *planes[1], a, seg_col, seg_row, shift, shift)
+    )(place, *halves_view(planes[0]), *halves_view(planes[1]), a, seg_col, seg_row, shift, shift)
 
 
 def ffn_fwd_kernel(near_first, halves, place_ref, *refs):
@@ -270,8 +291,8 @@
 
     @pl.when(step == 0)
     def _():
-        loads.start(0, 0, 0, 16)
-        loads.start(1, 0, 0, 4)
+        loads.start(0, 0)
+        loads.start(1, 0)
 
     @pl.when(step == 0)
     def _():
@@ -279,16 +300,16 @@
         h1[...] = hidden.astype(BF)
         acc[...] = hidden + shift_ref[5:6]
 
-    loads.wait(0, step, 0, 16)
+    loads.wait(0, step)
 
     @pl.when(step + 1 < units)
     def _():
-        loads.start(0, step + 1, 0, 16)
-        loads.start(1, 0, 4 * (step + 1), 4)
-
-    loads.wait(1, 0, 4 * step, 4)
+        loads.start(0, step + 1)
+        loads.start(1, step + 1)
+
+    loads.wait(1, step)
     up = up_w[step].reshape(width, width)
-    down = down_w[step].reshape(width, width)
+    down = down_w[step >> 1, step & 1].reshape(width, width)
     wide = 256
     parts = h1.shape[1] // wide
 
@@ -322,8 +343,8 @@
     length, width = n1.shape
     units = cup.shape[0]
     column = pl.BlockSpec((length, width), lambda g: (0, g))
-    up = (units, 4, 4, width // 16, width)
-    down = (4, 4, units * width // 16, width)
+    up = (units, 2, 2, 2, 2, width // 16, width)
+    down = (2, 2, 2, 2, units * width // 16, width)
     halves = len(planes[0])
     return pl.pallas_call(
         lambda *refs: ffn_fwd_kernel(near_first, halves, *refs),
@@ -344,11 +365,11 @@
             pltpu.VMEM((length, width), F32),
             pltpu.VMEM(up, BF),
             pltpu.VMEM(down, BF),
-            pltpu.SemaphoreType.DMA((2, units, 16)),
+            pltpu.SemaphoreType.DMA((2, units, 4)),
         ],
         cost_estimate=NO_COST,
         name="ffn_fwd",
-    )(place, *planes[0], *planes[1], n1, cup, gain, shift)
+    )(place, *halves_view(planes[0]), *halves_view(planes[1]), n1, cup, gain, shift)
 
 
 def by_section(section, action):
@@ -359,15 +380,15 @@
 def ffn_bwd_kernel(near_first, halves, place_ref, *refs):
     own, other = refs[:halves], refs[halves : 2 * halves]
     dy_ref, n2_ref, t2_ref, g_ref, gp_ref, n1_ref, t1_ref, gain_ref, shift_ref = refs[2 * halves : 2 * halves + 9]
-    keep_ref, send_ref, dr1_ref, sums_ref, cup_ref = refs[2 * halves + 9 : 2 * halves + 14]
-    h1, df, acc, gup, gdown, up_w, down_w, sem, load_sem = refs[2 * halves + 14 :]
+    keep_ref, high_ref, low_ref, dr1_ref, sums_ref, cup_ref = refs[2 * halves + 9 : 2 * halves + 15]
+    h1, df, acc, gup, gdown, up_w, down_w, sem, load_sem = refs[2 * halves + 15 :]
     step = pl.program_id(0)
     loads = Loads(near_first, place_ref, own, other, (up_w, down_w), load_sem)
 
     @pl.when(step == 0)
     def _():
-        loads.start(1, 0, 0, 4)
-        loads.start(0, 0, 0, 16)
+        loads.start(1, 0)
+        loads.start(0, 0)
 
     last = pl.num_programs(0) - 1
     quads = outer = 4
@@ -388,35 +409,54 @@
         sums_ref[2:3] = colsum(dy)
         sums_ref[3:4] = colsum(low.astype(F32))
 
-    loads.wait(1, 0, 4 * step, 4)
-    loads.wait(0, step, 0, 16)
+    loads.wait(1, step)
+    loads.wait(0, step)
 
     @pl.when(step < last)
     def _():
-        loads.start(1, 0, 4 * (step + 1), 4)
-        loads.start(0, step + 1, 0, 16)
+        loads.start(1, step + 1)
+        loads.start(0, step + 1)
 
     d = df[...]
     down = dot(g_ref[...], d, 0, 0).astype(BF)
-    gdown[step] = down.reshape(quads, width // quads, width)
-    du = (dot(d, down_w[step].reshape(width, width), 1, 1) * gp_ref[...].astype(F32)).astype(BF)
+    tall = width // quads
+    for q in range(quads):
+        gdown[send_index(step, q, place_ref[0], 1, near_first)] = down[q * tall : (q + 1) * tall]
+    du = (dot(d, down_w[step >> 1, step & 1].reshape(width, width), 1, 1) * gp_ref[...].astype(F32)).astype(BF)
     cup_ref[0] = colsum(du.astype(F32))
     up = dot(h1[...], du, 0, 0).astype(BF)
-    gup[step] = up.reshape(outer, quads, size, width)
+    for chip in range(quads * outer):
+        at = send_index(chip // quads, chip % quads, place_ref[0], 0, near_first)
+        gup[step, at] = up[chip * size : (chip + 1) * size]
     acc[...] += dot(du, up_w[step].reshape(width, width), 1, 1)
 
-    def up_copy(section, j, chip):
-        to = (keep_ref if section == 0 else send_ref).at[send_index(chip >> 2, chip & 3, place_ref[0], 0, near_first)]
+    def up_copies(section, j):
         rows = pl.ds(pl.multiple_of(j * size, PAD), size)
-        return pltpu.make_async_copy(gup.at[j, chip >> 2, chip & 3], to.at[rows, :], sem.at[j, chip])
-
-    def down_copy(section, j, q):
-        to = (send_ref if section == 0 else keep_ref).at[send_index(j, q, place_ref[0], 1, near_first)]
-        return pltpu.make_async_copy(gdown.at[j, q], to, sem.at[j, 16 + q])
+        if section == 0:
+            return [pltpu.make_async_copy(gup.at[j], keep_ref.at[:, rows, :], sem.at[j, 0])]
+        return [
+            pltpu.make_async_copy(gup.at[j, :8], low_ref.at[:, rows, :], sem.at[j, 0]),
+            pltpu.make_async_copy(gup.at[j, 8:], high_ref.at[:, rows, :], sem.at[j, 1]),
+        ]
+
+    def down_copies(section, j, start):
+        for q in range(quads):
+            at = send_index(j, q, place_ref[0], 1, near_first)
+            if section == 1:
+                copy = pltpu.make_async_copy(gdown.at[at], keep_ref.at[at], sem.at[j, 2 + q])
+                copy.start() if start else copy.wait()
+            elif not start:
+                pltpu.make_async_copy(gdown.at[at], low_ref.at[0], sem.at[j, 2 + q]).wait()
+            else:
+                for part, ref in enumerate((low_ref, high_ref)):
+                    @pl.when(at >> 3 == part)
+                    def _():
+                        pltpu.make_async_copy(gdown.at[at], ref.at[at & 7], sem.at[j, 2 + q]).start()
 
     def begin(section):
-        each(16, lambda chip: up_copy(section, step, chip).start())
-        each(4, lambda q: down_copy(section, step, q).start())
+        for item in up_copies(section, step):
+            item.start()
+        down_copies(section, step, True)
 
     by_section(place_ref[1], begin)
 
@@ -430,8 +470,9 @@
 
         def finish(section):
             def one(j):
-                each(16, lambda chip: up_copy(section, j, chip).wait())
-                each(4, lambda q: down_copy(section, j, q).wait())
+                for item in up_copies(section, j):
+                    item.wait()
+                down_copies(section, j, False)
 
             each(gup.shape[0], one)
 
@@ -443,10 +484,10 @@
     units = g.shape[1] // width
     outer, size = 4, width // 16
     halves = len(planes[0])
-    up = (units, outer, 4, size, width)
-    down = (outer, 4, units * size, width)
+    up = (units, 2, 2, 2, 2, size, width)
+    down = (2, 2, 2, 2, units * size, width)
     column = pl.BlockSpec((length, width), lambda g: (0, g))
-    chunk = shape_of((16, units * size, width), BF)
+    chunk, half_chunk = [shape_of((n, units * size, width), BF) for n in (16, 8)]
     return pl.pallas_call(
         lambda *refs: ffn_bwd_kernel(near_first, halves, *refs),
         grid=(units,),
@@ -464,41 +505,42 @@
             whole_block(8, width),
         ],
         out_specs=[
-            pl.BlockSpec(memory_space=pl.ANY),
-            pl.BlockSpec(memory_space=pl.ANY),
+            ANYWHERE,
+            ANYWHERE,
+            ANYWHERE,
             whole_block(length, width),
             whole_block(8, width),
             pl.BlockSpec((1, 1, width), lambda g: (g, 0, 0)),
         ],
-        out_shape=[chunk, chunk, shape_of((length, width), F32), shape_of((8, width), F32), shape_of((units, 1, width), F32)],
+        out_shape=[chunk, half_chunk, half_chunk, shape_of((length, width), F32), shape_of((8, width), F32), shape_of((units, 1, width), F32)],
         scratch_shapes=[
             pltpu.VMEM((length, width), BF),
             pltpu.VMEM((length, width), BF),
             pltpu.VMEM((length, width), F32),
-            pltpu.VMEM((units, outer, 4, size, width), BF),
-            pltpu.VMEM((units, 4, width // 4, width), BF),
+            pltpu.VMEM((units, 16, size, width), BF),
+            pltpu.VMEM((16, units * size, width), BF),
             pltpu.VMEM(up, BF),
             pltpu.VMEM(down, BF),
-            pltpu.SemaphoreType.DMA((units, 20)),
-            pltpu.SemaphoreType.DMA((2, units, 16)),
+            pltpu.SemaphoreType.DMA((units, 6)),
+            pltpu.SemaphoreType.DMA((2, units, 4)),
         ],
         cost_estimate=NO_COST,
         name="ffn_bwd",
-    )(place, *planes[0], *planes[1], dy, n2, t2, g, gp, n1, t1, gain, shift)
+    )(place, *halves_view(planes[0]), *halves_view(planes[1]), dy, n2, t2, g, gp, n1, t1, gain, shift)
 
 
 def attn_bwd_kernel(near_first, halves, place_ref, *refs):
     own, other = refs[:halves], refs[halves : 2 * halves]
     dr_ref, a_ref, sq_ref, sk_ref, q_ref, k_ref, v_ref, o_ref = refs[2 * halves : 2 * halves + 8]
-    keep_ref, send_ref, da_ref, sums_ref, sumo_ref = refs[2 * halves + 8 : 2 * halves + 13]
-    dat, do_sc, dq, dk, dv, grads, low_w, high_w, sem, load_sem = refs[2 * halves + 13 :]
+    keep_ref, high_ref, low_ref, da_ref, sums_ref, sumo_ref = refs[2 * halves + 8 : 2 * halves + 14]
+    dat, do_sc, dq, dk, dv, grads, low_w, high_w, sem, load_sem = refs[2 * halves + 14 :]
     step = pl.program_id(0)
     loads = Loads(near_first, place_ref, own, other, (low_w, high_w), load_sem)
 
     @pl.when(step == 0)
     def _():
         for plane, unit in ((1, 1), (0, 0), (0, 1), (1, 0)):
-            loads.start(plane, unit, 0, 16)
+            loads.start(plane, unit)
 
     length, width = a_ref.shape
     blocks = length // BLOCK
@@ -519,7 +561,7 @@
 
     @pl.when(step == 0)
     def _():
-        loads.wait(1, 1, 0, 16)
+        loads.wait(1, 1)
 
     now = pl.ds(pl.multiple_of(step * cols, cols), cols)
     do_sc[...] = dot(d, high_w.at[1].reshape(width, width)[now, :], 1, 1).astype(BF)
@@ -561,40 +603,49 @@
     @pl.when(step == 0)
     def _():
         for plane, unit in ((0, 0), (0, 1), (1, 0)):
-            loads.wait(plane, unit, 0, 16)
+            loads.wait(plane, unit)
 
     for low, (w_ref, j) in zip(lows, ((low_w, 0), (low_w, 1), (high_w, 0))):
         made.append(dot(a, low, 0, 0).astype(BF))
-        out = out + dot(low, w_ref[j, :, :, :, now].reshape(width, cols), 1, 1)
+        out = out + dot(low, w_ref[j, :, :, :, :, :, now].reshape(width, cols), 1, 1)
     da_ref[...] = out
     sums_ref[...] = jnp.zeros_like(sums_ref)
     sums_ref[0:1] = colsum(lows[0].astype(F32))
     sums_ref[1:2] = colsum(lows[2].astype(F32))
     steps = HEADS // GROUP
+
+    def place_of(chip, core):
+        return send_index(chip // quads, chip % quads, place_ref[0], core, near_first)
+
+    for unit in range(3):
+        for chip in range(quads * outer):
+            grads[unit, place_of(chip, unit // 2), :, now] = made[unit][chip * size : (chip + 1) * size]
     for j in range(steps):
         @pl.when(step == j)
         def _(j=j):
-            here = slice(j * cols, (j + 1) * cols)
-            for unit in range(3):
-                grads[unit, :, here] = made[unit]
-            grads[3, here, :] = grad_o
+            for chip in range(quads * outer):
+                start, end = max(chip * size, j * cols), min((chip + 1) * size, (j + 1) * cols)
+                if start < end:
+                    rows = slice(start - chip * size, end - chip * size)
+                    grads[3, place_of(chip, 1), rows, :] = grad_o[start - j * cols : end - j * cols]
 
     @pl.when(step == steps - 1)
     def _():
-        def copy(section, unit, chip):
-            core = unit // 2
-            to = (keep_ref if core == section else send_ref).at[
-                send_index(chip >> 2, chip & 3, place_ref[0], core, near_first)
-            ]
-            rows = pl.ds(pl.multiple_of(chip * size, PAD), size)
-            at = (unit % 2) * size
-            return pltpu.make_async_copy(grads.at[unit, rows, :], to.at[at : at + size, :], sem.at[unit, chip])
-
         def move(section):
+            copies = []
             for unit in range(4):
-                each(16, lambda chip: copy(section, unit, chip).start())
-            for unit in range(4):
-                each(16, lambda chip: copy(section, unit, chip).wait())
+                rows = slice((unit % 2) * size, (unit % 2 + 1) * size)
+                if unit // 2 == section:
+                    copies.append(pltpu.make_async_copy(grads.at[unit], keep_ref.at[:, rows, :], sem.at[unit, 0]))
+                else:
+                    copies += [
+                        pltpu.make_async_copy(grads.at[unit, :8], low_ref.at[:, rows, :], sem.at[unit, 0]),
+                        pltpu.make_async_copy(grads.at[unit, 8:], high_ref.at[:, rows, :], sem.at[unit, 1]),
+                    ]
+            for item in copies:
+                item.start()
+            for item in copies:
+                item.wait()
 
         by_section(place_ref[1], move)
 
@@ -603,10 +654,10 @@
     length, width = a.shape
     outer, size = 4, width // 16
     halves = len(planes[0])
-    half = (2, outer, 4, size, width)
+    half = (2, 2, 2, 2, 2, size, width)
     cols = GROUP * HDIM
     group = pl.BlockSpec((length, cols), lambda g: (0, g))
-    chunk = shape_of((16, 2 * size + more, width), BF)
+    chunk, half_chunk = [shape_of((n, 2 * size + more, width), BF) for n in (16, 8)]
     return pl.pallas_call(
         lambda *refs: attn_bwd_kernel(near_first, halves, *refs),
         grid=(HEADS // GROUP,),
@@ -620,20 +671,21 @@
         ]
         + [group] * 4,
         out_specs=[
-            pl.BlockSpec(memory_space=pl.ANY),
-            pl.BlockSpec(memory_space=pl.ANY),
+            ANYWHERE,
+            ANYWHERE,
+            ANYWHERE,
             whole_block(length, width),
             pl.BlockSpec((8, cols), lambda g: (0, g)),
             whole_block(8, width),
         ],
-        out_shape=[chunk, chunk, shape_of((length, width), F32), shape_of((8, width), F32), shape_of((8, width), F32)],
+        out_shape=[chunk, half_chunk, half_chunk, shape_of((length, width), F32), shape_of((8, width), F32), shape_of((8, width), F32)],
         scratch_shapes=[pltpu.VMEM((length, width), BF), pltpu.VMEM((length, cols), BF)]
         + [pltpu.VMEM((length, cols), F32)] * 3
-        + [pltpu.VMEM((4, width, width), BF), pltpu.VMEM(half, BF), pltpu.VMEM(half, BF)]
-        + [pltpu.SemaphoreType.DMA((4, 4 * outer)), pltpu.SemaphoreType.DMA((2, 2, 16))],
+        + [pltpu.VMEM((4, 16, size, width), BF), pltpu.VMEM(half, BF), pltpu.VMEM(half, BF)]
+        + [pltpu.SemaphoreType.DMA((4, 2)), pltpu.SemaphoreType.DMA((2, 2, 8))],
         cost_estimate=NO_COST,
         name="attn_bwd",
-    )(place, *planes[0], *planes[1], dr, a, seg_row, seg_col, q, k, v, o)
+    )(place, *halves_view(planes[0]), *halves_view(planes[1]), dr, a, seg_row, seg_col, q, k, v, o)
 
 
 def flip(value, mask, other=None):
@@ -701,7 +753,7 @@
         self.other_own = swap(self.order.now(self.own))
 
     def swap_got(self):
-        self.other_got = swap(self.order.now(self.got))
+        self.other_got = jax.tree.map(lambda item: swap(self.order.now(item)), self.got)
 
     def halves(self, place, units, size):
         pairs = tuple(
@@ -792,7 +844,7 @@
 
 def pack_kernel(cut, place_ref, *refs):
     sums = (refs[0:4], refs[4:8])
-    head_ref, _, _, keep_ref, send_ref, pieces, sem = refs[8:]
+    head_ref, _, _, _, keep_ref, high_ref, low_ref, pieces, sem = refs[8:]
     width = pieces.shape[3]
     size = width // 16
     height = head_ref.shape[0] // 32
@@ -810,31 +862,39 @@
                 pieces[plane, chip, :8, 384 + 128 * k : 512 + 128 * k] = head_ref[row : row + 8, :].astype(BF)
 
     def move(section):
-        for start in (True, False):
-            for plane in range(2):
-                to = keep_ref if plane == section else send_ref
-
-                def by_chip(chip):
-                    at = send_index(chip >> 2, chip & 3, place_ref[0], plane, False)
-                    copy = pltpu.make_async_copy(pieces.at[plane, chip], to.at[at, cut:, :], sem.at[plane, chip])
-                    copy.start() if start else copy.wait()
-
-                each(16, by_chip)
+        for plane in range(2):
+            def by_chip(chip):
+                at = send_index(chip >> 2, chip & 3, place_ref[0], plane, False)
+                source, this = pieces.at[plane, chip], sem.at[plane, chip]
+                if plane == section:
+                    pltpu.make_async_copy(source, keep_ref.at[at, cut:, :], this).start()
+                    return
+                for part, ref in enumerate((low_ref, high_ref)):
+                    @pl.when(at >> 3 == part)
+                    def _():
+                        pltpu.make_async_copy(source, ref.at[at & 7, cut:, :], this).start()
+
+            each(16, by_chip)
+        for plane in range(2):
+            def wait(chip):
+                pltpu.make_async_copy(pieces.at[plane, chip], keep_ref.at[0, cut:, :], sem.at[plane, chip]).wait()
+
+            each(16, wait)
 
     by_section(place_ref[1], move)
 
 
-def pack_tails(place, cut, layer0, layer1, g_head, keep, send):
+def pack_tails(place, cut, layer0, layer1, g_head, chunk):
     return pl.pallas_call(
         lambda *refs: pack_kernel(cut, *refs),
-        in_specs=[SCALARS] + [pl.BlockSpec(memory_space=pltpu.VMEM)] * 9 + [ANYWHERE] * 2,
-        out_specs=[ANYWHERE] * 2,
-        out_shape=[shape_of(keep.shape, BF)] * 2,
-        input_output_aliases={10: 0, 11: 1},
-        scratch_shapes=[pltpu.VMEM((2, 16, PAD, keep.shape[2]), BF), pltpu.SemaphoreType.DMA((2, 16))],
+        in_specs=[SCALARS] + [pl.BlockSpec(memory_space=pltpu.VMEM)] * 9 + [ANYWHERE] * 3,
+        out_specs=[ANYWHERE] * 3,
+        out_shape=[shape_of(item.shape, BF) for item in chunk],
+        input_output_aliases={10: 0, 11: 1, 12: 2},
+        scratch_shapes=[pltpu.VMEM((2, 16, PAD, chunk[0].shape[2]), BF), pltpu.SemaphoreType.DMA((2, 16))],
         cost_estimate=NO_COST,
         name="pack",
-    )(place, *layer0, *layer1, g_head, keep, send)
+    )(place, *layer0, *layer1, g_head, *chunk)
 
 
 def in_chips(chunk, place, units, count, core, near_first):
@@ -850,14 +910,20 @@
     return relative(natural, place, core, near_first)
 
 
-def in_planes(keep, send, place, units, count, near_first):
+def in_planes(keep, high, low_half, place, units, count, near_first):
     if is_small(count):
-        return keep, send
+        return keep, high, low_half
+    send = jnp.concatenate([low_half, high])
     first = place[1] == 0
     keeps, sends = [
         [in_chips(item, place, units[core], count, core, near_first) for core in range(2)] for item in (keep, send)
     ]
-    return jnp.where(first, *keeps), jnp.where(first, sends[1], sends[0])
+    return (jnp.where(first, *keeps),) + in_halves(jnp.where(first, sends[1], sends[0]))
+
+
+def in_halves(send):
+    half = send.shape[0] // 2
+    return send[half:], send[:half]
 
 
 def relative(block, place, core, near_first=False):
@@ -876,28 +942,40 @@
 
 
 class Reduce:
-    def __init__(self, order, keep, send, near_first=False):
+    def __init__(self, order, chunk, near_first=False):
+        keep, high, low_half = chunk
         self.order = order
         self.left = list(zip(*[steps_of(lax.axis_size("dp"), core, near_first) for core in range(2)]))
-        self.terms = [keep]
-        self.got = swap(order.now(send))
+        self.keep = keep
+        self.got = swap(order.now(high))
+        self.there = swap(order.now(low_half))
+        self.terms = None
 
     def wait(self):
         self.got = self.order.wait(self.got)
 
     def start(self):
-        self.terms.append(self.got)
-        half = self.got.shape[0] // 2
-        self.got = flip(self.order.now(add_low(self.terms, half, half)), *self.left.pop())
+        if self.terms is None:
+            half = self.got.shape[0]
+            sent = add_low([self.keep[half:], self.got], 0, half)
+            self.terms = [self.keep[:half], self.there]
+        else:
+            self.terms.append(self.got)
+            half = self.got.shape[0] // 2
+            sent = add_low(self.terms, half, half)
+        self.got = flip(self.order.now(sent), *self.left.pop())
 
     def start_upper(self):
-        self.terms.append(self.got)
-        self.part = self.got.shape[0] // 4
+        self.half = self.got.shape[0]
+        self.part = self.half // 2
         self.masks = self.left.pop()
-        self.upper = flip(self.order.now(add_low(self.terms, 3 * self.part, self.part)), *self.masks)
+        sent = add_low([self.keep[self.half :], self.got], self.part, self.part)
+        self.upper = flip(self.order.now(sent), *self.masks)
 
     def start_lower(self):
-        self.got = flip(self.order.now(add_low(self.terms, 2 * self.part, self.part)), *self.masks)
+        sent = add_low([self.keep[self.half :], self.got], 0, self.part)
+        self.got = flip(self.order.now(sent), *self.masks)
+        self.terms = [self.keep[: self.half], self.there]
 
     def start_from_upper(self):
         part = self.part
@@ -1002,6 +1080,7 @@
     a1_g.done()
     f1_g.done()
     f1_g.start()
+    a1_part = a1_g.start_part(0)
     a0_g.swap_got()
     a0_g.other_got = order.wait(a0_g.other_got)
     a0_half = a0_g.halves(place, 2, size)
@@ -1034,10 +1113,10 @@
 
     a0 = order.now([own[r] for r in rows])
     kept_a0 = [attn_fwd(False, place, a0[r], seg_col[r], seg_row[r], a0_half, shift0) for r in rows]
-    kept_a0, f0_g.got, f1_g.got = order.wait(kept_a0, f0_g.got, f1_g.got)
+    kept_a0, f0_g.got, f1_g.got, a1_part = order.wait(kept_a0, f0_g.got, f1_g.got, a1_part)
     f0_g.swap_own()
     f0_g.swap_got()
-    a1_g.start()
+    a1_g.got = (a1_part, a1_g.start_part(1))
     f1_g.done()
     f1_g.start()
     f0_g.other_own, f0_g.other_got = order.wait(f0_g.other_own, f0_g.other_got)
@@ -1081,43 +1160,44 @@
             ffn_bwd(near_first, grad_place, d_out[r], *kept_f[r][2:4], *kept_f[r][:2], planes, *kept_a[r][4:6], gain, shift)
             for r in rows
         ]
-        keep, send, sums, cup = total([(o[0], o[1], o[3], o[4]) for o in outs])
-        keep, send = in_planes(keep, send, place, (units, 0), count, near_first)
-        return keep, send, [o[2] for o in outs], sums, cup
+        *chunk, sums, cup = total([(*o[:3], o[4], o[5]) for o in outs])
+        return in_planes(*chunk, place, (units, 0), count, near_first), [o[3] for o in outs], sums, cup
 
     def attn_back(near_first, more, d_out, a, kept, planes):
         outs = [attn_bwd(near_first, more, grad_place, d_out[r], a[r], seg_col[r], seg_row[r], *kept[r][:4], planes) for r in rows]
-        keep, send, sums, sumo = total([(o[0], o[1], o[3], o[4]) for o in outs])
-        keep, send = in_planes(keep, send, place, (2, 2), count, near_first)
-        return keep, send, [o[2] for o in outs], sums, sumo
-
-    keep, send, d_r, sums_f1, g_cup1 = ffn_back(False, d_y1, kept_a1, kept_f1, f1_half, gain1, shift1)
-    f1_r = Reduce(order, keep, send)
+        *chunk, sums, sumo = total([(*o[:3], o[4], o[5]) for o in outs])
+        return in_planes(*chunk, place, (2, 2), count, near_first), [o[3] for o in outs], sums, sumo
+
+    chunk, d_r, sums_f1, g_cup1 = ffn_back(False, d_y1, kept_a1, kept_f1, f1_half, gain1, shift1)
+    f1_r = Reduce(order, chunk)
     f1_r.wait()
     f1_r.start_upper()
     d_r = order.now(d_r)
-    keep, send, d_a1, sums_a1, sumo_a1 = attn_back(True, 0, d_r, a1, kept_a1, a1_half)
-    d_a1, f1_r.upper = order.wait(d_a1, f1_r.upper)
-    a1_r = Reduce(order, keep, send, True)
+    chunk, d_a1, sums_a1, sumo_a1 = attn_back(True, 0, d_r, a1, kept_a1, a1_half)
+    d_a1, f1_r.upper, f1_r.there = order.wait(d_a1, f1_r.upper, f1_r.there)
+    a1_r = Reduce(order, chunk, True)
     f1_r.start_lower()
     f1_r.start_from_upper()
     a1_r.wait()
     a1_r.spare(4)
     a1_r.start_upper()
     d_y0 = order.now([low(item) for item in d_a1])
-    keep, send, d_r, sums_f0, g_cup0 = ffn_back(False, d_y0, kept_a0, kept_f0, f0_half, gain0, shift0)
-    d_r, f1_r.got, f1_r.ahead, a1_r.upper = order.wait(d_r, f1_r.got, f1_r.ahead, a1_r.upper)
-    f0_r = Reduce(order, keep, send)
+    chunk, d_r, sums_f0, g_cup0 = ffn_back(False, d_y0, kept_a0, kept_f0, f0_half, gain0, shift0)
+    d_r, f1_r.got, f1_r.ahead, a1_r.upper, a1_r.there = order.wait(
+        d_r, f1_r.got, f1_r.ahead, a1_r.upper, a1_r.there
+    )
+    f0_r = Reduce(order, chunk)
     f1_r.join()
     f1_r.start()
     a1_r.start_lower()
     f0_r.wait()
     f0_r.start()
     d_r = order.now(d_r)
-    keep, send, d_a0, sums_a0, sumo_a0 = attn_back(
+    chunk, d_a0, sums_a0, sumo_a0 = attn_back(
         False, PAD if is_small(count) else 0, d_r, a0, kept_a0, a0_half
     )
-    d_a0, a1_r.got, f1_r.got, f0_r.got = order.wait(d_a0, a1_r.got, f1_r.got, f0_r.got)
+    d_a0, a1_r.got, f1_r.got, f0_r.got, there = order.wait(d_a0, a1_r.got, f1_r.got, f0_r.got, f0_r.there)
+    f0_r.terms[1] = there
 
     def small_block(sums_a, sumo, sums_f, g_cup, head_part, core):
         gains = jnp.stack([sums_f[0], sums_f[1]]).reshape(2, count, size).transpose(1, 0, 2)
@@ -1141,14 +1221,14 @@
     if is_small(count):
         layer0 = (sums_a0, sumo_a0, sums_f0, g_cup0)
         layer1 = (sums_a1, sumo_a1, sums_f1, g_cup1)
-        keep, send = pack_tails(place, cut, layer0, layer1, g_head, keep, send)
+        chunk = pack_tails(place, cut, layer0, layer1, g_head, chunk)
     else:
         half_head = g_head.reshape(2, -1, head_w.shape[1])
         tail0 = small_block(sums_a0, sumo_a0, sums_f0, g_cup0, half_head[0], 0)
         tail1 = small_block(sums_a1, sumo_a1, sums_f1, g_cup1, half_head[1], 1)
-        keep = jnp.concatenate([keep, jnp.where(first, tail0, tail1)], axis=1)
-        send = jnp.concatenate([send, jnp.where(first, tail1, tail0)], axis=1)
-    a0_r = Reduce(order, keep, send)
+        tails = (jnp.where(first, tail0, tail1),) + in_halves(jnp.where(first, tail1, tail0))
+        chunk = [jnp.concatenate(pair, axis=1) for pair in zip(chunk, tails)]
+    a0_r = Reduce(order, chunk)
     a0_r.wait()
     a0_r.start()
     f0_r.start()

time: 451 us -> 429 us (0.951)
  Pallas kernels: 169 us -> 153 us
  waiting for transfers between devices: 145 us -> 134 us
  starting transfers between devices: 52.2 us -> 59.4 us
    ppermute x16 -> x21, waiting for transfers between devices: 30.5 us -> 22.6 us  [swap(): return lax.ppermute(value, BOTH, pairs)]
    pallas_call x2, Pallas kernels: 46.1 us -> 38.5 us  [ffn_bwd(): pl.pallas_call(lambda *refs: ffn_bwd_kernel(near_first, halves, *refs), g...]
    ppermute x34 -> x35, starting transfers between devices: 45.6 us -> 50.6 us  [flip(): return lax.ppermute(value, BOTH, pairs)]
    ppermute x34 -> x35, waiting for transfers between devices: 115 us -> 111 us  [flip(): return lax.ppermute(value, BOTH, pairs)]
  transfers between devices with their start and end apart: 52 -> 58, of which waited for: 27 -> 27; matrix products, arithmetic and copies ran while one was open for 11% -> 13% of each run, Pallas kernels for 29% -> 28%
where the time goes in v5:
time: 429 us; the launch traced here: 423 us
  Pallas kernels  153 us (36%)
  waiting for transfers between devices  134 us (31%)
  starting transfers between devices  59.4 us (14%)
  other arithmetic  57.1 us (13%)
  local copies, waits for them, and re-layouts  13.2 us (3%)
    ppermute x35, waiting for transfers between devices, flip(): return lax.ppermute(value, BOTH, pairs)  111 us
    ppermute x35, starting transfers between devices, flip(): return lax.ppermute(value, BOTH, pairs)  50.6 us
    pallas_call x2, Pallas kernels, attn_bwd(): pl.pallas_call(lambda *refs: attn_bwd_kernel(near_first, halves, *refs),...  44.1 us
    pallas_call x2, Pallas kernels, ffn_bwd(): pl.pallas_call(lambda *refs: ffn_bwd_kernel(near_first, halves, *refs), g...  38.5 us
    pallas_call x2, Pallas kernels, ffn_fwd(): pl.pallas_call(lambda *refs: ffn_fwd_kernel(near_first, halves, *refs), g...  32.9 us
    pallas_call x2, Pallas kernels, attn_fwd(): pl.pallas_call(lambda *refs: attn_fwd_kernel(near_first, halves, *refs),...  32.3 us
    convert_element_type x23, other arithmetic, low(): return value.astype(BF)  30.9 us
    ppermute x21, waiting for transfers between devices, swap(): return lax.ppermute(value, BOTH, pairs)  22.6 us
  transfers between devices with their start and end apart: 58, of which 27 were waited for; matrix products, arithmetic and copies ran while one was open for 13% of the time, Pallas kernels for 28%

profile of v5, /device:TPU:0, one launch (start us, length us, event | category | flops | bytes accessed | tf_op | source)
XLA Modules:
  0.0 423.3 jit_solution(785676686696230987)
XLA Ops:
  12.5 3.8 collective-permute-done.1
  22.4 8.8 %collective-permute-done.5 = bf16[1,192,768]{2,1,0:T(8,128)(2,1)} collective-permute-done((bf16[1,192,768]{2,1,0:T(8,128)(2,1)S(1)}, bf16[1,192,768]{2,1,0:T(8,128)(2,1)}, u32[]{:S(2)}, u32[]{:S(2)}) %collective-permute-start.5) | collective-permute-done | bytes 294944 | tf_op jit(solution)/shard_map/ppermute | solution.py:695
  31.2 3.5 collective-permute-done.3
  37.3 15.8 %collective-permute-done.8 = bf16[2,192,768]{2,1,0:T(8,128)(2,1)S(1)} collective-permute-done((bf16[2,192,768]{2,1,0:T(8,128)(2,1)S(1)}, bf16[2,192,768]{2,1,0:T(8,128)(2,1)S(1)}, u32[]{:S(2)}, u32[]{:S(2)}) %collective-permute-start.8) | collective-permute-done | bytes 589856 | tf_op jit(solution)/shard_map/ppermute | solution.py:695
  60.3 20.5 %collective-permute-done.13 = bf16[1,192,768]{2,1,0:T(8,128)(2,1)S(1)} collective-permute-done((bf16[1,192,768]{2,1,0:T(8,128)(2,1)S(1)}, bf16[1,192,768]{2,1,0:T(8,128)(2,1)S(1)}, u32[]{:S(2)}, u32[]{:S(2)}) %collective-permute-start.13) | collective-permute-done | bytes 294944 | tf_op jit(solution)/shard_map/ppermute | solution.py:695
  80.8 3.4 collective-permute-done.10
  84.3 3.6 maximum_select_fusion.1
  101.5 16.4 %attn_fwd.2 = (bf16[512,768]{1,0:T(8,128)(2,1)}, bf16[512,768]{1,0:T(8,128)(2,1)}, bf16[512,768]{1,0:T(8,128)(2,1)}, bf16[512,768]{1,0:T(8,128)(2,1)}, f32[512,768]{1,0:T(8,128)}, /*index=5*/f32[512,128]{1,0:T(8,128)}) custom-call(s32[2]{0:T(128)} %pad_add_fusion.refs_0_, bf16[2,2,2,112,768]{4,3,2,1,0:T(8,128)(2,1)} %bitcast.91, ...), custom_call_target="tpu_custom_call" | custom-call | tf_op jit(solution)/shard_map/attn_fwd/pallas_call | solution.py:261
  130.2 16.4 %ffn_fwd.2 = (bf16[512,3072]{1,0:T(8,128)(2,1)}, bf16[512,3072]{1,0:T(8,128)(2,1)}, f32[512,768]{1,0:T(8,128)}, f32[512,128]{1,0:T(8,128)}, bf16[512,768]{1,0:T(8,128)(2,1)}) custom-call(s32[2]{0:T(128)} %pad_add_fusion.refs_0_, bf16[2,2,2,192,768]{4,3,2,1,0:T(8,128)(2,1)} %bitcast.16.refs_1_, bf16[2,2,2,192,768]{4,3,2,1,0:T(8,128)(2,1)} %bitcast.20.refs_2_, ...), custom_call_target="tpu_custom_call" | custom-call | tf_op jit(solution)/shard_map/ffn_fwd/pallas_call | solution.py:349
  151.5 15.9 %attn_fwd.3 = (bf16[512,768]{1,0:T(8,128)(2,1)}, bf16[512,768]{1,0:T(8,128)(2,1)}, bf16[512,768]{1,0:T(8,128)(2,1)}, bf16[512,768]{1,0:T(8,128)(2,1)}, f32[512,768]{1,0:T(8,128)}, /*index=5*/f32[512,128]{1,0:T(8,128)}) custom-call(s32[2]{0:T(128)} %pad_add_fusion.refs_0_, bf16[2,2,2,96,768]{4,3,2,1,0:T(8,128)(2,1)} %bitcast.95, ...), custom_call_target="tpu_custom_call" | custom-call | tf_op jit(solution)/shard_map/attn_fwd/pallas_call | solution.py:261
  167.4 11.3 %collective-permute-done.26 = bf16[8,192,768]{2,1,0:T(8,128)(2,1)} collective-permute-done((bf16[8,192,768]{2,1,0:T(8,128)(2,1)S(1)}, bf16[8,192,768]{2,1,0:T(8,128)(2,1)}, u32[]{:S(2)}, u32[]{:S(2)}) %collective-permute-start.26) | collective-permute-done | bytes 2359328 | tf_op jit(solution)/shard_map/ppermute | solution.py:695
  179.8 3.7 collective-permute-done.27
  185.0 16.6 %ffn_fwd.3 = (bf16[512,3072]{1,0:T(8,128)(2,1)}, bf16[512,3072]{1,0:T(8,128)(2,1)}, f32[512,768]{1,0:T(8,128)}, f32[512,128]{1,0:T(8,128)}, bf16[512,768]{1,0:T(8,128)(2,1)}) custom-call(s32[2]{0:T(128)} %pad_add_fusion.refs_0_, bf16[2,2,2,192,768]{4,3,2,1,0:T(8,128)(2,1)} %bitcast.93, bf16[2,2,2,192,768]{4,3,2,1,0:T(8,128)(2,1)} %bitcast.32.refs_2_, ...), custom_call_target="tpu_custom_call" | custom-call | tf_op jit(solution)/shard_map/ffn_fwd/pallas_call | solution.py:349
  204.8 19.3 %ffn_bwd.2 = (bf16[16,192,768]{2,1,0:T(8,128)(2,1)}, bf16[8,192,768]{2,1,0:T(8,128)(2,1)}, bf16[8,192,768]{2,1,0:T(8,128)(2,1)}, f32[512,768]{1,0:T(8,128)}, f32[8,768]{1,0:T(8,128)}, /*index=5*/f32[4,1,768]{2,1,0:T(1,128)}) custom-call(s32[2]{0:T(128)} %pad_add_fusion.refs_0_, bf16[2,2,2,192,768]{4,3,2,1,0:T(8,128)(2,1)} %bitcast.94, ...), custom_call_target="tpu_custom_call" | custom-call | tf_op jit(solution)/shard_map/ffn_bwd/pallas_call | solution.py:491
  224.6 4.3 %collective-permute-done.28 = bf16[8,192,768]{2,1,0:T(8,128)(2,1)S(1)} collective-permute-done((bf16[8,192,768]{2,1,0:T(8,128)(2,1)}, bf16[8,192,768]{2,1,0:T(8,128)(2,1)S(1)}, u32[]{:S(2)}, u32[]{:S(2)}) %collective-permute-start.28) | collective-permute-done | bytes 2359328 | tf_op jit(solution)/shard_map/ppermute | solution.py:701
  232.6 22.2 %attn_bwd.2 = (bf16[16,96,768]{2,1,0:T(8,128)(2,1)}, bf16[8,96,768]{2,1,0:T(8,128)(2,1)}, bf16[8,96,768]{2,1,0:T(8,128)(2,1)}, f32[512,768]{1,0:T(8,128)}, f32[8,768]{1,0:T(8,128)}, /*index=5*/f32[8,768]{1,0:T(8,128)}) custom-call(s32[2]{0:T(128)} %pad_add_fusion.refs_0_, bf16[2,2,2,96,768]{4,3,2,1,0:T(8,128)(2,1)} %bitcast.96, ...), custom_call_target="tpu_custom_call" | custom-call | tf_op jit(solution)/shard_map/attn_bwd/pallas_call | solution.py:661
  255.0 4.0 add_convert_fusion.3
  266.1 19.2 %ffn_bwd.3 = (bf16[16,192,768]{2,1,0:T(8,128)(2,1)}, bf16[8,192,768]{2,1,0:T(8,128)(2,1)}, bf16[8,192,768]{2,1,0:T(8,128)(2,1)}, f32[512,768]{1,0:T(8,128)}, f32[8,768]{1,0:T(8,128)}, /*index=5*/f32[4,1,768]{2,1,0:T(1,128)}) custom-call(s32[2]{0:T(128)} %pad_add_fusion.refs_0_, bf16[2,2,2,192,768]{4,3,2,1,0:T(8,128)(2,1)} %bitcast.16.refs_1_, ...), custom_call_target="tpu_custom_call" | custom-call | tf_op jit(solution)/shard_map/ffn_bwd/pallas_call | solution.py:491
  287.9 6.0 %collective-permute-done.36 = bf16[8,192,768]{2,1,0:T(8,128)(2,1)S(1)} collective-permute-done((bf16[8,192,768]{2,1,0:T(8,128)(2,1)}, bf16[8,192,768]{2,1,0:T(8,128)(2,1)S(1)}, u32[]{:S(2)}, u32[]{:S(2)}) %collective-permute-start.36) | collective-permute-done | bytes 2359328 | tf_op jit(solution)/shard_map/ppermute | solution.py:701
  293.9 3.6 add_convert_fusion
  307.3 21.9 %attn_bwd.3 = (bf16[16,112,768]{2,1,0:T(8,128)(2,1)}, bf16[8,112,768]{2,1,0:T(8,128)(2,1)}, bf16[8,112,768]{2,1,0:T(8,128)(2,1)}, f32[512,768]{1,0:T(8,128)}, f32[8,768]{1,0:T(8,128)}, /*index=5*/f32[8,768]{1,0:T(8,128)}) custom-call(s32[2]{0:T(128)} %pad_add_fusion.refs_0_, bf16[2,2,2,112,768]{4,3,2,1,0:T(8,128)(2,1)} %bitcast.92, ...), custom_call_target="tpu_custom_call" | custom-call | tf_op jit(solution)/shard_map/attn_bwd/pallas_call | solution.py:661
  347.0 18.3 %collective-permute-done.45 = bf16[1,192,768]{2,1,0:T(8,128)(2,1)S(1)} collective-permute-done((bf16[1,192,768]{2,1,0:T(8,128)(2,1)S(1)}, bf16[1,192,768]{2,1,0:T(8,128)(2,1)S(1)}, u32[]{:S(2)}, u32[]{:S(2)}) %collective-permute-start.45) | collective-permute-done | bytes 294944 | tf_op jit(solution)/shard_map/ppermute | solution.py:695
  369.2 3.5 collective-permute-start.53
  400.2 7.5 %collective-permute-done.49 = bf16[2,112,768]{2,1,0:T(8,128)(2,1)S(1)} collective-permute-done((bf16[2,112,768]{2,1,0:T(8,128)(2,1)S(1)}, bf16[2,112,768]{2,1,0:T(8,128)(2,1)S(1)}, u32[]{:S(2)}, u32[]{:S(2)}) %collective-permute-start.49) | collective-permute-done | bytes 344096 | tf_op jit(solution)/shard_map/ppermute | solution.py:695
  (240 shorter events, 151.8 us)
Async XLA Ops:
  53.4 30.9 %collective-permute-start.12 = (bf16[8,112,768]{2,1,0:T(8,128)(2,1)S(1)}, bf16[8,112,768]{2,1,0:T(8,128)(2,1)}, u32[]{:S(2)}, u32[]{:S(2)}) collective-permute-start(bf16[8,112,768]{2,1,0:T(8,128)(2,1)S(1)} %maximum_select_fusion.3.refs_1_), channel_id=1, source_target_pairs={{0,16},{1,17},{2,18},{3,19},{4,20},{5,21},{6,22},{7,23},{8,24},{9,... | collective-permute-start | bytes 4128776 | tf_op jit(solution)/shard_map/ppermute | solution.py:701
  53.5 30.8 %collective-permute-start.9 = (bf16[8,112,768]{2,1,0:T(8,128)(2,1)S(1)}, bf16[8,112,768]{2,1,0:T(8,128)(2,1)}, u32[]{:S(2)}, u32[]{:S(2)}) collective-permute-start(bf16[8,112,768]{2,1,0:T(8,128)(2,1)S(1)} %maximum_select_fusion.3.refs_1_), channel_id=1, source_target_pairs={{0,2},{1,3},{2,0},{3,1},{4,6},{5,7},{6,4},{7,5},{8,10},{9,11},{10,... | collective-permute-start | bytes 4128776 | tf_op jit(solution)/shard_map/ppermute | solution.py:695
  56.6 27.7 %collective-permute-start.10 = (bf16[4,192,768]{2,1,0:T(8,128)(2,1)}, bf16[4,192,768]{2,1,0:T(8,128)(2,1)}, u32[]{:S(2)}, u32[]{:S(2)}) collective-permute-start(bf16[4,192,768]{2,1,0:T(8,128)(2,1)} %maximum_select_fusion.4), channel_id=1, source_target_pairs={{0,1},{1,0},{2,3},{3,2},{4,5},{5,4},{6,7},{7,6},{8,9},{9,8},{10,11... | collective-permute-start | bytes 3538952 | tf_op jit(solution)/shard_map/ppermute | solution.py:695
  87.9 31.9 %collective-permute-start.15 = (bf16[8,192,768]{2,1,0:T(8,128)(2,1)}, bf16[8,192,768]{2,1,0:T(8,128)(2,1)}, u32[]{:S(2)}, u32[]{:S(2)}) collective-permute-start(bf16[8,192,768]{2,1,0:T(8,128)(2,1)} %maximum_select_fusion.1), channel_id=1, source_target_pairs={{0,2},{1,3},{2,0},{3,1},{4,6},{5,7},{6,4},{7,5},{8,10},{9,11},{10,... | collective-permute-start | bytes 7077896 | tf_op jit(solution)/shard_map/ppermute | solution.py:695
  90.2 27.7 %collective-permute-start.16 = (bf16[2,192,768]{2,1,0:T(8,128)(2,1)S(1)}, bf16[2,192,768]{2,1,0:T(8,128)(2,1)}, u32[]{:S(2)}, u32[]{:S(2)}) collective-permute-start(bf16[2,192,768]{2,1,0:T(8,128)(2,1)S(1)} %maximum_select_fusion.10), channel_id=1, source_target_pairs={{0,8},{1,9},{2,10},{3,11},{4,12},{5,13},{6,14},{7,15},{8,0},{9,1},... | collective-permute-start | bytes 1769480 | tf_op jit(solution)/shard_map/ppermute | solution.py:695
  91.7 28.1 %collective-permute-start.17 = (bf16[4,96,768]{2,1,0:T(8,128)(2,1)}, bf16[4,96,768]{2,1,0:T(8,128)(2,1)}, u32[]{:S(2)}, u32[]{:S(2)}) collective-permute-start(bf16[4,96,768]{2,1,0:T(8,128)(2,1)} %get-tuple-element.260), channel_id=1, source_target_pairs={{0,8},{1,9},{2,10},{3,11},{4,12},{5,13},{6,14},{7,15},{8,0},{9,1},... | collective-permute-start | bytes 1769480 | tf_op jit(solution)/shard_map/ppermute | solution.py:695
  123.1 23.5 %collective-permute-start.22 = (bf16[4,192,768]{2,1,0:T(8,128)(2,1)}, bf16[4,192,768]{2,1,0:T(8,128)(2,1)}, u32[]{:S(2)}, u32[]{:S(2)}) collective-permute-start(bf16[4,192,768]{2,1,0:T(8,128)(2,1)} %maximum_select_fusion.6), channel_id=1, source_target_pairs={{0,1},{1,0},{2,3},{3,2},{4,5},{5,4},{6,7},{7,6},{8,9},{9,8},{10,11... | collective-permute-start | bytes 3538952 | tf_op jit(solution)/shard_map/ppermute | solution.py:695
  149.7 29.0 %collective-permute-start.26 = (bf16[8,192,768]{2,1,0:T(8,128)(2,1)S(1)}, bf16[8,192,768]{2,1,0:T(8,128)(2,1)}, u32[]{:S(2)}, u32[]{:S(2)}) collective-permute-start(bf16[8,192,768]{2,1,0:T(8,128)(2,1)S(1)} %maximum_select_fusion.2), channel_id=1, source_target_pairs={{0,2},{1,3},{2,0},{3,1},{4,6},{5,7},{6,4},{7,5},{8,10},{9,11},{10,... | collective-permute-start | bytes 7077896 | tf_op jit(solution)/shard_map/ppermute | solution.py:695
  150.4 28.4 %collective-permute-start.25 = (bf16[8,192,768]{2,1,0:T(8,128)(2,1)S(1)}, bf16[8,192,768]{2,1,0:T(8,128)(2,1)}, u32[]{:S(2)}, u32[]{:S(2)}) collective-permute-start(bf16[8,192,768]{2,1,0:T(8,128)(2,1)S(1)} %maximum_select_fusion.2), channel_id=1, source_target_pairs={{0,16},{1,17},{2,18},{3,19},{4,20},{5,21},{6,22},{7,23},{8,24},{9,... | collective-permute-start | bytes 7077896 | tf_op jit(solution)/shard_map/ppermute | solution.py:701
  224.5 30.4 %collective-permute-start.30 = (bf16[8,192,768]{2,1,0:T(8,128)(2,1)}, bf16[8,192,768]{2,1,0:T(8,128)(2,1)S(1)}, u32[]{:S(2)}, u32[]{:S(2)}) collective-permute-start(bf16[8,192,768]{2,1,0:T(8,128)(2,1)} %get-tuple-element.327), channel_id=1, source_target_pairs={{0,16},{1,17},{2,18},{3,19},{4,20},{5,21},{6,22},{7,23},{8,24},{9,... | collective-permute-start | bytes 7077896 | tf_op jit(solution)/shard_map/ppermute | solution.py:701
  232.1 22.8 %collective-permute-start.29 = (bf16[4,192,768]{2,1,0:T(8,128)(2,1)}, bf16[4,192,768]{2,1,0:T(8,128)(2,1)}, u32[]{:S(2)}, u32[]{:S(2)}) collective-permute-start(bf16[4,192,768]{2,1,0:T(8,128)(2,1)} %get-tuple-element.325), channel_id=1, source_target_pairs={{0,2},{1,3},{2,0},{3,1},{4,6},{5,7},{6,4},{7,5},{8,10},{9,11},{10,... | collective-permute-start | bytes 3538952 | tf_op jit(solution)/shard_map/ppermute | solution.py:695
  258.9 27.8 %collective-permute-start.32 = (bf16[4,192,768]{2,1,0:T(8,128)(2,1)S(1)}, bf16[4,192,768]{2,1,0:T(8,128)(2,1)}, u32[]{:S(2)}, u32[]{:S(2)}) collective-permute-start(bf16[4,192,768]{2,1,0:T(8,128)(2,1)S(1)} %get-tuple-element.340), channel_id=1, source_target_pairs={{0,2},{1,3},{2,0},{3,1},{4,6},{5,7},{6,4},{7,5},{8,10},{9,11},{10,... | collective-permute-start | bytes 3538952 | tf_op jit(solution)/shard_map/ppermute | solution.py:695
  260.6 26.2 %collective-permute-start.35 = (bf16[8,96,768]{2,1,0:T(8,128)(2,1)}, bf16[8,96,768]{2,1,0:T(8,128)(2,1)}, u32[]{:S(2)}, u32[]{:S(2)}) collective-permute-start(bf16[8,96,768]{2,1,0:T(8,128)(2,1)} %get-tuple-element.348), channel_id=1, source_target_pairs={{0,16},{1,17},{2,18},{3,19},{4,20},{5,21},{6,22},{7,23},{8,24},{9,... | collective-permute-start | bytes 3538952 | tf_op jit(solution)/shard_map/ppermute | solution.py:701
  260.7 26.6 %collective-permute-start.33 = (bf16[4,192,768]{2,1,0:T(8,128)(2,1)}, bf16[4,192,768]{2,1,0:T(8,128)(2,1)}, u32[]{:S(2)}, u32[]{:S(2)}) collective-permute-start(bf16[4,192,768]{2,1,0:T(8,128)(2,1)} %add_convert_fusion.3), channel_id=1, source_target_pairs={{0,1},{1,0},{2,3},{3,2},{4,5},{5,4},{6,7},{7,6},{8,9},{9,8},{10,11... | collective-permute-start | bytes 3538952 | tf_op jit(solution)/shard_map/ppermute | solution.py:695
  262.3 25.1 %collective-permute-start.34 = (bf16[4,96,768]{2,1,0:T(8,128)(2,1)S(1)}, bf16[4,96,768]{2,1,0:T(8,128)(2,1)}, u32[]{:S(2)}, u32[]{:S(2)}) collective-permute-start(bf16[4,96,768]{2,1,0:T(8,128)(2,1)S(1)} %get-tuple-element.346), channel_id=1, source_target_pairs={{0,8},{1,9},{2,10},{3,11},{4,12},{5,13},{6,14},{7,15},{8,0},{9,1},... | collective-permute-start | bytes 1769480 | tf_op jit(solution)/shard_map/ppermute | solution.py:695
  287.7 44.1 %collective-permute-start.40 = (bf16[8,192,768]{2,1,0:T(8,128)(2,1)}, bf16[8,192,768]{2,1,0:T(8,128)(2,1)}, u32[]{:S(2)}, u32[]{:S(2)}) collective-permute-start(bf16[8,192,768]{2,1,0:T(8,128)(2,1)} %get-tuple-element.381), channel_id=1, source_target_pairs={{0,16},{1,17},{2,18},{3,19},{4,20},{5,21},{6,22},{7,23},{8,24},{9,... | collective-permute-start | bytes 7077896 | tf_op jit(solution)/shard_map/ppermute | solution.py:701
  297.5 34.3 %collective-permute-start.39 = (bf16[8,192,768]{2,1,0:T(8,128)(2,1)}, bf16[8,192,768]{2,1,0:T(8,128)(2,1)}, u32[]{:S(2)}, u32[]{:S(2)}) collective-permute-start(bf16[8,192,768]{2,1,0:T(8,128)(2,1)} %add_convert_fusion), channel_id=1, source_target_pairs={{0,2},{1,3},{2,0},{3,1},{4,6},{5,7},{6,4},{7,5},{8,10},{9,11},{10,... | collective-permute-start | bytes 7077896 | tf_op jit(solution)/shard_map/ppermute | solution.py:695
  303.2 28.6 %collective-permute-start.38 = (bf16[2,192,768]{2,1,0:T(8,128)(2,1)}, bf16[2,192,768]{2,1,0:T(8,128)(2,1)S(1)}, u32[]{:S(2)}, u32[]{:S(2)}) collective-permute-start(bf16[2,192,768]{2,1,0:T(8,128)(2,1)} %add_convert_fusion.9), channel_id=1, source_target_pairs={{0,8},{1,9},{2,10},{3,11},{4,12},{5,13},{6,14},{7,15},{8,0},{9,1},... | collective-permute-start | bytes 1769480 | tf_op jit(solution)/shard_map/ppermute | solution.py:695
  306.0 25.8 %collective-permute-start.37 = (bf16[4,96,768]{2,1,0:T(8,128)(2,1)S(1)}, bf16[4,96,768]{2,1,0:T(8,128)(2,1)S(1)}, u32[]{:S(2)}, u32[]{:S(2)}) collective-permute-start(bf16[4,96,768]{2,1,0:T(8,128)(2,1)S(1)} %copy-done.22), channel_id=1, source_target_pairs={{0,8},{1,9},{2,10},{3,11},{4,12},{5,13},{6,14},{7,15},{8,0},{9,1},... | collective-permute-start | bytes 1769480 | tf_op jit(solution)/shard_map/ppermute | solution.py:695
  331.9 40.9 %collective-permute-start.41 = (bf16[8,112,768]{2,1,0:T(8,128)(2,1)}, bf16[8,112,768]{2,1,0:T(8,128)(2,1)S(1)}, u32[]{:S(2)}, u32[]{:S(2)}) collective-permute-start(bf16[8,112,768]{2,1,0:T(8,128)(2,1)} %get-tuple-element.383), channel_id=1, source_target_pairs={{0,16},{1,17},{2,18},{3,19},{4,20},{5,21},{6,22},{7,23},{8,24},{9,... | collective-permute-start | bytes 4128776 | tf_op jit(solution)/shard_map/ppermute | solution.py:701
  336.9 31.0 %collective-permute-start.43 = (bf16[8,112,768]{2,1,0:T(8,128)(2,1)S(1)}, bf16[8,112,768]{2,1,0:T(8,128)(2,1)S(1)}, u32[]{:S(2)}, u32[]{:S(2)}) collective-permute-start(bf16[8,112,768]{2,1,0:T(8,128)(2,1)S(1)} %add_convert_fusion.1), channel_id=1, source_target_pairs={{0,2},{1,3},{2,0},{3,1},{4,6},{5,7},{6,4},{7,5},{8,10},{9,11},{10,... | collective-permute-start | bytes 4128776 | tf_op jit(solution)/shard_map/ppermute | solution.py:695
  339.6 28.4 %collective-permute-start.47 = (bf16[4,192,768]{2,1,0:T(8,128)(2,1)S(1)}, bf16[4,192,768]{2,1,0:T(8,128)(2,1)S(1)}, u32[]{:S(2)}, u32[]{:S(2)}) collective-permute-start(bf16[4,192,768]{2,1,0:T(8,128)(2,1)S(1)} %add_convert_fusion.2), channel_id=1, source_target_pairs={{0,1},{1,0},{2,3},{3,2},{4,5},{5,4},{6,7},{7,6},{8,9},{9,8},{10,11... | collective-permute-start | bytes 3538952 | tf_op jit(solution)/shard_map/ppermute | solution.py:695
  367.9 26.2 %collective-permute-start.52 = (f32[1,512,768]{2,1,0:T(8,128)S(1)}, f32[1,512,768]{2,1,0:T(8,128)S(1)}, u32[]{:S(2)}, u32[]{:S(2)}) collective-permute-start(f32[1,512,768]{2,1,0:T(8,128)S(1)} %bitcast.114), channel_id=1, source_target_pairs={{16,0},{17,1},{18,2},{19,3},{20,4},{21,5},{22,6},{23,7},{24,8},{25... | collective-permute-start | bytes 4718600 | tf_op jit(solution)/shard_map/ppermute | solution.py:706
  369.2 24.9 %collective-permute-start.53 = (f32[1,512,768]{2,1,0:T(8,128)S(1)}, f32[1,512,768]{2,1,0:T(8,128)S(1)}, u32[]{:S(2)}, u32[]{:S(2)}) collective-permute-start(f32[1,512,768]{2,1,0:T(8,128)S(1)} %bitcast.103), channel_id=1, source_target_pairs={{0,16},{1,17},{2,18},{3,19},{4,20},{5,21},{6,22},{7,23},{8,24},{9,... | collective-permute-start | bytes 4718600 | tf_op jit(solution)/shard_map/ppermute | solution.py:706
  (64 other events, 685.3 us)

commit v6 on v5

--- a/solution.py
+++ b/solution.py
@@ -377,8 +377,11 @@
         pl.when(section == plane)(lambda plane=plane: action(plane))
 
 
-def ffn_bwd_kernel(near_first, halves, place_ref, *refs):
+def ffn_bwd_kernel(near_first, halves, head, place_ref, *refs):
     own, other = refs[:halves], refs[halves : 2 * halves]
+    if head:
+        y_ref, cot_ref, head_ref, g_head_ref = refs[2 * halves], refs[2 * halves + 1], refs[2 * halves + 2], refs[2 * halves + 17]
+        refs = refs[: 2 * halves] + (None,) + refs[2 * halves + 3 : 2 * halves + 17] + refs[2 * halves + 18 :]
     dy_ref, n2_ref, t2_ref, g_ref, gp_ref, n1_ref, t1_ref, gain_ref, shift_ref = refs[2 * halves : 2 * halves + 9]
     keep_ref, high_ref, low_ref, dr1_ref, sums_ref, cup_ref = refs[2 * halves + 9 : 2 * halves + 15]
     h1, df, acc, gup, gdown, up_w, down_w, sem, load_sem = refs[2 * halves + 15 :]
@@ -398,7 +401,17 @@
     @pl.when(step == 0)
     def _():
         n2 = n2_ref[...]
-        dy = dy_ref[...].astype(F32)
+        if head:
+            y = y_ref[...]
+            proj = dot(y, head_ref[...])
+            rho = lax.rsqrt(jnp.sum(proj * proj, axis=-1, keepdims=True) + norm_eps)
+            cot = cot_ref[...].astype(F32)
+            along = jnp.sum(proj * cot, axis=-1, keepdims=True)
+            d_proj = (rho * cot - rho * rho * rho * proj * along).astype(BF)
+            g_head_ref[...] = dot(y, d_proj, 0, 0)
+            dy = dot(d_proj, head_ref[...], 1, 1)
+        else:
+            dy = dy_ref[...].astype(F32)
         dr2 = norm_back(dy, n2, t2_ref[:, 0:1], gain_ref[1:2])
         low = dr2.astype(BF)
         df[...] = low
@@ -479,22 +492,23 @@
         by_section(place_ref[1], finish)
 
 
-def ffn_bwd(near_first, place, dy, n2, t2, g, gp, planes, n1, t1, gain, shift):
+def ffn_bwd(near_first, place, given, n2, t2, g, gp, planes, n1, t1, gain, shift):
     length, width = n1.shape
     units = g.shape[1] // width
     outer, size = 4, width // 16
     halves = len(planes[0])
+    head = len(given) == 3
     up = (units, 2, 2, 2, 2, size, width)
     down = (2, 2, 2, 2, units * size, width)
     column = pl.BlockSpec((length, width), lambda g: (0, g))
     chunk, half_chunk = [shape_of((n, units * size, width), BF) for n in (16, 8)]
     return pl.pallas_call(
-        lambda *refs: ffn_bwd_kernel(near_first, halves, *refs),
+        lambda *refs: ffn_bwd_kernel(near_first, halves, head, *refs),
         grid=(units,),
         in_specs=[
             SCALARS,
             *[ANYWHERE] * (2 * halves),
-            whole_block(length, width),
+            *[whole_block(*item.shape) for item in given],
             whole_block(length, width),
             whole_block(length, 128),
             column,
@@ -511,8 +525,10 @@
             whole_block(length, width),
             whole_block(8, width),
             pl.BlockSpec((1, 1, width), lambda g: (g, 0, 0)),
-        ],
-        out_shape=[chunk, half_chunk, half_chunk, shape_of((length, width), F32), shape_of((8, width), F32), shape_of((units, 1, width), F32)],
+        ]
+        + [whole_block(*item.shape) for item in given[2:]],
+        out_shape=[chunk, half_chunk, half_chunk, shape_of((length, width), F32), shape_of((8, width), F32), shape_of((units, 1, width), F32)]
+        + [shape_of(item.shape, F32) for item in given[2:]],
         scratch_shapes=[
             pltpu.VMEM((length, width), BF),
             pltpu.VMEM((length, width), BF),
@@ -526,7 +542,7 @@
         ],
         cost_estimate=NO_COST,
         name="ffn_bwd",
-    )(place, *halves_view(planes[0]), *halves_view(planes[1]), dy, n2, t2, g, gp, n1, t1, gain, shift)
+    )(place, *halves_view(planes[0]), *halves_view(planes[1]), *given, n2, t2, g, gp, n1, t1, gain, shift)
 
 
 def attn_bwd_kernel(near_first, halves, place_ref, *refs):
@@ -629,25 +645,42 @@
                     rows = slice(start - chip * size, end - chip * size)
                     grads[3, place_of(chip, 1), rows, :] = grad_o[start - j * cols : end - j * cols]
 
+    def copies(section, j, units):
+        out = []
+        for unit in units:
+            rows = slice((unit % 2) * size, (unit % 2 + 1) * size)
+            lanes = pl.ds(pl.multiple_of(j * cols, cols), cols) if unit < 3 else slice(None)
+            if unit // 2 == section:
+                pairs = [(grads.at[unit, :, :, lanes], keep_ref.at[:, rows, lanes])]
+            else:
+                pairs = [
+                    (grads.at[unit, :8, :, lanes], low_ref.at[:, rows, lanes]),
+                    (grads.at[unit, 8:, :, lanes], high_ref.at[:, rows, lanes]),
+                ]
+            out += [pltpu.make_async_copy(*pair, sem.at[unit, part, j]) for part, pair in enumerate(pairs)]
+        return out
+
+    def begin(section):
+        for item in copies(section, step, range(3)):
+            item.start()
+
+    by_section(place_ref[1], begin)
+
     @pl.when(step == steps - 1)
     def _():
-        def move(section):
-            copies = []
-            for unit in range(4):
-                rows = slice((unit % 2) * size, (unit % 2 + 1) * size)
-                if unit // 2 == section:
-                    copies.append(pltpu.make_async_copy(grads.at[unit], keep_ref.at[:, rows, :], sem.at[unit, 0]))
-                else:
-                    copies += [
-                        pltpu.make_async_copy(grads.at[unit, :8], low_ref.at[:, rows, :], sem.at[unit, 0]),
-                        pltpu.make_async_copy(grads.at[unit, 8:], high_ref.at[:, rows, :], sem.at[unit, 1]),
-                    ]
-            for item in copies:
+        def finish(section):
+            for item in copies(section, 0, (3,)):
                 item.start()
-            for item in copies:
+
+            def one(j):
+                for item in copies(section, j, range(3)):
+                    item.wait()
+
+            each(steps, one)
+            for item in copies(section, 0, (3,)):
                 item.wait()
 
-        by_section(place_ref[1], move)
+        by_section(place_ref[1], finish)
 
 
 def attn_bwd(near_first, more, place, dr, a, seg_col, seg_row, q, k, v, o, planes):
@@ -682,7 +715,7 @@
         scratch_shapes=[pltpu.VMEM((length, width), BF), pltpu.VMEM((length, cols), BF)]
         + [pltpu.VMEM((length, cols), F32)] * 3
         + [pltpu.VMEM((4, 16, size, width), BF), pltpu.VMEM(half, BF), pltpu.VMEM(half, BF)]
-        + [pltpu.SemaphoreType.DMA((4, 2)), pltpu.SemaphoreType.DMA((2, 2, 8))],
+        + [pltpu.SemaphoreType.DMA((4, 2, HEADS // GROUP)), pltpu.SemaphoreType.DMA((2, 2, 8))],
         cost_estimate=NO_COST,
         name="attn_bwd",
     )(place, *halves_view(planes[0]), *halves_view(planes[1]), dr, a, seg_row, seg_col, q, k, v, o)
@@ -1139,36 +1172,28 @@
     f1_half = f1_g.halves(place, units, size)
     kept_f1 = [ffn_fwd(False, place, n1[r], f1_half, cup1, gain1, shift1) for r in rows]
 
-    d_y1, g_head = [], 0.0
-    for r in rows:
-        y1 = kept_f1[r][4]
-        proj = dot(y1, head)
-        rho = lax.rsqrt(jnp.sum(proj * proj, axis=-1, keepdims=True) + norm_eps)
-        c = cot[r].astype(F32)
-        d_proj = low(rho * c - rho * rho * rho * proj * jnp.sum(proj * c, axis=-1, keepdims=True))
-        g_head = g_head + dot(y1, d_proj, 0, 0)
-        d_y1.append(dot(d_proj, head, 1, 1))
-
     def total(items):
         out = items[0]
         for item in items[1:]:
             out = jax.tree.map(lambda x, y: (x.astype(F32) + y.astype(F32)).astype(x.dtype), out, item)
         return out
 
-    def ffn_back(near_first, d_out, kept_a, kept_f, planes, gain, shift):
+    def ffn_back(near_first, given, kept_a, kept_f, planes, gain, shift):
         outs = [
-            ffn_bwd(near_first, grad_place, d_out[r], *kept_f[r][2:4], *kept_f[r][:2], planes, *kept_a[r][4:6], gain, shift)
+            ffn_bwd(near_first, grad_place, given[r], *kept_f[r][2:4], *kept_f[r][:2], planes, *kept_a[r][4:6], gain, shift)
             for r in rows
         ]
         *chunk, sums, cup = total([(*o[:3], o[4], o[5]) for o in outs])
-        return in_planes(*chunk, place, (units, 0), count, near_first), [o[3] for o in outs], sums, cup
+        rest = (total([o[6:] for o in outs]),) if outs[0][6:] else ()
+        return in_planes(*chunk, place, (units, 0), count, near_first), [o[3] for o in outs], sums, cup, *rest
 
     def attn_back(near_first, more, d_out, a, kept, planes):
         outs = [attn_bwd(near_first, more, grad_place, d_out[r], a[r], seg_col[r], seg_row[r], *kept[r][:4], planes) for r in rows]
         *chunk, sums, sumo = total([(*o[:3], o[4], o[5]) for o in outs])
         return in_planes(*chunk, place, (2, 2), count, near_first), [o[3] for o in outs], sums, sumo
 
-    chunk, d_r, sums_f1, g_cup1 = ffn_back(False, d_y1, kept_a1, kept_f1, f1_half, gain1, shift1)
+    given = [(kept_f1[r][4], cot[r], head) for r in rows]
+    chunk, d_r, sums_f1, g_cup1, (g_head,) = ffn_back(False, given, kept_a1, kept_f1, f1_half, gain1, shift1)
     f1_r = Reduce(order, chunk)
     f1_r.wait()
     f1_r.start_upper()
@@ -1182,7 +1207,7 @@
     a1_r.spare(4)
     a1_r.start_upper()
     d_y0 = order.now([low(item) for item in d_a1])
-    chunk, d_r, sums_f0, g_cup0 = ffn_back(False, d_y0, kept_a0, kept_f0, f0_half, gain0, shift0)
+    chunk, d_r, sums_f0, g_cup0 = ffn_back(False, [(item,) for item in d_y0], kept_a0, kept_f0, f0_half, gain0, shift0)
     d_r, f1_r.got, f1_r.ahead, a1_r.upper, a1_r.there = order.wait(
         d_r, f1_r.got, f1_r.ahead, a1_r.upper, a1_r.there
     )

time: 429 us -> 427 us (level)
  starting transfers between devices: 59.4 us -> 54.4 us
  waiting for transfers between devices: 134 us -> 139 us
    ppermute x35, waiting for transfers between devices: 111 us -> 119 us  [flip(): return lax.ppermute(value, BOTH, pairs)]
    ppermute x35, starting transfers between devices: 50.6 us -> 45.7 us  [flip(): return lax.ppermute(value, BOTH, pairs)]
  transfers between devices with their start and end apart: 58 -> 58, of which waited for: 27 -> 28; matrix products, arithmetic and copies ran while one was open for 13% -> 14% of each run, Pallas kernels for 28% -> 28%
where the time goes in v6:
time: 427 us; the launch traced here: 420 us
  Pallas kernels  153 us (36%)
  waiting for transfers between devices  139 us (33%)
  other arithmetic  58.7 us (14%)
  starting transfers between devices  54.4 us (13%)
  local copies, waits for them, and re-layouts  13.7 us (3%)
    ppermute x35, waiting for transfers between devices, flip(): return lax.ppermute(value, BOTH, pairs)  119 us
    ppermute x35, starting transfers between devices, flip(): return lax.ppermute(value, BOTH, pairs)  45.7 us
    pallas_call x2, Pallas kernels, attn_bwd(): pl.pallas_call(lambda *refs: attn_bwd_kernel(near_first, halves, *refs),...  43.2 us
    pallas_call x2, Pallas kernels, ffn_bwd(): pl.pallas_call(lambda *refs: ffn_bwd_kernel(near_first, halves, head, *re...  39 us
    pallas_call x2, Pallas kernels, ffn_fwd(): pl.pallas_call(lambda *refs: ffn_fwd_kernel(near_first, halves, *refs), g...  32.8 us
    convert_element_type x23, other arithmetic, low(): return value.astype(BF)  32.6 us
    pallas_call x2, Pallas kernels, attn_fwd(): pl.pallas_call(lambda *refs: attn_fwd_kernel(near_first, halves, *refs),...  32.2 us
    ppermute x21, waiting for transfers between devices, swap(): return lax.ppermute(value, BOTH, pairs)  19.7 us
  transfers between devices with their start and end apart: 58, of which 28 were waited for; matrix products, arithmetic and copies ran while one was open for 14% of the time, Pallas kernels for 28%

profile of v6, /device:TPU:0, one launch (start us, length us, event | category | flops | bytes accessed | tf_op | source)
XLA Modules:
  0.0 420.3 jit_solution(18201562726517443490)
XLA Ops:
  12.5 3.8 collective-permute-done.1
  22.4 8.8 %collective-permute-done.5 = bf16[1,192,768]{2,1,0:T(8,128)(2,1)} collective-permute-done((bf16[1,192,768]{2,1,0:T(8,128)(2,1)S(1)}, bf16[1,192,768]{2,1,0:T(8,128)(2,1)}, u32[]{:S(2)}, u32[]{:S(2)}) %collective-permute-start.5) | collective-permute-done | bytes 294944 | tf_op jit(solution)/shard_map/ppermute | solution.py:728
  37.3 15.8 %collective-permute-done.8 = bf16[2,192,768]{2,1,0:T(8,128)(2,1)S(1)} collective-permute-done((bf16[2,192,768]{2,1,0:T(8,128)(2,1)S(1)}, bf16[2,192,768]{2,1,0:T(8,128)(2,1)S(1)}, u32[]{:S(2)}, u32[]{:S(2)}) %collective-permute-start.8) | collective-permute-done | bytes 589856 | tf_op jit(solution)/shard_map/ppermute | solution.py:728
  60.3 20.5 %collective-permute-done.13 = bf16[1,192,768]{2,1,0:T(8,128)(2,1)S(1)} collective-permute-done((bf16[1,192,768]{2,1,0:T(8,128)(2,1)S(1)}, bf16[1,192,768]{2,1,0:T(8,128)(2,1)S(1)}, u32[]{:S(2)}, u32[]{:S(2)}) %collective-permute-start.13) | collective-permute-done | bytes 294944 | tf_op jit(solution)/shard_map/ppermute | solution.py:728
  84.3 3.6 maximum_select_fusion.1
  101.5 16.3 %attn_fwd.2 = (bf16[512,768]{1,0:T(8,128)(2,1)}, bf16[512,768]{1,0:T(8,128)(2,1)}, bf16[512,768]{1,0:T(8,128)(2,1)}, bf16[512,768]{1,0:T(8,128)(2,1)}, f32[512,768]{1,0:T(8,128)}, /*index=5*/f32[512,128]{1,0:T(8,128)}) custom-call(s32[2]{0:T(128)} %pad_add_fusion.refs_0_, bf16[2,2,2,112,768]{4,3,2,1,0:T(8,128)(2,1)} %bitcast.85, ...), custom_call_target="tpu_custom_call" | custom-call | tf_op jit(solution)/shard_map/attn_fwd/pallas_call | solution.py:261
  130.2 16.4 %ffn_fwd.2 = (bf16[512,3072]{1,0:T(8,128)(2,1)}, bf16[512,3072]{1,0:T(8,128)(2,1)}, f32[512,768]{1,0:T(8,128)}, f32[512,128]{1,0:T(8,128)}, bf16[512,768]{1,0:T(8,128)(2,1)}) custom-call(s32[2]{0:T(128)} %pad_add_fusion.refs_0_, bf16[2,2,2,192,768]{4,3,2,1,0:T(8,128)(2,1)} %bitcast.16.refs_1_, bf16[2,2,2,192,768]{4,3,2,1,0:T(8,128)(2,1)} %bitcast.20.refs_2_, ...), custom_call_target="tpu_custom_call" | custom-call | tf_op jit(solution)/shard_map/ffn_fwd/pallas_call | solution.py:349
  151.6 15.9 %attn_fwd.3 = (bf16[512,768]{1,0:T(8,128)(2,1)}, bf16[512,768]{1,0:T(8,128)(2,1)}, bf16[512,768]{1,0:T(8,128)(2,1)}, bf16[512,768]{1,0:T(8,128)(2,1)}, f32[512,768]{1,0:T(8,128)}, /*index=5*/f32[512,128]{1,0:T(8,128)}) custom-call(s32[2]{0:T(128)} %pad_add_fusion.refs_0_, bf16[2,2,2,96,768]{4,3,2,1,0:T(8,128)(2,1)} %bitcast.89, ...), custom_call_target="tpu_custom_call" | custom-call | tf_op jit(solution)/shard_map/attn_fwd/pallas_call | solution.py:261
  167.5 11.3 %collective-permute-done.26 = bf16[8,192,768]{2,1,0:T(8,128)(2,1)} collective-permute-done((bf16[8,192,768]{2,1,0:T(8,128)(2,1)S(1)}, bf16[8,192,768]{2,1,0:T(8,128)(2,1)}, u32[]{:S(2)}, u32[]{:S(2)}) %collective-permute-start.26) | collective-permute-done | bytes 2359328 | tf_op jit(solution)/shard_map/ppermute | solution.py:728
  185.0 16.4 %ffn_fwd.3 = (bf16[512,3072]{1,0:T(8,128)(2,1)}, bf16[512,3072]{1,0:T(8,128)(2,1)}, f32[512,768]{1,0:T(8,128)}, f32[512,128]{1,0:T(8,128)}, bf16[512,768]{1,0:T(8,128)(2,1)}) custom-call(s32[2]{0:T(128)} %pad_add_fusion.refs_0_, bf16[2,2,2,192,768]{4,3,2,1,0:T(8,128)(2,1)} %bitcast.87, bf16[2,2,2,192,768]{4,3,2,1,0:T(8,128)(2,1)} %bitcast.32.refs_2_, ...), custom_call_target="tpu_custom_call" | custom-call | tf_op jit(solution)/shard_map/ffn_fwd/pallas_call | solution.py:349
  201.4 19.8 %ffn_bwd.2 = (bf16[16,192,768]{2,1,0:T(8,128)(2,1)}, bf16[8,192,768]{2,1,0:T(8,128)(2,1)}, bf16[8,192,768]{2,1,0:T(8,128)(2,1)}, f32[512,768]{1,0:T(8,128)}, f32...) custom-call(s32[2]{0:T(128)} %pad_add_fusion.refs_0_, bf16[2,2,2,192,768]{4,3,2,1,0:T(8,128)(2,1)} %bitcast.88, ...), custom_call_target="tpu_custom_call" | custom-call | tf_op jit(solution)/shard_map/ffn_bwd/pallas_call | solution.py:505
  221.8 4.3 %collective-permute-done.28 = bf16[8,192,768]{2,1,0:T(8,128)(2,1)S(1)} collective-permute-done((bf16[8,192,768]{2,1,0:T(8,128)(2,1)}, bf16[8,192,768]{2,1,0:T(8,128)(2,1)S(1)}, u32[]{:S(2)}, u32[]{:S(2)}) %collective-permute-start.28) | collective-permute-done | bytes 2359328 | tf_op jit(solution)/shard_map/ppermute | solution.py:734
  229.9 21.7 %attn_bwd.2 = (bf16[16,96,768]{2,1,0:T(8,128)(2,1)}, bf16[8,96,768]{2,1,0:T(8,128)(2,1)}, bf16[8,96,768]{2,1,0:T(8,128)(2,1)}, f32[512,768]{1,0:T(8,128)}, f32[8,768]{1,0:T(8,128)}, /*index=5*/f32[8,768]{1,0:T(8,128)}) custom-call(s32[2]{0:T(128)} %pad_add_fusion.refs_0_, bf16[2,2,2,96,768]{4,3,2,1,0:T(8,128)(2,1)} %bitcast.90, ...), custom_call_target="tpu_custom_call" | custom-call | tf_op jit(solution)/shard_map/attn_bwd/pallas_call | solution.py:694
  251.7 4.0 add_convert_fusion.3
  262.8 19.2 %ffn_bwd.3 = (bf16[16,192,768]{2,1,0:T(8,128)(2,1)}, bf16[8,192,768]{2,1,0:T(8,128)(2,1)}, bf16[8,192,768]{2,1,0:T(8,128)(2,1)}, f32[512,768]{1,0:T(8,128)}, f32[8,768]{1,0:T(8,128)}, /*index=5*/f32[4,1,768]{2,1,0:T(1,128)}) custom-call(s32[2]{0:T(128)} %pad_add_fusion.refs_0_, bf16[2,2,2,192,768]{4,3,2,1,0:T(8,128)(2,1)} %bitcast.16.refs_1_, ...), custom_call_target="tpu_custom_call" | custom-call | tf_op jit(solution)/shard_map/ffn_bwd/pallas_call | solution.py:505
  284.7 5.1 %collective-permute-done.36 = bf16[8,192,768]{2,1,0:T(8,128)(2,1)S(1)} collective-permute-done((bf16[8,192,768]{2,1,0:T(8,128)(2,1)}, bf16[8,192,768]{2,1,0:T(8,128)(2,1)S(1)}, u32[]{:S(2)}, u32[]{:S(2)}) %collective-permute-start.36) | collective-permute-done | bytes 2359328 | tf_op jit(solution)/shard_map/ppermute | solution.py:734
  289.8 3.6 add_convert_fusion
  293.4 4.0 collective-permute-start.39
  303.1 21.4 %attn_bwd.3 = (bf16[16,112,768]{2,1,0:T(8,128)(2,1)}, bf16[8,112,768]{2,1,0:T(8,128)(2,1)}, bf16[8,112,768]{2,1,0:T(8,128)(2,1)}, f32[512,768]{1,0:T(8,128)}, f32[8,768]{1,0:T(8,128)}, /*index=5*/f32[8,768]{1,0:T(8,128)}) custom-call(s32[2]{0:T(128)} %pad_add_fusion.refs_0_, bf16[2,2,2,112,768]{4,3,2,1,0:T(8,128)(2,1)} %bitcast.86, ...), custom_call_target="tpu_custom_call" | custom-call | tf_op jit(solution)/shard_map/attn_bwd/pallas_call | solution.py:694
  343.7 18.8 %collective-permute-done.45 = bf16[1,192,768]{2,1,0:T(8,128)(2,1)S(1)} collective-permute-done((bf16[1,192,768]{2,1,0:T(8,128)(2,1)S(1)}, bf16[1,192,768]{2,1,0:T(8,128)(2,1)S(1)}, u32[]{:S(2)}, u32[]{:S(2)}) %collective-permute-start.45) | collective-permute-done | bytes 294944 | tf_op jit(solution)/shard_map/ppermute | solution.py:728
  362.5 3.6 collective-permute-done.43
  378.8 3.6 collective-permute-done.48
  387.5 3.7 collective-permute-done.51
  396.8 8.0 %collective-permute-done.49 = bf16[2,112,768]{2,1,0:T(8,128)(2,1)S(1)} collective-permute-done((bf16[2,112,768]{2,1,0:T(8,128)(2,1)S(1)}, bf16[2,112,768]{2,1,0:T(8,128)(2,1)S(1)}, u32[]{:S(2)}, u32[]{:S(2)}) %collective-permute-start.49) | collective-permute-done | bytes 344096 | tf_op jit(solution)/shard_map/ppermute | solution.py:728
  (227 shorter events, 148.7 us)
Async XLA Ops:
  53.4 30.9 %collective-permute-start.12 = (bf16[8,112,768]{2,1,0:T(8,128)(2,1)S(1)}, bf16[8,112,768]{2,1,0:T(8,128)(2,1)}, u32[]{:S(2)}, u32[]{:S(2)}) collective-permute-start(bf16[8,112,768]{2,1,0:T(8,128)(2,1)S(1)} %maximum_select_fusion.3.refs_1_), channel_id=1, source_target_pairs={{0,16},{1,17},{2,18},{3,19},{4,20},{5,21},{6,22},{7,23},{8,24},{9,... | collective-permute-start | bytes 4128776 | tf_op jit(solution)/shard_map/ppermute | solution.py:734
  53.5 30.8 %collective-permute-start.9 = (bf16[8,112,768]{2,1,0:T(8,128)(2,1)S(1)}, bf16[8,112,768]{2,1,0:T(8,128)(2,1)}, u32[]{:S(2)}, u32[]{:S(2)}) collective-permute-start(bf16[8,112,768]{2,1,0:T(8,128)(2,1)S(1)} %maximum_select_fusion.3.refs_1_), channel_id=1, source_target_pairs={{0,2},{1,3},{2,0},{3,1},{4,6},{5,7},{6,4},{7,5},{8,10},{9,11},{10,... | collective-permute-start | bytes 4128776 | tf_op jit(solution)/shard_map/ppermute | solution.py:728
  56.6 27.7 %collective-permute-start.10 = (bf16[4,192,768]{2,1,0:T(8,128)(2,1)}, bf16[4,192,768]{2,1,0:T(8,128)(2,1)}, u32[]{:S(2)}, u32[]{:S(2)}) collective-permute-start(bf16[4,192,768]{2,1,0:T(8,128)(2,1)} %maximum_select_fusion.4), channel_id=1, source_target_pairs={{0,1},{1,0},{2,3},{3,2},{4,5},{5,4},{6,7},{7,6},{8,9},{9,8},{10,11... | collective-permute-start | bytes 3538952 | tf_op jit(solution)/shard_map/ppermute | solution.py:728
  58.2 22.6 %collective-permute-start.11 = (bf16[4,96,768]{2,1,0:T(8,128)(2,1)S(1)}, bf16[4,96,768]{2,1,0:T(8,128)(2,1)S(1)}, u32[]{:S(2)}, u32[]{:S(2)}) collective-permute-start(bf16[4,96,768]{2,1,0:T(8,128)(2,1)S(1)} %maximum_select_fusion.9), channel_id=1, source_target_pairs={{0,4},{1,5},{2,6},{3,7},{4,0},{5,1},{6,2},{7,3},{8,12},{9,13},{10,... | collective-permute-start | bytes 1769480 | tf_op jit(solution)/shard_map/ppermute | solution.py:728
  87.9 31.9 %collective-permute-start.15 = (bf16[8,192,768]{2,1,0:T(8,128)(2,1)}, bf16[8,192,768]{2,1,0:T(8,128)(2,1)}, u32[]{:S(2)}, u32[]{:S(2)}) collective-permute-start(bf16[8,192,768]{2,1,0:T(8,128)(2,1)} %maximum_select_fusion.1), channel_id=1, source_target_pairs={{0,2},{1,3},{2,0},{3,1},{4,6},{5,7},{6,4},{7,5},{8,10},{9,11},{10,... | collective-permute-start | bytes 7077896 | tf_op jit(solution)/shard_map/ppermute | solution.py:728
  90.2 27.7 %collective-permute-start.16 = (bf16[2,192,768]{2,1,0:T(8,128)(2,1)S(1)}, bf16[2,192,768]{2,1,0:T(8,128)(2,1)}, u32[]{:S(2)}, u32[]{:S(2)}) collective-permute-start(bf16[2,192,768]{2,1,0:T(8,128)(2,1)S(1)} %maximum_select_fusion.10), channel_id=1, source_target_pairs={{0,8},{1,9},{2,10},{3,11},{4,12},{5,13},{6,14},{7,15},{8,0},{9,1},... | collective-permute-start | bytes 1769480 | tf_op jit(solution)/shard_map/ppermute | solution.py:728
  91.7 28.1 %collective-permute-start.17 = (bf16[4,96,768]{2,1,0:T(8,128)(2,1)}, bf16[4,96,768]{2,1,0:T(8,128)(2,1)}, u32[]{:S(2)}, u32[]{:S(2)}) collective-permute-start(bf16[4,96,768]{2,1,0:T(8,128)(2,1)} %get-tuple-element.261), channel_id=1, source_target_pairs={{0,8},{1,9},{2,10},{3,11},{4,12},{5,13},{6,14},{7,15},{8,0},{9,1},... | collective-permute-start | bytes 1769480 | tf_op jit(solution)/shard_map/ppermute | solution.py:728
  123.2 23.5 %collective-permute-start.22 = (bf16[4,192,768]{2,1,0:T(8,128)(2,1)}, bf16[4,192,768]{2,1,0:T(8,128)(2,1)}, u32[]{:S(2)}, u32[]{:S(2)}) collective-permute-start(bf16[4,192,768]{2,1,0:T(8,128)(2,1)} %maximum_select_fusion.6), channel_id=1, source_target_pairs={{0,1},{1,0},{2,3},{3,2},{4,5},{5,4},{6,7},{7,6},{8,9},{9,8},{10,11... | collective-permute-start | bytes 3538952 | tf_op jit(solution)/shard_map/ppermute | solution.py:728
  149.8 29.0 %collective-permute-start.26 = (bf16[8,192,768]{2,1,0:T(8,128)(2,1)S(1)}, bf16[8,192,768]{2,1,0:T(8,128)(2,1)}, u32[]{:S(2)}, u32[]{:S(2)}) collective-permute-start(bf16[8,192,768]{2,1,0:T(8,128)(2,1)S(1)} %maximum_select_fusion.2), channel_id=1, source_target_pairs={{0,2},{1,3},{2,0},{3,1},{4,6},{5,7},{6,4},{7,5},{8,10},{9,11},{10,... | collective-permute-start | bytes 7077896 | tf_op jit(solution)/shard_map/ppermute | solution.py:728
  150.4 28.4 %collective-permute-start.25 = (bf16[8,192,768]{2,1,0:T(8,128)(2,1)S(1)}, bf16[8,192,768]{2,1,0:T(8,128)(2,1)}, u32[]{:S(2)}, u32[]{:S(2)}) collective-permute-start(bf16[8,192,768]{2,1,0:T(8,128)(2,1)S(1)} %maximum_select_fusion.2), channel_id=1, source_target_pairs={{0,16},{1,17},{2,18},{3,19},{4,20},{5,21},{6,22},{7,23},{8,24},{9,... | collective-permute-start | bytes 7077896 | tf_op jit(solution)/shard_map/ppermute | solution.py:734
  221.7 29.9 %collective-permute-start.30 = (bf16[8,192,768]{2,1,0:T(8,128)(2,1)}, bf16[8,192,768]{2,1,0:T(8,128)(2,1)S(1)}, u32[]{:S(2)}, u32[]{:S(2)}) collective-permute-start(bf16[8,192,768]{2,1,0:T(8,128)(2,1)} %get-tuple-element.328), channel_id=1, source_target_pairs={{0,16},{1,17},{2,18},{3,19},{4,20},{5,21},{6,22},{7,23},{8,24},{9,... | collective-permute-start | bytes 7077896 | tf_op jit(solution)/shard_map/ppermute | solution.py:734
  255.7 28.1 %collective-permute-start.32 = (bf16[4,192,768]{2,1,0:T(8,128)(2,1)S(1)}, bf16[4,192,768]{2,1,0:T(8,128)(2,1)}, u32[]{:S(2)}, u32[]{:S(2)}) collective-permute-start(bf16[4,192,768]{2,1,0:T(8,128)(2,1)S(1)} %get-tuple-element.341), channel_id=1, source_target_pairs={{0,2},{1,3},{2,0},{3,1},{4,6},{5,7},{6,4},{7,5},{8,10},{9,11},{10,... | collective-permute-start | bytes 3538952 | tf_op jit(solution)/shard_map/ppermute | solution.py:728
  257.5 26.3 %collective-permute-start.35 = (bf16[8,96,768]{2,1,0:T(8,128)(2,1)}, bf16[8,96,768]{2,1,0:T(8,128)(2,1)}, u32[]{:S(2)}, u32[]{:S(2)}) collective-permute-start(bf16[8,96,768]{2,1,0:T(8,128)(2,1)} %get-tuple-element.349), channel_id=1, source_target_pairs={{0,16},{1,17},{2,18},{3,19},{4,20},{5,21},{6,22},{7,23},{8,24},{9,... | collective-permute-start | bytes 3538952 | tf_op jit(solution)/shard_map/ppermute | solution.py:734
  257.6 26.6 %collective-permute-start.33 = (bf16[4,192,768]{2,1,0:T(8,128)(2,1)}, bf16[4,192,768]{2,1,0:T(8,128)(2,1)}, u32[]{:S(2)}, u32[]{:S(2)}) collective-permute-start(bf16[4,192,768]{2,1,0:T(8,128)(2,1)} %add_convert_fusion.3), channel_id=1, source_target_pairs={{0,1},{1,0},{2,3},{3,2},{4,5},{5,4},{6,7},{7,6},{8,9},{9,8},{10,11... | collective-permute-start | bytes 3538952 | tf_op jit(solution)/shard_map/ppermute | solution.py:728
  259.1 25.1 %collective-permute-start.34 = (bf16[4,96,768]{2,1,0:T(8,128)(2,1)S(1)}, bf16[4,96,768]{2,1,0:T(8,128)(2,1)}, u32[]{:S(2)}, u32[]{:S(2)}) collective-permute-start(bf16[4,96,768]{2,1,0:T(8,128)(2,1)S(1)} %get-tuple-element.347), channel_id=1, source_target_pairs={{0,8},{1,9},{2,10},{3,11},{4,12},{5,13},{6,14},{7,15},{8,0},{9,1},... | collective-permute-start | bytes 1769480 | tf_op jit(solution)/shard_map/ppermute | solution.py:728
  284.5 45.7 %collective-permute-start.40 = (bf16[8,192,768]{2,1,0:T(8,128)(2,1)}, bf16[8,192,768]{2,1,0:T(8,128)(2,1)}, u32[]{:S(2)}, u32[]{:S(2)}) collective-permute-start(bf16[8,192,768]{2,1,0:T(8,128)(2,1)} %get-tuple-element.383), channel_id=1, source_target_pairs={{0,16},{1,17},{2,18},{3,19},{4,20},{5,21},{6,22},{7,23},{8,24},{9,... | collective-permute-start | bytes 7077896 | tf_op jit(solution)/shard_map/ppermute | solution.py:734
  293.4 36.7 %collective-permute-start.39 = (bf16[8,192,768]{2,1,0:T(8,128)(2,1)}, bf16[8,192,768]{2,1,0:T(8,128)(2,1)}, u32[]{:S(2)}, u32[]{:S(2)}) collective-permute-start(bf16[8,192,768]{2,1,0:T(8,128)(2,1)} %add_convert_fusion), channel_id=1, source_target_pairs={{0,2},{1,3},{2,0},{3,1},{4,6},{5,7},{6,4},{7,5},{8,10},{9,11},{10,... | collective-permute-start | bytes 7077896 | tf_op jit(solution)/shard_map/ppermute | solution.py:728
  300.2 27.0 %collective-permute-start.38 = (bf16[2,192,768]{2,1,0:T(8,128)(2,1)}, bf16[2,192,768]{2,1,0:T(8,128)(2,1)S(1)}, u32[]{:S(2)}, u32[]{:S(2)}) collective-permute-start(bf16[2,192,768]{2,1,0:T(8,128)(2,1)} %add_convert_fusion.9), channel_id=1, source_target_pairs={{0,8},{1,9},{2,10},{3,11},{4,12},{5,13},{6,14},{7,15},{8,0},{9,1},... | collective-permute-start | bytes 1769480 | tf_op jit(solution)/shard_map/ppermute | solution.py:728
  302.8 27.4 %collective-permute-start.37 = (bf16[4,96,768]{2,1,0:T(8,128)(2,1)S(1)}, bf16[4,96,768]{2,1,0:T(8,128)(2,1)S(1)}, u32[]{:S(2)}, u32[]{:S(2)}) collective-permute-start(bf16[4,96,768]{2,1,0:T(8,128)(2,1)S(1)} %copy-done.18), channel_id=1, source_target_pairs={{0,8},{1,9},{2,10},{3,11},{4,12},{5,13},{6,14},{7,15},{8,0},{9,1},... | collective-permute-start | bytes 1769480 | tf_op jit(solution)/shard_map/ppermute | solution.py:728
  330.2 40.8 %collective-permute-start.41 = (bf16[8,112,768]{2,1,0:T(8,128)(2,1)}, bf16[8,112,768]{2,1,0:T(8,128)(2,1)S(1)}, u32[]{:S(2)}, u32[]{:S(2)}) collective-permute-start(bf16[8,112,768]{2,1,0:T(8,128)(2,1)} %get-tuple-element.385), channel_id=1, source_target_pairs={{0,16},{1,17},{2,18},{3,19},{4,20},{5,21},{6,22},{7,23},{8,24},{9,... | collective-permute-start | bytes 4128776 | tf_op jit(solution)/shard_map/ppermute | solution.py:734
  335.2 30.9 %collective-permute-start.43 = (bf16[8,112,768]{2,1,0:T(8,128)(2,1)S(1)}, bf16[8,112,768]{2,1,0:T(8,128)(2,1)S(1)}, u32[]{:S(2)}, u32[]{:S(2)}) collective-permute-start(bf16[8,112,768]{2,1,0:T(8,128)(2,1)S(1)} %add_convert_fusion.1), channel_id=1, source_target_pairs={{0,2},{1,3},{2,0},{3,1},{4,6},{5,7},{6,4},{7,5},{8,10},{9,11},{10,... | collective-permute-start | bytes 4128776 | tf_op jit(solution)/shard_map/ppermute | solution.py:728
  337.9 28.3 %collective-permute-start.47 = (bf16[4,192,768]{2,1,0:T(8,128)(2,1)S(1)}, bf16[4,192,768]{2,1,0:T(8,128)(2,1)S(1)}, u32[]{:S(2)}, u32[]{:S(2)}) collective-permute-start(bf16[4,192,768]{2,1,0:T(8,128)(2,1)S(1)} %add_convert_fusion.2), channel_id=1, source_target_pairs={{0,1},{1,0},{2,3},{3,2},{4,5},{5,4},{6,7},{7,6},{8,9},{9,8},{10,11... | collective-permute-start | bytes 3538952 | tf_op jit(solution)/shard_map/ppermute | solution.py:728
  366.2 25.0 %collective-permute-start.52 = (f32[1,512,768]{2,1,0:T(8,128)S(1)}, f32[1,512,768]{2,1,0:T(8,128)S(1)}, u32[]{:S(2)}, u32[]{:S(2)}) collective-permute-start(f32[1,512,768]{2,1,0:T(8,128)S(1)} %bitcast.108), channel_id=1, source_target_pairs={{16,0},{17,1},{18,2},{19,3},{20,4},{21,5},{22,6},{23,7},{24,8},{25... | collective-permute-start | bytes 4718600 | tf_op jit(solution)/shard_map/ppermute | solution.py:739
  367.4 23.7 %collective-permute-start.53 = (f32[1,512,768]{2,1,0:T(8,128)S(1)}, f32[1,512,768]{2,1,0:T(8,128)S(1)}, u32[]{:S(2)}, u32[]{:S(2)}) collective-permute-start(f32[1,512,768]{2,1,0:T(8,128)S(1)} %bitcast.97), channel_id=1, source_target_pairs={{0,16},{1,17},{2,18},{3,19},{4,20},{5,21},{6,22},{7,23},{8,24},{9,... | collective-permute-start | bytes 4718600 | tf_op jit(solution)/shard_map/ppermute | solution.py:739
  (60 other events, 653.0 us)

commit v7 on v6

--- a/solution.py
+++ b/solution.py
@@ -1217,11 +1217,15 @@
     a1_r.start_lower()
     f0_r.wait()
     f0_r.start()
+    d_second = jnp.stack(d_a1)
+    from_second = across(order.now(d_second), 0)
     d_r = order.now(d_r)
     chunk, d_a0, sums_a0, sumo_a0 = attn_back(
         False, PAD if is_small(count) else 0, d_r, a0, kept_a0, a0_half
     )
-    d_a0, a1_r.got, f1_r.got, f0_r.got, there = order.wait(d_a0, a1_r.got, f1_r.got, f0_r.got, f0_r.there)
+    d_a0, a1_r.got, f1_r.got, f0_r.got, there, from_second = order.wait(
+        d_a0, a1_r.got, f1_r.got, f0_r.got, f0_r.there, from_second
+    )
     f0_r.terms[1] = there
 
     def small_block(sums_a, sumo, sums_f, g_cup, head_part, core):
@@ -1260,23 +1264,23 @@
     f1_r.spare(1)
     f1_r.start()
     a1_r.start_from_upper()
-    d_first, d_second = jnp.stack(d_a0), jnp.stack(d_a1)
+    d_first = jnp.stack(d_a0)
     a0_r.got, a1_r.ahead, f1_r.got = order.wait(a0_r.got, a1_r.ahead, f1_r.got)
     a0_r.start()
     a1_r.join()
     f0_r.wait()
     f0_r.start()
     a1_r.start()
-    got = across(order.now(d_first), 1), across(order.now(d_second), 0)
+    from_first = across(order.now(d_first), 1)
     a0_r.got, a1_r.got = order.wait(a0_r.got, a1_r.got)
     a0_r.spare(2)
     a0_r.start()
     done_f1 = f1_r.finish()
     a1_r.start()
-    f0_r.got, got, done_f1 = order.wait(f0_r.got, got, done_f1)
+    f0_r.got, from_first, done_f1 = order.wait(f0_r.got, from_first, done_f1)
     f0_r.spare(1)
     f0_r.start()
-    input_grads = jnp.where(first, jnp.concatenate([d_first, got[0]]), jnp.concatenate([got[1], d_second]))
+    input_grads = jnp.where(first, jnp.concatenate([d_first, from_first]), jnp.concatenate([from_second, d_second]))
     a0_r.got, a1_r.got, input_grads = order.wait(a0_r.got, a1_r.got, input_grads)
     a0_r.spare(1)
     a0_r.start()

time: 427 us -> 425 us (level)
  no operation moved by 1% of the time
where the time goes in v7:
time: 425 us; the launch traced here: 420 us
  Pallas kernels  152 us (36%)
  waiting for transfers between devices  141 us (33%)
  other arithmetic  58.9 us (14%)
  starting transfers between devices  52.1 us (12%)
  local copies, waits for them, and re-layouts  13.7 us (3%)
    ppermute x35, waiting for transfers between devices, flip(): return lax.ppermute(value, BOTH, pairs)  121 us
    ppermute x35, starting transfers between devices, flip(): return lax.ppermute(value, BOTH, pairs)  44.9 us
    pallas_call x2, Pallas kernels, attn_bwd(): pl.pallas_call(lambda *refs: attn_bwd_kernel(near_first, halves, *refs),...  43.1 us
    pallas_call x2, Pallas kernels, ffn_bwd(): pl.pallas_call(lambda *refs: ffn_bwd_kernel(near_first, halves, head, *re...  38.7 us
    pallas_call x2, Pallas kernels, ffn_fwd(): pl.pallas_call(lambda *refs: ffn_fwd_kernel(near_first, halves, *refs), g...  32.8 us
    convert_element_type x23, other arithmetic, low(): return value.astype(BF)  32.7 us
    pallas_call x2, Pallas kernels, attn_fwd(): pl.pallas_call(lambda *refs: attn_fwd_kernel(near_first, halves, *refs),...  32.2 us
    ppermute x21, waiting for transfers between devices, swap(): return lax.ppermute(value, BOTH, pairs)  20.3 us
  transfers between devices with their start and end apart: 58, of which 28 were waited for; matrix products, arithmetic and copies ran while one was open for 14% of the time, Pallas kernels for 28%

profile of v7, /device:TPU:0, one launch (start us, length us, event | category | flops | bytes accessed | tf_op | source)
XLA Modules:
  0.0 420.3 jit_solution(5004293650475883112)
XLA Ops:
  12.5 3.8 collective-permute-done.1
  22.4 8.8 %collective-permute-done.5 = bf16[1,192,768]{2,1,0:T(8,128)(2,1)} collective-permute-done((bf16[1,192,768]{2,1,0:T(8,128)(2,1)S(1)}, bf16[1,192,768]{2,1,0:T(8,128)(2,1)}, u32[]{:S(2)}, u32[]{:S(2)}) %collective-permute-start.5) | collective-permute-done | bytes 294944 | tf_op jit(solution)/shard_map/ppermute | solution.py:728
  31.2 3.5 collective-permute-done.3
  37.3 15.8 %collective-permute-done.8 = bf16[2,192,768]{2,1,0:T(8,128)(2,1)S(1)} collective-permute-done((bf16[2,192,768]{2,1,0:T(8,128)(2,1)S(1)}, bf16[2,192,768]{2,1,0:T(8,128)(2,1)S(1)}, u32[]{:S(2)}, u32[]{:S(2)}) %collective-permute-start.8) | collective-permute-done | bytes 589856 | tf_op jit(solution)/shard_map/ppermute | solution.py:728
  60.3 20.5 %collective-permute-done.13 = bf16[1,192,768]{2,1,0:T(8,128)(2,1)S(1)} collective-permute-done((bf16[1,192,768]{2,1,0:T(8,128)(2,1)S(1)}, bf16[1,192,768]{2,1,0:T(8,128)(2,1)S(1)}, u32[]{:S(2)}, u32[]{:S(2)}) %collective-permute-start.13) | collective-permute-done | bytes 294944 | tf_op jit(solution)/shard_map/ppermute | solution.py:728
  84.3 3.6 maximum_select_fusion.1
  101.5 16.3 %attn_fwd.2 = (bf16[512,768]{1,0:T(8,128)(2,1)}, bf16[512,768]{1,0:T(8,128)(2,1)}, bf16[512,768]{1,0:T(8,128)(2,1)}, bf16[512,768]{1,0:T(8,128)(2,1)}, f32[512,768]{1,0:T(8,128)}, /*index=5*/f32[512,128]{1,0:T(8,128)}) custom-call(s32[2]{0:T(128)} %pad_add_fusion.refs_0_, bf16[2,2,2,112,768]{4,3,2,1,0:T(8,128)(2,1)} %bitcast.85, ...), custom_call_target="tpu_custom_call" | custom-call | tf_op jit(solution)/shard_map/attn_fwd/pallas_call | solution.py:261
  130.2 16.4 %ffn_fwd.2 = (bf16[512,3072]{1,0:T(8,128)(2,1)}, bf16[512,3072]{1,0:T(8,128)(2,1)}, f32[512,768]{1,0:T(8,128)}, f32[512,128]{1,0:T(8,128)}, bf16[512,768]{1,0:T(8,128)(2,1)}) custom-call(s32[2]{0:T(128)} %pad_add_fusion.refs_0_, bf16[2,2,2,192,768]{4,3,2,1,0:T(8,128)(2,1)} %bitcast.16.refs_1_, bf16[2,2,2,192,768]{4,3,2,1,0:T(8,128)(2,1)} %bitcast.20.refs_2_, ...), custom_call_target="tpu_custom_call" | custom-call | tf_op jit(solution)/shard_map/ffn_fwd/pallas_call | solution.py:349
  151.5 15.9 %attn_fwd.3 = (bf16[512,768]{1,0:T(8,128)(2,1)}, bf16[512,768]{1,0:T(8,128)(2,1)}, bf16[512,768]{1,0:T(8,128)(2,1)}, bf16[512,768]{1,0:T(8,128)(2,1)}, f32[512,768]{1,0:T(8,128)}, /*index=5*/f32[512,128]{1,0:T(8,128)}) custom-call(s32[2]{0:T(128)} %pad_add_fusion.refs_0_, bf16[2,2,2,96,768]{4,3,2,1,0:T(8,128)(2,1)} %bitcast.89, ...), custom_call_target="tpu_custom_call" | custom-call | tf_op jit(solution)/shard_map/attn_fwd/pallas_call | solution.py:261
  167.4 11.3 %collective-permute-done.26 = bf16[8,192,768]{2,1,0:T(8,128)(2,1)} collective-permute-done((bf16[8,192,768]{2,1,0:T(8,128)(2,1)S(1)}, bf16[8,192,768]{2,1,0:T(8,128)(2,1)}, u32[]{:S(2)}, u32[]{:S(2)}) %collective-permute-start.26) | collective-permute-done | bytes 2359328 | tf_op jit(solution)/shard_map/ppermute | solution.py:728
  185.0 16.4 %ffn_fwd.3 = (bf16[512,3072]{1,0:T(8,128)(2,1)}, bf16[512,3072]{1,0:T(8,128)(2,1)}, f32[512,768]{1,0:T(8,128)}, f32[512,128]{1,0:T(8,128)}, bf16[512,768]{1,0:T(8,128)(2,1)}) custom-call(s32[2]{0:T(128)} %pad_add_fusion.refs_0_, bf16[2,2,2,192,768]{4,3,2,1,0:T(8,128)(2,1)} %bitcast.87, bf16[2,2,2,192,768]{4,3,2,1,0:T(8,128)(2,1)} %bitcast.32.refs_2_, ...), custom_call_target="tpu_custom_call" | custom-call | tf_op jit(solution)/shard_map/ffn_fwd/pallas_call | solution.py:349
  201.4 19.6 %ffn_bwd.2 = (bf16[16,192,768]{2,1,0:T(8,128)(2,1)}, bf16[8,192,768]{2,1,0:T(8,128)(2,1)}, bf16[8,192,768]{2,1,0:T(8,128)(2,1)}, f32[512,768]{1,0:T(8,128)}, f32...) custom-call(s32[2]{0:T(128)} %pad_add_fusion.refs_0_, bf16[2,2,2,192,768]{4,3,2,1,0:T(8,128)(2,1)} %bitcast.88, ...), custom_call_target="tpu_custom_call" | custom-call | tf_op jit(solution)/shard_map/ffn_bwd/pallas_call | solution.py:505
  221.6 4.3 %collective-permute-done.28 = bf16[8,192,768]{2,1,0:T(8,128)(2,1)S(1)} collective-permute-done((bf16[8,192,768]{2,1,0:T(8,128)(2,1)}, bf16[8,192,768]{2,1,0:T(8,128)(2,1)S(1)}, u32[]{:S(2)}, u32[]{:S(2)}) %collective-permute-start.28) | collective-permute-done | bytes 2359328 | tf_op jit(solution)/shard_map/ppermute | solution.py:734
  229.6 21.7 %attn_bwd.2 = (bf16[16,96,768]{2,1,0:T(8,128)(2,1)}, bf16[8,96,768]{2,1,0:T(8,128)(2,1)}, bf16[8,96,768]{2,1,0:T(8,128)(2,1)}, f32[512,768]{1,0:T(8,128)}, f32[8,768]{1,0:T(8,128)}, /*index=5*/f32[8,768]{1,0:T(8,128)}) custom-call(s32[2]{0:T(128)} %pad_add_fusion.refs_0_, bf16[2,2,2,96,768]{4,3,2,1,0:T(8,128)(2,1)} %bitcast.90, ...), custom_call_target="tpu_custom_call" | custom-call | tf_op jit(solution)/shard_map/attn_bwd/pallas_call | solution.py:694
  251.4 4.0 add_convert_fusion.3
  262.6 19.1 %ffn_bwd.3 = (bf16[16,192,768]{2,1,0:T(8,128)(2,1)}, bf16[8,192,768]{2,1,0:T(8,128)(2,1)}, bf16[8,192,768]{2,1,0:T(8,128)(2,1)}, f32[512,768]{1,0:T(8,128)}, f32[8,768]{1,0:T(8,128)}, /*index=5*/f32[4,1,768]{2,1,0:T(1,128)}) custom-call(s32[2]{0:T(128)} %pad_add_fusion.refs_0_, bf16[2,2,2,192,768]{4,3,2,1,0:T(8,128)(2,1)} %bitcast.16.refs_1_, ...), custom_call_target="tpu_custom_call" | custom-call | tf_op jit(solution)/shard_map/ffn_bwd/pallas_call | solution.py:505
  284.5 5.1 %collective-permute-done.36 = bf16[8,192,768]{2,1,0:T(8,128)(2,1)S(1)} collective-permute-done((bf16[8,192,768]{2,1,0:T(8,128)(2,1)}, bf16[8,192,768]{2,1,0:T(8,128)(2,1)S(1)}, u32[]{:S(2)}, u32[]{:S(2)}) %collective-permute-start.36) | collective-permute-done | bytes 2359328 | tf_op jit(solution)/shard_map/ppermute | solution.py:734
  289.5 3.6 add_convert_fusion
  293.1 4.0 collective-permute-start.39
  304.4 21.4 %attn_bwd.3 = (bf16[16,112,768]{2,1,0:T(8,128)(2,1)}, bf16[8,112,768]{2,1,0:T(8,128)(2,1)}, bf16[8,112,768]{2,1,0:T(8,128)(2,1)}, f32[512,768]{1,0:T(8,128)}, f32[8,768]{1,0:T(8,128)}, /*index=5*/f32[8,768]{1,0:T(8,128)}) custom-call(s32[2]{0:T(128)} %pad_add_fusion.refs_0_, bf16[2,2,2,112,768]{4,3,2,1,0:T(8,128)(2,1)} %bitcast.86, ...), custom_call_target="tpu_custom_call" | custom-call | tf_op jit(solution)/shard_map/attn_bwd/pallas_call | solution.py:694
  347.1 18.9 %collective-permute-done.46 = bf16[1,192,768]{2,1,0:T(8,128)(2,1)S(1)} collective-permute-done((bf16[1,192,768]{2,1,0:T(8,128)(2,1)S(1)}, bf16[1,192,768]{2,1,0:T(8,128)(2,1)S(1)}, u32[]{:S(2)}, u32[]{:S(2)}) %collective-permute-start.46) | collective-permute-done | bytes 294944 | tf_op jit(solution)/shard_map/ppermute | solution.py:728
  377.3 3.7 collective-permute-done.49
  385.7 6.3 %collective-permute-done.52 = bf16[2,192,768]{2,1,0:T(8,128)(2,1)S(1)} collective-permute-done((bf16[2,192,768]{2,1,0:T(8,128)(2,1)S(1)}, bf16[2,192,768]{2,1,0:T(8,128)(2,1)S(1)}, u32[]{:S(2)}, u32[]{:S(2)}) %collective-permute-start.52) | collective-permute-done | bytes 589856 | tf_op jit(solution)/shard_map/ppermute | solution.py:728
  395.9 8.9 %collective-permute-done.50 = bf16[2,112,768]{2,1,0:T(8,128)(2,1)S(1)} collective-permute-done((bf16[2,112,768]{2,1,0:T(8,128)(2,1)S(1)}, bf16[2,112,768]{2,1,0:T(8,128)(2,1)S(1)}, u32[]{:S(2)}, u32[]{:S(2)}) %collective-permute-start.50) | collective-permute-done | bytes 344096 | tf_op jit(solution)/shard_map/ppermute | solution.py:728
  (225 shorter events, 145.6 us)
Async XLA Ops:
  53.4 30.9 %collective-permute-start.12 = (bf16[8,112,768]{2,1,0:T(8,128)(2,1)S(1)}, bf16[8,112,768]{2,1,0:T(8,128)(2,1)}, u32[]{:S(2)}, u32[]{:S(2)}) collective-permute-start(bf16[8,112,768]{2,1,0:T(8,128)(2,1)S(1)} %maximum_select_fusion.3.refs_1_), channel_id=1, source_target_pairs={{0,16},{1,17},{2,18},{3,19},{4,20},{5,21},{6,22},{7,23},{8,24},{9,... | collective-permute-start | bytes 4128776 | tf_op jit(solution)/shard_map/ppermute | solution.py:734
  53.5 30.8 %collective-permute-start.9 = (bf16[8,112,768]{2,1,0:T(8,128)(2,1)S(1)}, bf16[8,112,768]{2,1,0:T(8,128)(2,1)}, u32[]{:S(2)}, u32[]{:S(2)}) collective-permute-start(bf16[8,112,768]{2,1,0:T(8,128)(2,1)S(1)} %maximum_select_fusion.3.refs_1_), channel_id=1, source_target_pairs={{0,2},{1,3},{2,0},{3,1},{4,6},{5,7},{6,4},{7,5},{8,10},{9,11},{10,... | collective-permute-start | bytes 4128776 | tf_op jit(solution)/shard_map/ppermute | solution.py:728
  56.6 27.7 %collective-permute-start.10 = (bf16[4,192,768]{2,1,0:T(8,128)(2,1)}, bf16[4,192,768]{2,1,0:T(8,128)(2,1)}, u32[]{:S(2)}, u32[]{:S(2)}) collective-permute-start(bf16[4,192,768]{2,1,0:T(8,128)(2,1)} %maximum_select_fusion.4), channel_id=1, source_target_pairs={{0,1},{1,0},{2,3},{3,2},{4,5},{5,4},{6,7},{7,6},{8,9},{9,8},{10,11... | collective-permute-start | bytes 3538952 | tf_op jit(solution)/shard_map/ppermute | solution.py:728
  58.2 22.6 %collective-permute-start.11 = (bf16[4,96,768]{2,1,0:T(8,128)(2,1)S(1)}, bf16[4,96,768]{2,1,0:T(8,128)(2,1)S(1)}, u32[]{:S(2)}, u32[]{:S(2)}) collective-permute-start(bf16[4,96,768]{2,1,0:T(8,128)(2,1)S(1)} %maximum_select_fusion.9), channel_id=1, source_target_pairs={{0,4},{1,5},{2,6},{3,7},{4,0},{5,1},{6,2},{7,3},{8,12},{9,13},{10,... | collective-permute-start | bytes 1769480 | tf_op jit(solution)/shard_map/ppermute | solution.py:728
  87.9 31.9 %collective-permute-start.15 = (bf16[8,192,768]{2,1,0:T(8,128)(2,1)}, bf16[8,192,768]{2,1,0:T(8,128)(2,1)}, u32[]{:S(2)}, u32[]{:S(2)}) collective-permute-start(bf16[8,192,768]{2,1,0:T(8,128)(2,1)} %maximum_select_fusion.1), channel_id=1, source_target_pairs={{0,2},{1,3},{2,0},{3,1},{4,6},{5,7},{6,4},{7,5},{8,10},{9,11},{10,... | collective-permute-start | bytes 7077896 | tf_op jit(solution)/shard_map/ppermute | solution.py:728
  90.2 27.7 %collective-permute-start.16 = (bf16[2,192,768]{2,1,0:T(8,128)(2,1)S(1)}, bf16[2,192,768]{2,1,0:T(8,128)(2,1)}, u32[]{:S(2)}, u32[]{:S(2)}) collective-permute-start(bf16[2,192,768]{2,1,0:T(8,128)(2,1)S(1)} %maximum_select_fusion.10), channel_id=1, source_target_pairs={{0,8},{1,9},{2,10},{3,11},{4,12},{5,13},{6,14},{7,15},{8,0},{9,1},... | collective-permute-start | bytes 1769480 | tf_op jit(solution)/shard_map/ppermute | solution.py:728
  91.7 28.1 %collective-permute-start.17 = (bf16[4,96,768]{2,1,0:T(8,128)(2,1)}, bf16[4,96,768]{2,1,0:T(8,128)(2,1)}, u32[]{:S(2)}, u32[]{:S(2)}) collective-permute-start(bf16[4,96,768]{2,1,0:T(8,128)(2,1)} %get-tuple-element.261), channel_id=1, source_target_pairs={{0,8},{1,9},{2,10},{3,11},{4,12},{5,13},{6,14},{7,15},{8,0},{9,1},... | collective-permute-start | bytes 1769480 | tf_op jit(solution)/shard_map/ppermute | solution.py:728
  123.1 23.5 %collective-permute-start.22 = (bf16[4,192,768]{2,1,0:T(8,128)(2,1)}, bf16[4,192,768]{2,1,0:T(8,128)(2,1)}, u32[]{:S(2)}, u32[]{:S(2)}) collective-permute-start(bf16[4,192,768]{2,1,0:T(8,128)(2,1)} %maximum_select_fusion.6), channel_id=1, source_target_pairs={{0,1},{1,0},{2,3},{3,2},{4,5},{5,4},{6,7},{7,6},{8,9},{9,8},{10,11... | collective-permute-start | bytes 3538952 | tf_op jit(solution)/shard_map/ppermute | solution.py:728
  149.7 29.0 %collective-permute-start.26 = (bf16[8,192,768]{2,1,0:T(8,128)(2,1)S(1)}, bf16[8,192,768]{2,1,0:T(8,128)(2,1)}, u32[]{:S(2)}, u32[]{:S(2)}) collective-permute-start(bf16[8,192,768]{2,1,0:T(8,128)(2,1)S(1)} %maximum_select_fusion.2), channel_id=1, source_target_pairs={{0,2},{1,3},{2,0},{3,1},{4,6},{5,7},{6,4},{7,5},{8,10},{9,11},{10,... | collective-permute-start | bytes 7077896 | tf_op jit(solution)/shard_map/ppermute | solution.py:728
  150.4 28.4 %collective-permute-start.25 = (bf16[8,192,768]{2,1,0:T(8,128)(2,1)S(1)}, bf16[8,192,768]{2,1,0:T(8,128)(2,1)}, u32[]{:S(2)}, u32[]{:S(2)}) collective-permute-start(bf16[8,192,768]{2,1,0:T(8,128)(2,1)S(1)} %maximum_select_fusion.2), channel_id=1, source_target_pairs={{0,16},{1,17},{2,18},{3,19},{4,20},{5,21},{6,22},{7,23},{8,24},{9,... | collective-permute-start | bytes 7077896 | tf_op jit(solution)/shard_map/ppermute | solution.py:734
  221.5 29.8 %collective-permute-start.30 = (bf16[8,192,768]{2,1,0:T(8,128)(2,1)}, bf16[8,192,768]{2,1,0:T(8,128)(2,1)S(1)}, u32[]{:S(2)}, u32[]{:S(2)}) collective-permute-start(bf16[8,192,768]{2,1,0:T(8,128)(2,1)} %get-tuple-element.328), channel_id=1, source_target_pairs={{0,16},{1,17},{2,18},{3,19},{4,20},{5,21},{6,22},{7,23},{8,24},{9,... | collective-permute-start | bytes 7077896 | tf_op jit(solution)/shard_map/ppermute | solution.py:734
  255.4 28.1 %collective-permute-start.32 = (bf16[4,192,768]{2,1,0:T(8,128)(2,1)S(1)}, bf16[4,192,768]{2,1,0:T(8,128)(2,1)}, u32[]{:S(2)}, u32[]{:S(2)}) collective-permute-start(bf16[4,192,768]{2,1,0:T(8,128)(2,1)S(1)} %get-tuple-element.341), channel_id=1, source_target_pairs={{0,2},{1,3},{2,0},{3,1},{4,6},{5,7},{6,4},{7,5},{8,10},{9,11},{10,... | collective-permute-start | bytes 3538952 | tf_op jit(solution)/shard_map/ppermute | solution.py:728
  257.2 26.3 %collective-permute-start.35 = (bf16[8,96,768]{2,1,0:T(8,128)(2,1)}, bf16[8,96,768]{2,1,0:T(8,128)(2,1)}, u32[]{:S(2)}, u32[]{:S(2)}) collective-permute-start(bf16[8,96,768]{2,1,0:T(8,128)(2,1)} %get-tuple-element.349), channel_id=1, source_target_pairs={{0,16},{1,17},{2,18},{3,19},{4,20},{5,21},{6,22},{7,23},{8,24},{9,... | collective-permute-start | bytes 3538952 | tf_op jit(solution)/shard_map/ppermute | solution.py:734
  257.3 26.6 %collective-permute-start.33 = (bf16[4,192,768]{2,1,0:T(8,128)(2,1)}, bf16[4,192,768]{2,1,0:T(8,128)(2,1)}, u32[]{:S(2)}, u32[]{:S(2)}) collective-permute-start(bf16[4,192,768]{2,1,0:T(8,128)(2,1)} %add_convert_fusion.3), channel_id=1, source_target_pairs={{0,1},{1,0},{2,3},{3,2},{4,5},{5,4},{6,7},{7,6},{8,9},{9,8},{10,11... | collective-permute-start | bytes 3538952 | tf_op jit(solution)/shard_map/ppermute | solution.py:728
  258.9 25.1 %collective-permute-start.34 = (bf16[4,96,768]{2,1,0:T(8,128)(2,1)S(1)}, bf16[4,96,768]{2,1,0:T(8,128)(2,1)}, u32[]{:S(2)}, u32[]{:S(2)}) collective-permute-start(bf16[4,96,768]{2,1,0:T(8,128)(2,1)S(1)} %get-tuple-element.347), channel_id=1, source_target_pairs={{0,8},{1,9},{2,10},{3,11},{4,12},{5,13},{6,14},{7,15},{8,0},{9,1},... | collective-permute-start | bytes 1769480 | tf_op jit(solution)/shard_map/ppermute | solution.py:728
  284.2 47.4 %collective-permute-start.40 = (bf16[8,192,768]{2,1,0:T(8,128)(2,1)}, bf16[8,192,768]{2,1,0:T(8,128)(2,1)}, u32[]{:S(2)}, u32[]{:S(2)}) collective-permute-start(bf16[8,192,768]{2,1,0:T(8,128)(2,1)} %get-tuple-element.383), channel_id=1, source_target_pairs={{0,16},{1,17},{2,18},{3,19},{4,20},{5,21},{6,22},{7,23},{8,24},{9,... | collective-permute-start | bytes 7077896 | tf_op jit(solution)/shard_map/ppermute | solution.py:734
  293.1 38.5 %collective-permute-start.39 = (bf16[8,192,768]{2,1,0:T(8,128)(2,1)}, bf16[8,192,768]{2,1,0:T(8,128)(2,1)}, u32[]{:S(2)}, u32[]{:S(2)}) collective-permute-start(bf16[8,192,768]{2,1,0:T(8,128)(2,1)} %add_convert_fusion), channel_id=1, source_target_pairs={{0,2},{1,3},{2,0},{3,1},{4,6},{5,7},{6,4},{7,5},{8,10},{9,11},{10,... | collective-permute-start | bytes 7077896 | tf_op jit(solution)/shard_map/ppermute | solution.py:728
  297.1 34.5 %collective-permute-start.41 = (f32[1,512,768]{2,1,0:T(8,128)S(1)}, f32[1,512,768]{2,1,0:T(8,128)S(1)}, u32[]{:S(2)}, u32[]{:S(2)}) collective-permute-start(f32[1,512,768]{2,1,0:T(8,128)S(1)} %bitcast.97), channel_id=1, source_target_pairs={{0,16},{1,17},{2,18},{3,19},{4,20},{5,21},{6,22},{7,23},{8,24},{9,... | collective-permute-start | bytes 4718600 | tf_op jit(solution)/shard_map/ppermute | solution.py:739
  301.5 26.9 %collective-permute-start.38 = (bf16[2,192,768]{2,1,0:T(8,128)(2,1)}, bf16[2,192,768]{2,1,0:T(8,128)(2,1)}, u32[]{:S(2)}, u32[]{:S(2)}) collective-permute-start(bf16[2,192,768]{2,1,0:T(8,128)(2,1)} %add_convert_fusion.9), channel_id=1, source_target_pairs={{0,8},{1,9},{2,10},{3,11},{4,12},{5,13},{6,14},{7,15},{8,0},{9,1},... | collective-permute-start | bytes 1769480 | tf_op jit(solution)/shard_map/ppermute | solution.py:728
  304.2 27.4 %collective-permute-start.37 = (bf16[4,96,768]{2,1,0:T(8,128)(2,1)}, bf16[4,96,768]{2,1,0:T(8,128)(2,1)}, u32[]{:S(2)}, u32[]{:S(2)}) collective-permute-start(bf16[4,96,768]{2,1,0:T(8,128)(2,1)} %get-tuple-element.375), channel_id=1, source_target_pairs={{0,8},{1,9},{2,10},{3,11},{4,12},{5,13},{6,14},{7,15},{8,0},{9,1},... | collective-permute-start | bytes 1769480 | tf_op jit(solution)/shard_map/ppermute | solution.py:728
  331.7 37.4 %collective-permute-start.42 = (bf16[8,112,768]{2,1,0:T(8,128)(2,1)}, bf16[8,112,768]{2,1,0:T(8,128)(2,1)S(1)}, u32[]{:S(2)}, u32[]{:S(2)}) collective-permute-start(bf16[8,112,768]{2,1,0:T(8,128)(2,1)} %get-tuple-element.386), channel_id=1, source_target_pairs={{0,16},{1,17},{2,18},{3,19},{4,20},{5,21},{6,22},{7,23},{8,24},{9,... | collective-permute-start | bytes 4128776 | tf_op jit(solution)/shard_map/ppermute | solution.py:734
  336.7 30.8 %collective-permute-start.44 = (bf16[8,112,768]{2,1,0:T(8,128)(2,1)S(1)}, bf16[8,112,768]{2,1,0:T(8,128)(2,1)S(1)}, u32[]{:S(2)}, u32[]{:S(2)}) collective-permute-start(bf16[8,112,768]{2,1,0:T(8,128)(2,1)S(1)} %add_convert_fusion.1), channel_id=1, source_target_pairs={{0,2},{1,3},{2,0},{3,1},{4,6},{5,7},{6,4},{7,5},{8,10},{9,11},{10,... | collective-permute-start | bytes 4128776 | tf_op jit(solution)/shard_map/ppermute | solution.py:728
  340.6 26.9 %collective-permute-start.48 = (bf16[4,192,768]{2,1,0:T(8,128)(2,1)S(1)}, bf16[4,192,768]{2,1,0:T(8,128)(2,1)S(1)}, u32[]{:S(2)}, u32[]{:S(2)}) collective-permute-start(bf16[4,192,768]{2,1,0:T(8,128)(2,1)S(1)} %add_convert_fusion.2), channel_id=1, source_target_pairs={{0,1},{1,0},{2,3},{3,2},{4,5},{5,4},{6,7},{7,6},{8,9},{9,8},{10,11... | collective-permute-start | bytes 3538952 | tf_op jit(solution)/shard_map/ppermute | solution.py:728
  367.5 24.4 %collective-permute-start.53 = (f32[1,512,768]{2,1,0:T(8,128)S(1)}, f32[1,512,768]{2,1,0:T(8,128)S(1)}, u32[]{:S(2)}, u32[]{:S(2)}) collective-permute-start(f32[1,512,768]{2,1,0:T(8,128)S(1)} %bitcast.108), channel_id=1, source_target_pairs={{16,0},{17,1},{18,2},{19,3},{20,4},{21,5},{22,6},{23,7},{24,8},{25... | collective-permute-start | bytes 4718600 | tf_op jit(solution)/shard_map/ppermute | solution.py:739
  (59 other events, 646.9 us)

commit v8 on v7

--- a/solution.py
+++ b/solution.py
@@ -334,7 +334,7 @@
     @pl.when(step == pl.num_programs(0) - 1)
     def _():
         n, t = norm_stats(acc[...])
-        n_ref[...] = n
+        n_ref[...] = n.astype(BF)
         t_ref[...] = jnp.broadcast_to(t, t_ref.shape)
         y_ref[...] = (n * gain_ref[1:2] + shift_ref[7:8]).astype(BF)
 
@@ -359,7 +359,7 @@
         ],
         out_specs=[column, column, whole_block(length, width), whole_block(length, 128), whole_block(length, width)],
         out_shape=[shape_of((length, units * width), BF)] * 2
-        + [shape_of((length, width), F32), shape_of((length, 128), F32), shape_of((length, width), BF)],
+        + [shape_of((length, width), BF), shape_of((length, 128), F32), shape_of((length, width), BF)],
         scratch_shapes=[
             pltpu.VMEM((length, width), BF),
             pltpu.VMEM((length, width), F32),
@@ -400,7 +400,7 @@
 
     @pl.when(step == 0)
     def _():
-        n2 = n2_ref[...]
+        n2 = n2_ref[...].astype(F32)
         if head:
             y = y_ref[...]
             proj = dot(y, head_ref[...])

time: 425 us -> 423 us (level)
  no operation moved by 1% of the time
where the time goes in v8:
time: 423 us; the launch traced here: 419 us
  Pallas kernels  151 us (36%)
  waiting for transfers between devices  141 us (33%)
  other arithmetic  59.2 us (14%)
  starting transfers between devices  51.8 us (12%)
  local copies, waits for them, and re-layouts  13.5 us (3%)
    ppermute x35, waiting for transfers between devices, flip(): return lax.ppermute(value, BOTH, pairs)  119 us
    ppermute x35, starting transfers between devices, flip(): return lax.ppermute(value, BOTH, pairs)  44.4 us
    pallas_call x2, Pallas kernels, attn_bwd(): pl.pallas_call(lambda *refs: attn_bwd_kernel(near_first, halves, *refs),...  43.1 us
    pallas_call x2, Pallas kernels, ffn_bwd(): pl.pallas_call(lambda *refs: ffn_bwd_kernel(near_first, halves, head, *re...  38.1 us
    convert_element_type x23, other arithmetic, low(): return value.astype(BF)  32.6 us
    pallas_call x2, Pallas kernels, ffn_fwd(): pl.pallas_call(lambda *refs: ffn_fwd_kernel(near_first, halves, *refs), g...  32.3 us
    pallas_call x2, Pallas kernels, attn_fwd(): pl.pallas_call(lambda *refs: attn_fwd_kernel(near_first, halves, *refs),...  32.2 us
    ppermute x21, waiting for transfers between devices, swap(): return lax.ppermute(value, BOTH, pairs)  22 us
  transfers between devices with their start and end apart: 58, of which 28 were waited for; matrix products, arithmetic and copies ran while one was open for 14% of the time, Pallas kernels for 28%

profile of v8, /device:TPU:0, one launch (start us, length us, event | category | flops | bytes accessed | tf_op | source)
XLA Modules:
  0.0 418.5 jit_solution(16141318340869248698)
XLA Ops:
  12.5 3.8 collective-permute-done.1
  22.4 8.8 %collective-permute-done.5 = bf16[1,192,768]{2,1,0:T(8,128)(2,1)} collective-permute-done((bf16[1,192,768]{2,1,0:T(8,128)(2,1)S(1)}, bf16[1,192,768]{2,1,0:T(8,128)(2,1)}, u32[]{:S(2)}, u32[]{:S(2)}) %collective-permute-start.5) | collective-permute-done | bytes 294944 | tf_op jit(solution)/shard_map/ppermute | solution.py:728
  31.2 3.5 collective-permute-done.3
  37.3 15.8 %collective-permute-done.8 = bf16[2,192,768]{2,1,0:T(8,128)(2,1)S(1)} collective-permute-done((bf16[2,192,768]{2,1,0:T(8,128)(2,1)S(1)}, bf16[2,192,768]{2,1,0:T(8,128)(2,1)S(1)}, u32[]{:S(2)}, u32[]{:S(2)}) %collective-permute-start.8) | collective-permute-done | bytes 589856 | tf_op jit(solution)/shard_map/ppermute | solution.py:728
  60.3 20.5 %collective-permute-done.13 = bf16[1,192,768]{2,1,0:T(8,128)(2,1)S(1)} collective-permute-done((bf16[1,192,768]{2,1,0:T(8,128)(2,1)S(1)}, bf16[1,192,768]{2,1,0:T(8,128)(2,1)S(1)}, u32[]{:S(2)}, u32[]{:S(2)}) %collective-permute-start.13) | collective-permute-done | bytes 294944 | tf_op jit(solution)/shard_map/ppermute | solution.py:728
  80.8 3.4 collective-permute-done.10
  84.3 3.5 maximum_select_fusion.1
  101.4 16.3 %attn_fwd.2 = (bf16[512,768]{1,0:T(8,128)(2,1)}, bf16[512,768]{1,0:T(8,128)(2,1)}, bf16[512,768]{1,0:T(8,128)(2,1)}, bf16[512,768]{1,0:T(8,128)(2,1)}, f32[512,768]{1,0:T(8,128)}, /*index=5*/f32[512,128]{1,0:T(8,128)}) custom-call(s32[2]{0:T(128)} %pad_add_fusion.refs_0_, bf16[2,2,2,112,768]{4,3,2,1,0:T(8,128)(2,1)} %bitcast.85, ...), custom_call_target="tpu_custom_call" | custom-call | tf_op jit(solution)/shard_map/attn_fwd/pallas_call | solution.py:261
  130.1 16.2 %ffn_fwd.2 = (bf16[512,3072]{1,0:T(8,128)(2,1)}, bf16[512,3072]{1,0:T(8,128)(2,1)}, bf16[512,768]{1,0:T(8,128)(2,1)}, f32[512,128]{1,0:T(8,128)}, bf16[512,768]{1,0:T(8,128)(2,1)}) custom-call(s32[2]{0:T(128)} %pad_add_fusion.refs_0_, bf16[2,2,2,192,768]{4,3,2,1,0:T(8,128)(2,1)} %bitcast.16.refs_1_, bf16[2,2,2,192,768]{4,3,2,1,0:T(8,128)(2,1)} %bitcast.20.refs_2_, ...), custom_call_target="tpu_custom_call" | custom-call | tf_op jit(solution)/shard_map/ffn_fwd/pallas_call | solution.py:349
  151.5 15.9 %attn_fwd.3 = (bf16[512,768]{1,0:T(8,128)(2,1)}, bf16[512,768]{1,0:T(8,128)(2,1)}, bf16[512,768]{1,0:T(8,128)(2,1)}, bf16[512,768]{1,0:T(8,128)(2,1)}, f32[512,768]{1,0:T(8,128)}, /*index=5*/f32[512,128]{1,0:T(8,128)}) custom-call(s32[2]{0:T(128)} %pad_add_fusion.refs_0_, bf16[2,2,2,96,768]{4,3,2,1,0:T(8,128)(2,1)} %bitcast.89, ...), custom_call_target="tpu_custom_call" | custom-call | tf_op jit(solution)/shard_map/attn_fwd/pallas_call | solution.py:261
  167.5 11.3 %collective-permute-done.26 = bf16[8,192,768]{2,1,0:T(8,128)(2,1)} collective-permute-done((bf16[8,192,768]{2,1,0:T(8,128)(2,1)S(1)}, bf16[8,192,768]{2,1,0:T(8,128)(2,1)}, u32[]{:S(2)}, u32[]{:S(2)}) %collective-permute-start.26) | collective-permute-done | bytes 2359328 | tf_op jit(solution)/shard_map/ppermute | solution.py:728
  184.9 16.2 %ffn_fwd.3 = (bf16[512,3072]{1,0:T(8,128)(2,1)}, bf16[512,3072]{1,0:T(8,128)(2,1)}, bf16[512,768]{1,0:T(8,128)(2,1)}, f32[512,128]{1,0:T(8,128)}, bf16[512,768]{1,0:T(8,128)(2,1)}) custom-call(s32[2]{0:T(128)} %pad_add_fusion.refs_0_, bf16[2,2,2,192,768]{4,3,2,1,0:T(8,128)(2,1)} %bitcast.87, bf16[2,2,2,192,768]{4,3,2,1,0:T(8,128)(2,1)} %bitcast.32.refs_2_, ...), custom_call_target="tpu_custom_call" | custom-call | tf_op jit(solution)/shard_map/ffn_fwd/pallas_call | solution.py:349
  201.1 19.3 %ffn_bwd.2 = (bf16[16,192,768]{2,1,0:T(8,128)(2,1)}, bf16[8,192,768]{2,1,0:T(8,128)(2,1)}, bf16[8,192,768]{2,1,0:T(8,128)(2,1)}, f32[512,768]{1,0:T(8,128)}, f32...) custom-call(s32[2]{0:T(128)} %pad_add_fusion.refs_0_, bf16[2,2,2,192,768]{4,3,2,1,0:T(8,128)(2,1)} %bitcast.88, ...), custom_call_target="tpu_custom_call" | custom-call | tf_op jit(solution)/shard_map/ffn_bwd/pallas_call | solution.py:505
  221.0 4.3 %collective-permute-done.28 = bf16[8,192,768]{2,1,0:T(8,128)(2,1)S(1)} collective-permute-done((bf16[8,192,768]{2,1,0:T(8,128)(2,1)}, bf16[8,192,768]{2,1,0:T(8,128)(2,1)S(1)}, u32[]{:S(2)}, u32[]{:S(2)}) %collective-permute-start.28) | collective-permute-done | bytes 2359328 | tf_op jit(solution)/shard_map/ppermute | solution.py:734
  229.2 21.7 %attn_bwd.2 = (bf16[16,96,768]{2,1,0:T(8,128)(2,1)}, bf16[8,96,768]{2,1,0:T(8,128)(2,1)}, bf16[8,96,768]{2,1,0:T(8,128)(2,1)}, f32[512,768]{1,0:T(8,128)}, f32[8,768]{1,0:T(8,128)}, /*index=5*/f32[8,768]{1,0:T(8,128)}) custom-call(s32[2]{0:T(128)} %pad_add_fusion.refs_0_, bf16[2,2,2,96,768]{4,3,2,1,0:T(8,128)(2,1)} %bitcast.90, ...), custom_call_target="tpu_custom_call" | custom-call | tf_op jit(solution)/shard_map/attn_bwd/pallas_call | solution.py:694
  251.0 4.0 add_convert_fusion.3
  261.9 18.8 %ffn_bwd.3 = (bf16[16,192,768]{2,1,0:T(8,128)(2,1)}, bf16[8,192,768]{2,1,0:T(8,128)(2,1)}, bf16[8,192,768]{2,1,0:T(8,128)(2,1)}, f32[512,768]{1,0:T(8,128)}, f32[8,768]{1,0:T(8,128)}, /*index=5*/f32[4,1,768]{2,1,0:T(1,128)}) custom-call(s32[2]{0:T(128)} %pad_add_fusion.refs_0_, bf16[2,2,2,192,768]{4,3,2,1,0:T(8,128)(2,1)} %bitcast.16.refs_1_, ...), custom_call_target="tpu_custom_call" | custom-call | tf_op jit(solution)/shard_map/ffn_bwd/pallas_call | solution.py:505
  283.8 7.0 %collective-permute-done.36 = bf16[8,192,768]{2,1,0:T(8,128)(2,1)S(1)} collective-permute-done((bf16[8,192,768]{2,1,0:T(8,128)(2,1)}, bf16[8,192,768]{2,1,0:T(8,128)(2,1)S(1)}, u32[]{:S(2)}, u32[]{:S(2)}) %collective-permute-start.36) | collective-permute-done | bytes 2359328 | tf_op jit(solution)/shard_map/ppermute | solution.py:734
  290.8 3.6 add_convert_fusion
  303.6 21.4 %attn_bwd.3 = (bf16[16,112,768]{2,1,0:T(8,128)(2,1)}, bf16[8,112,768]{2,1,0:T(8,128)(2,1)}, bf16[8,112,768]{2,1,0:T(8,128)(2,1)}, f32[512,768]{1,0:T(8,128)}, f32[8,768]{1,0:T(8,128)}, /*index=5*/f32[8,768]{1,0:T(8,128)}) custom-call(s32[2]{0:T(128)} %pad_add_fusion.refs_0_, bf16[2,2,2,112,768]{4,3,2,1,0:T(8,128)(2,1)} %bitcast.86, ...), custom_call_target="tpu_custom_call" | custom-call | tf_op jit(solution)/shard_map/attn_bwd/pallas_call | solution.py:694
  346.2 18.9 %collective-permute-done.46 = bf16[1,192,768]{2,1,0:T(8,128)(2,1)S(1)} collective-permute-done((bf16[1,192,768]{2,1,0:T(8,128)(2,1)S(1)}, bf16[1,192,768]{2,1,0:T(8,128)(2,1)S(1)}, u32[]{:S(2)}, u32[]{:S(2)}) %collective-permute-start.46) | collective-permute-done | bytes 294944 | tf_op jit(solution)/shard_map/ppermute | solution.py:728
  376.5 3.9 collective-permute-done.49
  385.2 5.2 %collective-permute-done.52 = bf16[2,192,768]{2,1,0:T(8,128)(2,1)S(1)} collective-permute-done((bf16[2,192,768]{2,1,0:T(8,128)(2,1)S(1)}, bf16[2,192,768]{2,1,0:T(8,128)(2,1)S(1)}, u32[]{:S(2)}, u32[]{:S(2)}) %collective-permute-start.52) | collective-permute-done | bytes 589856 | tf_op jit(solution)/shard_map/ppermute | solution.py:728
  395.1 8.1 %collective-permute-done.50 = bf16[2,112,768]{2,1,0:T(8,128)(2,1)S(1)} collective-permute-done((bf16[2,112,768]{2,1,0:T(8,128)(2,1)S(1)}, bf16[2,112,768]{2,1,0:T(8,128)(2,1)S(1)}, u32[]{:S(2)}, u32[]{:S(2)}) %collective-permute-start.50) | collective-permute-done | bytes 344096 | tf_op jit(solution)/shard_map/ppermute | solution.py:728
  (225 shorter events, 145.3 us)
Async XLA Ops:
  53.4 30.9 %collective-permute-start.12 = (bf16[8,112,768]{2,1,0:T(8,128)(2,1)S(1)}, bf16[8,112,768]{2,1,0:T(8,128)(2,1)}, u32[]{:S(2)}, u32[]{:S(2)}) collective-permute-start(bf16[8,112,768]{2,1,0:T(8,128)(2,1)S(1)} %maximum_select_fusion.3.refs_1_), channel_id=1, source_target_pairs={{0,16},{1,17},{2,18},{3,19},{4,20},{5,21},{6,22},{7,23},{8,24},{9,... | collective-permute-start | bytes 4128776 | tf_op jit(solution)/shard_map/ppermute | solution.py:734
  53.5 30.8 %collective-permute-start.9 = (bf16[8,112,768]{2,1,0:T(8,128)(2,1)S(1)}, bf16[8,112,768]{2,1,0:T(8,128)(2,1)}, u32[]{:S(2)}, u32[]{:S(2)}) collective-permute-start(bf16[8,112,768]{2,1,0:T(8,128)(2,1)S(1)} %maximum_select_fusion.3.refs_1_), channel_id=1, source_target_pairs={{0,2},{1,3},{2,0},{3,1},{4,6},{5,7},{6,4},{7,5},{8,10},{9,11},{10,... | collective-permute-start | bytes 4128776 | tf_op jit(solution)/shard_map/ppermute | solution.py:728
  56.6 27.7 %collective-permute-start.10 = (bf16[4,192,768]{2,1,0:T(8,128)(2,1)}, bf16[4,192,768]{2,1,0:T(8,128)(2,1)}, u32[]{:S(2)}, u32[]{:S(2)}) collective-permute-start(bf16[4,192,768]{2,1,0:T(8,128)(2,1)} %maximum_select_fusion.4), channel_id=1, source_target_pairs={{0,1},{1,0},{2,3},{3,2},{4,5},{5,4},{6,7},{7,6},{8,9},{9,8},{10,11... | collective-permute-start | bytes 3538952 | tf_op jit(solution)/shard_map/ppermute | solution.py:728
  58.2 22.6 %collective-permute-start.11 = (bf16[4,96,768]{2,1,0:T(8,128)(2,1)S(1)}, bf16[4,96,768]{2,1,0:T(8,128)(2,1)S(1)}, u32[]{:S(2)}, u32[]{:S(2)}) collective-permute-start(bf16[4,96,768]{2,1,0:T(8,128)(2,1)S(1)} %maximum_select_fusion.9), channel_id=1, source_target_pairs={{0,4},{1,5},{2,6},{3,7},{4,0},{5,1},{6,2},{7,3},{8,12},{9,13},{10,... | collective-permute-start | bytes 1769480 | tf_op jit(solution)/shard_map/ppermute | solution.py:728
  87.8 31.9 %collective-permute-start.15 = (bf16[8,192,768]{2,1,0:T(8,128)(2,1)}, bf16[8,192,768]{2,1,0:T(8,128)(2,1)}, u32[]{:S(2)}, u32[]{:S(2)}) collective-permute-start(bf16[8,192,768]{2,1,0:T(8,128)(2,1)} %maximum_select_fusion.1), channel_id=1, source_target_pairs={{0,2},{1,3},{2,0},{3,1},{4,6},{5,7},{6,4},{7,5},{8,10},{9,11},{10,... | collective-permute-start | bytes 7077896 | tf_op jit(solution)/shard_map/ppermute | solution.py:728
  90.1 27.6 %collective-permute-start.16 = (bf16[2,192,768]{2,1,0:T(8,128)(2,1)S(1)}, bf16[2,192,768]{2,1,0:T(8,128)(2,1)}, u32[]{:S(2)}, u32[]{:S(2)}) collective-permute-start(bf16[2,192,768]{2,1,0:T(8,128)(2,1)S(1)} %maximum_select_fusion.10), channel_id=1, source_target_pairs={{0,8},{1,9},{2,10},{3,11},{4,12},{5,13},{6,14},{7,15},{8,0},{9,1},... | collective-permute-start | bytes 1769480 | tf_op jit(solution)/shard_map/ppermute | solution.py:728
  91.6 28.1 %collective-permute-start.17 = (bf16[4,96,768]{2,1,0:T(8,128)(2,1)}, bf16[4,96,768]{2,1,0:T(8,128)(2,1)}, u32[]{:S(2)}, u32[]{:S(2)}) collective-permute-start(bf16[4,96,768]{2,1,0:T(8,128)(2,1)} %get-tuple-element.261), channel_id=1, source_target_pairs={{0,8},{1,9},{2,10},{3,11},{4,12},{5,13},{6,14},{7,15},{8,0},{9,1},... | collective-permute-start | bytes 1769480 | tf_op jit(solution)/shard_map/ppermute | solution.py:728
  123.2 23.3 %collective-permute-start.22 = (bf16[4,192,768]{2,1,0:T(8,128)(2,1)}, bf16[4,192,768]{2,1,0:T(8,128)(2,1)}, u32[]{:S(2)}, u32[]{:S(2)}) collective-permute-start(bf16[4,192,768]{2,1,0:T(8,128)(2,1)} %maximum_select_fusion.6), channel_id=1, source_target_pairs={{0,1},{1,0},{2,3},{3,2},{4,5},{5,4},{6,7},{7,6},{8,9},{9,8},{10,11... | collective-permute-start | bytes 3538952 | tf_op jit(solution)/shard_map/ppermute | solution.py:728
  149.7 29.0 %collective-permute-start.26 = (bf16[8,192,768]{2,1,0:T(8,128)(2,1)S(1)}, bf16[8,192,768]{2,1,0:T(8,128)(2,1)}, u32[]{:S(2)}, u32[]{:S(2)}) collective-permute-start(bf16[8,192,768]{2,1,0:T(8,128)(2,1)S(1)} %maximum_select_fusion.2), channel_id=1, source_target_pairs={{0,2},{1,3},{2,0},{3,1},{4,6},{5,7},{6,4},{7,5},{8,10},{9,11},{10,... | collective-permute-start | bytes 7077896 | tf_op jit(solution)/shard_map/ppermute | solution.py:728
  150.5 28.3 %collective-permute-start.25 = (bf16[8,192,768]{2,1,0:T(8,128)(2,1)S(1)}, bf16[8,192,768]{2,1,0:T(8,128)(2,1)}, u32[]{:S(2)}, u32[]{:S(2)}) collective-permute-start(bf16[8,192,768]{2,1,0:T(8,128)(2,1)S(1)} %maximum_select_fusion.2), channel_id=1, source_target_pairs={{0,16},{1,17},{2,18},{3,19},{4,20},{5,21},{6,22},{7,23},{8,24},{9,... | collective-permute-start | bytes 7077896 | tf_op jit(solution)/shard_map/ppermute | solution.py:734
  220.9 30.0 %collective-permute-start.30 = (bf16[8,192,768]{2,1,0:T(8,128)(2,1)}, bf16[8,192,768]{2,1,0:T(8,128)(2,1)S(1)}, u32[]{:S(2)}, u32[]{:S(2)}) collective-permute-start(bf16[8,192,768]{2,1,0:T(8,128)(2,1)} %get-tuple-element.328), channel_id=1, source_target_pairs={{0,16},{1,17},{2,18},{3,19},{4,20},{5,21},{6,22},{7,23},{8,24},{9,... | collective-permute-start | bytes 7077896 | tf_op jit(solution)/shard_map/ppermute | solution.py:734
  255.0 27.7 %collective-permute-start.32 = (bf16[4,192,768]{2,1,0:T(8,128)(2,1)S(1)}, bf16[4,192,768]{2,1,0:T(8,128)(2,1)}, u32[]{:S(2)}, u32[]{:S(2)}) collective-permute-start(bf16[4,192,768]{2,1,0:T(8,128)(2,1)S(1)} %get-tuple-element.341), channel_id=1, source_target_pairs={{0,2},{1,3},{2,0},{3,1},{4,6},{5,7},{6,4},{7,5},{8,10},{9,11},{10,... | collective-permute-start | bytes 3538952 | tf_op jit(solution)/shard_map/ppermute | solution.py:728
  256.5 26.1 %collective-permute-start.35 = (bf16[8,96,768]{2,1,0:T(8,128)(2,1)}, bf16[8,96,768]{2,1,0:T(8,128)(2,1)}, u32[]{:S(2)}, u32[]{:S(2)}) collective-permute-start(bf16[8,96,768]{2,1,0:T(8,128)(2,1)} %get-tuple-element.349), channel_id=1, source_target_pairs={{0,16},{1,17},{2,18},{3,19},{4,20},{5,21},{6,22},{7,23},{8,24},{9,... | collective-permute-start | bytes 3538952 | tf_op jit(solution)/shard_map/ppermute | solution.py:734
  256.7 26.6 %collective-permute-start.33 = (bf16[4,192,768]{2,1,0:T(8,128)(2,1)}, bf16[4,192,768]{2,1,0:T(8,128)(2,1)}, u32[]{:S(2)}, u32[]{:S(2)}) collective-permute-start(bf16[4,192,768]{2,1,0:T(8,128)(2,1)} %add_convert_fusion.3), channel_id=1, source_target_pairs={{0,1},{1,0},{2,3},{3,2},{4,5},{5,4},{6,7},{7,6},{8,9},{9,8},{10,11... | collective-permute-start | bytes 3538952 | tf_op jit(solution)/shard_map/ppermute | solution.py:728
  258.3 25.0 %collective-permute-start.34 = (bf16[4,96,768]{2,1,0:T(8,128)(2,1)S(1)}, bf16[4,96,768]{2,1,0:T(8,128)(2,1)}, u32[]{:S(2)}, u32[]{:S(2)}) collective-permute-start(bf16[4,96,768]{2,1,0:T(8,128)(2,1)S(1)} %get-tuple-element.347), channel_id=1, source_target_pairs={{0,8},{1,9},{2,10},{3,11},{4,12},{5,13},{6,14},{7,15},{8,0},{9,1},... | collective-permute-start | bytes 1769480 | tf_op jit(solution)/shard_map/ppermute | solution.py:728
  283.7 47.1 %collective-permute-start.40 = (bf16[8,192,768]{2,1,0:T(8,128)(2,1)}, bf16[8,192,768]{2,1,0:T(8,128)(2,1)}, u32[]{:S(2)}, u32[]{:S(2)}) collective-permute-start(bf16[8,192,768]{2,1,0:T(8,128)(2,1)} %get-tuple-element.383), channel_id=1, source_target_pairs={{0,16},{1,17},{2,18},{3,19},{4,20},{5,21},{6,22},{7,23},{8,24},{9,... | collective-permute-start | bytes 7077896 | tf_op jit(solution)/shard_map/ppermute | solution.py:734
  294.4 36.4 %collective-permute-start.39 = (bf16[8,192,768]{2,1,0:T(8,128)(2,1)}, bf16[8,192,768]{2,1,0:T(8,128)(2,1)}, u32[]{:S(2)}, u32[]{:S(2)}) collective-permute-start(bf16[8,192,768]{2,1,0:T(8,128)(2,1)} %add_convert_fusion), channel_id=1, source_target_pairs={{0,2},{1,3},{2,0},{3,1},{4,6},{5,7},{6,4},{7,5},{8,10},{9,11},{10,... | collective-permute-start | bytes 7077896 | tf_op jit(solution)/shard_map/ppermute | solution.py:728
  296.3 34.5 %collective-permute-start.41 = (f32[1,512,768]{2,1,0:T(8,128)S(1)}, f32[1,512,768]{2,1,0:T(8,128)S(1)}, u32[]{:S(2)}, u32[]{:S(2)}) collective-permute-start(f32[1,512,768]{2,1,0:T(8,128)S(1)} %bitcast.97), channel_id=1, source_target_pairs={{0,16},{1,17},{2,18},{3,19},{4,20},{5,21},{6,22},{7,23},{8,24},{9,... | collective-permute-start | bytes 4718600 | tf_op jit(solution)/shard_map/ppermute | solution.py:739
  300.6 27.1 %collective-permute-start.38 = (bf16[2,192,768]{2,1,0:T(8,128)(2,1)}, bf16[2,192,768]{2,1,0:T(8,128)(2,1)}, u32[]{:S(2)}, u32[]{:S(2)}) collective-permute-start(bf16[2,192,768]{2,1,0:T(8,128)(2,1)} %add_convert_fusion.9), channel_id=1, source_target_pairs={{0,8},{1,9},{2,10},{3,11},{4,12},{5,13},{6,14},{7,15},{8,0},{9,1},... | collective-permute-start | bytes 1769480 | tf_op jit(solution)/shard_map/ppermute | solution.py:728
  303.6 27.2 %collective-permute-start.37 = (bf16[4,96,768]{2,1,0:T(8,128)(2,1)}, bf16[4,96,768]{2,1,0:T(8,128)(2,1)}, u32[]{:S(2)}, u32[]{:S(2)}) collective-permute-start(bf16[4,96,768]{2,1,0:T(8,128)(2,1)} %get-tuple-element.375), channel_id=1, source_target_pairs={{0,8},{1,9},{2,10},{3,11},{4,12},{5,13},{6,14},{7,15},{8,0},{9,1},... | collective-permute-start | bytes 1769480 | tf_op jit(solution)/shard_map/ppermute | solution.py:728
  330.9 37.2 %collective-permute-start.42 = (bf16[8,112,768]{2,1,0:T(8,128)(2,1)}, bf16[8,112,768]{2,1,0:T(8,128)(2,1)S(1)}, u32[]{:S(2)}, u32[]{:S(2)}) collective-permute-start(bf16[8,112,768]{2,1,0:T(8,128)(2,1)} %get-tuple-element.386), channel_id=1, source_target_pairs={{0,16},{1,17},{2,18},{3,19},{4,20},{5,21},{6,22},{7,23},{8,24},{9,... | collective-permute-start | bytes 4128776 | tf_op jit(solution)/shard_map/ppermute | solution.py:734
  335.9 30.6 %collective-permute-start.44 = (bf16[8,112,768]{2,1,0:T(8,128)(2,1)S(1)}, bf16[8,112,768]{2,1,0:T(8,128)(2,1)S(1)}, u32[]{:S(2)}, u32[]{:S(2)}) collective-permute-start(bf16[8,112,768]{2,1,0:T(8,128)(2,1)S(1)} %add_convert_fusion.1), channel_id=1, source_target_pairs={{0,2},{1,3},{2,0},{3,1},{4,6},{5,7},{6,4},{7,5},{8,10},{9,11},{10,... | collective-permute-start | bytes 4128776 | tf_op jit(solution)/shard_map/ppermute | solution.py:728
  340.1 26.4 %collective-permute-start.48 = (bf16[4,192,768]{2,1,0:T(8,128)(2,1)S(1)}, bf16[4,192,768]{2,1,0:T(8,128)(2,1)S(1)}, u32[]{:S(2)}, u32[]{:S(2)}) collective-permute-start(bf16[4,192,768]{2,1,0:T(8,128)(2,1)S(1)} %add_convert_fusion.2), channel_id=1, source_target_pairs={{0,1},{1,0},{2,3},{3,2},{4,5},{5,4},{6,7},{7,6},{8,9},{9,8},{10,11... | collective-permute-start | bytes 3538952 | tf_op jit(solution)/shard_map/ppermute | solution.py:728
  366.5 23.8 %collective-permute-start.53 = (f32[1,512,768]{2,1,0:T(8,128)S(1)}, f32[1,512,768]{2,1,0:T(8,128)S(1)}, u32[]{:S(2)}, u32[]{:S(2)}) collective-permute-start(f32[1,512,768]{2,1,0:T(8,128)S(1)} %bitcast.108), channel_id=1, source_target_pairs={{16,0},{17,1},{18,2},{19,3},{20,4},{21,5},{22,6},{23,7},{24,8},{25... | collective-permute-start | bytes 4718600 | tf_op jit(solution)/shard_map/ppermute | solution.py:739
  (59 other events, 646.1 us)
